TPU v7x, 256 devices: a whole 4x4x8 slice. The times are simulated.
256 devices in a mesh: row: 16 (over x, z_hi), col: 16 (over y, z_lo, core).
Axes of the slice: x: 4, y: 4, z: 8 (z_hi: 4, z_lo: 2; z = z_hi * 2 + z_lo), core: 2. Of those that a mesh axis runs over, the one named last changes fastest.
Arguments:
- amplitudes: bfloat16 [1280, 32768], P('row', 'col'), may hold values from -6 to 6
- integrals: bfloat16 [32768, 16384], P('col', 'row'), may hold values from -0.046875 to 0.046875
Outputs:
- ladder: bfloat16 [16384, 1280], P(('row', 'col'))
All inputs are finite; a program needn't handle non-finite values.
Results may differ from a plain program's by a relative error of at most 0.001.
Values may be sent and summed in bfloat16 or wider, within the bound.
No kernel may reach another device: no remote copies, remote signals or barrier semaphores. Data moves between devices by JAX's collectives and lax.ppermute only.
A program may use at most 64 MiB of HBM per device.

v0:
```python
import jax
import jax.numpy as jnp
from jax import lax
from jax.sharding import PartitionSpec as P


def local(amplitudes, integrals):
    partial_value = jnp.dot(
        lax.all_gather(amplitudes, "row", axis=0, tiled=True),
        integrals,
        preferred_element_type=jnp.float32,
    )
    summed = lax.psum_scatter(partial_value, "col", scatter_dimension=0, tiled=True)
    turned = summed.astype(jnp.bfloat16).T
    return lax.all_to_all(turned, "col", split_axis=0, concat_axis=1, tiled=True)


def solution(mesh):
    placed = (P("row", "col"), P("col", "row"))
    return jax.shard_map(
        local, mesh=mesh, in_specs=placed, out_specs=P(("row", "col"), None), check_vma=False
    )
```

profile of v0, /device:TPU:64, one launch (start us, length us, event | category | flops | bytes accessed | tf_op | source)
XLA Modules:
  0.0 204.0 jit_solution(17190738923694836563)
XLA Ops:
  6.5 0.0 all-gather.2.cloned.1.call-start
  6.5 0.7 all-gather.2.cloned.1.call-update
  7.3 0.0 reduce-scatter.2.cloned.1.call-start
  7.3 92.4 %all-gather.2.cloned.1.call-done = bf16[1280,2048]{1,0:T(8,128)(2,1)} async-done(((bf16[80,2048]{1,0:T(8,128)(2,1)}), bf16[1280,2048]{1,0:T(8,128)(2,1)}) %all-gather.2.cloned.1.call-update) | async-done | bytes 5242896 | tf_op jit(solution)/shard_map/all_gather | solution.py:9
  99.7 10.2 %fusion = f32[1280,1024]{1,0:T(8,128)} fusion(bf16[1280,2048]{1,0:T(8,128)(2,1)} %all-gather.2.cloned.1.call-done, bf16[2048,1024]{1,0:T(8,128)(2,1)} %param.3), kind=kOutput, calls=%fused_computation.1 | convolution fusion | flops 5368709120 | bytes 14680064 | tf_op jit(solution)/shard_map/dot_general | solution.py:8
  110.0 0.0 reduce-scatter.2.cloned.1.call-update
  110.0 73.8 %reduce-scatter.2.cloned.1.call-done = f32[80,1024]{1,0:T(8,128)} async-done(((f32[1280,1024]{1,0:T(8,128)}), f32[80,1024]{1,0:T(8,128)}) %reduce-scatter.2.cloned.1.call-update) | async-done | bytes 327696 | tf_op jit(solution)/shard_map/reduce_scatter | solution.py:13
  183.8 1.0 convert_bitcast_fusion
  184.8 0.2 copy.7
  184.9 11.1 %all_to_all.19 = bf16[16,64,80]{2,1,0:T(8,128)(2,1)S(1)} all-to-all(bf16[16,64,80]{2,1,0:T(8,128)(2,1)S(1)} %bitcast.7), channel_id=1, replica_groups=mesh['row'=16,'col'=16] {'col'}, dimensions={0} | all-to-all | bytes 327680 | tf_op jit(solution)/shard_map/all_to_all | solution.py:15
  196.1 0.2 copy.6
  196.2 0.9 all_to_all.17
Async XLA Ops:
  6.5 93.2 %all-gather.2.cloned.1.call-start = ((), (), s32[]{:S(2)}) async-start(), calls=%async_computation.2 | async-start | bytes 5570560 | tf_op jit(solution)/shard_map/all_gather | solution.py:9
  7.3 176.5 %reduce-scatter.2.cloned.1.call-start = ((), (), s32[]{:S(2)}) async-start(), calls=%async_computation.3 | async-start | bytes 5570560 | tf_op jit(solution)/shard_map/reduce_scatter | solution.py:13
Sparse Core Ops, SparseCore 0:
  9.8 89.8 all-gather.1
  110.1 73.6 reduce-scatter.1
where the time goes:
time: 206 us; the launch traced here: 204 us
  waiting for transfers between devices  167 us (81%)
  between operations  13.4 us (7%)
  blocking collectives  11.1 us (5%)
  matrix products  10.2 us (5%)
    all_gather x1, waiting for transfers between devices, local(): lax.all_gather(amplitudes, 'row', axis=0, tiled=True)  92.4 us
    reduce_scatter x1, waiting for transfers between devices, local(): lax.psum_scatter(partial_value, 'col', scatter_dimension=0, tiled=True)  73.8 us
    all_to_all x1, blocking collectives, local(): lax.all_to_all(turned, 'col', split_axis=0, concat_axis=1, tiled=True)  11.1 us
    dot_general x1, matrix products, local(): jnp.dot(lax.all_gather(amplitudes, 'row', axis=0, tiled=True), integrals,...  10.2 us
  transfers between devices with their start and end apart: 2, of which 2 were waited for; matrix products, arithmetic and copies ran while one was open for 0% of the time, Pallas kernels for 0%

commit v1 on v0

v1 whole, which is shorter than its diff:
```python
import jax
import jax.numpy as jnp
from jax import lax
from jax.sharding import PartitionSpec as P


def local(amplitudes, integrals):
    gathered = lax.all_gather(amplitudes, "row", axis=0, tiled=True)
    partial_value = lax.dot_general(
        integrals, gathered, (((0,), (1,)), ((), ())), preferred_element_type=jnp.float32
    )
    summed = lax.psum_scatter(partial_value, "col", scatter_dimension=0, tiled=True)
    return summed.astype(jnp.bfloat16)


def solution(mesh):
    placed = (P("row", "col"), P("col", "row"))
    return jax.shard_map(
        local, mesh=mesh, in_specs=placed, out_specs=P(("row", "col"), None), check_vma=False
    )
```

time: 206 us -> 194 us (0.942)
  blocking collectives: 11.1 us -> 0 us
    all_to_all x1 -> x0, blocking collectives: 11.1 us -> none  [local(): lax.all_to_all(turned, 'col', split_axis=0, concat_axis=1, tiled=True)]
where the time goes in v1:
time: 194 us; the launch traced here: 193 us
  waiting for transfers between devices  167 us (86%)
  between operations  13.4 us (7%)
  matrix products  10.5 us (5%)
    all_gather x1, waiting for transfers between devices, local(): gathered = lax.all_gather(amplitudes, 'row', axis=0, tiled=True)  92.4 us
    reduce_scatter x1, waiting for transfers between devices, local(): lax.psum_scatter(partial_value, 'col', scatter_dimension=0, tiled=True)  74.3 us
    dot_general x1, matrix products, local(): lax.dot_general(integrals, gathered, (((0,), (1,)), ((), ())), preferred_...  10.5 us
  transfers between devices with their start and end apart: 2, of which 2 were waited for; matrix products, arithmetic and copies ran while one was open for 0% of the time, Pallas kernels for 0%

profile of v1, /device:TPU:64, one launch (start us, length us, event | category | flops | bytes accessed | tf_op | source)
XLA Modules:
  0.0 193.1 jit_solution(12885800077939433936)
XLA Ops:
  6.5 0.0 all-gather.2.cloned.1.call-start
  6.5 0.7 all-gather.2.cloned.1.call-update
  7.3 0.0 reduce-scatter.2.cloned.1.call-start
  7.3 92.4 %all-gather.2.cloned.1.call-done = bf16[1280,2048]{1,0:T(8,128)(2,1)} async-done(((bf16[80,2048]{1,0:T(8,128)(2,1)}), bf16[1280,2048]{1,0:T(8,128)(2,1)}) %all-gather.2.cloned.1.call-update) | async-done | bytes 5242896 | tf_op jit(solution)/shard_map/all_gather | solution.py:8
  99.7 10.5 %fusion = f32[1024,1280]{1,0:T(8,128)} fusion(bf16[2048,1024]{1,0:T(8,128)(2,1)} %param.3, bf16[1280,2048]{1,0:T(8,128)(2,1)} %all-gather.2.cloned.1.call-done), kind=kOutput, calls=%fused_computation | convolution fusion | flops 5368709120 | bytes 14680064 | tf_op jit(solution)/shard_map/dot_general | solution.py:9
  110.2 0.0 reduce-scatter.2.cloned.1.call-update
  110.2 74.3 %reduce-scatter.2.cloned.1.call-done = f32[64,1280]{1,0:T(8,128)} async-done(((f32[1024,1280]{1,0:T(8,128)}), f32[64,1280]{1,0:T(8,128)}) %reduce-scatter.2.cloned.1.call-update) | async-done | bytes 327696 | tf_op jit(solution)/shard_map/reduce_scatter | solution.py:12
  184.6 1.7 convert_element_type.3
Async XLA Ops:
  6.5 93.2 %all-gather.2.cloned.1.call-start = ((), (), s32[]{:S(2)}) async-start(), calls=%async_computation.1 | async-start | bytes 5570560 | tf_op jit(solution)/shard_map/all_gather | solution.py:8
  7.3 177.3 %reduce-scatter.2.cloned.1.call-start = ((), (), s32[]{:S(2)}) async-start(), calls=%async_computation.2 | async-start | bytes 5570560 | tf_op jit(solution)/shard_map/reduce_scatter | solution.py:12
Sparse Core Ops, SparseCore 0:
  9.8 89.8 all-gather.1
  110.4 74.1 reduce-scatter.1

commit v2 on v1

v2 whole, which is shorter than its diff:
```python
import jax
import jax.numpy as jnp
from jax import lax
from jax.sharding import Mesh, PartitionSpec as P

ROWS = 80
F32 = jnp.float32
BF16 = jnp.bfloat16


def shift(value, axis, size, by):
    return lax.ppermute(value, axis, [(i, (i + by) % size) for i in range(size)])


def near(block, axis):
    return shift(block, axis, 4, 1), shift(block, axis, 4, -1)


def opposite(before, after, axis):
    half = before.shape[0] // 2
    return shift(after[:half], axis, 4, -1), shift(before[half:], axis, 4, 1)


def local(amplitudes, integrals):
    x, zh, zl, core = (lax.axis_index(n) for n in ("x", "zh", "zl", "core"))

    out_col = lax.broadcasted_iota(jnp.int32, (1024, 1024), 1)
    in_col = lax.broadcasted_iota(jnp.int32, (1024, 1024), 0)
    owner = jnp.where(out_col < 512, 1 - core, core)
    inside = out_col % 512
    source = (inside // 64) * 128 + owner * 64 + inside % 64
    order = (in_col == source).astype(BF16)
    columns = jnp.dot(integrals, order, preferred_element_type=F32).astype(BF16)
    theirs, mine = columns[:, :512], columns[:, 512:]

    def reduced(rows):
        away = jnp.dot(rows, theirs, preferred_element_type=F32)
        kept = jnp.dot(rows, mine, preferred_element_type=F32)
        pair = kept + lax.ppermute(away, "core", [(0, 1), (1, 0)])
        split = pair.reshape(rows.shape[0], 4, 128).transpose(1, 0, 2)
        spread = lax.all_to_all(split, "y", split_axis=0, concat_axis=0, tiled=True)
        over_y = jnp.sum(spread, axis=0)
        total = over_y + lax.ppermute(over_y, "zl", [(0, 1), (1, 0)])
        return total.astype(BF16)

    def block(dx, dz, first=0, count=ROWS):
        start = (((x + dx) % 4) * 4 + (zh + dz) % 4) * ROWS + first
        return start + jnp.arange(count)

    own = amplitudes
    zm, zp = near(own, "zh")
    own_xm, own_xp = near(own, "x")
    own_far = opposite(own_xm, own_xp, "x")
    far = jnp.concatenate(opposite(zm, zp, "zh"), axis=0)
    side = jnp.concatenate([zm, zp], axis=0)
    side_xm, side_xp = near(side, "x")
    far_xm, far_xp = near(far, "x")
    side_far = opposite(side_xm, side_xp, "x")
    far_far = opposite(far_xm, far_xp, "x")

    def pair_at(dx):
        return [block(dx, -1), block(dx, 1)]

    groups = [
        ([own, own_xm, own_xp], [block(0, 0), block(-1, 0), block(1, 0)]),
        ([side, *own_far], [*pair_at(0), block(2, 0, 0, 40), block(2, 0, 40, 40)]),
        ([side_xm, side_xp, far], [*pair_at(-1), *pair_at(1), block(0, 2)]),
        ([far_xm, far_xp, *side_far], [block(-1, 2), block(1, 2), *pair_at(2)]),
        ([*far_far], [block(2, 2, 0, 40), block(2, 2, 40, 40)]),
    ]
    sums = [reduced(jnp.concatenate(parts, axis=0)) for parts, _ in groups]
    places = jnp.concatenate([p for _, ps in groups for p in ps])
    total = jnp.concatenate(sums, axis=0)
    place = (places[:, None] == jnp.arange(1280)[None, :]).astype(BF16)
    turned = lax.dot_general(total, place, (((0,), (0,)), ((), ())), preferred_element_type=F32)
    return lax.dynamic_slice_in_dim(turned, zl * 64, 64, axis=0).astype(BF16)


def solution(mesh):
    split = Mesh(mesh.devices.reshape(4, 4, 4, 2, 2), ("x", "zh", "y", "zl", "core"))
    row, col = ("x", "zh"), ("y", "zl", "core")
    return jax.shard_map(
        local,
        mesh=split,
        in_specs=(P(row, col), P(col, row)),
        out_specs=P(row + col, None),
        check_vma=False,
    )
```

time: 194 us -> 144 us (0.74)
  waiting for transfers between devices: 167 us -> 60.7 us
  starting transfers between devices: 0.04 us -> 49.5 us
  matrix products: 10.5 us -> 26.6 us
  between operations: 13.4 us -> 0.78 us
  local copies, waits for them, and re-layouts: 0 us -> 5.53 us
    all_gather x1 -> x0, waiting for transfers between devices: 92.4 us -> none  [local(): gathered = lax.all_gather(amplitudes, 'row', axis=0, tiled=True)]
    reduce_scatter x1 -> x0, waiting for transfers between devices: 74.3 us -> none  [local(): lax.psum_scatter(partial_value, 'col', scatter_dimension=0, tiled=True)]
    ppermute x0 -> x26, waiting for transfers between devices: none -> 43.3 us  [the longest x16 34.9 us: shift(): lax.ppermute(value, axis, [(i, (i + by) % size) for i in range(size)])]
    ppermute x0 -> x26, starting transfers between devices: none -> 29.7 us  [the longest x16 26.6 us: shift(): lax.ppermute(value, axis, [(i, (i + by) % size) for i in range(size)])]
    all_to_all x0 -> x5, starting transfers between devices: none -> 19.8 us  [reduced(): spread = lax.all_to_all(split, 'y', split_axis=0, concat_axis=0, tiled=True)]
    all_to_all x0 -> x5, waiting for transfers between devices: none -> 17.4 us  [reduced(): spread = lax.all_to_all(split, 'y', split_axis=0, concat_axis=0, tiled=True)]
    dot_general x1 -> x12, matrix products: 10.5 us -> 26.6 us  [the longest x5 9.35 us: reduced(): kept = jnp.dot(rows, mine, preferred_element_type=F32)]
    reshape x0 -> x5, local copies, waits for them, and re-layouts: none -> 4.15 us  [reduced(): split = pair.reshape(rows.shape[0], 4, 128).transpose(1, 0, 2)]
  transfers between devices with their start and end apart: 2 -> 31, of which waited for: 2 -> 13; matrix products, arithmetic and copies ran while one was open for 0% -> 21% of each run, Pallas kernels for 0% -> 0%
where the time goes in v2:
time: 144 us; the launch traced here: 143 us
  waiting for transfers between devices  60.7 us (42%)
  starting transfers between devices  49.5 us (34%)
  matrix products  26.6 us (18%)
  local copies, waits for them, and re-layouts  5.53 us (4%)
    ppermute x16, waiting for transfers between devices, shift(): lax.ppermute(value, axis, [(i, (i + by) % size) for i in range(size)])  34.9 us
    ppermute x16, starting transfers between devices, shift(): lax.ppermute(value, axis, [(i, (i + by) % size) for i in range(size)])  26.6 us
    all_to_all x5, starting transfers between devices, reduced(): spread = lax.all_to_all(split, 'y', split_axis=0, concat_axis=0, tiled=True)  19.8 us
    all_to_all x5, waiting for transfers between devices, reduced(): spread = lax.all_to_all(split, 'y', split_axis=0, concat_axis=0, tiled=True)  17.4 us
    dot_general x5, matrix products, reduced(): kept = jnp.dot(rows, mine, preferred_element_type=F32)  9.35 us
    dot_general x5, matrix products, reduced(): away = jnp.dot(rows, theirs, preferred_element_type=F32)  8.59 us
    ppermute x5, waiting for transfers between devices, reduced(): total = over_y + lax.ppermute(over_y, 'zl', [(0, 1), (1, 0)])  8.3 us
    dot_general x1, matrix products, local(): columns = jnp.dot(integrals, order, preferred_element_type=F32).astype(BF16)  7.1 us
  transfers between devices with their start and end apart: 31, of which 13 were waited for; matrix products, arithmetic and copies ran while one was open for 21% of the time, Pallas kernels for 0%

profile of v2, /device:TPU:64, one launch (start us, length us, event | category | flops | bytes accessed | tf_op | source)
XLA Modules:
  0.0 143.4 jit_solution(9079288194015083039)
XLA Ops:
  0.0 1.5 %collective-permute-start = (bf16[80,2048]{1,0:T(8,128)(2,1)}, bf16[80,2048]{1,0:T(8,128)(2,1)S(1)}, u32[]{:S(2)}, u32[]{:S(2)}) collective-permute-start(bf16[80,2048]{1,0:T(8,128)(2,1)} %param.2), channel_id=1, source_target_pairs={{0,64},{64,128},{128,192},{192,0},{1,65},{65,129},{129,193},{193,1... | collective-permute-start | bytes 983048 | tf_op jit(solution)/shard_map/ppermute | solution.py:12
  1.5 1.7 %collective-permute-start.1 = (bf16[80,2048]{1,0:T(8,128)(2,1)}, bf16[80,2048]{1,0:T(8,128)(2,1)S(1)}, u32[]{:S(2)}, u32[]{:S(2)}) collective-permute-start(bf16[80,2048]{1,0:T(8,128)(2,1)} %param.2), channel_id=1, source_target_pairs={{0,192},{64,0},{128,64},{192,128},{1,193},{65,1},{129,65},{193,129... | collective-permute-start | bytes 983048 | tf_op jit(solution)/shard_map/ppermute | solution.py:12
  3.2 4.5 %collective-permute-start.4 = (bf16[80,2048]{1,0:T(8,128)(2,1)}, bf16[80,2048]{1,0:T(8,128)(2,1)S(1)}, u32[]{:S(2)}, u32[]{:S(2)}) collective-permute-start(bf16[80,2048]{1,0:T(8,128)(2,1)} %param.2), channel_id=1, source_target_pairs={{0,16},{16,32},{32,48},{48,0},{1,17},{17,33},{33,49},{49,1},{2,18}... | collective-permute-start | bytes 983048 | tf_op jit(solution)/shard_map/ppermute | solution.py:12
  8.0 7.1 %convert_bitcast_fusion = bf16[2048,1024]{0,1:T(8,128)(2,1)S(1)} fusion(bf16[2048,1024]{1,0:T(8,128)(2,1)} %param.3, s32[1024]{0:T(1024)S(1)} %get-tuple-element.13, s32[1024]{0:T(1024)S(1)} %get-tuple-element.14, s32[1024]{0:T(1024)S(1)} %fusion.47, pred[1024]{0:T(1024)(128)(4,1)S(1)} %fusion.50), kind=kOutput, calls=%fused_computation.17 | convolution fusion | flops 4323278848 | bytes 8401920 | tf_op jit(solution)/shard_map/dot_general | solution.py:33
  15.1 6.2 %collective-permute-done.4 = bf16[80,2048]{1,0:T(8,128)(2,1)S(1)} collective-permute-done((bf16[80,2048]{1,0:T(8,128)(2,1)}, bf16[80,2048]{1,0:T(8,128)(2,1)S(1)}, u32[]{:S(2)}, u32[]{:S(2)}) %collective-permute-start.4) | collective-permute-done | bytes 327712 | tf_op jit(solution)/shard_map/ppermute | solution.py:12
  21.4 4.2 %collective-permute-done.5 = bf16[80,2048]{1,0:T(8,128)(2,1)S(1)} collective-permute-done((bf16[80,2048]{1,0:T(8,128)(2,1)}, bf16[80,2048]{1,0:T(8,128)(2,1)S(1)}, u32[]{:S(2)}, u32[]{:S(2)}) %collective-permute-start.5) | collective-permute-done | bytes 327712 | tf_op jit(solution)/shard_map/ppermute | solution.py:12
  26.0 3.0 %collective-permute-start.11 = (bf16[160,2048]{1,0:T(8,128)(2,1)S(1)}, bf16[160,2048]{1,0:T(8,128)(2,1)S(1)}, u32[]{:S(2)}, u32[]{:S(2)}) collective-permute-start(bf16[160,2048]{1,0:T(8,128)(2,1)S(1)} %get-tuple-element.5), channel_id=1, source_target_pairs={{0,192},{64,0},{128,64},{192,128},{1,193},{65,1},{129,65},{193,129... | collective-permute-start | bytes 1966088 | tf_op jit(solution)/shard_map/ppermute | solution.py:12
  29.0 0.4 collective-permute-start.6
  29.4 0.7 fusion.36
  30.3 1.8 %collective-permute-start.7 = (bf16[40,2048]{1,0:T(8,128)(2,1)S(1)}, bf16[40,2048]{1,0:T(8,128)(2,1)S(1)}, u32[]{:S(2)}, u32[]{:S(2)}) collective-permute-start(bf16[40,2048]{1,0:T(8,128)(2,1)S(1)} %slice.43), channel_id=1, source_target_pairs={{0,64},{64,128},{128,192},{192,0},{1,65},{65,129},{129,193},{193,1... | collective-permute-start | bytes 491528 | tf_op jit(solution)/shard_map/ppermute | solution.py:12
  32.1 13.2 %collective-permute-done.6 = bf16[40,2048]{1,0:T(8,128)(2,1)S(1)} collective-permute-done((bf16[40,2048]{1,0:T(8,128)(2,1)S(1)}, bf16[40,2048]{1,0:T(8,128)(2,1)S(1)}, u32[]{:S(2)}, u32[]{:S(2)}) %collective-permute-start.6) | collective-permute-done | bytes 163872 | tf_op jit(solution)/shard_map/ppermute | solution.py:12
  45.4 0.7 collective-permute-done.7
  46.1 3.7 %collective-permute-start.13 = (bf16[40,2048]{1,0:T(8,128)(2,1)S(1)}, bf16[40,2048]{1,0:T(8,128)(2,1)S(1)}, u32[]{:S(2)}, u32[]{:S(2)}) collective-permute-start(bf16[40,2048]{1,0:T(8,128)(2,1)S(1)} %slice.45), channel_id=1, source_target_pairs={{0,16},{16,32},{32,48},{48,0},{1,17},{17,33},{33,49},{49,1},{2,18}... | collective-permute-start | bytes 491528 | tf_op jit(solution)/shard_map/ppermute | solution.py:12
  49.8 1.6 %fusion.34 = f32[240,512]{1,0:T(8,128)} fusion(bf16[240,2048]{1,0:T(8,128)(2,1)S(1)} %constant_dynamic-update-slice_fusion.3, bf16[2048,1024]{0,1:T(8,128)(2,1)S(1)} %convert_bitcast_fusion), kind=kOutput, calls=%fused_computation.48 | convolution fusion | flops 503316480 | bytes 3571712 | tf_op jit(solution)/shard_map/dot_general | solution.py:37
  51.4 0.7 fusion.26
  52.2 0.8 copy.21
  53.0 4.5 %all-to-all-start = ((f32[4,240,128]{2,1,0:T(8,128)}), f32[4,240,128]{2,1,0:T(8,128)S(1)}, u32[]{:S(2)}, u32[]{:S(2)}) async-start(f32[4,240,128]{2,1,0:T(8,128)} %bitcast.51), calls=%async_computation | async-start | bytes 983040 | tf_op jit(solution)/shard_map/all_to_all | solution.py:41
  57.7 1.1 collective-permute-start.16
  58.8 2.8 %collective-permute-start.17 = (bf16[80,2048]{1,0:T(8,128)(2,1)S(1)}, bf16[80,2048]{1,0:T(8,128)(2,1)S(1)}, u32[]{:S(2)}, u32[]{:S(2)}) collective-permute-start(bf16[80,2048]{1,0:T(8,128)(2,1)S(1)} %get-tuple-element.9), channel_id=1, source_target_pairs={{0,192},{64,0},{128,64},{192,128},{1,193},{65,1},{129,65},{193,129... | collective-permute-start | bytes 983048 | tf_op jit(solution)/shard_map/ppermute | solution.py:12
  61.5 2.4 %fusion.25 = f32[30,4,8,128]{3,2,1,0:T(8,128)S(1)} fusion(f32[240,512]{1,0:T(8,128)} %collective-permute-done.8, bf16[240,2048]{1,0:T(8,128)(2,1)S(1)} %copy-done.4, bf16[2048,1024]{0,1:T(8,128)(2,1)} %copy-done.7), kind=kOutput, calls=%fused_computation.37 | convolution fusion | flops 503439360 | bytes 4063232 | tf_op jit(solution)/shard_map/dot_general | solution.py:38
  63.9 0.8 copy.20
  64.8 2.0 %fusion.32 = f32[400,512]{1,0:T(8,128)} fusion(bf16[400,2048]{1,0:T(8,128)(2,1)S(1)} %get-tuple-element.10, bf16[2048,1024]{0,1:T(8,128)(2,1)S(1)} %copy-done.8), kind=kOutput, calls=%fused_computation.46 | convolution fusion | flops 838860800 | bytes 4554752 | tf_op jit(solution)/shard_map/dot_general | solution.py:37
  66.8 2.0 %collective-permute-start.18 = (bf16[80,2048]{1,0:T(8,128)(2,1)S(1)}, bf16[80,2048]{1,0:T(8,128)(2,1)S(1)}, u32[]{:S(2)}, u32[]{:S(2)}) collective-permute-start(bf16[80,2048]{1,0:T(8,128)(2,1)S(1)} %slice.46), channel_id=1, source_target_pairs={{0,192},{64,0},{128,64},{192,128},{1,193},{65,1},{129,65},{193,129... | collective-permute-start | bytes 983048 | tf_op jit(solution)/shard_map/ppermute | solution.py:12
  69.0 3.6 %collective-permute-start.22 = (bf16[40,2048]{1,0:T(8,128)(2,1)S(1)}, bf16[40,2048]{1,0:T(8,128)(2,1)S(1)}, u32[]{:S(2)}, u32[]{:S(2)}) collective-permute-start(bf16[40,2048]{1,0:T(8,128)(2,1)S(1)} %slice.48), channel_id=1, source_target_pairs={{0,192},{64,0},{128,64},{192,128},{1,193},{65,1},{129,65},{193,129... | collective-permute-start | bytes 491528 | tf_op jit(solution)/shard_map/ppermute | solution.py:12
  72.8 4.6 %collective-permute-done.18 = bf16[80,2048]{1,0:T(8,128)(2,1)S(1)} collective-permute-done((bf16[80,2048]{1,0:T(8,128)(2,1)S(1)}, bf16[80,2048]{1,0:T(8,128)(2,1)S(1)}, u32[]{:S(2)}, u32[]{:S(2)}) %collective-permute-start.18) | collective-permute-done | bytes 327712 | tf_op jit(solution)/shard_map/ppermute | solution.py:12
  77.4 3.3 %collective-permute-done.19 = bf16[80,2048]{1,0:T(8,128)(2,1)S(1)} collective-permute-done((bf16[80,2048]{1,0:T(8,128)(2,1)S(1)}, bf16[80,2048]{1,0:T(8,128)(2,1)S(1)}, u32[]{:S(2)}, u32[]{:S(2)}) %collective-permute-start.19) | collective-permute-done | bytes 327712 | tf_op jit(solution)/shard_map/ppermute | solution.py:12
  80.7 2.7 %collective-permute-done.23 = bf16[40,2048]{1,0:T(8,128)(2,1)S(1)} collective-permute-done((bf16[40,2048]{1,0:T(8,128)(2,1)S(1)}, bf16[40,2048]{1,0:T(8,128)(2,1)S(1)}, u32[]{:S(2)}, u32[]{:S(2)}) %collective-permute-start.23) | collective-permute-done | bytes 163872 | tf_op jit(solution)/shard_map/ppermute | solution.py:12
  83.5 0.8 fusion.28
  84.4 4.8 %all-to-all-start.1 = ((f32[4,240,128]{2,1,0:T(8,128)}), f32[4,240,128]{2,1,0:T(8,128)S(1)}, u32[]{:S(2)}, u32[]{:S(2)}) async-start(f32[4,240,128]{2,1,0:T(8,128)} %bitcast.49), calls=%async_computation.1 | async-start | bytes 983040 | tf_op jit(solution)/shard_map/all_to_all | solution.py:41
  89.2 3.5 %fusion.30 = f32[320,512]{1,0:T(8,128)} fusion(bf16[320,2048]{1,0:T(8,128)(2,1)S(1)} %constant_dynamic-update-slice_fusion.15, bf16[2048,1024]{0,1:T(8,128)(2,1)} %copy-done.7), kind=kOutput, calls=%fused_computation.44 | convolution fusion | flops 671088640 | bytes 4063232 | tf_op jit(solution)/shard_map/dot_general | solution.py:37
  92.9 0.8 fusion.27
  93.7 0.7 copy.22
  94.3 4.6 %all-to-all-done.1 = f32[4,240,128]{2,1,0:T(8,128)S(1)} async-done(((f32[4,240,128]{2,1,0:T(8,128)}), f32[4,240,128]{2,1,0:T(8,128)S(1)}, u32[]{:S(2)}, u32[]{:S(2)}) %all-to-all-start.1) | async-done | bytes 491552 | tf_op jit(solution)/shard_map/all_to_all | solution.py:41
  99.0 3.6 %all-to-all-start.4 = ((f32[4,80,128]{2,1,0:T(8,128)}), f32[4,80,128]{2,1,0:T(8,128)S(1)}, u32[]{:S(2)}, u32[]{:S(2)}) async-start(f32[4,80,128]{2,1,0:T(8,128)} %bitcast.53), calls=%async_computation.4 | async-start | bytes 327680 | tf_op jit(solution)/shard_map/all_to_all | solution.py:41
  102.6 2.8 %fusion.24 = f32[50,4,8,128]{3,2,1,0:T(8,128)S(1)} fusion(f32[400,512]{1,0:T(8,128)} %collective-permute-done.14, bf16[400,2048]{1,0:T(8,128)(2,1)S(1)} %copy-done.2, bf16[2048,1024]{0,1:T(8,128)(2,1)} %copy-done.7), kind=kOutput, calls=%fused_computation.35 | convolution fusion | flops 839065600 | bytes 5373952 | tf_op jit(solution)/shard_map/dot_general | solution.py:38
  105.4 1.0 copy.18
  106.4 2.3 %all-to-all-done.4 = f32[4,80,128]{2,1,0:T(8,128)S(1)} async-done(((f32[4,80,128]{2,1,0:T(8,128)}), f32[4,80,128]{2,1,0:T(8,128)S(1)}, u32[]{:S(2)}, u32[]{:S(2)}) %all-to-all-start.4) | async-done | bytes 163872 | tf_op jit(solution)/shard_map/all_to_all | solution.py:41
  108.6 3.5 %all-to-all-start.2 = ((f32[4,400,128]{2,1,0:T(8,128)}), f32[4,400,128]{2,1,0:T(8,128)S(1)}, u32[]{:S(2)}, u32[]{:S(2)}) async-start(f32[4,400,128]{2,1,0:T(8,128)} %bitcast.45), calls=%async_computation.2 | async-start | bytes 1638400 | tf_op jit(solution)/shard_map/all_to_all | solution.py:41
  112.4 2.6 %fusion.23 = f32[40,4,8,128]{3,2,1,0:T(8,128)S(1)} fusion(f32[320,512]{1,0:T(8,128)} %collective-permute-done.20, bf16[320,2048]{1,0:T(8,128)(2,1)S(1)} %copy-done.6, bf16[2048,1024]{0,1:T(8,128)(2,1)} %copy-done.7), kind=kOutput, calls=%fused_computation.33 | convolution fusion | flops 671252480 | bytes 4718592 | tf_op jit(solution)/shard_map/dot_general | solution.py:38
  115.0 0.9 copy.19
  115.9 7.6 %all-to-all-done.2 = f32[4,400,128]{2,1,0:T(8,128)S(1)} async-done(((f32[4,400,128]{2,1,0:T(8,128)}), f32[4,400,128]{2,1,0:T(8,128)S(1)}, u32[]{:S(2)}, u32[]{:S(2)}) %all-to-all-start.2) | async-done | bytes 819232 | tf_op jit(solution)/shard_map/all_to_all | solution.py:41
  123.4 3.5 %all-to-all-start.3 = ((f32[4,320,128]{2,1,0:T(8,128)}), f32[4,320,128]{2,1,0:T(8,128)S(1)}, u32[]{:S(2)}, u32[]{:S(2)}) async-start(f32[4,320,128]{2,1,0:T(8,128)} %bitcast.47), calls=%async_computation.3 | async-start | bytes 1310720 | tf_op jit(solution)/shard_map/all_to_all | solution.py:41
  127.2 2.1 %collective-permute-start.15 = (f32[400,128]{1,0:T(8,128)S(1)}, f32[400,128]{1,0:T(8,128)S(1)}, u32[]{:S(2)}, u32[]{:S(2)}) collective-permute-start(f32[400,128]{1,0:T(8,128)S(1)} %reduce_sum.47), channel_id=1, source_target_pairs={{0,2},{2,0},{1,3},{3,1},{4,6},{6,4},{5,7},{7,5},{8,10},{10,8},{9,1... | collective-permute-start | bytes 614408 | tf_op jit(solution)/shard_map/ppermute | solution.py:43
  129.3 3.0 %collective-permute-done.9 = f32[240,128]{1,0:T(8,128)S(1)} collective-permute-done((f32[240,128]{1,0:T(8,128)S(1)}, f32[240,128]{1,0:T(8,128)S(1)}, u32[]{:S(2)}, u32[]{:S(2)}) %collective-permute-start.9) | collective-permute-done | bytes 122912 | tf_op jit(solution)/shard_map/ppermute | solution.py:43
  132.7 2.9 %all-to-all-done.3 = f32[4,320,128]{2,1,0:T(8,128)S(1)} async-done(((f32[4,320,128]{2,1,0:T(8,128)}), f32[4,320,128]{2,1,0:T(8,128)S(1)}, u32[]{:S(2)}, u32[]{:S(2)}) %all-to-all-start.3) | async-done | bytes 655392 | tf_op jit(solution)/shard_map/all_to_all | solution.py:41
  135.9 5.3 %collective-permute-done.21 = f32[320,128]{1,0:T(8,128)S(1)} collective-permute-done((f32[320,128]{1,0:T(8,128)S(1)}, f32[320,128]{1,0:T(8,128)S(1)}, u32[]{:S(2)}, u32[]{:S(2)}) %collective-permute-start.21) | collective-permute-done | bytes 163872 | tf_op jit(solution)/shard_map/ppermute | solution.py:43
  141.2 1.6 %fusion = bf16[128,1280]{1,0:T(8,128)(2,1)S(1)} fusion(bf16[1280,128]{1,0:T(8,128)(2,1)S(1)} %constant_dynamic-update-slice_fusion.21, s32[1280]{0:T(1024)S(1)} %concatenate.37), kind=kOutput, calls=%fused_computation.5 | convolution fusion | flops 421068800 | bytes 660480 | tf_op jit(solution)/shard_map/dot_general | solution.py:75
  142.7 0.7 dynamic-slice_convert_fusion
  (100 shorter events, 2.7 us)
Async XLA Ops:
  0.0 29.4 %collective-permute-start = (bf16[80,2048]{1,0:T(8,128)(2,1)}, bf16[80,2048]{1,0:T(8,128)(2,1)S(1)}, u32[]{:S(2)}, u32[]{:S(2)}) collective-permute-start(bf16[80,2048]{1,0:T(8,128)(2,1)} %param.2), channel_id=1, source_target_pairs={{0,64},{64,128},{128,192},{192,0},{1,65},{65,129},{129,193},{193,1... | collective-permute-start | bytes 983048 | tf_op jit(solution)/shard_map/ppermute | solution.py:12
  1.5 27.5 %collective-permute-start.1 = (bf16[80,2048]{1,0:T(8,128)(2,1)}, bf16[80,2048]{1,0:T(8,128)(2,1)S(1)}, u32[]{:S(2)}, u32[]{:S(2)}) collective-permute-start(bf16[80,2048]{1,0:T(8,128)(2,1)} %param.2), channel_id=1, source_target_pairs={{0,192},{64,0},{128,64},{192,128},{1,193},{65,1},{129,65},{193,129... | collective-permute-start | bytes 983048 | tf_op jit(solution)/shard_map/ppermute | solution.py:12
  3.2 18.1 %collective-permute-start.4 = (bf16[80,2048]{1,0:T(8,128)(2,1)}, bf16[80,2048]{1,0:T(8,128)(2,1)S(1)}, u32[]{:S(2)}, u32[]{:S(2)}) collective-permute-start(bf16[80,2048]{1,0:T(8,128)(2,1)} %param.2), channel_id=1, source_target_pairs={{0,16},{16,32},{32,48},{48,0},{1,17},{17,33},{33,49},{49,1},{2,18}... | collective-permute-start | bytes 983048 | tf_op jit(solution)/shard_map/ppermute | solution.py:12
  7.7 17.9 %collective-permute-start.5 = (bf16[80,2048]{1,0:T(8,128)(2,1)}, bf16[80,2048]{1,0:T(8,128)(2,1)S(1)}, u32[]{:S(2)}, u32[]{:S(2)}) collective-permute-start(bf16[80,2048]{1,0:T(8,128)(2,1)} %param.2), channel_id=1, source_target_pairs={{0,48},{16,0},{32,16},{48,32},{1,49},{17,1},{33,17},{49,33},{2,50}... | collective-permute-start | bytes 983048 | tf_op jit(solution)/shard_map/ppermute | solution.py:12
  7.9 7.1 %copy-start = (bf16[80,2048]{1,0:T(8,128)(2,1)S(1)}, bf16[80,2048]{1,0:T(8,128)(2,1)}, u32[]{:S(2)}) copy-start(bf16[80,2048]{1,0:T(8,128)(2,1)} %param.2) | copy-start | bytes 983044
  15.1 36.3 %copy-start.7 = (bf16[2048,1024]{0,1:T(8,128)(2,1)}, bf16[2048,1024]{0,1:T(8,128)(2,1)S(1)}, u32[]{:S(2)}) copy-start(bf16[2048,1024]{0,1:T(8,128)(2,1)S(1)} %convert_bitcast_fusion) | copy-start | bytes 12582916
  25.6 31.8 %collective-permute-start.10 = (bf16[160,2048]{1,0:T(8,128)(2,1)S(1)}, bf16[160,2048]{1,0:T(8,128)(2,1)S(1)}, u32[]{:S(2)}, u32[]{:S(2)}) collective-permute-start(bf16[160,2048]{1,0:T(8,128)(2,1)S(1)} %get-tuple-element.5), channel_id=1, source_target_pairs={{0,64},{64,128},{128,192},{192,0},{1,65},{65,129},{129,193},{193,1... | collective-permute-start | bytes 1966088 | tf_op jit(solution)/shard_map/ppermute | solution.py:12
  26.0 31.5 %collective-permute-start.11 = (bf16[160,2048]{1,0:T(8,128)(2,1)S(1)}, bf16[160,2048]{1,0:T(8,128)(2,1)S(1)}, u32[]{:S(2)}, u32[]{:S(2)}) collective-permute-start(bf16[160,2048]{1,0:T(8,128)(2,1)S(1)} %get-tuple-element.5), channel_id=1, source_target_pairs={{0,192},{64,0},{128,64},{192,128},{1,193},{65,1},{129,65},{193,129... | collective-permute-start | bytes 1966088 | tf_op jit(solution)/shard_map/ppermute | solution.py:12
  29.0 16.4 %collective-permute-start.6 = (bf16[40,2048]{1,0:T(8,128)(2,1)S(1)}, bf16[40,2048]{1,0:T(8,128)(2,1)S(1)}, u32[]{:S(2)}, u32[]{:S(2)}) collective-permute-start(bf16[40,2048]{1,0:T(8,128)(2,1)S(1)} %slice.42), channel_id=1, source_target_pairs={{0,192},{64,0},{128,64},{192,128},{1,193},{65,1},{129,65},{193,129... | collective-permute-start | bytes 491528 | tf_op jit(solution)/shard_map/ppermute | solution.py:12
  30.2 21.2 %collective-permute-start.2 = (f32[240,512]{1,0:T(8,128)S(1)}, f32[240,512]{1,0:T(8,128)S(1)}, u32[]{:S(2)}, u32[]{:S(2)}) collective-permute-start(f32[240,512]{1,0:T(8,128)S(1)} %fusion.36), channel_id=1, source_target_pairs={{0,1},{1,0},{2,3},{3,2},{4,5},{5,4},{6,7},{7,6},{8,9},{9,8},{10,11... | collective-permute-start | bytes 1474568 | tf_op jit(solution)/shard_map/ppermute | solution.py:39
  30.3 15.8 %collective-permute-start.7 = (bf16[40,2048]{1,0:T(8,128)(2,1)S(1)}, bf16[40,2048]{1,0:T(8,128)(2,1)S(1)}, u32[]{:S(2)}, u32[]{:S(2)}) collective-permute-start(bf16[40,2048]{1,0:T(8,128)(2,1)S(1)} %slice.43), channel_id=1, source_target_pairs={{0,64},{64,128},{128,192},{192,0},{1,65},{65,129},{129,193},{193,1... | collective-permute-start | bytes 491528 | tf_op jit(solution)/shard_map/ppermute | solution.py:12
  45.4 12.2 %collective-permute-start.12 = (bf16[40,2048]{1,0:T(8,128)(2,1)S(1)}, bf16[40,2048]{1,0:T(8,128)(2,1)S(1)}, u32[]{:S(2)}, u32[]{:S(2)}) collective-permute-start(bf16[40,2048]{1,0:T(8,128)(2,1)S(1)} %slice.44), channel_id=1, source_target_pairs={{0,48},{16,0},{32,16},{48,32},{1,49},{17,1},{33,17},{49,33},{2,50}... | collective-permute-start | bytes 491528 | tf_op jit(solution)/shard_map/ppermute | solution.py:12
  46.1 11.5 %collective-permute-start.13 = (bf16[40,2048]{1,0:T(8,128)(2,1)S(1)}, bf16[40,2048]{1,0:T(8,128)(2,1)S(1)}, u32[]{:S(2)}, u32[]{:S(2)}) collective-permute-start(bf16[40,2048]{1,0:T(8,128)(2,1)S(1)} %slice.45), channel_id=1, source_target_pairs={{0,16},{16,32},{32,48},{48,0},{1,17},{17,33},{33,49},{49,1},{2,18}... | collective-permute-start | bytes 491528 | tf_op jit(solution)/shard_map/ppermute | solution.py:12
  49.8 1.6 %copy-start.3 = (bf16[240,2048]{1,0:T(8,128)(2,1)}, bf16[240,2048]{1,0:T(8,128)(2,1)S(1)}, u32[]{:S(2)}) copy-start(bf16[240,2048]{1,0:T(8,128)(2,1)S(1)} %constant_dynamic-update-slice_fusion.3) | copy-start | bytes 2949124
  51.4 10.1 %collective-permute-start.8 = (f32[240,512]{1,0:T(8,128)}, f32[240,512]{1,0:T(8,128)}, u32[]{:S(2)}, u32[]{:S(2)}) collective-permute-start(f32[240,512]{1,0:T(8,128)} %fusion.34), channel_id=1, source_target_pairs={{0,1},{1,0},{2,3},{3,2},{4,5},{5,4},{6,7},{7,6},{8,9},{9,8},{10,11... | collective-permute-start | bytes 1474568 | tf_op jit(solution)/shard_map/ppermute | solution.py:39
  53.0 31.4 %all-to-all-start = ((f32[4,240,128]{2,1,0:T(8,128)}), f32[4,240,128]{2,1,0:T(8,128)S(1)}, u32[]{:S(2)}, u32[]{:S(2)}) async-start(f32[4,240,128]{2,1,0:T(8,128)} %bitcast.51), calls=%async_computation | async-start | bytes 983040 | tf_op jit(solution)/shard_map/all_to_all | solution.py:41
  57.4 4.1 %copy-start.4 = (bf16[240,2048]{1,0:T(8,128)(2,1)S(1)}, bf16[240,2048]{1,0:T(8,128)(2,1)}, u32[]{:S(2)}) copy-start(bf16[240,2048]{1,0:T(8,128)(2,1)} %copy-done.3) | copy-start | bytes 2949124
  57.6 7.1 %copy-start.1 = (bf16[400,2048]{1,0:T(8,128)(2,1)}, bf16[400,2048]{1,0:T(8,128)(2,1)S(1)}, u32[]{:S(2)}) copy-start(bf16[400,2048]{1,0:T(8,128)(2,1)S(1)} %get-tuple-element.10) | copy-start | bytes 4915204
  57.7 7.1 %copy-start.8 = (bf16[2048,1024]{0,1:T(8,128)(2,1)S(1)}, bf16[2048,1024]{0,1:T(8,128)(2,1)}, u32[]{:S(2)}) copy-start(bf16[2048,1024]{0,1:T(8,128)(2,1)} %copy-done.7) | copy-start | bytes 12582916
  57.7 15.0 %collective-permute-start.16 = (bf16[80,2048]{1,0:T(8,128)(2,1)S(1)}, bf16[80,2048]{1,0:T(8,128)(2,1)S(1)}, u32[]{:S(2)}, u32[]{:S(2)}) collective-permute-start(bf16[80,2048]{1,0:T(8,128)(2,1)S(1)} %get-tuple-element.9), channel_id=1, source_target_pairs={{0,64},{64,128},{128,192},{192,0},{1,65},{65,129},{129,193},{193,1... | collective-permute-start | bytes 983048 | tf_op jit(solution)/shard_map/ppermute | solution.py:12
  58.8 10.3 %collective-permute-start.17 = (bf16[80,2048]{1,0:T(8,128)(2,1)S(1)}, bf16[80,2048]{1,0:T(8,128)(2,1)S(1)}, u32[]{:S(2)}, u32[]{:S(2)}) collective-permute-start(bf16[80,2048]{1,0:T(8,128)(2,1)S(1)} %get-tuple-element.9), channel_id=1, source_target_pairs={{0,192},{64,0},{128,64},{192,128},{1,193},{65,1},{129,65},{193,129... | collective-permute-start | bytes 983048 | tf_op jit(solution)/shard_map/ppermute | solution.py:12
  66.8 35.8 %collective-permute-start.14 = (f32[400,512]{1,0:T(8,128)}, f32[400,512]{1,0:T(8,128)}, u32[]{:S(2)}, u32[]{:S(2)}) collective-permute-start(f32[400,512]{1,0:T(8,128)} %fusion.32), channel_id=1, source_target_pairs={{0,1},{1,0},{2,3},{3,2},{4,5},{5,4},{6,7},{7,6},{8,9},{9,8},{10,11... | collective-permute-start | bytes 2457608 | tf_op jit(solution)/shard_map/ppermute | solution.py:39
  66.8 10.6 %collective-permute-start.18 = (bf16[80,2048]{1,0:T(8,128)(2,1)S(1)}, bf16[80,2048]{1,0:T(8,128)(2,1)S(1)}, u32[]{:S(2)}, u32[]{:S(2)}) collective-permute-start(bf16[80,2048]{1,0:T(8,128)(2,1)S(1)} %slice.46), channel_id=1, source_target_pairs={{0,192},{64,0},{128,64},{192,128},{1,193},{65,1},{129,65},{193,129... | collective-permute-start | bytes 983048 | tf_op jit(solution)/shard_map/ppermute | solution.py:12
  68.8 11.8 %collective-permute-start.19 = (bf16[80,2048]{1,0:T(8,128)(2,1)S(1)}, bf16[80,2048]{1,0:T(8,128)(2,1)S(1)}, u32[]{:S(2)}, u32[]{:S(2)}) collective-permute-start(bf16[80,2048]{1,0:T(8,128)(2,1)S(1)} %slice.47), channel_id=1, source_target_pairs={{0,64},{64,128},{128,192},{192,0},{1,65},{65,129},{129,193},{193,1... | collective-permute-start | bytes 983048 | tf_op jit(solution)/shard_map/ppermute | solution.py:12
  69.0 11.7 %collective-permute-start.22 = (bf16[40,2048]{1,0:T(8,128)(2,1)S(1)}, bf16[40,2048]{1,0:T(8,128)(2,1)S(1)}, u32[]{:S(2)}, u32[]{:S(2)}) collective-permute-start(bf16[40,2048]{1,0:T(8,128)(2,1)S(1)} %slice.48), channel_id=1, source_target_pairs={{0,192},{64,0},{128,64},{192,128},{1,193},{65,1},{129,65},{193,129... | collective-permute-start | bytes 491528 | tf_op jit(solution)/shard_map/ppermute | solution.py:12
  72.7 10.8 %collective-permute-start.23 = (bf16[40,2048]{1,0:T(8,128)(2,1)S(1)}, bf16[40,2048]{1,0:T(8,128)(2,1)S(1)}, u32[]{:S(2)}, u32[]{:S(2)}) collective-permute-start(bf16[40,2048]{1,0:T(8,128)(2,1)S(1)} %slice.49), channel_id=1, source_target_pairs={{0,64},{64,128},{128,192},{192,0},{1,65},{65,129},{129,193},{193,1... | collective-permute-start | bytes 491528 | tf_op jit(solution)/shard_map/ppermute | solution.py:12
  80.7 8.5 %copy-start.5 = (bf16[320,2048]{1,0:T(8,128)(2,1)}, bf16[320,2048]{1,0:T(8,128)(2,1)S(1)}, u32[]{:S(2)}) copy-start(bf16[320,2048]{1,0:T(8,128)(2,1)S(1)} %constant_dynamic-update-slice_fusion.15) | copy-start | bytes 3932164
  84.3 8.6 %collective-permute-start.24 = (f32[80,512]{1,0:T(8,128)S(1)}, f32[80,512]{1,0:T(8,128)S(1)}, u32[]{:S(2)}, u32[]{:S(2)}) collective-permute-start(f32[80,512]{1,0:T(8,128)S(1)} %fusion.28), channel_id=1, source_target_pairs={{0,1},{1,0},{2,3},{3,2},{4,5},{5,4},{6,7},{7,6},{8,9},{9,8},{10,11... | collective-permute-start | bytes 491528 | tf_op jit(solution)/shard_map/ppermute | solution.py:39
  84.4 14.6 %all-to-all-start.1 = ((f32[4,240,128]{2,1,0:T(8,128)}), f32[4,240,128]{2,1,0:T(8,128)S(1)}, u32[]{:S(2)}, u32[]{:S(2)}) async-start(f32[4,240,128]{2,1,0:T(8,128)} %bitcast.49), calls=%async_computation.1 | async-start | bytes 983040 | tf_op jit(solution)/shard_map/all_to_all | solution.py:41
  89.2 3.7 %copy-start.9 = (bf16[2048,1024]{0,1:T(8,128)(2,1)S(1)}, bf16[2048,1024]{0,1:T(8,128)(2,1)}, u32[]{:S(2)}) copy-start(bf16[2048,1024]{0,1:T(8,128)(2,1)} %copy-done.7) | copy-start | bytes 12582916
  92.7 9.9 %copy-start.2 = (bf16[400,2048]{1,0:T(8,128)(2,1)S(1)}, bf16[400,2048]{1,0:T(8,128)(2,1)}, u32[]{:S(2)}) copy-start(bf16[400,2048]{1,0:T(8,128)(2,1)} %copy-done.1) | copy-start | bytes 4915204
  92.7 19.7 %collective-permute-start.20 = (f32[320,512]{1,0:T(8,128)}, f32[320,512]{1,0:T(8,128)}, u32[]{:S(2)}, u32[]{:S(2)}) collective-permute-start(f32[320,512]{1,0:T(8,128)} %fusion.30), channel_id=1, source_target_pairs={{0,1},{1,0},{2,3},{3,2},{4,5},{5,4},{6,7},{7,6},{8,9},{9,8},{10,11... | collective-permute-start | bytes 1966088 | tf_op jit(solution)/shard_map/ppermute | solution.py:39
  99.0 9.7 %all-to-all-start.4 = ((f32[4,80,128]{2,1,0:T(8,128)}), f32[4,80,128]{2,1,0:T(8,128)S(1)}, u32[]{:S(2)}, u32[]{:S(2)}) async-start(f32[4,80,128]{2,1,0:T(8,128)} %bitcast.53), calls=%async_computation.4 | async-start | bytes 327680 | tf_op jit(solution)/shard_map/all_to_all | solution.py:41
  105.4 7.0 %copy-start.6 = (bf16[320,2048]{1,0:T(8,128)(2,1)S(1)}, bf16[320,2048]{1,0:T(8,128)(2,1)}, u32[]{:S(2)}) copy-start(bf16[320,2048]{1,0:T(8,128)(2,1)} %copy-done.5) | copy-start | bytes 3932164
  108.6 14.8 %all-to-all-start.2 = ((f32[4,400,128]{2,1,0:T(8,128)}), f32[4,400,128]{2,1,0:T(8,128)S(1)}, u32[]{:S(2)}, u32[]{:S(2)}) async-start(f32[4,400,128]{2,1,0:T(8,128)} %bitcast.45), calls=%async_computation.2 | async-start | bytes 1638400 | tf_op jit(solution)/shard_map/all_to_all | solution.py:41
  112.2 14.9 %collective-permute-start.3 = (f32[240,128]{1,0:T(8,128)S(1)}, f32[240,128]{1,0:T(8,128)S(1)}, u32[]{:S(2)}, u32[]{:S(2)}) collective-permute-start(f32[240,128]{1,0:T(8,128)S(1)} %reduce_sum.45), channel_id=1, source_target_pairs={{0,2},{2,0},{1,3},{3,1},{4,6},{6,4},{5,7},{7,5},{8,10},{10,8},{9,1... | collective-permute-start | bytes 368648 | tf_op jit(solution)/shard_map/ppermute | solution.py:43
  123.4 12.2 %all-to-all-start.3 = ((f32[4,320,128]{2,1,0:T(8,128)}), f32[4,320,128]{2,1,0:T(8,128)S(1)}, u32[]{:S(2)}, u32[]{:S(2)}) async-start(f32[4,320,128]{2,1,0:T(8,128)} %bitcast.47), calls=%async_computation.3 | async-start | bytes 1310720 | tf_op jit(solution)/shard_map/all_to_all | solution.py:41
  127.1 5.3 %collective-permute-start.9 = (f32[240,128]{1,0:T(8,128)S(1)}, f32[240,128]{1,0:T(8,128)S(1)}, u32[]{:S(2)}, u32[]{:S(2)}) collective-permute-start(f32[240,128]{1,0:T(8,128)S(1)} %reduce_sum.46), channel_id=1, source_target_pairs={{0,2},{2,0},{1,3},{3,1},{4,6},{6,4},{5,7},{7,5},{8,10},{10,8},{9,1... | collective-permute-start | bytes 368648 | tf_op jit(solution)/shard_map/ppermute | solution.py:43
  127.2 8.6 %collective-permute-start.15 = (f32[400,128]{1,0:T(8,128)S(1)}, f32[400,128]{1,0:T(8,128)S(1)}, u32[]{:S(2)}, u32[]{:S(2)}) collective-permute-start(f32[400,128]{1,0:T(8,128)S(1)} %reduce_sum.47), channel_id=1, source_target_pairs={{0,2},{2,0},{1,3},{3,1},{4,6},{6,4},{5,7},{7,5},{8,10},{10,8},{9,1... | collective-permute-start | bytes 614408 | tf_op jit(solution)/shard_map/ppermute | solution.py:43
  132.4 8.7 %collective-permute-start.25 = (f32[80,128]{1,0:T(8,128)S(1)}, f32[80,128]{1,0:T(8,128)S(1)}, u32[]{:S(2)}, u32[]{:S(2)}) collective-permute-start(f32[80,128]{1,0:T(8,128)S(1)} %reduce_sum.49), channel_id=1, source_target_pairs={{0,2},{2,0},{1,3},{3,1},{4,6},{6,4},{5,7},{7,5},{8,10},{10,8},{9,1... | collective-permute-start | bytes 122888 | tf_op jit(solution)/shard_map/ppermute | solution.py:43
  135.7 5.4 %collective-permute-start.21 = (f32[320,128]{1,0:T(8,128)S(1)}, f32[320,128]{1,0:T(8,128)S(1)}, u32[]{:S(2)}, u32[]{:S(2)}) collective-permute-start(f32[320,128]{1,0:T(8,128)S(1)} %reduce_sum.48), channel_id=1, source_target_pairs={{0,2},{2,0},{1,3},{3,1},{4,6},{6,4},{5,7},{7,5},{8,10},{10,8},{9,1... | collective-permute-start | bytes 491528 | tf_op jit(solution)/shard_map/ppermute | solution.py:43

commit v3 on v1

v3 whole, which is shorter than its diff:
```python
import jax
import jax.numpy as jnp
from jax import lax
from jax.sharding import Mesh, PartitionSpec as P

ROWS = 80
F32 = jnp.float32
BF16 = jnp.bfloat16


def shift(value, axis, size, by):
    return lax.ppermute(value, axis, [(i, (i + by) % size) for i in range(size)])


def to_both(value, axis):
    return shift(value, axis, 4, 1), shift(value, axis, 4, -1)


def swap(value, axis):
    return lax.ppermute(value, axis, [(0, 1), (1, 0)])


def joined(*parts):
    return jnp.concatenate(parts, axis=0)


def local(amplitudes, integrals):
    x, zh, y, zl, core = (lax.axis_index(n) for n in ("x", "zh", "y", "zl", "core"))

    out_col = lax.broadcasted_iota(jnp.int32, (1024, 1024), 1)
    in_col = lax.broadcasted_iota(jnp.int32, (1024, 1024), 0)
    owner = jnp.where(out_col < 512, 1 - core, core)
    level = jnp.where(out_col & 64 == 0, zl, 1 - zl)
    source = ((out_col >> 7) & 3) * 256 + level * 128 + owner * 64 + (out_col & 63)
    order = (in_col == source).astype(BF16)
    columns = jnp.dot(integrals, order, preferred_element_type=F32).astype(BF16)
    theirs, mine = columns[:, :512], columns[:, 512:]

    def paired(rows):
        away = swap(jnp.dot(rows, theirs, preferred_element_type=F32), "core")
        return jnp.dot(rows, mine, preferred_element_type=F32) + away

    def over_y(pair):
        split = pair.reshape(pair.shape[0], 4, 128).transpose(1, 0, 2)
        return jnp.sum(lax.all_to_all(split, "y", split_axis=0, concat_axis=0, tiled=True), axis=0)

    def over_y_at_once(pair):
        part = lambda d: lax.dynamic_slice_in_dim(pair, ((y + d) % 4) * 128, 128, axis=1)
        others = [shift(part(d), "y", 4, d) for d in (1, 3, 2)]
        return part(0) + others[0] + others[1] + others[2]

    def over_zl(some):
        return (some[:, :64] + swap(some, "zl")[:, 64:]).astype(BF16)

    def block(dx, dz, first=0, count=ROWS):
        start = (((x + dx) % 4) * 4 + (zh + dz) % 4) * ROWS + first
        return start + jnp.arange(count)

    own = amplitudes
    zm, zp = to_both(own, "zh")
    own_xm, own_xp = to_both(own, "x")
    side = joined(zm, zp)
    side_xm, side_xp = to_both(side, "x")
    far = joined(shift(zp[:40], "zh", 4, -1), shift(zm[40:], "zh", 4, 1))
    first = paired(joined(own, own_xm, own_xp, side))
    after_xm, after_xp, first = lax.optimization_barrier(
        (joined(far, own_xm[40:]), joined(far, own_xp[:40]), first)
    )
    from_xm, from_xp = shift(after_xm, "x", 4, 1), shift(after_xp, "x", 4, -1)
    second = paired(joined(side_xm, side_xp, far))
    after_xm, after_xp, second = lax.optimization_barrier(
        (joined(side_xm[80:], from_xm[40:80]), joined(side_xp[:80], from_xp[:40]), second)
    )
    last_xm, last_xp = shift(after_xm, "x", 4, 1), shift(after_xp, "x", 4, -1)
    third = paired(joined(from_xm, from_xp))
    last_xm, last_xp, third = lax.optimization_barrier((last_xm, last_xp, third))
    fourth = paired(joined(last_xm, last_xp))

    sums = [over_zl(over_y(pair)) for pair in (first, second, third)]
    sums.append(over_zl(over_y_at_once(fourth)))
    sites = [
        [block(0, 0), block(-1, 0), block(1, 0), block(0, -1), block(0, 1)],
        [block(-1, -1), block(-1, 1), block(1, -1), block(1, 1), block(0, 2)],
        [block(-1, 2), block(2, 0, 40, 40), block(1, 2), block(2, 0, 0, 40)],
        [block(2, 1), block(2, 2, 40, 40), block(2, -1), block(2, 2, 0, 40)],
    ]
    places = joined(*[p for ps in sites for p in ps])
    place = (places[:, None] == jnp.arange(1280)[None, :]).astype(BF16)
    turned = lax.dot_general(
        joined(*sums), place, (((0,), (0,)), ((), ())), preferred_element_type=F32
    )
    return turned.astype(BF16)


def solution(mesh):
    split = Mesh(mesh.devices.reshape(4, 4, 4, 2, 2), ("x", "zh", "y", "zl", "core"))
    row, col = ("x", "zh"), ("y", "zl", "core")
    return jax.shard_map(
        local,
        mesh=split,
        in_specs=(P(row, col), P(col, row)),
        out_specs=P(row + col, None),
        check_vma=False,
    )
```

time: 194 us -> 119 us (0.61)
  waiting for transfers between devices: 167 us -> 36.7 us
  starting transfers between devices: 0.04 us -> 42.1 us
  matrix products: 10.5 us -> 30.4 us
  between operations: 13.4 us -> 0.54 us
  local copies, waits for them, and re-layouts: 0 us -> 6.09 us
    all_gather x1 -> x0, waiting for transfers between devices: 92.4 us -> none  [local(): gathered = lax.all_gather(amplitudes, 'row', axis=0, tiled=True)]
    reduce_scatter x1 -> x0, waiting for transfers between devices: 74.3 us -> none  [local(): lax.psum_scatter(partial_value, 'col', scatter_dimension=0, tiled=True)]
    ppermute x0 -> x23, waiting for transfers between devices: none -> 30.8 us  [the longest x15 26.4 us: shift(): lax.ppermute(value, axis, [(i, (i + by) % size) for i in range(size)])]
    ppermute x0 -> x23, starting transfers between devices: none -> 30.7 us  [the longest x15 26 us: shift(): lax.ppermute(value, axis, [(i, (i + by) % size) for i in range(size)])]
    dot_general x1 -> x10, matrix products: 10.5 us -> 30.4 us  [the longest x4 10.3 us: paired(): away = swap(jnp.dot(rows, theirs, preferred_element_type=F32), 'core')]
    all_to_all x0 -> x3, starting transfers between devices: none -> 11.4 us  [over_y(): lax.all_to_all(split, 'y', split_axis=0, concat_axis=0, tiled=True)]
    all_to_all x0 -> x3, waiting for transfers between devices: none -> 5.82 us  [over_y(): lax.all_to_all(split, 'y', split_axis=0, concat_axis=0, tiled=True)]
    transpose x0 -> x3, local copies, waits for them, and re-layouts: none -> 2.75 us  [over_y(): split = pair.reshape(pair.shape[0], 4, 128).transpose(1, 0, 2)]
  transfers between devices with their start and end apart: 2 -> 26, of which waited for: 2 -> 14; matrix products, arithmetic and copies ran while one was open for 0% -> 28% of each run, Pallas kernels for 0% -> 0%
where the time goes in v3:
time: 119 us; the launch traced here: 118 us
  starting transfers between devices  42.1 us (35%)
  waiting for transfers between devices  36.7 us (31%)
  matrix products  30.4 us (26%)
  local copies, waits for them, and re-layouts  6.09 us (5%)
  other arithmetic  2.51 us (2%)
    ppermute x15, waiting for transfers between devices, shift(): lax.ppermute(value, axis, [(i, (i + by) % size) for i in range(size)])  26.4 us
    ppermute x15, starting transfers between devices, shift(): lax.ppermute(value, axis, [(i, (i + by) % size) for i in range(size)])  26 us
    all_to_all x3, starting transfers between devices, over_y(): lax.all_to_all(split, 'y', split_axis=0, concat_axis=0, tiled=True)  11.4 us
    dot_general x4, matrix products, paired(): away = swap(jnp.dot(rows, theirs, preferred_element_type=F32), 'core')  10.3 us
    dot_general x4, matrix products, paired(): return jnp.dot(rows, mine, preferred_element_type=F32) + away  9.54 us
    dot_general x1, matrix products, local(): columns = jnp.dot(integrals, order, preferred_element_type=F32).astype(BF16)  8.39 us
    all_to_all x3, waiting for transfers between devices, over_y(): lax.all_to_all(split, 'y', split_axis=0, concat_axis=0, tiled=True)  5.82 us
    ppermute x8, starting transfers between devices, swap(): return lax.ppermute(value, axis, [(0, 1), (1, 0)])  4.64 us
  transfers between devices with their start and end apart: 26, of which 14 were waited for; matrix products, arithmetic and copies ran while one was open for 28% of the time, Pallas kernels for 0%

profile of v3, /device:TPU:64, one launch (start us, length us, event | category | flops | bytes accessed | tf_op | source)
XLA Modules:
  0.0 118.3 jit_solution(2755518627239369380)
XLA Ops:
  0.0 2.8 %collective-permute-start.5 = (bf16[80,2048]{1,0:T(8,128)(2,1)}, bf16[80,2048]{1,0:T(8,128)(2,1)S(1)}, u32[]{:S(2)}, u32[]{:S(2)}) collective-permute-start(bf16[80,2048]{1,0:T(8,128)(2,1)} %param.2), channel_id=1, source_target_pairs={{0,192},{64,0},{128,64},{192,128},{1,193},{65,1},{129,65},{193,129... | collective-permute-start | bytes 983048 | tf_op jit(solution)/shard_map/ppermute | solution.py:12
  2.8 4.5 %collective-permute-start.2 = (bf16[80,2048]{1,0:T(8,128)(2,1)}, bf16[80,2048]{1,0:T(8,128)(2,1)S(1)}, u32[]{:S(2)}, u32[]{:S(2)}) collective-permute-start(bf16[80,2048]{1,0:T(8,128)(2,1)} %param.2), channel_id=1, source_target_pairs={{0,16},{16,32},{32,48},{48,0},{1,17},{17,33},{33,49},{49,1},{2,18}... | collective-permute-start | bytes 983048 | tf_op jit(solution)/shard_map/ppermute | solution.py:12
  7.4 8.4 %convert_bitcast_fusion = bf16[2048,1024]{0,1:T(8,128)(2,1)} fusion(bf16[2048,1024]{1,0:T(8,128)(2,1)} %param.3, s32[1024]{0:T(1024)S(1)} %and_add_fusion), kind=kOutput, calls=%fused_computation.2 | convolution fusion | flops 4299161600 | bytes 8392704 | tf_op jit(solution)/shard_map/dot_general | solution.py:36
  15.8 1.8 %collective-permute-done.4 = bf16[80,2048]{1,0:T(8,128)(2,1)S(1)} collective-permute-done((bf16[80,2048]{1,0:T(8,128)(2,1)}, bf16[80,2048]{1,0:T(8,128)(2,1)S(1)}, u32[]{:S(2)}, u32[]{:S(2)}) %collective-permute-start.4) | collective-permute-done | bytes 327712 | tf_op jit(solution)/shard_map/ppermute | solution.py:12
  17.6 3.5 %collective-permute-done.2 = bf16[80,2048]{1,0:T(8,128)(2,1)S(1)} collective-permute-done((bf16[80,2048]{1,0:T(8,128)(2,1)}, bf16[80,2048]{1,0:T(8,128)(2,1)S(1)}, u32[]{:S(2)}, u32[]{:S(2)}) %collective-permute-start.2) | collective-permute-done | bytes 327712 | tf_op jit(solution)/shard_map/ppermute | solution.py:12
  21.2 0.8 constant_dynamic-update-slice_fusion.6
  22.0 3.4 %collective-permute-done = bf16[80,2048]{1,0:T(8,128)(2,1)S(1)} collective-permute-done((bf16[80,2048]{1,0:T(8,128)(2,1)}, bf16[80,2048]{1,0:T(8,128)(2,1)S(1)}, u32[]{:S(2)}, u32[]{:S(2)}) %collective-permute-start) | collective-permute-done | bytes 327712 | tf_op jit(solution)/shard_map/ppermute | solution.py:12
  25.4 0.8 constant_dynamic-update-slice_fusion.5
  26.2 1.2 copy-done.5
  27.4 3.2 %collective-permute-start.10 = (bf16[160,2048]{1,0:T(8,128)(2,1)}, bf16[160,2048]{1,0:T(8,128)(2,1)S(1)}, u32[]{:S(2)}, u32[]{:S(2)}) collective-permute-start(bf16[160,2048]{1,0:T(8,128)(2,1)} %get-tuple-element.26), channel_id=1, source_target_pairs={{0,192},{64,0},{128,64},{192,128},{1,193},{65,1},{129,65},{193,129... | collective-permute-start | bytes 1966088 | tf_op jit(solution)/shard_map/ppermute | solution.py:12
  30.6 1.1 collective-permute-start.3
  31.8 1.9 %collective-permute-start.1 = (bf16[40,2048]{1,0:T(8,128)(2,1)S(1)}, bf16[40,2048]{1,0:T(8,128)(2,1)S(1)}, u32[]{:S(2)}, u32[]{:S(2)}) collective-permute-start(bf16[40,2048]{1,0:T(8,128)(2,1)S(1)} %slice.72), channel_id=1, source_target_pairs={{0,48},{16,0},{32,16},{48,32},{1,49},{17,1},{33,17},{49,33},{2,50}... | collective-permute-start | bytes 491528 | tf_op jit(solution)/shard_map/ppermute | solution.py:12
  33.7 3.3 %fusion.12 = f32[400,512]{1,0:T(8,128)S(1)} fusion(bf16[400,2048]{1,0:T(8,128)(2,1)} %copy-done.5, bf16[2048,1024]{0,1:T(8,128)(2,1)} %convert_bitcast_fusion), kind=kOutput, calls=%fused_computation.14 | convolution fusion | flops 838860800 | bytes 4554752 | tf_op jit(solution)/shard_map/dot_general | solution.py:40
  37.1 2.1 %collective-permute-done.3 = bf16[40,2048]{1,0:T(8,128)(2,1)S(1)} collective-permute-done((bf16[40,2048]{1,0:T(8,128)(2,1)S(1)}, bf16[40,2048]{1,0:T(8,128)(2,1)S(1)}, u32[]{:S(2)}, u32[]{:S(2)}) %collective-permute-start.3) | collective-permute-done | bytes 163872 | tf_op jit(solution)/shard_map/ppermute | solution.py:12
  39.2 1.2 collective-permute-done.1
  40.4 0.9 pad_maximum_fusion.2
  41.3 3.2 %collective-permute-done.8 = bf16[160,2048]{1,0:T(8,128)(2,1)S(1)} collective-permute-done((bf16[160,2048]{1,0:T(8,128)(2,1)}, bf16[160,2048]{1,0:T(8,128)(2,1)S(1)}, u32[]{:S(2)}, u32[]{:S(2)}) %collective-permute-start.8) | collective-permute-done | bytes 655392 | tf_op jit(solution)/shard_map/ppermute | solution.py:12
  44.6 1.0 fusion.22
  46.0 2.0 %fusion.10 = f32[400,512]{1,0:T(8,128)} fusion(bf16[400,2048]{1,0:T(8,128)(2,1)S(1)} %constant_dynamic-update-slice_fusion.7, bf16[2048,1024]{0,1:T(8,128)(2,1)S(1)} %copy-done.7), kind=kOutput, calls=%fused_computation.12 | convolution fusion | flops 838860800 | bytes 4554752 | tf_op jit(solution)/shard_map/dot_general | solution.py:40
  48.0 3.3 %collective-permute-start.11 = (bf16[120,2048]{1,0:T(8,128)(2,1)S(1)}, bf16[120,2048]{1,0:T(8,128)(2,1)S(1)}, u32[]{:S(2)}, u32[]{:S(2)}) collective-permute-start(bf16[120,2048]{1,0:T(8,128)(2,1)S(1)} %get-tuple-element.16), channel_id=1, source_target_pairs={{0,192},{64,0},{128,64},{192,128},{1,193},{65,1},{129,65},{193,129... | collective-permute-start | bytes 1474568 | tf_op jit(solution)/shard_map/ppermute | solution.py:12
  51.3 1.0 bitcast_bitcast_fusion.1
  52.2 4.5 %all-to-all-start = ((f32[4,400,128]{2,1,0:T(8,128)}), f32[4,400,128]{2,1,0:T(8,128)S(1)}, u32[]{:S(2)}, u32[]{:S(2)}) async-start(f32[4,400,128]{2,1,0:T(8,128)} %bitcast_bitcast_fusion.1), calls=%async_computation | async-start | bytes 1638400 | tf_op jit(solution)/shard_map/all_to_all | solution.py:45
  56.7 1.9 %collective-permute-done.9 = bf16[120,2048]{1,0:T(8,128)(2,1)S(1)} collective-permute-done((bf16[120,2048]{1,0:T(8,128)(2,1)}, bf16[120,2048]{1,0:T(8,128)(2,1)S(1)}, u32[]{:S(2)}, u32[]{:S(2)}) %collective-permute-start.9) | collective-permute-done | bytes 491552 | tf_op jit(solution)/shard_map/ppermute | solution.py:12
  58.7 3.7 %collective-permute-done.11 = bf16[120,2048]{1,0:T(8,128)(2,1)S(1)} collective-permute-done((bf16[120,2048]{1,0:T(8,128)(2,1)S(1)}, bf16[120,2048]{1,0:T(8,128)(2,1)S(1)}, u32[]{:S(2)}, u32[]{:S(2)}) %collective-permute-start.11) | collective-permute-done | bytes 491552 | tf_op jit(solution)/shard_map/ppermute | solution.py:12
  62.4 3.5 %fusion.8 = f32[240,512]{1,0:T(8,128)} fusion(bf16[240,2048]{1,0:T(8,128)(2,1)S(1)} %constant_dynamic-update-slice_fusion.11, bf16[2048,1024]{0,1:T(8,128)(2,1)} %convert_bitcast_fusion), kind=kOutput, calls=%fused_computation.10 | convolution fusion | flops 503316480 | bytes 3571712 | tf_op jit(solution)/shard_map/dot_general | solution.py:40
  66.1 3.6 %all-to-all-done = f32[4,400,128]{2,1,0:T(8,128)S(1)} async-done(((f32[4,400,128]{2,1,0:T(8,128)}), f32[4,400,128]{2,1,0:T(8,128)S(1)}, u32[]{:S(2)}, u32[]{:S(2)}) %all-to-all-start) | async-done | bytes 819232 | tf_op jit(solution)/shard_map/all_to_all | solution.py:45
  69.8 3.3 %fusion.25 = f32[400,512]{1,0:T(8,128)S(1)} fusion(f32[400,512]{1,0:T(8,128)} %collective-permute-done.12, bf16[400,2048]{1,0:T(8,128)(2,1)} %copy-done.3, bf16[2048,1024]{0,1:T(8,128)(2,1)} %convert_bitcast_fusion), kind=kOutput, calls=%fused_computation.25 | convolution fusion | flops 839065600 | bytes 5373952 | tf_op jit(solution)/shard_map/dot_general | solution.py:41
  73.2 3.2 %collective-permute-start.15 = (bf16[120,2048]{1,0:T(8,128)(2,1)S(1)}, bf16[120,2048]{1,0:T(8,128)(2,1)S(1)}, u32[]{:S(2)}, u32[]{:S(2)}) collective-permute-start(bf16[120,2048]{1,0:T(8,128)(2,1)S(1)} %pad_maximum_fusion.4), channel_id=1, source_target_pairs={{0,192},{64,0},{128,64},{192,128},{1,193},{65,1},{129,65},{193,129... | collective-permute-start | bytes 1474568 | tf_op jit(solution)/shard_map/ppermute | solution.py:12
  76.4 1.0 bitcast_bitcast_fusion
  77.4 3.5 %all-to-all-start.1 = ((f32[4,400,128]{2,1,0:T(8,128)}), f32[4,400,128]{2,1,0:T(8,128)S(1)}, u32[]{:S(2)}, u32[]{:S(2)}) async-start(f32[4,400,128]{2,1,0:T(8,128)} %bitcast_bitcast_fusion), calls=%async_computation.1 | async-start | bytes 1638400 | tf_op jit(solution)/shard_map/all_to_all | solution.py:45
  80.9 2.8 %fusion.28 = f32[240,512]{1,0:T(8,128)S(1)} fusion(f32[240,512]{1,0:T(8,128)} %collective-permute-done.16, bf16[240,2048]{1,0:T(8,128)(2,1)} %copy-done.4, bf16[2048,1024]{0,1:T(8,128)(2,1)} %convert_bitcast_fusion), kind=kOutput, calls=%fused_computation.26 | convolution fusion | flops 503439360 | bytes 4063232 | tf_op jit(solution)/shard_map/dot_general | solution.py:41
  83.8 2.8 %collective-permute-done.14 = bf16[120,2048]{1,0:T(8,128)(2,1)S(1)} collective-permute-done((bf16[120,2048]{1,0:T(8,128)(2,1)S(1)}, bf16[120,2048]{1,0:T(8,128)(2,1)S(1)}, u32[]{:S(2)}, u32[]{:S(2)}) %collective-permute-start.14) | collective-permute-done | bytes 491552 | tf_op jit(solution)/shard_map/ppermute | solution.py:12
  86.7 1.5 %fusion.6 = f32[240,512]{1,0:T(8,128)} fusion(bf16[240,2048]{1,0:T(8,128)(2,1)S(1)} %constant_dynamic-update-slice_fusion.13, bf16[2048,1024]{0,1:T(8,128)(2,1)S(1)} %copy-done.8), kind=kOutput, calls=%fused_computation.8 | convolution fusion | flops 503316480 | bytes 3571712 | tf_op jit(solution)/shard_map/dot_general | solution.py:40
  88.3 1.0 fusion.42
  89.4 0.8 bitcast_bitcast_fusion.2
  90.2 2.2 %all-to-all-done.1 = f32[4,400,128]{2,1,0:T(8,128)S(1)} async-done(((f32[4,400,128]{2,1,0:T(8,128)}), f32[4,400,128]{2,1,0:T(8,128)S(1)}, u32[]{:S(2)}, u32[]{:S(2)}) %all-to-all-start.1) | async-done | bytes 819232 | tf_op jit(solution)/shard_map/all_to_all | solution.py:45
  92.4 3.5 %all-to-all-start.2 = ((f32[4,240,128]{2,1,0:T(8,128)}), f32[4,240,128]{2,1,0:T(8,128)S(1)}, u32[]{:S(2)}, u32[]{:S(2)}) async-start(f32[4,240,128]{2,1,0:T(8,128)} %bitcast_bitcast_fusion.2), calls=%async_computation.2 | async-start | bytes 983040 | tf_op jit(solution)/shard_map/all_to_all | solution.py:45
  95.9 1.8 %collective-permute-start.13 = (f32[400,128]{1,0:T(8,128)S(1)}, f32[400,128]{1,0:T(8,128)S(1)}, u32[]{:S(2)}, u32[]{:S(2)}) collective-permute-start(f32[400,128]{1,0:T(8,128)S(1)} %reduce_sum.28), channel_id=1, source_target_pairs={{0,2},{2,0},{1,3},{3,1},{4,6},{6,4},{5,7},{7,5},{8,10},{10,8},{9,1... | collective-permute-start | bytes 614408 | tf_op jit(solution)/shard_map/ppermute | solution.py:20
  97.8 2.3 %fusion.31 = f32[240,512]{1,0:T(8,128)S(1)} fusion(f32[240,512]{1,0:T(8,128)S(1)} %collective-permute-done.18, bf16[240,2048]{1,0:T(8,128)(2,1)S(1)} %constant_dynamic-update-slice_fusion.13, bf16[2048,1024]{0,1:T(8,128)(2,1)} %convert_bitcast_fusion), kind=kOutput, calls=%fused_computation.27 | convolution fusion | flops 503439360 | bytes 4063232 | tf_op jit(solution)/shard_map/dot_general | solution.py:41
  100.2 3.6 %collective-permute-start.21 = (f32[240,128]{1,0:T(8,128)S(1)}, f32[240,128]{1,0:T(8,128)S(1)}, u32[]{:S(2)}, u32[]{:S(2)}) collective-permute-start(f32[240,128]{1,0:T(8,128)S(1)} %get-tuple-element.24), channel_id=1, source_target_pairs={{0,8},{4,12},{8,0},{12,4},{1,9},{5,13},{9,1},{13,5},{2,10},{6,14},... | collective-permute-start | bytes 368648 | tf_op jit(solution)/shard_map/ppermute | solution.py:12
  103.7 1.2 collective-permute-start.20
  104.9 0.9 collective-permute-start.19
  105.9 2.2 %collective-permute-start.17 = (f32[240,128]{1,0:T(8,128)S(1)}, f32[240,128]{1,0:T(8,128)S(1)}, u32[]{:S(2)}, u32[]{:S(2)}) collective-permute-start(f32[240,128]{1,0:T(8,128)S(1)} %reduce_sum.29), channel_id=1, source_target_pairs={{0,2},{2,0},{1,3},{3,1},{4,6},{6,4},{5,7},{7,5},{8,10},{10,8},{9,1... | collective-permute-start | bytes 368648 | tf_op jit(solution)/shard_map/ppermute | solution.py:20
  108.2 0.4 collective-permute-done.20
  108.6 2.4 %collective-permute-done.19 = f32[240,128]{1,0:T(8,128)S(1)} collective-permute-done((f32[240,128]{1,0:T(8,128)S(1)}, f32[240,128]{1,0:T(8,128)S(1)}, u32[]{:S(2)}, u32[]{:S(2)}) %collective-permute-start.19) | collective-permute-done | bytes 122912 | tf_op jit(solution)/shard_map/ppermute | solution.py:12
  111.0 0.4 collective-permute-start.22
  111.5 4.5 %collective-permute-done.22 = f32[240,128]{1,0:T(8,128)S(1)} collective-permute-done((f32[240,128]{1,0:T(8,128)S(1)}, f32[240,128]{1,0:T(8,128)S(1)}, u32[]{:S(2)}, u32[]{:S(2)}) %collective-permute-start.22) | collective-permute-done | bytes 122912 | tf_op jit(solution)/shard_map/ppermute | solution.py:20
  116.1 2.2 %fusion.3 = bf16[64,1280]{1,0:T(8,128)(2,1)} fusion(s32[1280]{0:T(1024)S(1)} %concatenate.48, bf16[240,64]{1,0:T(8,128)(2,1)S(1)} %fusion.43, bf16[240,64]{1,0:T(8,128)(2,1)S(1)} %fusion.44, bf16[400,64]{1,0:T(8,128)(2,1)S(1)} %fusion.41, bf16[400,64]{1,0:T(8,128)(2,1)S(1)} %fusion.42), kind=kOutput, calls=%fused_computation.6 | convolution fusion | flops 212090880 | bytes 332800 | tf_op jit(solution)/shard_map/dot_general | solution.py:89
  (81 shorter events, 1.7 us)
Async XLA Ops:
  0.0 17.6 %collective-permute-start.5 = (bf16[80,2048]{1,0:T(8,128)(2,1)}, bf16[80,2048]{1,0:T(8,128)(2,1)S(1)}, u32[]{:S(2)}, u32[]{:S(2)}) collective-permute-start(bf16[80,2048]{1,0:T(8,128)(2,1)} %param.2), channel_id=1, source_target_pairs={{0,192},{64,0},{128,64},{192,128},{1,193},{65,1},{129,65},{193,129... | collective-permute-start | bytes 983048 | tf_op jit(solution)/shard_map/ppermute | solution.py:12
  2.8 18.4 %collective-permute-start.2 = (bf16[80,2048]{1,0:T(8,128)(2,1)}, bf16[80,2048]{1,0:T(8,128)(2,1)S(1)}, u32[]{:S(2)}, u32[]{:S(2)}) collective-permute-start(bf16[80,2048]{1,0:T(8,128)(2,1)} %param.2), channel_id=1, source_target_pairs={{0,16},{16,32},{32,48},{48,0},{1,17},{17,33},{33,49},{49,1},{2,18}... | collective-permute-start | bytes 983048 | tf_op jit(solution)/shard_map/ppermute | solution.py:12
  7.2 18.1 %collective-permute-start = (bf16[80,2048]{1,0:T(8,128)(2,1)}, bf16[80,2048]{1,0:T(8,128)(2,1)S(1)}, u32[]{:S(2)}, u32[]{:S(2)}) collective-permute-start(bf16[80,2048]{1,0:T(8,128)(2,1)} %param.2), channel_id=1, source_target_pairs={{0,48},{16,0},{32,16},{48,32},{1,49},{17,1},{33,17},{49,33},{2,50}... | collective-permute-start | bytes 983048 | tf_op jit(solution)/shard_map/ppermute | solution.py:12
  7.2 10.3 %collective-permute-start.4 = (bf16[80,2048]{1,0:T(8,128)(2,1)}, bf16[80,2048]{1,0:T(8,128)(2,1)S(1)}, u32[]{:S(2)}, u32[]{:S(2)}) collective-permute-start(bf16[80,2048]{1,0:T(8,128)(2,1)} %param.2), channel_id=1, source_target_pairs={{0,64},{64,128},{128,192},{192,0},{1,65},{65,129},{129,193},{193,1... | collective-permute-start | bytes 983048 | tf_op jit(solution)/shard_map/ppermute | solution.py:12
  7.3 8.4 %copy-start.2 = (bf16[80,2048]{1,0:T(8,128)(2,1)S(1)}, bf16[80,2048]{1,0:T(8,128)(2,1)}, u32[]{:S(2)}) copy-start(bf16[80,2048]{1,0:T(8,128)(2,1)} %param.2) | copy-start | bytes 983044
  26.2 1.2 copy-start.5
  27.4 17.1 %collective-permute-start.8 = (bf16[160,2048]{1,0:T(8,128)(2,1)}, bf16[160,2048]{1,0:T(8,128)(2,1)S(1)}, u32[]{:S(2)}, u32[]{:S(2)}) collective-permute-start(bf16[160,2048]{1,0:T(8,128)(2,1)} %get-tuple-element.26), channel_id=1, source_target_pairs={{0,64},{64,128},{128,192},{192,0},{1,65},{65,129},{129,193},{193,1... | collective-permute-start | bytes 1966088 | tf_op jit(solution)/shard_map/ppermute | solution.py:12
  27.4 17.1 %collective-permute-start.10 = (bf16[160,2048]{1,0:T(8,128)(2,1)}, bf16[160,2048]{1,0:T(8,128)(2,1)S(1)}, u32[]{:S(2)}, u32[]{:S(2)}) collective-permute-start(bf16[160,2048]{1,0:T(8,128)(2,1)} %get-tuple-element.26), channel_id=1, source_target_pairs={{0,192},{64,0},{128,64},{192,128},{1,193},{65,1},{129,65},{193,129... | collective-permute-start | bytes 1966088 | tf_op jit(solution)/shard_map/ppermute | solution.py:12
  30.6 8.6 %collective-permute-start.3 = (bf16[40,2048]{1,0:T(8,128)(2,1)S(1)}, bf16[40,2048]{1,0:T(8,128)(2,1)S(1)}, u32[]{:S(2)}, u32[]{:S(2)}) collective-permute-start(bf16[40,2048]{1,0:T(8,128)(2,1)S(1)} %slice.73), channel_id=1, source_target_pairs={{0,16},{16,32},{32,48},{48,0},{1,17},{17,33},{33,49},{49,1},{2,18}... | collective-permute-start | bytes 491528 | tf_op jit(solution)/shard_map/ppermute | solution.py:12
  31.8 8.6 %collective-permute-start.1 = (bf16[40,2048]{1,0:T(8,128)(2,1)S(1)}, bf16[40,2048]{1,0:T(8,128)(2,1)S(1)}, u32[]{:S(2)}, u32[]{:S(2)}) collective-permute-start(bf16[40,2048]{1,0:T(8,128)(2,1)S(1)} %slice.72), channel_id=1, source_target_pairs={{0,48},{16,0},{32,16},{48,32},{1,49},{17,1},{33,17},{49,33},{2,50}... | collective-permute-start | bytes 491528 | tf_op jit(solution)/shard_map/ppermute | solution.py:12
  33.7 10.9 %copy-start.7 = (bf16[2048,1024]{0,1:T(8,128)(2,1)S(1)}, bf16[2048,1024]{0,1:T(8,128)(2,1)}, u32[]{:S(2)}) copy-start(bf16[2048,1024]{0,1:T(8,128)(2,1)} %convert_bitcast_fusion) | copy-start | bytes 12582916
  37.0 7.6 %collective-permute-start.6 = (f32[400,512]{1,0:T(8,128)S(1)}, f32[400,512]{1,0:T(8,128)S(1)}, u32[]{:S(2)}, u32[]{:S(2)}) collective-permute-start(f32[400,512]{1,0:T(8,128)S(1)} %fusion.12), channel_id=1, source_target_pairs={{0,1},{1,0},{2,3},{3,2},{4,5},{5,4},{6,7},{7,6},{8,9},{9,8},{10,11... | collective-permute-start | bytes 2457608 | tf_op jit(solution)/shard_map/ppermute | solution.py:20
  37.1 7.5 %copy-start.6 = (bf16[400,2048]{1,0:T(8,128)(2,1)S(1)}, bf16[400,2048]{1,0:T(8,128)(2,1)}, u32[]{:S(2)}) copy-start(bf16[400,2048]{1,0:T(8,128)(2,1)} %copy-done.5) | copy-start | bytes 4915204
  44.4 3.5 %copy-start = (bf16[160,2048]{1,0:T(8,128)(2,1)}, bf16[160,2048]{1,0:T(8,128)(2,1)S(1)}, u32[]{:S(2)}) copy-start(bf16[160,2048]{1,0:T(8,128)(2,1)S(1)} %collective-permute-done.8) | copy-start | bytes 1966084
  44.5 3.5 %copy-start.1 = (bf16[160,2048]{1,0:T(8,128)(2,1)}, bf16[160,2048]{1,0:T(8,128)(2,1)S(1)}, u32[]{:S(2)}) copy-start(bf16[160,2048]{1,0:T(8,128)(2,1)S(1)} %collective-permute-done.10) | copy-start | bytes 1966084
  44.6 1.4 %copy-start.3 = (bf16[400,2048]{1,0:T(8,128)(2,1)}, bf16[400,2048]{1,0:T(8,128)(2,1)S(1)}, u32[]{:S(2)}) copy-start(bf16[400,2048]{1,0:T(8,128)(2,1)S(1)} %constant_dynamic-update-slice_fusion.7) | copy-start | bytes 4915204
  45.7 12.9 %collective-permute-start.9 = (bf16[120,2048]{1,0:T(8,128)(2,1)}, bf16[120,2048]{1,0:T(8,128)(2,1)S(1)}, u32[]{:S(2)}, u32[]{:S(2)}) collective-permute-start(bf16[120,2048]{1,0:T(8,128)(2,1)} %get-tuple-element.15), channel_id=1, source_target_pairs={{0,64},{64,128},{128,192},{192,0},{1,65},{65,129},{129,193},{193,1... | collective-permute-start | bytes 1474568 | tf_op jit(solution)/shard_map/ppermute | solution.py:12
  48.0 21.8 %collective-permute-start.12 = (f32[400,512]{1,0:T(8,128)}, f32[400,512]{1,0:T(8,128)}, u32[]{:S(2)}, u32[]{:S(2)}) collective-permute-start(f32[400,512]{1,0:T(8,128)} %fusion.10), channel_id=1, source_target_pairs={{0,1},{1,0},{2,3},{3,2},{4,5},{5,4},{6,7},{7,6},{8,9},{9,8},{10,11... | collective-permute-start | bytes 2457608 | tf_op jit(solution)/shard_map/ppermute | solution.py:20
  48.0 14.4 %collective-permute-start.11 = (bf16[120,2048]{1,0:T(8,128)(2,1)S(1)}, bf16[120,2048]{1,0:T(8,128)(2,1)S(1)}, u32[]{:S(2)}, u32[]{:S(2)}) collective-permute-start(bf16[120,2048]{1,0:T(8,128)(2,1)S(1)} %get-tuple-element.16), channel_id=1, source_target_pairs={{0,192},{64,0},{128,64},{192,128},{1,193},{65,1},{129,65},{193,129... | collective-permute-start | bytes 1474568 | tf_op jit(solution)/shard_map/ppermute | solution.py:12
  52.2 17.4 %all-to-all-start = ((f32[4,400,128]{2,1,0:T(8,128)}), f32[4,400,128]{2,1,0:T(8,128)S(1)}, u32[]{:S(2)}, u32[]{:S(2)}) async-start(f32[4,400,128]{2,1,0:T(8,128)} %bitcast_bitcast_fusion.1), calls=%async_computation | async-start | bytes 1638400 | tf_op jit(solution)/shard_map/all_to_all | solution.py:45
  62.4 3.5 %copy-start.4 = (bf16[240,2048]{1,0:T(8,128)(2,1)}, bf16[240,2048]{1,0:T(8,128)(2,1)S(1)}, u32[]{:S(2)}) copy-start(bf16[240,2048]{1,0:T(8,128)(2,1)S(1)} %constant_dynamic-update-slice_fusion.11) | copy-start | bytes 2949124
  62.4 3.6 %slice-start = ((bf16[160,2048]{1,0:T(8,128)(2,1)}), bf16[80,2048]{1,0:T(8,128)(2,1)S(1)}, s32[]{:S(2)}) async-start(bf16[160,2048]{1,0:T(8,128)(2,1)} %copy-done), calls=%async_computation.3 | async-start | bytes 655360 | tf_op jit(solution)/shard_map/slice | solution.py:72
  62.4 3.6 %slice-start.1 = ((bf16[160,2048]{1,0:T(8,128)(2,1)}), bf16[80,2048]{1,0:T(8,128)(2,1)S(1)}, s32[]{:S(2)}) async-start(bf16[160,2048]{1,0:T(8,128)(2,1)} %copy-done.1), calls=%async_computation.4 | async-start | bytes 655360 | tf_op jit(solution)/shard_map/slice | solution.py:72
  65.9 15.0 %collective-permute-start.16 = (f32[240,512]{1,0:T(8,128)}, f32[240,512]{1,0:T(8,128)}, u32[]{:S(2)}, u32[]{:S(2)}) collective-permute-start(f32[240,512]{1,0:T(8,128)} %fusion.8), channel_id=1, source_target_pairs={{0,1},{1,0},{2,3},{3,2},{4,5},{5,4},{6,7},{7,6},{8,9},{9,8},{10,11... | collective-permute-start | bytes 1474568 | tf_op jit(solution)/shard_map/ppermute | solution.py:20
  69.7 18.6 %collective-permute-start.7 = (f32[400,128]{1,0:T(8,128)S(1)}, f32[400,128]{1,0:T(8,128)}, u32[]{:S(2)}, u32[]{:S(2)}) collective-permute-start(f32[400,128]{1,0:T(8,128)S(1)} %reduce_sum.27), channel_id=1, source_target_pairs={{0,2},{2,0},{1,3},{3,1},{4,6},{6,4},{5,7},{7,5},{8,10},{10,8},{9,1... | collective-permute-start | bytes 614408 | tf_op jit(solution)/shard_map/ppermute | solution.py:20
  73.1 13.4 %collective-permute-start.14 = (bf16[120,2048]{1,0:T(8,128)(2,1)S(1)}, bf16[120,2048]{1,0:T(8,128)(2,1)S(1)}, u32[]{:S(2)}, u32[]{:S(2)}) collective-permute-start(bf16[120,2048]{1,0:T(8,128)(2,1)S(1)} %pad_maximum_fusion.3), channel_id=1, source_target_pairs={{0,64},{64,128},{128,192},{192,0},{1,65},{65,129},{129,193},{193,1... | collective-permute-start | bytes 1474568 | tf_op jit(solution)/shard_map/ppermute | solution.py:12
  73.2 13.3 %collective-permute-start.15 = (bf16[120,2048]{1,0:T(8,128)(2,1)S(1)}, bf16[120,2048]{1,0:T(8,128)(2,1)S(1)}, u32[]{:S(2)}, u32[]{:S(2)}) collective-permute-start(bf16[120,2048]{1,0:T(8,128)(2,1)S(1)} %pad_maximum_fusion.4), channel_id=1, source_target_pairs={{0,192},{64,0},{128,64},{192,128},{1,193},{65,1},{129,65},{193,129... | collective-permute-start | bytes 1474568 | tf_op jit(solution)/shard_map/ppermute | solution.py:12
  77.4 15.0 %all-to-all-start.1 = ((f32[4,400,128]{2,1,0:T(8,128)}), f32[4,400,128]{2,1,0:T(8,128)S(1)}, u32[]{:S(2)}, u32[]{:S(2)}) async-start(f32[4,400,128]{2,1,0:T(8,128)} %bitcast_bitcast_fusion), calls=%async_computation.1 | async-start | bytes 1638400 | tf_op jit(solution)/shard_map/all_to_all | solution.py:45
  80.9 5.7 %copy-start.8 = (bf16[2048,1024]{0,1:T(8,128)(2,1)S(1)}, bf16[2048,1024]{0,1:T(8,128)(2,1)}, u32[]{:S(2)}) copy-start(bf16[2048,1024]{0,1:T(8,128)(2,1)} %convert_bitcast_fusion) | copy-start | bytes 12582916
  88.2 9.6 %collective-permute-start.18 = (f32[240,512]{1,0:T(8,128)}, f32[240,512]{1,0:T(8,128)S(1)}, u32[]{:S(2)}, u32[]{:S(2)}) collective-permute-start(f32[240,512]{1,0:T(8,128)} %fusion.6), channel_id=1, source_target_pairs={{0,1},{1,0},{2,3},{3,2},{4,5},{5,4},{6,7},{7,6},{8,9},{9,8},{10,11... | collective-permute-start | bytes 1474568 | tf_op jit(solution)/shard_map/ppermute | solution.py:20
  92.4 13.5 %all-to-all-start.2 = ((f32[4,240,128]{2,1,0:T(8,128)}), f32[4,240,128]{2,1,0:T(8,128)S(1)}, u32[]{:S(2)}, u32[]{:S(2)}) async-start(f32[4,240,128]{2,1,0:T(8,128)} %bitcast_bitcast_fusion.2), calls=%async_computation.2 | async-start | bytes 983040 | tf_op jit(solution)/shard_map/all_to_all | solution.py:45
  95.9 9.8 %collective-permute-start.13 = (f32[400,128]{1,0:T(8,128)S(1)}, f32[400,128]{1,0:T(8,128)S(1)}, u32[]{:S(2)}, u32[]{:S(2)}) collective-permute-start(f32[400,128]{1,0:T(8,128)S(1)} %reduce_sum.28), channel_id=1, source_target_pairs={{0,2},{2,0},{1,3},{3,1},{4,6},{6,4},{5,7},{7,5},{8,10},{10,8},{9,1... | collective-permute-start | bytes 614408 | tf_op jit(solution)/shard_map/ppermute | solution.py:20
  100.2 8.0 %collective-permute-start.21 = (f32[240,128]{1,0:T(8,128)S(1)}, f32[240,128]{1,0:T(8,128)S(1)}, u32[]{:S(2)}, u32[]{:S(2)}) collective-permute-start(f32[240,128]{1,0:T(8,128)S(1)} %get-tuple-element.24), channel_id=1, source_target_pairs={{0,8},{4,12},{8,0},{12,4},{1,9},{5,13},{9,1},{13,5},{2,10},{6,14},... | collective-permute-start | bytes 368648 | tf_op jit(solution)/shard_map/ppermute | solution.py:12
  103.7 4.9 %collective-permute-start.20 = (f32[240,128]{1,0:T(8,128)S(1)}, f32[240,128]{1,0:T(8,128)S(1)}, u32[]{:S(2)}, u32[]{:S(2)}) collective-permute-start(f32[240,128]{1,0:T(8,128)S(1)} %get-tuple-element.25), channel_id=1, source_target_pairs={{0,12},{4,0},{8,4},{12,8},{1,13},{5,1},{9,5},{13,9},{2,14},{6,2},{... | collective-permute-start | bytes 368648 | tf_op jit(solution)/shard_map/ppermute | solution.py:12
  104.9 6.1 %collective-permute-start.19 = (f32[240,128]{1,0:T(8,128)S(1)}, f32[240,128]{1,0:T(8,128)S(1)}, u32[]{:S(2)}, u32[]{:S(2)}) collective-permute-start(f32[240,128]{1,0:T(8,128)S(1)} %get-tuple-element.23), channel_id=1, source_target_pairs={{0,4},{4,8},{8,12},{12,0},{1,5},{5,9},{9,13},{13,1},{2,6},{6,10},{... | collective-permute-start | bytes 368648 | tf_op jit(solution)/shard_map/ppermute | solution.py:12
  105.9 5.5 %collective-permute-start.17 = (f32[240,128]{1,0:T(8,128)S(1)}, f32[240,128]{1,0:T(8,128)S(1)}, u32[]{:S(2)}, u32[]{:S(2)}) collective-permute-start(f32[240,128]{1,0:T(8,128)S(1)} %reduce_sum.29), channel_id=1, source_target_pairs={{0,2},{2,0},{1,3},{3,1},{4,6},{6,4},{5,7},{7,5},{8,10},{10,8},{9,1... | collective-permute-start | bytes 368648 | tf_op jit(solution)/shard_map/ppermute | solution.py:20
  111.0 5.0 %collective-permute-start.22 = (f32[240,128]{1,0:T(8,128)S(1)}, f32[240,128]{1,0:T(8,128)S(1)}, u32[]{:S(2)}, u32[]{:S(2)}) collective-permute-start(f32[240,128]{1,0:T(8,128)S(1)} %add_add_fusion), channel_id=1, source_target_pairs={{0,2},{2,0},{1,3},{3,1},{4,6},{6,4},{5,7},{7,5},{8,10},{10,8},{9,1... | collective-permute-start | bytes 368648 | tf_op jit(solution)/shard_map/ppermute | solution.py:20

commit v4 on v3

v4 whole, which is shorter than its diff:
```python
import jax
import jax.numpy as jnp
from jax import lax
from jax.sharding import Mesh, PartitionSpec as P

ROWS = 80
F32 = jnp.float32
BF16 = jnp.bfloat16


def shift(value, axis, size, by):
    return lax.ppermute(value, axis, [(i, (i + by) % size) for i in range(size)])


def to_both(value, axis):
    return shift(value, axis, 4, 1), shift(value, axis, 4, -1)


def swap(value, axis):
    return lax.ppermute(value, axis, [(0, 1), (1, 0)])


def dot(left, right):
    return jnp.dot(left, right, preferred_element_type=F32)


def joined(*parts):
    return jnp.concatenate(parts, axis=0)


def local(amplitudes, integrals):
    x, zh, y, zl, core = (lax.axis_index(n) for n in ("x", "zh", "y", "zl", "core"))

    at = jnp.arange(1024)
    owner = jnp.where(at < 512, 1 - core, core)
    level = jnp.where(at & 64 == 0, zl, 1 - zl)
    source = ((at >> 7) & 3) * 256 + level * 128 + owner * 64 + (at & 63)

    def over_y(pair):
        split = pair.reshape(pair.shape[0], 4, 128).transpose(1, 0, 2)
        return jnp.sum(lax.all_to_all(split, "y", split_axis=0, concat_axis=0, tiled=True), axis=0)

    def over_y_at_once(pair):
        part = lambda d: lax.dynamic_slice_in_dim(pair, ((y + d) % 4) * 128, 128, axis=1)
        others = [shift(part(d), "y", 4, d) for d in (1, 3, 2)]
        return part(0) + others[0] + others[1] + others[2]

    def over_zl(some):
        return (some[:, :64] + swap(some, "zl")[:, 64:]).astype(BF16)

    def block(dx, dz, first=0, count=ROWS):
        start = (((x + dx) % 4) * 4 + (zh + dz) % 4) * ROWS + first
        return start + jnp.arange(count)

    own = amplitudes
    zm, zp = to_both(own, "zh")
    own, source = lax.optimization_barrier((own, source))
    order = (jnp.arange(1024)[:, None] == source[None, :]).astype(BF16)
    columns = dot(integrals, order).astype(BF16)
    own_xm, own_xp = to_both(own, "x")
    theirs, mine = columns[:, :512], columns[:, 512:]

    side = joined(zm, zp)
    side_xm, side_xp = to_both(side, "x")
    far = joined(shift(zp[:40], "zh", 4, -1), shift(zm[40:], "zh", 4, 1))
    early = joined(own, own_xm, own_xp, side)
    early_sum = dot(early, mine) + swap(dot(early, theirs), "core")

    late = joined(side_xm, side_xp)
    after_xm, after_xp, early_sum, away = lax.optimization_barrier(
        (joined(far, own_xm[40:]), joined(far, own_xp[:40]), early_sum, dot(late, theirs))
    )
    from_xm, from_xp = shift(after_xm, "x", 4, 1), shift(after_xp, "x", 4, -1)
    away = joined(swap(away[:160], "core"), swap(away[160:], "core"))
    late_sum = dot(late, mine) + away
    after_xm, after_xp, early_sum, late_sum = lax.optimization_barrier(
        (joined(side_xm[80:], from_xm[40:80]), joined(side_xp[:80], from_xp[:40]), early_sum, late_sum)
    )
    last_xm, last_xp = shift(after_xm, "x", 4, 1), shift(after_xp, "x", 4, -1)
    rows = joined(far, from_xm, from_xp)
    second = dot(rows, mine) + swap(dot(rows, theirs), "core")
    last_xm, last_xp, second = lax.optimization_barrier((last_xm, last_xp, second))
    rows = joined(last_xm, last_xp)
    third = dot(rows, mine) + swap(dot(rows, theirs), "core")

    sums = [over_zl(over_y(pair)) for pair in (joined(early_sum, late_sum), second)]
    sums.append(over_zl(over_y_at_once(third)))
    sites = [
        [block(0, 0), block(-1, 0), block(1, 0), block(0, -1), block(0, 1)],
        [block(-1, -1), block(-1, 1), block(1, -1), block(1, 1)],
        [block(0, 2), block(-1, 2), block(2, 0, 40, 40), block(1, 2), block(2, 0, 0, 40)],
        [block(2, 1), block(2, 2, 40, 40), block(2, -1), block(2, 2, 0, 40)],
    ]
    places = joined(*[p for ps in sites for p in ps])
    place = (places[:, None] == jnp.arange(1280)[None, :]).astype(BF16)
    turned = lax.dot_general(
        joined(*sums), place, (((0,), (0,)), ((), ())), preferred_element_type=F32
    )
    return turned.astype(BF16)


def solution(mesh):
    split = Mesh(mesh.devices.reshape(4, 4, 4, 2, 2), ("x", "zh", "y", "zl", "core"))
    row, col = ("x", "zh"), ("y", "zl", "core")
    return jax.shard_map(
        local,
        mesh=split,
        in_specs=(P(row, col), P(col, row)),
        out_specs=P(row + col, None),
        check_vma=False,
    )
```

time: 119 us -> 121 us (1.017)
  waiting for transfers between devices: 36.7 us -> 50 us
  matrix products: 30.4 us -> 23.9 us
  starting transfers between devices: 42.1 us -> 36.8 us
  other arithmetic: 2.51 us -> 3.78 us
    all_to_all x3 -> x2, waiting for transfers between devices: 5.82 us -> 14.2 us  [over_y(): lax.all_to_all(split, 'y', split_axis=0, concat_axis=0, tiled=True)]
    dot_general x9, matrix products: 28.2 us -> 21.7 us  [dot(): return jnp.dot(left, right, preferred_element_type=F32)]
    ppermute x8, starting transfers between devices: 4.64 us -> 1.15 us  [swap(): return lax.ppermute(value, axis, [(0, 1), (1, 0)])]
    all_to_all x3 -> x2, starting transfers between devices: 11.4 us -> 7.95 us  [over_y(): lax.all_to_all(split, 'y', split_axis=0, concat_axis=0, tiled=True)]
    ppermute x15, waiting for transfers between devices: 26.4 us -> 29.3 us  [shift(): lax.ppermute(value, axis, [(i, (i + by) % size) for i in range(size)])]
    ppermute x8, waiting for transfers between devices: 4.49 us -> 6.49 us  [swap(): return lax.ppermute(value, axis, [(0, 1), (1, 0)])]
    transpose x3 -> x1, local copies, waits for them, and re-layouts: 2.75 us -> 0.88 us  [over_y(): split = pair.reshape(pair.shape[0], 4, 128).transpose(1, 0, 2)]
    ppermute x15, starting transfers between devices: 26 us -> 27.7 us  [shift(): lax.ppermute(value, axis, [(i, (i + by) % size) for i in range(size)])]
  transfers between devices with their start and end apart: 26 -> 25, of which waited for: 14 -> 12; matrix products, arithmetic and copies ran while one was open for 28% -> 22% of each run, Pallas kernels for 0% -> 0%
where the time goes in v4:
time: 121 us
  waiting for transfers between devices  50 us (41%)
  starting transfers between devices  36.8 us (30%)
  matrix products  23.9 us (20%)
  local copies, waits for them, and re-layouts  5.92 us (5%)
  other arithmetic  3.78 us (3%)
    ppermute x15, waiting for transfers between devices, shift(): lax.ppermute(value, axis, [(i, (i + by) % size) for i in range(size)])  29.3 us
    ppermute x15, starting transfers between devices, shift(): lax.ppermute(value, axis, [(i, (i + by) % size) for i in range(size)])  27.7 us
    dot_general x9, matrix products, dot(): return jnp.dot(left, right, preferred_element_type=F32)  21.7 us
    all_to_all x2, waiting for transfers between devices, over_y(): lax.all_to_all(split, 'y', split_axis=0, concat_axis=0, tiled=True)  14.2 us
    all_to_all x2, starting transfers between devices, over_y(): lax.all_to_all(split, 'y', split_axis=0, concat_axis=0, tiled=True)  7.95 us
    ppermute x8, waiting for transfers between devices, swap(): return lax.ppermute(value, axis, [(0, 1), (1, 0)])  6.49 us
    unnamed x27, local copies, waits for them, and re-layouts  2.66 us
  transfers between devices with their start and end apart: 25, of which 12 were waited for; matrix products, arithmetic and copies ran while one was open for 22% of the time, Pallas kernels for 0%

profile of v4, /device:TPU:64, one launch (start us, length us, event | category | flops | bytes accessed | tf_op | source)
XLA Modules:
  0.0 121.0 jit_solution(3343402780275633260)
XLA Ops:
  0.0 1.6 %collective-permute-start.5 = (bf16[80,2048]{1,0:T(8,128)(2,1)}, bf16[80,2048]{1,0:T(8,128)(2,1)S(1)}, u32[]{:S(2)}, u32[]{:S(2)}) collective-permute-start(bf16[80,2048]{1,0:T(8,128)(2,1)} %param.2), channel_id=1, source_target_pairs={{0,64},{64,128},{128,192},{192,0},{1,65},{65,129},{129,193},{193,1... | collective-permute-start | bytes 983048 | tf_op jit(solution)/shard_map/ppermute | solution.py:12
  1.6 1.7 %collective-permute-start.6 = (bf16[80,2048]{1,0:T(8,128)(2,1)}, bf16[80,2048]{1,0:T(8,128)(2,1)S(1)}, u32[]{:S(2)}, u32[]{:S(2)}) collective-permute-start(bf16[80,2048]{1,0:T(8,128)(2,1)} %param.2), channel_id=1, source_target_pairs={{0,192},{64,0},{128,64},{192,128},{1,193},{65,1},{129,65},{193,129... | collective-permute-start | bytes 983048 | tf_op jit(solution)/shard_map/ppermute | solution.py:12
  3.3 4.5 %collective-permute-start = (bf16[80,2048]{1,0:T(8,128)(2,1)}, bf16[80,2048]{1,0:T(8,128)(2,1)S(1)}, u32[]{:S(2)}, u32[]{:S(2)}) collective-permute-start(bf16[80,2048]{1,0:T(8,128)(2,1)} %param.2), channel_id=1, source_target_pairs={{0,16},{16,32},{32,48},{48,0},{1,17},{17,33},{33,49},{49,1},{2,18}... | collective-permute-start | bytes 983048 | tf_op jit(solution)/shard_map/ppermute | solution.py:12
  7.9 8.4 %convert_bitcast_fusion = bf16[2048,1024]{0,1:T(8,128)(2,1)} fusion(bf16[2048,1024]{1,0:T(8,128)(2,1)} %param.3, s32[1024]{0:T(1024)S(1)} %and_add_fusion), kind=kOutput, calls=%fused_computation.2 | convolution fusion | flops 4299161600 | bytes 8392704 | tf_op jit(solution)/shard_map/dot_general | solution.py:24
  16.4 5.1 %collective-permute-done = bf16[80,2048]{1,0:T(8,128)(2,1)S(1)} collective-permute-done((bf16[80,2048]{1,0:T(8,128)(2,1)}, bf16[80,2048]{1,0:T(8,128)(2,1)S(1)}, u32[]{:S(2)}, u32[]{:S(2)}) %collective-permute-start) | collective-permute-done | bytes 327712 | tf_op jit(solution)/shard_map/ppermute | solution.py:12
  21.5 4.2 %collective-permute-done.1 = bf16[80,2048]{1,0:T(8,128)(2,1)S(1)} collective-permute-done((bf16[80,2048]{1,0:T(8,128)(2,1)}, bf16[80,2048]{1,0:T(8,128)(2,1)S(1)}, u32[]{:S(2)}, u32[]{:S(2)}) %collective-permute-start.1) | collective-permute-done | bytes 327712 | tf_op jit(solution)/shard_map/ppermute | solution.py:12
  25.7 1.1 copy-done.4
  26.9 0.3 collective-permute-start.2
  27.2 3.0 %collective-permute-start.8 = (bf16[160,2048]{1,0:T(8,128)(2,1)S(1)}, bf16[160,2048]{1,0:T(8,128)(2,1)S(1)}, u32[]{:S(2)}, u32[]{:S(2)}) collective-permute-start(bf16[160,2048]{1,0:T(8,128)(2,1)S(1)} %get-tuple-element.36), channel_id=1, source_target_pairs={{0,192},{64,0},{128,64},{192,128},{1,193},{65,1},{129,65},{193,129... | collective-permute-start | bytes 1966088 | tf_op jit(solution)/shard_map/ppermute | solution.py:12
  30.3 4.2 %collective-permute-start.4 = (bf16[40,2048]{1,0:T(8,128)(2,1)S(1)}, bf16[40,2048]{1,0:T(8,128)(2,1)S(1)}, u32[]{:S(2)}, u32[]{:S(2)}) collective-permute-start(bf16[40,2048]{1,0:T(8,128)(2,1)S(1)} %slice.74), channel_id=1, source_target_pairs={{0,16},{16,32},{32,48},{48,0},{1,17},{17,33},{33,49},{49,1},{2,18}... | collective-permute-start | bytes 491528 | tf_op jit(solution)/shard_map/ppermute | solution.py:12
  34.4 3.1 %fusion.12 = f32[400,512]{1,0:T(8,128)S(1)} fusion(bf16[400,2048]{1,0:T(8,128)(2,1)} %copy-done.4, bf16[2048,1024]{0,1:T(8,128)(2,1)} %convert_bitcast_fusion), kind=kOutput, calls=%fused_computation.16 | convolution fusion | flops 838860800 | bytes 4554752 | tf_op jit(solution)/shard_map/dot_general | solution.py:24
  37.6 0.3 collective-permute-start.7
  37.9 0.5 collective-permute-done.4
  38.5 5.3 %collective-permute-done.2 = bf16[160,2048]{1,0:T(8,128)(2,1)S(1)} collective-permute-done((bf16[160,2048]{1,0:T(8,128)(2,1)S(1)}, bf16[160,2048]{1,0:T(8,128)(2,1)S(1)}, u32[]{:S(2)}, u32[]{:S(2)}) %collective-permute-start.2) | collective-permute-done | bytes 655392 | tf_op jit(solution)/shard_map/ppermute | solution.py:12
  43.9 0.9 fusion.10
  44.8 0.9 copy-done.5
  45.7 1.0 fusion.28
  46.9 3.3 %collective-permute-start.10 = (bf16[120,2048]{1,0:T(8,128)(2,1)S(1)}, bf16[120,2048]{1,0:T(8,128)(2,1)S(1)}, u32[]{:S(2)}, u32[]{:S(2)}) collective-permute-start(bf16[120,2048]{1,0:T(8,128)(2,1)S(1)} %get-tuple-element.21), channel_id=1, source_target_pairs={{0,192},{64,0},{128,64},{192,128},{1,193},{65,1},{129,65},{193,129... | collective-permute-start | bytes 1474568 | tf_op jit(solution)/shard_map/ppermute | solution.py:12
  50.3 0.5 collective-permute-start.12
  50.8 8.4 %collective-permute-done.9 = bf16[120,2048]{1,0:T(8,128)(2,1)S(1)} collective-permute-done((bf16[120,2048]{1,0:T(8,128)(2,1)S(1)}, bf16[120,2048]{1,0:T(8,128)(2,1)S(1)}, u32[]{:S(2)}, u32[]{:S(2)}) %collective-permute-start.9) | collective-permute-done | bytes 491552 | tf_op jit(solution)/shard_map/ppermute | solution.py:12
  59.3 0.9 fusion.8
  60.2 0.2 copy-done.6
  60.4 0.9 fusion.22
  61.4 0.9 slice-done
  62.3 0.9 pad_maximum_fusion.3
  63.1 0.7 collective-permute-start.14
  63.8 2.6 %collective-permute-start.15 = (bf16[120,2048]{1,0:T(8,128)(2,1)S(1)}, bf16[120,2048]{1,0:T(8,128)(2,1)}, u32[]{:S(2)}, u32[]{:S(2)}) collective-permute-start(bf16[120,2048]{1,0:T(8,128)(2,1)S(1)} %pad_maximum_fusion.4), channel_id=1, source_target_pairs={{0,192},{64,0},{128,64},{192,128},{1,193},{65,1},{129,65},{193,129... | collective-permute-start | bytes 1474568 | tf_op jit(solution)/shard_map/ppermute | solution.py:12
  66.4 1.2 %bitcast_bitcast_fusion = f32[4,720,128]{2,1,0:T(8,128)} fusion(f32[320,512]{1,0:T(8,128)S(1)} %fusion.22, f32[400,512]{1,0:T(8,128)S(1)} %fusion.28), kind=kLoop, calls=%fused_computation.8 | loop fusion | flops 368640 | bytes 2949120 | tf_op jit(solution)/shard_map/transpose | solution.py:40
  67.6 4.5 %all-to-all-start = ((f32[4,720,128]{2,1,0:T(8,128)}), f32[4,720,128]{2,1,0:T(8,128)S(1)}, u32[]{:S(2)}, u32[]{:S(2)}) async-start(f32[4,720,128]{2,1,0:T(8,128)} %bitcast_bitcast_fusion), calls=%async_computation | async-start | bytes 2949120 | tf_op jit(solution)/shard_map/all_to_all | solution.py:41
  72.1 3.1 %fusion.25 = f32[320,512]{1,0:T(8,128)S(1)} fusion(f32[320,512]{1,0:T(8,128)} %collective-permute-done.16, bf16[320,2048]{1,0:T(8,128)(2,1)} %copy-done.6, bf16[2048,1024]{0,1:T(8,128)(2,1)} %convert_bitcast_fusion), kind=kOutput, calls=%fused_computation.27 | convolution fusion | flops 671252480 | bytes 4718592 | tf_op jit(solution)/shard_map/dot_general | solution.py:24
  75.2 3.0 %collective-permute-done.14 = bf16[120,2048]{1,0:T(8,128)(2,1)S(1)} collective-permute-done((bf16[120,2048]{1,0:T(8,128)(2,1)}, bf16[120,2048]{1,0:T(8,128)(2,1)S(1)}, u32[]{:S(2)}, u32[]{:S(2)}) %collective-permute-start.14) | collective-permute-done | bytes 491552 | tf_op jit(solution)/shard_map/ppermute | solution.py:12
  78.3 1.1 constant_dynamic-update-slice_fusion.13
  79.3 0.7 fusion.6
  80.1 0.2 copy-done.3
  80.3 0.9 bitcast_bitcast_fusion.1
  81.2 10.7 %all-to-all-done = f32[4,720,128]{2,1,0:T(8,128)S(1)} async-done(((f32[4,720,128]{2,1,0:T(8,128)}), f32[4,720,128]{2,1,0:T(8,128)S(1)}, u32[]{:S(2)}, u32[]{:S(2)}) %all-to-all-start) | async-done | bytes 1474592 | tf_op jit(solution)/shard_map/all_to_all | solution.py:41
  91.9 3.5 %all-to-all-start.1 = ((f32[4,320,128]{2,1,0:T(8,128)}), f32[4,320,128]{2,1,0:T(8,128)S(1)}, u32[]{:S(2)}, u32[]{:S(2)}) async-start(f32[4,320,128]{2,1,0:T(8,128)} %bitcast_bitcast_fusion.1), calls=%async_computation.1 | async-start | bytes 1310720 | tf_op jit(solution)/shard_map/all_to_all | solution.py:41
  95.4 2.6 %fusion.31 = f32[240,512]{1,0:T(8,128)S(1)} fusion(f32[240,512]{1,0:T(8,128)S(1)} %collective-permute-done.18, bf16[240,2048]{1,0:T(8,128)(2,1)} %copy-done.3, bf16[2048,1024]{0,1:T(8,128)(2,1)} %convert_bitcast_fusion), kind=kOutput, calls=%fused_computation.29 | convolution fusion | flops 503439360 | bytes 4063232 | tf_op jit(solution)/shard_map/dot_general | solution.py:24
  98.1 2.3 %collective-permute-start.19 = (f32[240,128]{1,0:T(8,128)S(1)}, f32[240,128]{1,0:T(8,128)S(1)}, u32[]{:S(2)}, u32[]{:S(2)}) collective-permute-start(f32[240,128]{1,0:T(8,128)S(1)} %get-tuple-element.33), channel_id=1, source_target_pairs={{0,4},{4,8},{8,12},{12,0},{1,5},{5,9},{9,13},{13,1},{2,6},{6,10},{... | collective-permute-start | bytes 368648 | tf_op jit(solution)/shard_map/ppermute | solution.py:12
  100.4 1.3 %collective-permute-start.20 = (f32[240,128]{1,0:T(8,128)S(1)}, f32[240,128]{1,0:T(8,128)}, u32[]{:S(2)}, u32[]{:S(2)}) collective-permute-start(f32[240,128]{1,0:T(8,128)S(1)} %get-tuple-element.35), channel_id=1, source_target_pairs={{0,12},{4,0},{8,4},{12,8},{1,13},{5,1},{9,5},{13,9},{2,14},{6,2},{... | collective-permute-start | bytes 368648 | tf_op jit(solution)/shard_map/ppermute | solution.py:12
  101.7 2.2 %collective-permute-start.21 = (f32[240,128]{1,0:T(8,128)S(1)}, f32[240,128]{1,0:T(8,128)}, u32[]{:S(2)}, u32[]{:S(2)}) collective-permute-start(f32[240,128]{1,0:T(8,128)S(1)} %get-tuple-element.34), channel_id=1, source_target_pairs={{0,8},{4,12},{8,0},{12,4},{1,9},{5,13},{9,1},{13,5},{2,10},{6,14},... | collective-permute-start | bytes 368648 | tf_op jit(solution)/shard_map/ppermute | solution.py:12
  104.2 3.5 %all-to-all-done.1 = f32[4,320,128]{2,1,0:T(8,128)S(1)} async-done(((f32[4,320,128]{2,1,0:T(8,128)}), f32[4,320,128]{2,1,0:T(8,128)S(1)}, u32[]{:S(2)}, u32[]{:S(2)}) %all-to-all-start.1) | async-done | bytes 655392 | tf_op jit(solution)/shard_map/all_to_all | solution.py:41
  107.9 1.5 %collective-permute-done.19 = f32[240,128]{1,0:T(8,128)S(1)} collective-permute-done((f32[240,128]{1,0:T(8,128)S(1)}, f32[240,128]{1,0:T(8,128)S(1)}, u32[]{:S(2)}, u32[]{:S(2)}) %collective-permute-start.19) | collective-permute-done | bytes 122912 | tf_op jit(solution)/shard_map/ppermute | solution.py:12
  109.4 1.4 %collective-permute-done.21 = f32[240,128]{1,0:T(8,128)} collective-permute-done((f32[240,128]{1,0:T(8,128)S(1)}, f32[240,128]{1,0:T(8,128)}, u32[]{:S(2)}, u32[]{:S(2)}) %collective-permute-start.21) | collective-permute-done | bytes 122912 | tf_op jit(solution)/shard_map/ppermute | solution.py:12
  110.8 1.0 add_add_fusion
  111.9 5.3 %collective-permute-done.17 = f32[320,128]{1,0:T(8,128)S(1)} collective-permute-done((f32[320,128]{1,0:T(8,128)S(1)}, f32[320,128]{1,0:T(8,128)S(1)}, u32[]{:S(2)}, u32[]{:S(2)}) %collective-permute-start.17) | collective-permute-done | bytes 163872 | tf_op jit(solution)/shard_map/ppermute | solution.py:20
  117.3 1.2 collective-permute-done.22
  118.8 2.2 %fusion.3 = bf16[64,1280]{1,0:T(8,128)(2,1)} fusion(s32[1280]{0:T(1024)S(1)} %concatenate.56, bf16[240,64]{1,0:T(8,128)(2,1)S(1)} %fusion.41, bf16[320,64]{1,0:T(8,128)(2,1)S(1)} %fusion.40, bf16[720,64]{1,0:T(8,128)(2,1)S(1)} %fusion.34), kind=kOutput, calls=%fused_computation.6 | convolution fusion | flops 211927040 | bytes 332800 | tf_op jit(solution)/shard_map/dot_general | solution.py:96
  (77 shorter events, 2.0 us)
Async XLA Ops:
  0.0 16.3 %collective-permute-start.5 = (bf16[80,2048]{1,0:T(8,128)(2,1)}, bf16[80,2048]{1,0:T(8,128)(2,1)S(1)}, u32[]{:S(2)}, u32[]{:S(2)}) collective-permute-start(bf16[80,2048]{1,0:T(8,128)(2,1)} %param.2), channel_id=1, source_target_pairs={{0,64},{64,128},{128,192},{192,0},{1,65},{65,129},{129,193},{193,1... | collective-permute-start | bytes 983048 | tf_op jit(solution)/shard_map/ppermute | solution.py:12
  1.6 14.8 %collective-permute-start.6 = (bf16[80,2048]{1,0:T(8,128)(2,1)}, bf16[80,2048]{1,0:T(8,128)(2,1)S(1)}, u32[]{:S(2)}, u32[]{:S(2)}) collective-permute-start(bf16[80,2048]{1,0:T(8,128)(2,1)} %param.2), channel_id=1, source_target_pairs={{0,192},{64,0},{128,64},{192,128},{1,193},{65,1},{129,65},{193,129... | collective-permute-start | bytes 983048 | tf_op jit(solution)/shard_map/ppermute | solution.py:12
  3.3 18.1 %collective-permute-start = (bf16[80,2048]{1,0:T(8,128)(2,1)}, bf16[80,2048]{1,0:T(8,128)(2,1)S(1)}, u32[]{:S(2)}, u32[]{:S(2)}) collective-permute-start(bf16[80,2048]{1,0:T(8,128)(2,1)} %param.2), channel_id=1, source_target_pairs={{0,16},{16,32},{32,48},{48,0},{1,17},{17,33},{33,49},{49,1},{2,18}... | collective-permute-start | bytes 983048 | tf_op jit(solution)/shard_map/ppermute | solution.py:12
  7.8 17.9 %collective-permute-start.1 = (bf16[80,2048]{1,0:T(8,128)(2,1)}, bf16[80,2048]{1,0:T(8,128)(2,1)S(1)}, u32[]{:S(2)}, u32[]{:S(2)}) collective-permute-start(bf16[80,2048]{1,0:T(8,128)(2,1)} %param.2), channel_id=1, source_target_pairs={{0,48},{16,0},{32,16},{48,32},{1,49},{17,1},{33,17},{49,33},{2,50}... | collective-permute-start | bytes 983048 | tf_op jit(solution)/shard_map/ppermute | solution.py:12
  7.8 8.4 %copy-start.2 = (bf16[80,2048]{1,0:T(8,128)(2,1)S(1)}, bf16[80,2048]{1,0:T(8,128)(2,1)}, u32[]{:S(2)}) copy-start(bf16[80,2048]{1,0:T(8,128)(2,1)} %param.2) | copy-start | bytes 983044
  25.7 1.2 copy-start.4
  26.9 16.9 %collective-permute-start.2 = (bf16[160,2048]{1,0:T(8,128)(2,1)S(1)}, bf16[160,2048]{1,0:T(8,128)(2,1)S(1)}, u32[]{:S(2)}, u32[]{:S(2)}) collective-permute-start(bf16[160,2048]{1,0:T(8,128)(2,1)S(1)} %get-tuple-element.36), channel_id=1, source_target_pairs={{0,64},{64,128},{128,192},{192,0},{1,65},{65,129},{129,193},{193,1... | collective-permute-start | bytes 1966088 | tf_op jit(solution)/shard_map/ppermute | solution.py:12
  27.2 16.6 %collective-permute-start.8 = (bf16[160,2048]{1,0:T(8,128)(2,1)S(1)}, bf16[160,2048]{1,0:T(8,128)(2,1)S(1)}, u32[]{:S(2)}, u32[]{:S(2)}) collective-permute-start(bf16[160,2048]{1,0:T(8,128)(2,1)S(1)} %get-tuple-element.36), channel_id=1, source_target_pairs={{0,192},{64,0},{128,64},{192,128},{1,193},{65,1},{129,65},{193,129... | collective-permute-start | bytes 1966088 | tf_op jit(solution)/shard_map/ppermute | solution.py:12
  30.1 7.8 %collective-permute-start.3 = (bf16[40,2048]{1,0:T(8,128)(2,1)S(1)}, bf16[40,2048]{1,0:T(8,128)(2,1)S(1)}, u32[]{:S(2)}, u32[]{:S(2)}) collective-permute-start(bf16[40,2048]{1,0:T(8,128)(2,1)S(1)} %slice.73), channel_id=1, source_target_pairs={{0,48},{16,0},{32,16},{48,32},{1,49},{17,1},{33,17},{49,33},{2,50}... | collective-permute-start | bytes 491528 | tf_op jit(solution)/shard_map/ppermute | solution.py:12
  30.3 8.1 %collective-permute-start.4 = (bf16[40,2048]{1,0:T(8,128)(2,1)S(1)}, bf16[40,2048]{1,0:T(8,128)(2,1)S(1)}, u32[]{:S(2)}, u32[]{:S(2)}) collective-permute-start(bf16[40,2048]{1,0:T(8,128)(2,1)S(1)} %slice.74), channel_id=1, source_target_pairs={{0,16},{16,32},{32,48},{48,0},{1,17},{17,33},{33,49},{49,1},{2,18}... | collective-permute-start | bytes 491528 | tf_op jit(solution)/shard_map/ppermute | solution.py:12
  37.6 7.2 %collective-permute-start.7 = (f32[400,512]{1,0:T(8,128)S(1)}, f32[400,512]{1,0:T(8,128)S(1)}, u32[]{:S(2)}, u32[]{:S(2)}) collective-permute-start(f32[400,512]{1,0:T(8,128)S(1)} %fusion.12), channel_id=1, source_target_pairs={{0,1},{1,0},{2,3},{3,2},{4,5},{5,4},{6,7},{7,6},{8,9},{9,8},{10,11... | collective-permute-start | bytes 2457608 | tf_op jit(solution)/shard_map/ppermute | solution.py:20
  38.4 5.5 %copy-start.7 = (bf16[2048,1024]{0,1:T(8,128)(2,1)S(1)}, bf16[2048,1024]{0,1:T(8,128)(2,1)}, u32[]{:S(2)}) copy-start(bf16[2048,1024]{0,1:T(8,128)(2,1)} %convert_bitcast_fusion) | copy-start | bytes 12582916
  43.8 6.4 %copy-start = (bf16[160,2048]{1,0:T(8,128)(2,1)}, bf16[160,2048]{1,0:T(8,128)(2,1)S(1)}, u32[]{:S(2)}) copy-start(bf16[160,2048]{1,0:T(8,128)(2,1)S(1)} %collective-permute-done.2) | copy-start | bytes 1966084
  43.8 6.3 %copy-start.1 = (bf16[160,2048]{1,0:T(8,128)(2,1)}, bf16[160,2048]{1,0:T(8,128)(2,1)S(1)}, u32[]{:S(2)}) copy-start(bf16[160,2048]{1,0:T(8,128)(2,1)S(1)} %collective-permute-done.8) | copy-start | bytes 1966084
  43.9 1.8 %copy-start.5 = (bf16[400,2048]{1,0:T(8,128)(2,1)S(1)}, bf16[400,2048]{1,0:T(8,128)(2,1)}, u32[]{:S(2)}) copy-start(bf16[400,2048]{1,0:T(8,128)(2,1)} %copy-done.4) | copy-start | bytes 4915204
  46.7 12.5 %collective-permute-start.9 = (bf16[120,2048]{1,0:T(8,128)(2,1)S(1)}, bf16[120,2048]{1,0:T(8,128)(2,1)S(1)}, u32[]{:S(2)}, u32[]{:S(2)}) collective-permute-start(bf16[120,2048]{1,0:T(8,128)(2,1)S(1)} %get-tuple-element.20), channel_id=1, source_target_pairs={{0,64},{64,128},{128,192},{192,0},{1,65},{65,129},{129,193},{193,1... | collective-permute-start | bytes 1474568 | tf_op jit(solution)/shard_map/ppermute | solution.py:12
  46.9 12.4 %collective-permute-start.10 = (bf16[120,2048]{1,0:T(8,128)(2,1)S(1)}, bf16[120,2048]{1,0:T(8,128)(2,1)S(1)}, u32[]{:S(2)}, u32[]{:S(2)}) collective-permute-start(bf16[120,2048]{1,0:T(8,128)(2,1)S(1)} %get-tuple-element.21), channel_id=1, source_target_pairs={{0,192},{64,0},{128,64},{192,128},{1,193},{65,1},{129,65},{193,129... | collective-permute-start | bytes 1474568 | tf_op jit(solution)/shard_map/ppermute | solution.py:12
  50.2 10.2 %collective-permute-start.11 = (f32[160,512]{1,0:T(8,128)S(1)}, f32[160,512]{1,0:T(8,128)S(1)}, u32[]{:S(2)}, u32[]{:S(2)}) collective-permute-start(f32[160,512]{1,0:T(8,128)S(1)} %get-tuple-element.31), channel_id=1, source_target_pairs={{0,1},{1,0},{2,3},{3,2},{4,5},{5,4},{6,7},{7,6},{8,9},{9,8},{10,11... | collective-permute-start | bytes 983048 | tf_op jit(solution)/shard_map/ppermute | solution.py:20
  50.3 10.1 %collective-permute-start.12 = (f32[160,512]{1,0:T(8,128)S(1)}, f32[160,512]{1,0:T(8,128)S(1)}, u32[]{:S(2)}, u32[]{:S(2)}) collective-permute-start(f32[160,512]{1,0:T(8,128)S(1)} %get-tuple-element.32), channel_id=1, source_target_pairs={{0,1},{1,0},{2,3},{3,2},{4,5},{5,4},{6,7},{7,6},{8,9},{9,8},{10,11... | collective-permute-start | bytes 983048 | tf_op jit(solution)/shard_map/ppermute | solution.py:20
  59.3 1.1 copy-start.6
  60.4 1.0 slice-start.1
  60.4 11.7 %collective-permute-start.16 = (f32[320,512]{1,0:T(8,128)S(1)}, f32[320,512]{1,0:T(8,128)}, u32[]{:S(2)}, u32[]{:S(2)}) collective-permute-start(f32[320,512]{1,0:T(8,128)S(1)} %fusion.8), channel_id=1, source_target_pairs={{0,1},{1,0},{2,3},{3,2},{4,5},{5,4},{6,7},{7,6},{8,9},{9,8},{10,11... | collective-permute-start | bytes 1966088 | tf_op jit(solution)/shard_map/ppermute | solution.py:20
  61.3 1.0 slice-start
  63.1 15.1 %collective-permute-start.14 = (bf16[120,2048]{1,0:T(8,128)(2,1)}, bf16[120,2048]{1,0:T(8,128)(2,1)S(1)}, u32[]{:S(2)}, u32[]{:S(2)}) collective-permute-start(bf16[120,2048]{1,0:T(8,128)(2,1)} %pad_maximum_fusion.3), channel_id=1, source_target_pairs={{0,64},{64,128},{128,192},{192,0},{1,65},{65,129},{129,193},{193,1... | collective-permute-start | bytes 1474568 | tf_op jit(solution)/shard_map/ppermute | solution.py:12
  63.8 14.4 %collective-permute-start.15 = (bf16[120,2048]{1,0:T(8,128)(2,1)S(1)}, bf16[120,2048]{1,0:T(8,128)(2,1)}, u32[]{:S(2)}, u32[]{:S(2)}) collective-permute-start(bf16[120,2048]{1,0:T(8,128)(2,1)S(1)} %pad_maximum_fusion.4), channel_id=1, source_target_pairs={{0,192},{64,0},{128,64},{192,128},{1,193},{65,1},{129,65},{193,129... | collective-permute-start | bytes 1474568 | tf_op jit(solution)/shard_map/ppermute | solution.py:12
  67.6 24.2 %all-to-all-start = ((f32[4,720,128]{2,1,0:T(8,128)}), f32[4,720,128]{2,1,0:T(8,128)S(1)}, u32[]{:S(2)}, u32[]{:S(2)}) async-start(f32[4,720,128]{2,1,0:T(8,128)} %bitcast_bitcast_fusion), calls=%async_computation | async-start | bytes 2949120 | tf_op jit(solution)/shard_map/all_to_all | solution.py:41
  72.1 7.2 %copy-start.8 = (bf16[2048,1024]{0,1:T(8,128)(2,1)S(1)}, bf16[2048,1024]{0,1:T(8,128)(2,1)}, u32[]{:S(2)}) copy-start(bf16[2048,1024]{0,1:T(8,128)(2,1)} %convert_bitcast_fusion) | copy-start | bytes 12582916
  79.3 1.0 copy-start.3
  80.3 15.1 %collective-permute-start.18 = (f32[240,512]{1,0:T(8,128)S(1)}, f32[240,512]{1,0:T(8,128)S(1)}, u32[]{:S(2)}, u32[]{:S(2)}) collective-permute-start(f32[240,512]{1,0:T(8,128)S(1)} %fusion.6), channel_id=1, source_target_pairs={{0,1},{1,0},{2,3},{3,2},{4,5},{5,4},{6,7},{7,6},{8,9},{9,8},{10,11... | collective-permute-start | bytes 1474568 | tf_op jit(solution)/shard_map/ppermute | solution.py:20
  91.9 15.9 %all-to-all-start.1 = ((f32[4,320,128]{2,1,0:T(8,128)}), f32[4,320,128]{2,1,0:T(8,128)S(1)}, u32[]{:S(2)}, u32[]{:S(2)}) async-start(f32[4,320,128]{2,1,0:T(8,128)} %bitcast_bitcast_fusion.1), calls=%async_computation.1 | async-start | bytes 1310720 | tf_op jit(solution)/shard_map/all_to_all | solution.py:41
  98.1 11.3 %collective-permute-start.19 = (f32[240,128]{1,0:T(8,128)S(1)}, f32[240,128]{1,0:T(8,128)S(1)}, u32[]{:S(2)}, u32[]{:S(2)}) collective-permute-start(f32[240,128]{1,0:T(8,128)S(1)} %get-tuple-element.33), channel_id=1, source_target_pairs={{0,4},{4,8},{8,12},{12,0},{1,5},{5,9},{9,13},{13,1},{2,6},{6,10},{... | collective-permute-start | bytes 368648 | tf_op jit(solution)/shard_map/ppermute | solution.py:12
  100.4 9.0 %collective-permute-start.20 = (f32[240,128]{1,0:T(8,128)S(1)}, f32[240,128]{1,0:T(8,128)}, u32[]{:S(2)}, u32[]{:S(2)}) collective-permute-start(f32[240,128]{1,0:T(8,128)S(1)} %get-tuple-element.35), channel_id=1, source_target_pairs={{0,12},{4,0},{8,4},{12,8},{1,13},{5,1},{9,5},{13,9},{2,14},{6,2},{... | collective-permute-start | bytes 368648 | tf_op jit(solution)/shard_map/ppermute | solution.py:12
  101.7 9.1 %collective-permute-start.21 = (f32[240,128]{1,0:T(8,128)S(1)}, f32[240,128]{1,0:T(8,128)}, u32[]{:S(2)}, u32[]{:S(2)}) collective-permute-start(f32[240,128]{1,0:T(8,128)S(1)} %get-tuple-element.34), channel_id=1, source_target_pairs={{0,8},{4,12},{8,0},{12,4},{1,9},{5,13},{9,1},{13,5},{2,10},{6,14},... | collective-permute-start | bytes 368648 | tf_op jit(solution)/shard_map/ppermute | solution.py:12
  104.1 14.5 %collective-permute-start.13 = (f32[720,128]{1,0:T(8,128)S(1)}, f32[720,128]{1,0:T(8,128)S(1)}, u32[]{:S(2)}, u32[]{:S(2)}) collective-permute-start(f32[720,128]{1,0:T(8,128)S(1)} %reduce_sum.18), channel_id=1, source_target_pairs={{0,2},{2,0},{1,3},{3,1},{4,6},{6,4},{5,7},{7,5},{8,10},{10,8},{9,1... | collective-permute-start | bytes 1105928 | tf_op jit(solution)/shard_map/ppermute | solution.py:20
  107.8 9.4 %collective-permute-start.17 = (f32[320,128]{1,0:T(8,128)S(1)}, f32[320,128]{1,0:T(8,128)S(1)}, u32[]{:S(2)}, u32[]{:S(2)}) collective-permute-start(f32[320,128]{1,0:T(8,128)S(1)} %reduce_sum.19), channel_id=1, source_target_pairs={{0,2},{2,0},{1,3},{3,1},{4,6},{6,4},{5,7},{7,5},{8,10},{10,8},{9,1... | collective-permute-start | bytes 491528 | tf_op jit(solution)/shard_map/ppermute | solution.py:20
  111.8 6.7 %collective-permute-start.22 = (f32[240,128]{1,0:T(8,128)S(1)}, f32[240,128]{1,0:T(8,128)S(1)}, u32[]{:S(2)}, u32[]{:S(2)}) collective-permute-start(f32[240,128]{1,0:T(8,128)S(1)} %add_add_fusion), channel_id=1, source_target_pairs={{0,2},{2,0},{1,3},{3,1},{4,6},{6,4},{5,7},{7,5},{8,10},{10,8},{9,1... | collective-permute-start | bytes 368648 | tf_op jit(solution)/shard_map/ppermute | solution.py:20

commit v5 on v4

--- a/solution.py
+++ b/solution.py
@@ -54,37 +54,37 @@
 
     own = amplitudes
     zm, zp = to_both(own, "zh")
-    own, source = lax.optimization_barrier((own, source))
+    own_xm, own_xp = to_both(own, "x")
     order = (jnp.arange(1024)[:, None] == source[None, :]).astype(BF16)
     columns = dot(integrals, order).astype(BF16)
-    own_xm, own_xp = to_both(own, "x")
     theirs, mine = columns[:, :512], columns[:, 512:]
 
-    side = joined(zm, zp)
+    def paired(rows):
+        return dot(rows, mine) + swap(dot(rows, theirs), "core")
+
+    side, own_xm, own_xp = lax.optimization_barrier((joined(zm, zp), own_xm, own_xp))
     side_xm, side_xp = to_both(side, "x")
     far = joined(shift(zp[:40], "zh", 4, -1), shift(zm[40:], "zh", 4, 1))
-    early = joined(own, own_xm, own_xp, side)
-    early_sum = dot(early, mine) + swap(dot(early, theirs), "core")
+    early = paired(joined(own, own_xm, own_xp, side))
 
-    late = joined(side_xm, side_xp)
-    after_xm, after_xp, early_sum, away = lax.optimization_barrier(
-        (joined(far, own_xm[40:]), joined(far, own_xp[:40]), early_sum, dot(late, theirs))
+    after_xm, after_xp, early = lax.optimization_barrier(
+        (joined(far, own_xm[40:]), joined(far, own_xp[:40]), early)
     )
     from_xm, from_xp = shift(after_xm, "x", 4, 1), shift(after_xp, "x", 4, -1)
-    away = joined(swap(away[:160], "core"), swap(away[160:], "core"))
-    late_sum = dot(late, mine) + away
-    after_xm, after_xp, early_sum, late_sum = lax.optimization_barrier(
-        (joined(side_xm[80:], from_xm[40:80]), joined(side_xp[:80], from_xp[:40]), early_sum, late_sum)
+    side_xm, side_xp, early = lax.optimization_barrier((side_xm, side_xp, early))
+    early = over_y(early)
+    late = paired(joined(side_xm, side_xp))
+    from_xm, from_xp, late = lax.optimization_barrier((from_xm, from_xp, late))
+    after_xm, after_xp, early = lax.optimization_barrier(
+        (joined(side_xm[80:], from_xm[40:80]), joined(side_xp[:80], from_xp[:40]), early)
     )
     last_xm, last_xp = shift(after_xm, "x", 4, 1), shift(after_xp, "x", 4, -1)
-    rows = joined(far, from_xm, from_xp)
-    second = dot(rows, mine) + swap(dot(rows, theirs), "core")
+    late = over_y(late)
+    second = paired(joined(far, from_xm, from_xp))
     last_xm, last_xp, second = lax.optimization_barrier((last_xm, last_xp, second))
-    rows = joined(last_xm, last_xp)
-    third = dot(rows, mine) + swap(dot(rows, theirs), "core")
-
-    sums = [over_zl(over_y(pair)) for pair in (joined(early_sum, late_sum), second)]
-    sums.append(over_zl(over_y_at_once(third)))
+    second = over_y(second)
+    third = over_y_at_once(paired(joined(last_xm, last_xp)))
+    sums = [over_zl(part) for part in (joined(early, late), second, third)]
     sites = [
         [block(0, 0), block(-1, 0), block(1, 0), block(0, -1), block(0, 1)],
         [block(-1, -1), block(-1, 1), block(1, -1), block(1, 1)],

time: 121 us -> 125 us (1.033)
  waiting for transfers between devices: 50 us -> 37.1 us
  matrix products: 23.9 us -> 32.2 us
  starting transfers between devices: 36.8 us -> 43.3 us
  local copies, waits for them, and re-layouts: 5.92 us -> 9.1 us
    dot_general x9, matrix products: 21.7 us -> 30 us  [dot(): return jnp.dot(left, right, preferred_element_type=F32)]
    all_to_all x2 -> x3, waiting for transfers between devices: 14.2 us -> 7.45 us  [over_y(): lax.all_to_all(split, 'y', split_axis=0, concat_axis=0, tiled=True)]
    all_to_all x2 -> x3, starting transfers between devices: 7.95 us -> 12.4 us  [over_y(): lax.all_to_all(split, 'y', split_axis=0, concat_axis=0, tiled=True)]
    ppermute x8 -> x7, waiting for transfers between devices: 6.49 us -> 3.4 us  [swap(): return lax.ppermute(value, axis, [(0, 1), (1, 0)])]
    ppermute x15, waiting for transfers between devices: 29.3 us -> 26.3 us  [shift(): lax.ppermute(value, axis, [(i, (i + by) % size) for i in range(size)])]
    ppermute x8 -> x7, starting transfers between devices: 1.15 us -> 3.67 us  [swap(): return lax.ppermute(value, axis, [(0, 1), (1, 0)])]
    unnamed x27 -> x34, local copies, waits for them, and re-layouts: 2.66 us -> 4.89 us
    transpose x1 -> x3, local copies, waits for them, and re-layouts: 0.88 us -> 2.75 us  [over_y(): split = pair.reshape(pair.shape[0], 4, 128).transpose(1, 0, 2)]
  transfers between devices with their start and end apart: 25 -> 25, of which waited for: 12 -> 14; matrix products, arithmetic and copies ran while one was open for 22% -> 26% of each run, Pallas kernels for 0% -> 0%
where the time goes in v5:
time: 125 us
  starting transfers between devices  43.3 us (35%)
  waiting for transfers between devices  37.1 us (30%)
  matrix products  32.2 us (26%)
  local copies, waits for them, and re-layouts  9.1 us (7%)
  other arithmetic  2.78 us (2%)
    dot_general x9, matrix products, dot(): return jnp.dot(left, right, preferred_element_type=F32)  30 us
    ppermute x15, starting transfers between devices, shift(): lax.ppermute(value, axis, [(i, (i + by) % size) for i in range(size)])  27.2 us
    ppermute x15, waiting for transfers between devices, shift(): lax.ppermute(value, axis, [(i, (i + by) % size) for i in range(size)])  26.3 us
    all_to_all x3, starting transfers between devices, over_y(): lax.all_to_all(split, 'y', split_axis=0, concat_axis=0, tiled=True)  12.4 us
    all_to_all x3, waiting for transfers between devices, over_y(): lax.all_to_all(split, 'y', split_axis=0, concat_axis=0, tiled=True)  7.45 us
    unnamed x34, local copies, waits for them, and re-layouts  4.89 us
    ppermute x7, starting transfers between devices, swap(): return lax.ppermute(value, axis, [(0, 1), (1, 0)])  3.67 us
    ppermute x7, waiting for transfers between devices, swap(): return lax.ppermute(value, axis, [(0, 1), (1, 0)])  3.4 us
  transfers between devices with their start and end apart: 25, of which 14 were waited for; matrix products, arithmetic and copies ran while one was open for 26% of the time, Pallas kernels for 0%

profile of v5, /device:TPU:64, one launch (start us, length us, event | category | flops | bytes accessed | tf_op | source)
XLA Modules:
  0.0 124.9 jit_solution(2850051572615292316)
XLA Ops:
  0.0 4.5 %collective-permute-start = (bf16[80,2048]{1,0:T(8,128)(2,1)}, bf16[80,2048]{1,0:T(8,128)(2,1)S(1)}, u32[]{:S(2)}, u32[]{:S(2)}) collective-permute-start(bf16[80,2048]{1,0:T(8,128)(2,1)} %param.2), channel_id=1, source_target_pairs={{0,16},{16,32},{32,48},{48,0},{1,17},{17,33},{33,49},{49,1},{2,18}... | collective-permute-start | bytes 983048 | tf_op jit(solution)/shard_map/ppermute | solution.py:12
  4.5 1.5 %collective-permute-start.2 = (bf16[80,2048]{1,0:T(8,128)(2,1)}, bf16[80,2048]{1,0:T(8,128)(2,1)S(1)}, u32[]{:S(2)}, u32[]{:S(2)}) collective-permute-start(bf16[80,2048]{1,0:T(8,128)(2,1)} %param.2), channel_id=1, source_target_pairs={{0,64},{64,128},{128,192},{192,0},{1,65},{65,129},{129,193},{193,1... | collective-permute-start | bytes 983048 | tf_op jit(solution)/shard_map/ppermute | solution.py:12
  6.0 1.7 %collective-permute-start.3 = (bf16[80,2048]{1,0:T(8,128)(2,1)}, bf16[80,2048]{1,0:T(8,128)(2,1)S(1)}, u32[]{:S(2)}, u32[]{:S(2)}) collective-permute-start(bf16[80,2048]{1,0:T(8,128)(2,1)} %param.2), channel_id=1, source_target_pairs={{0,192},{64,0},{128,64},{192,128},{1,193},{65,1},{129,65},{193,129... | collective-permute-start | bytes 983048 | tf_op jit(solution)/shard_map/ppermute | solution.py:12
  7.7 8.4 %convert_bitcast_fusion = bf16[2048,1024]{0,1:T(8,128)(2,1)} fusion(bf16[2048,1024]{1,0:T(8,128)(2,1)} %param.3, s32[1024]{0:T(1024)S(1)} %and_add_fusion), kind=kOutput, calls=%fused_computation.2 | convolution fusion | flops 4299161600 | bytes 8392704 | tf_op jit(solution)/shard_map/dot_general | solution.py:24
  16.9 1.8 %collective-permute-done = bf16[80,2048]{1,0:T(8,128)(2,1)S(1)} collective-permute-done((bf16[80,2048]{1,0:T(8,128)(2,1)}, bf16[80,2048]{1,0:T(8,128)(2,1)S(1)}, u32[]{:S(2)}, u32[]{:S(2)}) %collective-permute-start) | collective-permute-done | bytes 327712 | tf_op jit(solution)/shard_map/ppermute | solution.py:12
  18.7 4.2 %collective-permute-done.1 = bf16[80,2048]{1,0:T(8,128)(2,1)S(1)} collective-permute-done((bf16[80,2048]{1,0:T(8,128)(2,1)}, bf16[80,2048]{1,0:T(8,128)(2,1)S(1)}, u32[]{:S(2)}, u32[]{:S(2)}) %collective-permute-start.1) | collective-permute-done | bytes 327712 | tf_op jit(solution)/shard_map/ppermute | solution.py:12
  23.0 0.8 constant_dynamic-update-slice_fusion.2
  23.8 0.8 constant_dynamic-update-slice_fusion.1
  24.5 0.9 constant_dynamic-update-slice_fusion
  25.4 4.0 %fusion.12 = f32[400,512]{1,0:T(8,128)} fusion(bf16[400,2048]{1,0:T(8,128)(2,1)} %constant_dynamic-update-slice_fusion, bf16[2048,1024]{0,1:T(8,128)(2,1)} %convert_bitcast_fusion), kind=kOutput, calls=%fused_computation.14 | convolution fusion | flops 838860800 | bytes 4554752 | tf_op jit(solution)/shard_map/dot_general | solution.py:24
  29.6 4.2 %collective-permute-start.7 = (bf16[40,2048]{1,0:T(8,128)(2,1)S(1)}, bf16[40,2048]{1,0:T(8,128)(2,1)S(1)}, u32[]{:S(2)}, u32[]{:S(2)}) collective-permute-start(bf16[40,2048]{1,0:T(8,128)(2,1)S(1)} %slice.65), channel_id=1, source_target_pairs={{0,16},{16,32},{32,48},{48,0},{1,17},{17,33},{33,49},{49,1},{2,18}... | collective-permute-start | bytes 491528 | tf_op jit(solution)/shard_map/ppermute | solution.py:12
  33.8 1.5 %collective-permute-start.4 = (bf16[160,2048]{1,0:T(8,128)(2,1)S(1)}, bf16[160,2048]{1,0:T(8,128)(2,1)S(1)}, u32[]{:S(2)}, u32[]{:S(2)}) collective-permute-start(bf16[160,2048]{1,0:T(8,128)(2,1)S(1)} %pad_maximum_fusion), channel_id=1, source_target_pairs={{0,64},{64,128},{128,192},{192,0},{1,65},{65,129},{129,193},{193,1... | collective-permute-start | bytes 1966088 | tf_op jit(solution)/shard_map/ppermute | solution.py:12
  35.3 1.7 %collective-permute-start.5 = (bf16[160,2048]{1,0:T(8,128)(2,1)S(1)}, bf16[160,2048]{1,0:T(8,128)(2,1)S(1)}, u32[]{:S(2)}, u32[]{:S(2)}) collective-permute-start(bf16[160,2048]{1,0:T(8,128)(2,1)S(1)} %pad_maximum_fusion), channel_id=1, source_target_pairs={{0,192},{64,0},{128,64},{192,128},{1,193},{65,1},{129,65},{193,129... | collective-permute-start | bytes 1966088 | tf_op jit(solution)/shard_map/ppermute | solution.py:12
  37.1 2.0 %collective-permute-done.6 = bf16[40,2048]{1,0:T(8,128)(2,1)S(1)} collective-permute-done((bf16[40,2048]{1,0:T(8,128)(2,1)S(1)}, bf16[40,2048]{1,0:T(8,128)(2,1)S(1)}, u32[]{:S(2)}, u32[]{:S(2)}) %collective-permute-start.6) | collective-permute-done | bytes 163872 | tf_op jit(solution)/shard_map/ppermute | solution.py:12
  39.1 1.6 %collective-permute-done.7 = bf16[40,2048]{1,0:T(8,128)(2,1)S(1)} collective-permute-done((bf16[40,2048]{1,0:T(8,128)(2,1)S(1)}, bf16[40,2048]{1,0:T(8,128)(2,1)S(1)}, u32[]{:S(2)}, u32[]{:S(2)}) %collective-permute-start.7) | collective-permute-done | bytes 163872 | tf_op jit(solution)/shard_map/ppermute | solution.py:12
  40.7 1.1 pad_maximum_fusion.3
  41.8 3.0 %fusion.28 = f32[400,512]{1,0:T(8,128)S(1)} fusion(f32[400,512]{1,0:T(8,128)} %collective-permute-done.8, bf16[400,2048]{1,0:T(8,128)(2,1)S(1)} %copy-done.7, bf16[2048,1024]{0,1:T(8,128)(2,1)} %convert_bitcast_fusion), kind=kOutput, calls=%fused_computation.26 | convolution fusion | flops 839065600 | bytes 5373952 | tf_op jit(solution)/shard_map/dot_general | solution.py:24
  44.8 6.8 %collective-permute-done.4 = bf16[160,2048]{1,0:T(8,128)(2,1)S(1)} collective-permute-done((bf16[160,2048]{1,0:T(8,128)(2,1)S(1)}, bf16[160,2048]{1,0:T(8,128)(2,1)S(1)}, u32[]{:S(2)}, u32[]{:S(2)}) %collective-permute-start.4) | collective-permute-done | bytes 655392 | tf_op jit(solution)/shard_map/ppermute | solution.py:12
  51.7 1.8 %fusion.10 = f32[320,512]{1,0:T(8,128)} fusion(bf16[320,2048]{1,0:T(8,128)(2,1)S(1)} %constant_dynamic-update-slice_fusion.4, bf16[2048,1024]{0,1:T(8,128)(2,1)S(1)} %copy-done.10), kind=kOutput, calls=%fused_computation.12 | convolution fusion | flops 671088640 | bytes 4063232 | tf_op jit(solution)/shard_map/dot_general | solution.py:24
  54.9 3.0 %collective-permute-start.10 = (bf16[120,2048]{1,0:T(8,128)(2,1)}, bf16[120,2048]{1,0:T(8,128)(2,1)S(1)}, u32[]{:S(2)}, u32[]{:S(2)}) collective-permute-start(bf16[120,2048]{1,0:T(8,128)(2,1)} %get-tuple-element.29), channel_id=1, source_target_pairs={{0,192},{64,0},{128,64},{192,128},{1,193},{65,1},{129,65},{193,129... | collective-permute-start | bytes 1474568 | tf_op jit(solution)/shard_map/ppermute | solution.py:12
  57.9 1.0 bitcast_bitcast_fusion
  58.8 4.5 %all-to-all-start = ((f32[4,400,128]{2,1,0:T(8,128)}), f32[4,400,128]{2,1,0:T(8,128)S(1)}, u32[]{:S(2)}, u32[]{:S(2)}) async-start(f32[4,400,128]{2,1,0:T(8,128)} %bitcast_bitcast_fusion), calls=%async_computation | async-start | bytes 1638400 | tf_op jit(solution)/shard_map/all_to_all | solution.py:41
  63.3 4.0 %fusion.22 = f32[320,512]{1,0:T(8,128)} fusion(f32[320,512]{1,0:T(8,128)} %collective-permute-done.11, bf16[320,2048]{1,0:T(8,128)(2,1)} %copy-done.3, bf16[2048,1024]{0,1:T(8,128)(2,1)} %convert_bitcast_fusion), kind=kOutput, calls=%fused_computation.24 | convolution fusion | flops 671252480 | bytes 4718592 | tf_op jit(solution)/shard_map/dot_general | solution.py:24
  67.3 2.0 %collective-permute-done.10 = bf16[120,2048]{1,0:T(8,128)(2,1)S(1)} collective-permute-done((bf16[120,2048]{1,0:T(8,128)(2,1)}, bf16[120,2048]{1,0:T(8,128)(2,1)S(1)}, u32[]{:S(2)}, u32[]{:S(2)}) %collective-permute-start.10) | collective-permute-done | bytes 491552 | tf_op jit(solution)/shard_map/ppermute | solution.py:12
  69.3 3.3 %collective-permute-done.9 = bf16[120,2048]{1,0:T(8,128)(2,1)S(1)} collective-permute-done((bf16[120,2048]{1,0:T(8,128)(2,1)}, bf16[120,2048]{1,0:T(8,128)(2,1)S(1)}, u32[]{:S(2)}, u32[]{:S(2)}) %collective-permute-start.9) | collective-permute-done | bytes 491552 | tf_op jit(solution)/shard_map/ppermute | solution.py:12
  72.7 1.1 copy-done.9
  73.8 1.7 %fusion.8 = f32[320,512]{1,0:T(8,128)} fusion(bf16[320,2048]{1,0:T(8,128)(2,1)S(1)} %constant_dynamic-update-slice_fusion.6, bf16[2048,1024]{0,1:T(8,128)(2,1)S(1)} %copy-done.11), kind=kOutput, calls=%fused_computation.10 | convolution fusion | flops 671088640 | bytes 4063232 | tf_op jit(solution)/shard_map/dot_general | solution.py:24
  76.6 1.1 pad_maximum_fusion.4
  77.8 3.1 %collective-permute-start.14 = (bf16[120,2048]{1,0:T(8,128)(2,1)}, bf16[120,2048]{1,0:T(8,128)(2,1)S(1)}, u32[]{:S(2)}, u32[]{:S(2)}) collective-permute-start(bf16[120,2048]{1,0:T(8,128)(2,1)} %get-tuple-element.37), channel_id=1, source_target_pairs={{0,192},{64,0},{128,64},{192,128},{1,193},{65,1},{129,65},{193,129... | collective-permute-start | bytes 1474568 | tf_op jit(solution)/shard_map/ppermute | solution.py:12
  80.9 0.9 bitcast_bitcast_fusion.2
  81.8 4.5 %all-to-all-start.1 = ((f32[4,320,128]{2,1,0:T(8,128)}), f32[4,320,128]{2,1,0:T(8,128)S(1)}, u32[]{:S(2)}, u32[]{:S(2)}) async-start(f32[4,320,128]{2,1,0:T(8,128)} %bitcast_bitcast_fusion.2), calls=%async_computation.1 | async-start | bytes 1310720 | tf_op jit(solution)/shard_map/all_to_all | solution.py:41
  86.3 3.1 %fusion.25 = f32[320,512]{1,0:T(8,128)S(1)} fusion(f32[320,512]{1,0:T(8,128)} %collective-permute-done.15, bf16[320,2048]{1,0:T(8,128)(2,1)} %copy-done.9, bf16[2048,1024]{0,1:T(8,128)(2,1)} %convert_bitcast_fusion), kind=kOutput, calls=%fused_computation.25 | convolution fusion | flops 671252480 | bytes 4718592 | tf_op jit(solution)/shard_map/dot_general | solution.py:24
  89.4 3.3 %collective-permute-done.13 = bf16[120,2048]{1,0:T(8,128)(2,1)S(1)} collective-permute-done((bf16[120,2048]{1,0:T(8,128)(2,1)}, bf16[120,2048]{1,0:T(8,128)(2,1)S(1)}, u32[]{:S(2)}, u32[]{:S(2)}) %collective-permute-start.13) | collective-permute-done | bytes 491552 | tf_op jit(solution)/shard_map/ppermute | solution.py:12
  92.9 1.5 %fusion.6 = f32[240,512]{1,0:T(8,128)} fusion(bf16[240,2048]{1,0:T(8,128)(2,1)S(1)} %constant_dynamic-update-slice_fusion.10, bf16[2048,1024]{0,1:T(8,128)(2,1)S(1)} %copy-done.12), kind=kOutput, calls=%fused_computation.8 | convolution fusion | flops 503316480 | bytes 3571712 | tf_op jit(solution)/shard_map/dot_general | solution.py:24
  94.5 2.8 %all-to-all-done.1 = f32[4,320,128]{2,1,0:T(8,128)S(1)} async-done(((f32[4,320,128]{2,1,0:T(8,128)}), f32[4,320,128]{2,1,0:T(8,128)S(1)}, u32[]{:S(2)}, u32[]{:S(2)}) %all-to-all-start.1) | async-done | bytes 655392 | tf_op jit(solution)/shard_map/all_to_all | solution.py:41
  98.1 0.9 bitcast_bitcast_fusion.1
  99.0 3.5 %all-to-all-start.2 = ((f32[4,320,128]{2,1,0:T(8,128)}), f32[4,320,128]{2,1,0:T(8,128)S(1)}, u32[]{:S(2)}, u32[]{:S(2)}) async-start(f32[4,320,128]{2,1,0:T(8,128)} %bitcast_bitcast_fusion.1), calls=%async_computation.2 | async-start | bytes 1310720 | tf_op jit(solution)/shard_map/all_to_all | solution.py:41
  102.5 2.4 %fusion.31 = f32[240,512]{1,0:T(8,128)S(1)} fusion(f32[240,512]{1,0:T(8,128)} %collective-permute-done.17, bf16[240,2048]{1,0:T(8,128)(2,1)S(1)} %copy-done.6, bf16[2048,1024]{0,1:T(8,128)(2,1)} %convert_bitcast_fusion), kind=kOutput, calls=%fused_computation.27 | convolution fusion | flops 503439360 | bytes 4063232 | tf_op jit(solution)/shard_map/dot_general | solution.py:24
  105.0 2.3 %collective-permute-start.18 = (f32[240,128]{1,0:T(8,128)S(1)}, f32[240,128]{1,0:T(8,128)S(1)}, u32[]{:S(2)}, u32[]{:S(2)}) collective-permute-start(f32[240,128]{1,0:T(8,128)S(1)} %get-tuple-element.41), channel_id=1, source_target_pairs={{0,4},{4,8},{8,12},{12,0},{1,5},{5,9},{9,13},{13,1},{2,6},{6,10},{... | collective-permute-start | bytes 368648 | tf_op jit(solution)/shard_map/ppermute | solution.py:12
  107.3 1.3 %collective-permute-start.19 = (f32[240,128]{1,0:T(8,128)S(1)}, f32[240,128]{1,0:T(8,128)S(1)}, u32[]{:S(2)}, u32[]{:S(2)}) collective-permute-start(f32[240,128]{1,0:T(8,128)S(1)} %get-tuple-element.43), channel_id=1, source_target_pairs={{0,12},{4,0},{8,4},{12,8},{1,13},{5,1},{9,5},{13,9},{2,14},{6,2},{... | collective-permute-start | bytes 368648 | tf_op jit(solution)/shard_map/ppermute | solution.py:12
  108.6 2.2 %collective-permute-start.20 = (f32[240,128]{1,0:T(8,128)S(1)}, f32[240,128]{1,0:T(8,128)S(1)}, u32[]{:S(2)}, u32[]{:S(2)}) collective-permute-start(f32[240,128]{1,0:T(8,128)S(1)} %get-tuple-element.42), channel_id=1, source_target_pairs={{0,8},{4,12},{8,0},{12,4},{1,9},{5,13},{9,1},{13,5},{2,10},{6,14},... | collective-permute-start | bytes 368648 | tf_op jit(solution)/shard_map/ppermute | solution.py:12
  111.0 3.9 %all-to-all-done.2 = f32[4,320,128]{2,1,0:T(8,128)S(1)} async-done(((f32[4,320,128]{2,1,0:T(8,128)}), f32[4,320,128]{2,1,0:T(8,128)S(1)}, u32[]{:S(2)}, u32[]{:S(2)}) %all-to-all-start.2) | async-done | bytes 655392 | tf_op jit(solution)/shard_map/all_to_all | solution.py:41
  114.9 1.5 %collective-permute-start.16 = (f32[320,128]{1,0:T(8,128)S(1)}, f32[320,128]{1,0:T(8,128)S(1)}, u32[]{:S(2)}, u32[]{:S(2)}) collective-permute-start(f32[320,128]{1,0:T(8,128)S(1)} %reduce_sum.29), channel_id=1, source_target_pairs={{0,2},{2,0},{1,3},{3,1},{4,6},{6,4},{5,7},{7,5},{8,10},{10,8},{9,1... | collective-permute-start | bytes 491528 | tf_op jit(solution)/shard_map/ppermute | solution.py:20
  116.4 1.2 collective-permute-done.20
  117.6 1.5 %collective-permute-start.21 = (f32[240,128]{1,0:T(8,128)S(1)}, f32[240,128]{1,0:T(8,128)S(1)}, u32[]{:S(2)}, u32[]{:S(2)}) collective-permute-start(f32[240,128]{1,0:T(8,128)S(1)} %add_add_fusion), channel_id=1, source_target_pairs={{0,2},{2,0},{1,3},{3,1},{4,6},{6,4},{5,7},{7,5},{8,10},{10,8},{9,1... | collective-permute-start | bytes 368648 | tf_op jit(solution)/shard_map/ppermute | solution.py:20
  119.1 1.7 %collective-permute-done.16 = f32[320,128]{1,0:T(8,128)S(1)} collective-permute-done((f32[320,128]{1,0:T(8,128)S(1)}, f32[320,128]{1,0:T(8,128)S(1)}, u32[]{:S(2)}, u32[]{:S(2)}) %collective-permute-start.16) | collective-permute-done | bytes 163872 | tf_op jit(solution)/shard_map/ppermute | solution.py:20
  120.9 1.7 %collective-permute-done.21 = f32[240,128]{1,0:T(8,128)S(1)} collective-permute-done((f32[240,128]{1,0:T(8,128)S(1)}, f32[240,128]{1,0:T(8,128)S(1)}, u32[]{:S(2)}, u32[]{:S(2)}) %collective-permute-start.21) | collective-permute-done | bytes 122912 | tf_op jit(solution)/shard_map/ppermute | solution.py:20
  122.7 2.2 %fusion.3 = bf16[64,1280]{1,0:T(8,128)(2,1)} fusion(s32[1280]{0:T(1024)S(1)} %concatenate.51, bf16[240,64]{1,0:T(8,128)(2,1)S(1)} %fusion.43, bf16[320,64]{1,0:T(8,128)(2,1)S(1)} %fusion.42, bf16[720,64]{1,0:T(8,128)(2,1)S(1)} %fusion.36), kind=kOutput, calls=%fused_computation.6 | convolution fusion | flops 211927040 | bytes 332800 | tf_op jit(solution)/shard_map/dot_general | solution.py:96
  (86 shorter events, 5.2 us)
Async XLA Ops:
  0.0 18.7 %collective-permute-start = (bf16[80,2048]{1,0:T(8,128)(2,1)}, bf16[80,2048]{1,0:T(8,128)(2,1)S(1)}, u32[]{:S(2)}, u32[]{:S(2)}) collective-permute-start(bf16[80,2048]{1,0:T(8,128)(2,1)} %param.2), channel_id=1, source_target_pairs={{0,16},{16,32},{32,48},{48,0},{1,17},{17,33},{33,49},{49,1},{2,18}... | collective-permute-start | bytes 983048 | tf_op jit(solution)/shard_map/ppermute | solution.py:12
  4.5 18.4 %collective-permute-start.1 = (bf16[80,2048]{1,0:T(8,128)(2,1)}, bf16[80,2048]{1,0:T(8,128)(2,1)S(1)}, u32[]{:S(2)}, u32[]{:S(2)}) collective-permute-start(bf16[80,2048]{1,0:T(8,128)(2,1)} %param.2), channel_id=1, source_target_pairs={{0,48},{16,0},{32,16},{48,32},{1,49},{17,1},{33,17},{49,33},{2,50}... | collective-permute-start | bytes 983048 | tf_op jit(solution)/shard_map/ppermute | solution.py:12
  4.5 18.5 %collective-permute-start.2 = (bf16[80,2048]{1,0:T(8,128)(2,1)}, bf16[80,2048]{1,0:T(8,128)(2,1)S(1)}, u32[]{:S(2)}, u32[]{:S(2)}) collective-permute-start(bf16[80,2048]{1,0:T(8,128)(2,1)} %param.2), channel_id=1, source_target_pairs={{0,64},{64,128},{128,192},{192,0},{1,65},{65,129},{129,193},{193,1... | collective-permute-start | bytes 983048 | tf_op jit(solution)/shard_map/ppermute | solution.py:12
  6.0 17.0 %collective-permute-start.3 = (bf16[80,2048]{1,0:T(8,128)(2,1)}, bf16[80,2048]{1,0:T(8,128)(2,1)S(1)}, u32[]{:S(2)}, u32[]{:S(2)}) collective-permute-start(bf16[80,2048]{1,0:T(8,128)(2,1)} %param.2), channel_id=1, source_target_pairs={{0,192},{64,0},{128,64},{192,128},{1,193},{65,1},{129,65},{193,129... | collective-permute-start | bytes 983048 | tf_op jit(solution)/shard_map/ppermute | solution.py:12
  7.7 8.4 %copy-start.4 = (bf16[80,2048]{1,0:T(8,128)(2,1)S(1)}, bf16[80,2048]{1,0:T(8,128)(2,1)}, u32[]{:S(2)}) copy-start(bf16[80,2048]{1,0:T(8,128)(2,1)} %param.2) | copy-start | bytes 983044
  29.5 12.3 %collective-permute-start.8 = (f32[400,512]{1,0:T(8,128)}, f32[400,512]{1,0:T(8,128)}, u32[]{:S(2)}, u32[]{:S(2)}) collective-permute-start(f32[400,512]{1,0:T(8,128)} %fusion.12), channel_id=1, source_target_pairs={{0,1},{1,0},{2,3},{3,2},{4,5},{5,4},{6,7},{7,6},{8,9},{9,8},{10,11... | collective-permute-start | bytes 2457608 | tf_op jit(solution)/shard_map/ppermute | solution.py:20
  29.5 9.6 %collective-permute-start.6 = (bf16[40,2048]{1,0:T(8,128)(2,1)S(1)}, bf16[40,2048]{1,0:T(8,128)(2,1)S(1)}, u32[]{:S(2)}, u32[]{:S(2)}) collective-permute-start(bf16[40,2048]{1,0:T(8,128)(2,1)S(1)} %slice.64), channel_id=1, source_target_pairs={{0,48},{16,0},{32,16},{48,32},{1,49},{17,1},{33,17},{49,33},{2,50}... | collective-permute-start | bytes 491528 | tf_op jit(solution)/shard_map/ppermute | solution.py:12
  29.6 11.1 %collective-permute-start.7 = (bf16[40,2048]{1,0:T(8,128)(2,1)S(1)}, bf16[40,2048]{1,0:T(8,128)(2,1)S(1)}, u32[]{:S(2)}, u32[]{:S(2)}) collective-permute-start(bf16[40,2048]{1,0:T(8,128)(2,1)S(1)} %slice.65), channel_id=1, source_target_pairs={{0,16},{16,32},{32,48},{48,0},{1,17},{17,33},{33,49},{49,1},{2,18}... | collective-permute-start | bytes 491528 | tf_op jit(solution)/shard_map/ppermute | solution.py:12
  33.8 17.8 %collective-permute-start.4 = (bf16[160,2048]{1,0:T(8,128)(2,1)S(1)}, bf16[160,2048]{1,0:T(8,128)(2,1)S(1)}, u32[]{:S(2)}, u32[]{:S(2)}) collective-permute-start(bf16[160,2048]{1,0:T(8,128)(2,1)S(1)} %pad_maximum_fusion), channel_id=1, source_target_pairs={{0,64},{64,128},{128,192},{192,0},{1,65},{65,129},{129,193},{193,1... | collective-permute-start | bytes 1966088 | tf_op jit(solution)/shard_map/ppermute | solution.py:12
  35.3 16.3 %collective-permute-start.5 = (bf16[160,2048]{1,0:T(8,128)(2,1)S(1)}, bf16[160,2048]{1,0:T(8,128)(2,1)S(1)}, u32[]{:S(2)}, u32[]{:S(2)}) collective-permute-start(bf16[160,2048]{1,0:T(8,128)(2,1)S(1)} %pad_maximum_fusion), channel_id=1, source_target_pairs={{0,192},{64,0},{128,64},{192,128},{1,193},{65,1},{129,65},{193,129... | collective-permute-start | bytes 1966088 | tf_op jit(solution)/shard_map/ppermute | solution.py:12
  37.1 4.7 %copy-start.7 = (bf16[400,2048]{1,0:T(8,128)(2,1)S(1)}, bf16[400,2048]{1,0:T(8,128)(2,1)}, u32[]{:S(2)}) copy-start(bf16[400,2048]{1,0:T(8,128)(2,1)} %constant_dynamic-update-slice_fusion) | copy-start | bytes 4915204
  41.8 9.9 %copy-start.10 = (bf16[2048,1024]{0,1:T(8,128)(2,1)S(1)}, bf16[2048,1024]{0,1:T(8,128)(2,1)}, u32[]{:S(2)}) copy-start(bf16[2048,1024]{0,1:T(8,128)(2,1)} %convert_bitcast_fusion) | copy-start | bytes 12582916
  51.6 23.9 %copy-start = (bf16[160,2048]{1,0:T(8,128)(2,1)}, bf16[160,2048]{1,0:T(8,128)(2,1)S(1)}, u32[]{:S(2)}) copy-start(bf16[160,2048]{1,0:T(8,128)(2,1)S(1)} %collective-permute-done.4) | copy-start | bytes 1966084
  51.6 23.9 %copy-start.1 = (bf16[160,2048]{1,0:T(8,128)(2,1)}, bf16[160,2048]{1,0:T(8,128)(2,1)S(1)}, u32[]{:S(2)}) copy-start(bf16[160,2048]{1,0:T(8,128)(2,1)S(1)} %collective-permute-done.5) | copy-start | bytes 1966084
  51.7 1.8 %copy-start.3 = (bf16[320,2048]{1,0:T(8,128)(2,1)}, bf16[320,2048]{1,0:T(8,128)(2,1)S(1)}, u32[]{:S(2)}) copy-start(bf16[320,2048]{1,0:T(8,128)(2,1)S(1)} %constant_dynamic-update-slice_fusion.4) | copy-start | bytes 3932164
  53.5 9.7 %collective-permute-start.11 = (f32[320,512]{1,0:T(8,128)}, f32[320,512]{1,0:T(8,128)}, u32[]{:S(2)}, u32[]{:S(2)}) collective-permute-start(f32[320,512]{1,0:T(8,128)} %fusion.10), channel_id=1, source_target_pairs={{0,1},{1,0},{2,3},{3,2},{4,5},{5,4},{6,7},{7,6},{8,9},{9,8},{10,11... | collective-permute-start | bytes 1966088 | tf_op jit(solution)/shard_map/ppermute | solution.py:20
  54.9 14.4 %collective-permute-start.10 = (bf16[120,2048]{1,0:T(8,128)(2,1)}, bf16[120,2048]{1,0:T(8,128)(2,1)S(1)}, u32[]{:S(2)}, u32[]{:S(2)}) collective-permute-start(bf16[120,2048]{1,0:T(8,128)(2,1)} %get-tuple-element.29), channel_id=1, source_target_pairs={{0,192},{64,0},{128,64},{192,128},{1,193},{65,1},{129,65},{193,129... | collective-permute-start | bytes 1474568 | tf_op jit(solution)/shard_map/ppermute | solution.py:12
  57.9 14.8 %collective-permute-start.9 = (bf16[120,2048]{1,0:T(8,128)(2,1)}, bf16[120,2048]{1,0:T(8,128)(2,1)S(1)}, u32[]{:S(2)}, u32[]{:S(2)}) collective-permute-start(bf16[120,2048]{1,0:T(8,128)(2,1)} %get-tuple-element.28), channel_id=1, source_target_pairs={{0,64},{64,128},{128,192},{192,0},{1,65},{65,129},{129,193},{193,1... | collective-permute-start | bytes 1474568 | tf_op jit(solution)/shard_map/ppermute | solution.py:12
  58.8 17.5 %all-to-all-start = ((f32[4,400,128]{2,1,0:T(8,128)}), f32[4,400,128]{2,1,0:T(8,128)S(1)}, u32[]{:S(2)}, u32[]{:S(2)}) async-start(f32[4,400,128]{2,1,0:T(8,128)} %bitcast_bitcast_fusion), calls=%async_computation | async-start | bytes 1638400 | tf_op jit(solution)/shard_map/all_to_all | solution.py:41
  63.3 9.3 %copy-start.8 = (bf16[320,2048]{1,0:T(8,128)(2,1)S(1)}, bf16[320,2048]{1,0:T(8,128)(2,1)}, u32[]{:S(2)}) copy-start(bf16[320,2048]{1,0:T(8,128)(2,1)} %constant_dynamic-update-slice_fusion.8) | copy-start | bytes 3932164
  63.3 10.5 %copy-start.11 = (bf16[2048,1024]{0,1:T(8,128)(2,1)S(1)}, bf16[2048,1024]{0,1:T(8,128)(2,1)}, u32[]{:S(2)}) copy-start(bf16[2048,1024]{0,1:T(8,128)(2,1)} %convert_bitcast_fusion) | copy-start | bytes 12582916
  72.7 1.1 copy-start.9
  75.5 10.8 %collective-permute-start.15 = (f32[320,512]{1,0:T(8,128)}, f32[320,512]{1,0:T(8,128)}, u32[]{:S(2)}, u32[]{:S(2)}) collective-permute-start(f32[320,512]{1,0:T(8,128)} %fusion.8), channel_id=1, source_target_pairs={{0,1},{1,0},{2,3},{3,2},{4,5},{5,4},{6,7},{7,6},{8,9},{9,8},{10,11... | collective-permute-start | bytes 1966088 | tf_op jit(solution)/shard_map/ppermute | solution.py:20
  75.6 1.0 slice-start
  75.6 1.1 slice-start.1
  75.6 5.4 %copy-start.2 = (f32[320,512]{1,0:T(8,128)S(1)}, f32[320,512]{1,0:T(8,128)}, u32[]{:S(2)}) copy-start(f32[320,512]{1,0:T(8,128)} %fusion.22) | copy-start | bytes 1966084
  77.7 15.0 %collective-permute-start.13 = (bf16[120,2048]{1,0:T(8,128)(2,1)}, bf16[120,2048]{1,0:T(8,128)(2,1)S(1)}, u32[]{:S(2)}, u32[]{:S(2)}) collective-permute-start(bf16[120,2048]{1,0:T(8,128)(2,1)} %get-tuple-element.36), channel_id=1, source_target_pairs={{0,64},{64,128},{128,192},{192,0},{1,65},{65,129},{129,193},{193,1... | collective-permute-start | bytes 1474568 | tf_op jit(solution)/shard_map/ppermute | solution.py:12
  77.8 15.0 %collective-permute-start.14 = (bf16[120,2048]{1,0:T(8,128)(2,1)}, bf16[120,2048]{1,0:T(8,128)(2,1)S(1)}, u32[]{:S(2)}, u32[]{:S(2)}) collective-permute-start(bf16[120,2048]{1,0:T(8,128)(2,1)} %get-tuple-element.37), channel_id=1, source_target_pairs={{0,192},{64,0},{128,64},{192,128},{1,193},{65,1},{129,65},{193,129... | collective-permute-start | bytes 1474568 | tf_op jit(solution)/shard_map/ppermute | solution.py:12
  81.8 15.4 %all-to-all-start.1 = ((f32[4,320,128]{2,1,0:T(8,128)}), f32[4,320,128]{2,1,0:T(8,128)S(1)}, u32[]{:S(2)}, u32[]{:S(2)}) async-start(f32[4,320,128]{2,1,0:T(8,128)} %bitcast_bitcast_fusion.2), calls=%async_computation.1 | async-start | bytes 1310720 | tf_op jit(solution)/shard_map/all_to_all | solution.py:41
  86.3 6.5 %copy-start.12 = (bf16[2048,1024]{0,1:T(8,128)(2,1)S(1)}, bf16[2048,1024]{0,1:T(8,128)(2,1)}, u32[]{:S(2)}) copy-start(bf16[2048,1024]{0,1:T(8,128)(2,1)} %convert_bitcast_fusion) | copy-start | bytes 12582916
  92.8 1.5 %copy-start.5 = (bf16[240,2048]{1,0:T(8,128)(2,1)}, bf16[240,2048]{1,0:T(8,128)(2,1)S(1)}, u32[]{:S(2)}) copy-start(bf16[240,2048]{1,0:T(8,128)(2,1)S(1)} %constant_dynamic-update-slice_fusion.10) | copy-start | bytes 2949124
  94.4 8.1 %collective-permute-start.17 = (f32[240,512]{1,0:T(8,128)}, f32[240,512]{1,0:T(8,128)}, u32[]{:S(2)}, u32[]{:S(2)}) collective-permute-start(f32[240,512]{1,0:T(8,128)} %fusion.6), channel_id=1, source_target_pairs={{0,1},{1,0},{2,3},{3,2},{4,5},{5,4},{6,7},{7,6},{8,9},{9,8},{10,11... | collective-permute-start | bytes 1474568 | tf_op jit(solution)/shard_map/ppermute | solution.py:20
  97.3 5.2 %copy-start.6 = (bf16[240,2048]{1,0:T(8,128)(2,1)S(1)}, bf16[240,2048]{1,0:T(8,128)(2,1)}, u32[]{:S(2)}) copy-start(bf16[240,2048]{1,0:T(8,128)(2,1)} %copy-done.5) | copy-start | bytes 2949124
  97.4 13.4 %collective-permute-start.12 = (f32[720,128]{1,0:T(8,128)S(1)}, f32[720,128]{1,0:T(8,128)S(1)}, u32[]{:S(2)}, u32[]{:S(2)}) collective-permute-start(f32[720,128]{1,0:T(8,128)S(1)} %pad_maximum_fusion.6), channel_id=1, source_target_pairs={{0,2},{2,0},{1,3},{3,1},{4,6},{6,4},{5,7},{7,5},{8,10},{10,8},{9,1... | collective-permute-start | bytes 1105928 | tf_op jit(solution)/shard_map/ppermute | solution.py:20
  99.0 15.9 %all-to-all-start.2 = ((f32[4,320,128]{2,1,0:T(8,128)}), f32[4,320,128]{2,1,0:T(8,128)S(1)}, u32[]{:S(2)}, u32[]{:S(2)}) async-start(f32[4,320,128]{2,1,0:T(8,128)} %bitcast_bitcast_fusion.1), calls=%async_computation.2 | async-start | bytes 1310720 | tf_op jit(solution)/shard_map/all_to_all | solution.py:41
  105.0 11.4 %collective-permute-start.18 = (f32[240,128]{1,0:T(8,128)S(1)}, f32[240,128]{1,0:T(8,128)S(1)}, u32[]{:S(2)}, u32[]{:S(2)}) collective-permute-start(f32[240,128]{1,0:T(8,128)S(1)} %get-tuple-element.41), channel_id=1, source_target_pairs={{0,4},{4,8},{8,12},{12,0},{1,5},{5,9},{9,13},{13,1},{2,6},{6,10},{... | collective-permute-start | bytes 368648 | tf_op jit(solution)/shard_map/ppermute | solution.py:12
  107.3 9.2 %collective-permute-start.19 = (f32[240,128]{1,0:T(8,128)S(1)}, f32[240,128]{1,0:T(8,128)S(1)}, u32[]{:S(2)}, u32[]{:S(2)}) collective-permute-start(f32[240,128]{1,0:T(8,128)S(1)} %get-tuple-element.43), channel_id=1, source_target_pairs={{0,12},{4,0},{8,4},{12,8},{1,13},{5,1},{9,5},{13,9},{2,14},{6,2},{... | collective-permute-start | bytes 368648 | tf_op jit(solution)/shard_map/ppermute | solution.py:12
  108.6 9.0 %collective-permute-start.20 = (f32[240,128]{1,0:T(8,128)S(1)}, f32[240,128]{1,0:T(8,128)S(1)}, u32[]{:S(2)}, u32[]{:S(2)}) collective-permute-start(f32[240,128]{1,0:T(8,128)S(1)} %get-tuple-element.42), channel_id=1, source_target_pairs={{0,8},{4,12},{8,0},{12,4},{1,9},{5,13},{9,1},{13,5},{2,10},{6,14},... | collective-permute-start | bytes 368648 | tf_op jit(solution)/shard_map/ppermute | solution.py:12
  114.9 5.8 %collective-permute-start.16 = (f32[320,128]{1,0:T(8,128)S(1)}, f32[320,128]{1,0:T(8,128)S(1)}, u32[]{:S(2)}, u32[]{:S(2)}) collective-permute-start(f32[320,128]{1,0:T(8,128)S(1)} %reduce_sum.29), channel_id=1, source_target_pairs={{0,2},{2,0},{1,3},{3,1},{4,6},{6,4},{5,7},{7,5},{8,10},{10,8},{9,1... | collective-permute-start | bytes 491528 | tf_op jit(solution)/shard_map/ppermute | solution.py:20
  117.6 5.0 %collective-permute-start.21 = (f32[240,128]{1,0:T(8,128)S(1)}, f32[240,128]{1,0:T(8,128)S(1)}, u32[]{:S(2)}, u32[]{:S(2)}) collective-permute-start(f32[240,128]{1,0:T(8,128)S(1)} %add_add_fusion), channel_id=1, source_target_pairs={{0,2},{2,0},{1,3},{3,1},{4,6},{6,4},{5,7},{7,5},{8,10},{10,8},{9,1... | collective-permute-start | bytes 368648 | tf_op jit(solution)/shard_map/ppermute | solution.py:20

commit v6 on v5

--- a/solution.py
+++ b/solution.py
@@ -62,29 +62,28 @@
     def paired(rows):
         return dot(rows, mine) + swap(dot(rows, theirs), "core")
 
-    side, own_xm, own_xp = lax.optimization_barrier((joined(zm, zp), own_xm, own_xp))
+    side = joined(zm, zp)
     side_xm, side_xp = to_both(side, "x")
     far = joined(shift(zp[:40], "zh", 4, -1), shift(zm[40:], "zh", 4, 1))
-    early = paired(joined(own, own_xm, own_xp, side))
+    early = paired(joined(own, *lax.optimization_barrier((own_xm, own_xp, side))))
 
-    after_xm, after_xp, early = lax.optimization_barrier(
-        (joined(far, own_xm[40:]), joined(far, own_xp[:40]), early)
+    late_rows = joined(side_xm, side_xp)
+    after_xm, after_xp, early, away = lax.optimization_barrier(
+        (joined(far, own_xm[40:]), joined(far, own_xp[:40]), early, dot(late_rows, theirs))
     )
     from_xm, from_xp = shift(after_xm, "x", 4, 1), shift(after_xp, "x", 4, -1)
-    side_xm, side_xp, early = lax.optimization_barrier((side_xm, side_xp, early))
     early = over_y(early)
-    late = paired(joined(side_xm, side_xp))
+    late = dot(late_rows, mine) + joined(swap(away[:160], "core"), swap(away[160:], "core"))
     from_xm, from_xp, late = lax.optimization_barrier((from_xm, from_xp, late))
     after_xm, after_xp, early = lax.optimization_barrier(
         (joined(side_xm[80:], from_xm[40:80]), joined(side_xp[:80], from_xp[:40]), early)
     )
     last_xm, last_xp = shift(after_xm, "x", 4, 1), shift(after_xp, "x", 4, -1)
-    late = over_y(late)
     second = paired(joined(far, from_xm, from_xp))
     last_xm, last_xp, second = lax.optimization_barrier((last_xm, last_xp, second))
-    second = over_y(second)
+    second = over_y(joined(late, second))
     third = over_y_at_once(paired(joined(last_xm, last_xp)))
-    sums = [over_zl(part) for part in (joined(early, late), second, third)]
+    sums = [over_zl(part) for part in (early, second, third)]
     sites = [
         [block(0, 0), block(-1, 0), block(1, 0), block(0, -1), block(0, 1)],
         [block(-1, -1), block(-1, 1), block(1, -1), block(1, 1)],

time: 125 us -> 126 us (level)
  waiting for transfers between devices: 37.1 us -> 51.5 us
  matrix products: 32.2 us -> 25.6 us
  starting transfers between devices: 43.3 us -> 39.4 us
  local copies, waits for them, and re-layouts: 9.1 us -> 5.68 us
    ppermute x15, waiting for transfers between devices: 26.3 us -> 42.5 us  [shift(): lax.ppermute(value, axis, [(i, (i + by) % size) for i in range(size)])]
    all_to_all x3 -> x2, waiting for transfers between devices: 7.45 us -> 0.01 us  [over_y(): lax.all_to_all(split, 'y', split_axis=0, concat_axis=0, tiled=True)]
    dot_general x9, matrix products: 30 us -> 23.4 us  [dot(): return jnp.dot(left, right, preferred_element_type=F32)]
    ppermute x7 -> x8, waiting for transfers between devices: 3.4 us -> 8.99 us  [swap(): return lax.ppermute(value, axis, [(0, 1), (1, 0)])]
    all_to_all x3 -> x2, starting transfers between devices: 12.4 us -> 8.93 us  [over_y(): lax.all_to_all(split, 'y', split_axis=0, concat_axis=0, tiled=True)]
    unnamed x34 -> x21, local copies, waits for them, and re-layouts: 4.89 us -> 2.69 us
    transpose x3 -> x1, local copies, waits for them, and re-layouts: 2.75 us -> 0.95 us  [over_y(): split = pair.reshape(pair.shape[0], 4, 128).transpose(1, 0, 2)]
    ppermute x7 -> x8, starting transfers between devices: 3.67 us -> 3.15 us  [swap(): return lax.ppermute(value, axis, [(0, 1), (1, 0)])]
  transfers between devices with their start and end apart: 25 -> 25, of which waited for: 14 -> 12; matrix products, arithmetic and copies ran while one was open for 26% -> 23% of each run, Pallas kernels for 0% -> 0%
where the time goes in v6:
time: 126 us
  waiting for transfers between devices  51.5 us (41%)
  starting transfers between devices  39.4 us (31%)
  matrix products  25.6 us (20%)
  local copies, waits for them, and re-layouts  5.68 us (5%)
  other arithmetic  2.93 us (2%)
    ppermute x15, waiting for transfers between devices, shift(): lax.ppermute(value, axis, [(i, (i + by) % size) for i in range(size)])  42.5 us
    ppermute x15, starting transfers between devices, shift(): lax.ppermute(value, axis, [(i, (i + by) % size) for i in range(size)])  27.4 us
    dot_general x9, matrix products, dot(): return jnp.dot(left, right, preferred_element_type=F32)  23.4 us
    ppermute x8, waiting for transfers between devices, swap(): return lax.ppermute(value, axis, [(0, 1), (1, 0)])  8.99 us
    all_to_all x2, starting transfers between devices, over_y(): lax.all_to_all(split, 'y', split_axis=0, concat_axis=0, tiled=True)  8.93 us
    ppermute x8, starting transfers between devices, swap(): return lax.ppermute(value, axis, [(0, 1), (1, 0)])  3.15 us
    unnamed x21, local copies, waits for them, and re-layouts  2.69 us
  transfers between devices with their start and end apart: 25, of which 12 were waited for; matrix products, arithmetic and copies ran while one was open for 23% of the time, Pallas kernels for 0%

profile of v6, /device:TPU:64, one launch (start us, length us, event | category | flops | bytes accessed | tf_op | source)
XLA Modules:
  0.0 125.7 jit_solution(11125809982995788771)
XLA Ops:
  0.0 4.5 %collective-permute-start = (bf16[80,2048]{1,0:T(8,128)(2,1)}, bf16[80,2048]{1,0:T(8,128)(2,1)S(1)}, u32[]{:S(2)}, u32[]{:S(2)}) collective-permute-start(bf16[80,2048]{1,0:T(8,128)(2,1)} %param.2), channel_id=1, source_target_pairs={{0,16},{16,32},{32,48},{48,0},{1,17},{17,33},{33,49},{49,1},{2,18}... | collective-permute-start | bytes 983048 | tf_op jit(solution)/shard_map/ppermute | solution.py:12
  4.5 1.5 %collective-permute-start.5 = (bf16[80,2048]{1,0:T(8,128)(2,1)}, bf16[80,2048]{1,0:T(8,128)(2,1)S(1)}, u32[]{:S(2)}, u32[]{:S(2)}) collective-permute-start(bf16[80,2048]{1,0:T(8,128)(2,1)} %param.2), channel_id=1, source_target_pairs={{0,64},{64,128},{128,192},{192,0},{1,65},{65,129},{129,193},{193,1... | collective-permute-start | bytes 983048 | tf_op jit(solution)/shard_map/ppermute | solution.py:12
  6.0 1.7 %collective-permute-start.6 = (bf16[80,2048]{1,0:T(8,128)(2,1)}, bf16[80,2048]{1,0:T(8,128)(2,1)S(1)}, u32[]{:S(2)}, u32[]{:S(2)}) collective-permute-start(bf16[80,2048]{1,0:T(8,128)(2,1)} %param.2), channel_id=1, source_target_pairs={{0,192},{64,0},{128,64},{192,128},{1,193},{65,1},{129,65},{193,129... | collective-permute-start | bytes 983048 | tf_op jit(solution)/shard_map/ppermute | solution.py:12
  7.7 7.1 %convert_bitcast_fusion = bf16[2048,1024]{0,1:T(8,128)(2,1)S(1)} fusion(bf16[2048,1024]{1,0:T(8,128)(2,1)} %param.3, s32[1024]{0:T(1024)S(1)} %and_add_fusion), kind=kOutput, calls=%fused_computation.2 | convolution fusion | flops 4299161600 | bytes 8392704 | tf_op jit(solution)/shard_map/dot_general | solution.py:24
  14.9 3.8 %collective-permute-done = bf16[80,2048]{1,0:T(8,128)(2,1)S(1)} collective-permute-done((bf16[80,2048]{1,0:T(8,128)(2,1)}, bf16[80,2048]{1,0:T(8,128)(2,1)S(1)}, u32[]{:S(2)}, u32[]{:S(2)}) %collective-permute-start) | collective-permute-done | bytes 327712 | tf_op jit(solution)/shard_map/ppermute | solution.py:12
  18.7 4.2 %collective-permute-done.1 = bf16[80,2048]{1,0:T(8,128)(2,1)S(1)} collective-permute-done((bf16[80,2048]{1,0:T(8,128)(2,1)}, bf16[80,2048]{1,0:T(8,128)(2,1)S(1)}, u32[]{:S(2)}, u32[]{:S(2)}) %collective-permute-start.1) | collective-permute-done | bytes 327712 | tf_op jit(solution)/shard_map/ppermute | solution.py:12
  22.9 1.6 %collective-permute-start.2 = (bf16[160,2048]{1,0:T(8,128)(2,1)S(1)}, bf16[160,2048]{1,0:T(8,128)(2,1)S(1)}, u32[]{:S(2)}, u32[]{:S(2)}) collective-permute-start(bf16[160,2048]{1,0:T(8,128)(2,1)S(1)} %constant_dynamic-update-slice_fusion), channel_id=1, source_target_pairs={{0,64},{64,128},{128,192},{192,0},{1,65},{65,129},{129,193},{193,1... | collective-permute-start | bytes 1966088 | tf_op jit(solution)/shard_map/ppermute | solution.py:12
  24.5 1.7 %collective-permute-start.8 = (bf16[160,2048]{1,0:T(8,128)(2,1)S(1)}, bf16[160,2048]{1,0:T(8,128)(2,1)S(1)}, u32[]{:S(2)}, u32[]{:S(2)}) collective-permute-start(bf16[160,2048]{1,0:T(8,128)(2,1)S(1)} %constant_dynamic-update-slice_fusion), channel_id=1, source_target_pairs={{0,192},{64,0},{128,64},{192,128},{1,193},{65,1},{129,65},{193,129... | collective-permute-start | bytes 1966088 | tf_op jit(solution)/shard_map/ppermute | solution.py:12
  26.4 4.2 %collective-permute-start.4 = (bf16[40,2048]{1,0:T(8,128)(2,1)S(1)}, bf16[40,2048]{1,0:T(8,128)(2,1)S(1)}, u32[]{:S(2)}, u32[]{:S(2)}) collective-permute-start(bf16[40,2048]{1,0:T(8,128)(2,1)S(1)} %slice.74), channel_id=1, source_target_pairs={{0,16},{16,32},{32,48},{48,0},{1,17},{17,33},{33,49},{49,1},{2,18}... | collective-permute-start | bytes 491528 | tf_op jit(solution)/shard_map/ppermute | solution.py:12
  30.7 1.0 fusion.12
  31.7 0.3 collective-permute-start.7
  32.1 1.8 %collective-permute-done.3 = bf16[40,2048]{1,0:T(8,128)(2,1)S(1)} collective-permute-done((bf16[40,2048]{1,0:T(8,128)(2,1)S(1)}, bf16[40,2048]{1,0:T(8,128)(2,1)S(1)}, u32[]{:S(2)}, u32[]{:S(2)}) %collective-permute-start.3) | collective-permute-done | bytes 163872 | tf_op jit(solution)/shard_map/ppermute | solution.py:12
  33.9 0.5 collective-permute-done.4
  34.4 1.1 pad_maximum_fusion.2
  35.5 0.7 constant_dynamic-update-slice_fusion.11
  36.1 3.8 %collective-permute-done.2 = bf16[160,2048]{1,0:T(8,128)(2,1)S(1)} collective-permute-done((bf16[160,2048]{1,0:T(8,128)(2,1)S(1)}, bf16[160,2048]{1,0:T(8,128)(2,1)S(1)}, u32[]{:S(2)}, u32[]{:S(2)}) %collective-permute-start.2) | collective-permute-done | bytes 655392 | tf_op jit(solution)/shard_map/ppermute | solution.py:12
  40.1 0.9 fusion.10
  41.0 0.2 copy-done.1
  41.2 1.0 fusion.28
  42.3 0.8 fusion.43
  43.1 0.5 collective-permute-start.12
  43.6 0.7 constant_dynamic-update-slice_fusion.10
  44.2 2.9 %collective-permute-start.10 = (bf16[120,2048]{1,0:T(8,128)(2,1)}, bf16[120,2048]{1,0:T(8,128)(2,1)S(1)}, u32[]{:S(2)}, u32[]{:S(2)}) collective-permute-start(bf16[120,2048]{1,0:T(8,128)(2,1)} %get-tuple-element.25), channel_id=1, source_target_pairs={{0,192},{64,0},{128,64},{192,128},{1,193},{65,1},{129,65},{193,129... | collective-permute-start | bytes 1474568 | tf_op jit(solution)/shard_map/ppermute | solution.py:12
  47.1 1.0 bitcast_bitcast_fusion.1
  48.1 4.5 %all-to-all-start = ((f32[4,400,128]{2,1,0:T(8,128)}), f32[4,400,128]{2,1,0:T(8,128)S(1)}, u32[]{:S(2)}, u32[]{:S(2)}) async-start(f32[4,400,128]{2,1,0:T(8,128)} %bitcast_bitcast_fusion.1), calls=%async_computation | async-start | bytes 1638400 | tf_op jit(solution)/shard_map/all_to_all | solution.py:41
  52.6 4.0 %fusion.22 = f32[320,512]{1,0:T(8,128)} fusion(bf16[320,2048]{1,0:T(8,128)(2,1)} %copy-done.1, bf16[2048,1024]{0,1:T(8,128)(2,1)} %copy-done.3, f32[160,512]{1,0:T(8,128)} %collective-permute-done.12, f32[160,512]{1,0:T(8,128)} %collective-permute-done.11), kind=kOutput, calls=%fused_computation.26 | convolution fusion | flops 671416320 | bytes 4718592 | tf_op jit(solution)/shard_map/dot_general | solution.py:24
  56.6 1.5 %collective-permute-done.10 = bf16[120,2048]{1,0:T(8,128)(2,1)S(1)} collective-permute-done((bf16[120,2048]{1,0:T(8,128)(2,1)}, bf16[120,2048]{1,0:T(8,128)(2,1)S(1)}, u32[]{:S(2)}, u32[]{:S(2)}) %collective-permute-start.10) | collective-permute-done | bytes 491552 | tf_op jit(solution)/shard_map/ppermute | solution.py:12
  58.1 3.3 %collective-permute-done.9 = bf16[120,2048]{1,0:T(8,128)(2,1)S(1)} collective-permute-done((bf16[120,2048]{1,0:T(8,128)(2,1)}, bf16[120,2048]{1,0:T(8,128)(2,1)S(1)}, u32[]{:S(2)}, u32[]{:S(2)}) %collective-permute-start.9) | collective-permute-done | bytes 491552 | tf_op jit(solution)/shard_map/ppermute | solution.py:12
  61.4 0.8 constant_dynamic-update-slice_fusion.9
  62.2 0.8 constant_dynamic-update-slice_fusion.8
  63.1 3.1 %fusion.8 = f32[320,512]{1,0:T(8,128)} fusion(bf16[320,2048]{1,0:T(8,128)(2,1)} %constant_dynamic-update-slice_fusion.8, bf16[2048,1024]{0,1:T(8,128)(2,1)S(1)} %copy-done.4), kind=kOutput, calls=%fused_computation.10 | convolution fusion | flops 671088640 | bytes 4063232 | tf_op jit(solution)/shard_map/dot_general | solution.py:24
  66.5 3.2 %collective-permute-start.15 = (bf16[120,2048]{1,0:T(8,128)(2,1)S(1)}, bf16[120,2048]{1,0:T(8,128)(2,1)S(1)}, u32[]{:S(2)}, u32[]{:S(2)}) collective-permute-start(bf16[120,2048]{1,0:T(8,128)(2,1)S(1)} %get-tuple-element.33), channel_id=1, source_target_pairs={{0,192},{64,0},{128,64},{192,128},{1,193},{65,1},{129,65},{193,129... | collective-permute-start | bytes 1474568 | tf_op jit(solution)/shard_map/ppermute | solution.py:12
  69.7 3.1 %fusion.25 = f32[320,512]{1,0:T(8,128)S(1)} fusion(f32[320,512]{1,0:T(8,128)} %collective-permute-done.16, bf16[320,2048]{1,0:T(8,128)(2,1)} %constant_dynamic-update-slice_fusion.8, bf16[2048,1024]{0,1:T(8,128)(2,1)} %copy-done.3), kind=kOutput, calls=%fused_computation.27 | convolution fusion | flops 671252480 | bytes 4718592 | tf_op jit(solution)/shard_map/dot_general | solution.py:24
  72.9 8.4 %collective-permute-done.14 = bf16[120,2048]{1,0:T(8,128)(2,1)S(1)} collective-permute-done((bf16[120,2048]{1,0:T(8,128)(2,1)S(1)}, bf16[120,2048]{1,0:T(8,128)(2,1)S(1)}, u32[]{:S(2)}, u32[]{:S(2)}) %collective-permute-start.14) | collective-permute-done | bytes 491552 | tf_op jit(solution)/shard_map/ppermute | solution.py:12
  81.4 0.7 fusion.6
  82.5 1.2 bitcast_bitcast_fusion
  83.7 4.5 %all-to-all-start.1 = ((f32[4,640,128]{2,1,0:T(8,128)}), f32[4,640,128]{2,1,0:T(8,128)S(1)}, u32[]{:S(2)}, u32[]{:S(2)}) async-start(f32[4,640,128]{2,1,0:T(8,128)} %bitcast_bitcast_fusion), calls=%async_computation.1 | async-start | bytes 2621440 | tf_op jit(solution)/shard_map/all_to_all | solution.py:41
  88.2 2.4 %fusion.31 = f32[240,512]{1,0:T(8,128)S(1)} fusion(f32[240,512]{1,0:T(8,128)} %collective-permute-done.18, bf16[240,2048]{1,0:T(8,128)(2,1)S(1)} %constant_dynamic-update-slice_fusion.12, bf16[2048,1024]{0,1:T(8,128)(2,1)} %copy-done.3), kind=kOutput, calls=%fused_computation.29 | convolution fusion | flops 503439360 | bytes 4063232 | tf_op jit(solution)/shard_map/dot_general | solution.py:24
  90.6 2.3 %collective-permute-start.19 = (f32[240,128]{1,0:T(8,128)S(1)}, f32[240,128]{1,0:T(8,128)S(1)}, u32[]{:S(2)}, u32[]{:S(2)}) collective-permute-start(f32[240,128]{1,0:T(8,128)S(1)} %get-tuple-element.39), channel_id=1, source_target_pairs={{0,4},{4,8},{8,12},{12,0},{1,5},{5,9},{9,13},{13,1},{2,6},{6,10},{... | collective-permute-start | bytes 368648 | tf_op jit(solution)/shard_map/ppermute | solution.py:12
  93.0 1.3 %collective-permute-start.20 = (f32[240,128]{1,0:T(8,128)S(1)}, f32[240,128]{1,0:T(8,128)S(1)}, u32[]{:S(2)}, u32[]{:S(2)}) collective-permute-start(f32[240,128]{1,0:T(8,128)S(1)} %get-tuple-element.41), channel_id=1, source_target_pairs={{0,12},{4,0},{8,4},{12,8},{1,13},{5,1},{9,5},{13,9},{2,14},{6,2},{... | collective-permute-start | bytes 368648 | tf_op jit(solution)/shard_map/ppermute | solution.py:12
  94.3 2.2 %collective-permute-start.21 = (f32[240,128]{1,0:T(8,128)S(1)}, f32[240,128]{1,0:T(8,128)S(1)}, u32[]{:S(2)}, u32[]{:S(2)}) collective-permute-start(f32[240,128]{1,0:T(8,128)S(1)} %get-tuple-element.40), channel_id=1, source_target_pairs={{0,8},{4,12},{8,0},{12,4},{1,9},{5,13},{9,1},{13,5},{2,10},{6,14},... | collective-permute-start | bytes 368648 | tf_op jit(solution)/shard_map/ppermute | solution.py:12
  96.7 12.8 %collective-permute-done.19 = f32[240,128]{1,0:T(8,128)S(1)} collective-permute-done((f32[240,128]{1,0:T(8,128)S(1)}, f32[240,128]{1,0:T(8,128)S(1)}, u32[]{:S(2)}, u32[]{:S(2)}) %collective-permute-start.19) | collective-permute-done | bytes 122912 | tf_op jit(solution)/shard_map/ppermute | solution.py:12
  109.5 2.4 %collective-permute-done.21 = f32[240,128]{1,0:T(8,128)S(1)} collective-permute-done((f32[240,128]{1,0:T(8,128)S(1)}, f32[240,128]{1,0:T(8,128)S(1)}, u32[]{:S(2)}, u32[]{:S(2)}) %collective-permute-start.21) | collective-permute-done | bytes 122912 | tf_op jit(solution)/shard_map/ppermute | solution.py:12
  112.1 2.1 %collective-permute-start.17 = (f32[640,128]{1,0:T(8,128)S(1)}, f32[640,128]{1,0:T(8,128)S(1)}, u32[]{:S(2)}, u32[]{:S(2)}) collective-permute-start(f32[640,128]{1,0:T(8,128)S(1)} %reduce_sum.19), channel_id=1, source_target_pairs={{0,2},{2,0},{1,3},{3,1},{4,6},{6,4},{5,7},{7,5},{8,10},{10,8},{9,1... | collective-permute-start | bytes 983048 | tf_op jit(solution)/shard_map/ppermute | solution.py:20
  114.3 3.9 %collective-permute-done.22 = f32[240,128]{1,0:T(8,128)S(1)} collective-permute-done((f32[240,128]{1,0:T(8,128)S(1)}, f32[240,128]{1,0:T(8,128)S(1)}, u32[]{:S(2)}, u32[]{:S(2)}) %collective-permute-start.22) | collective-permute-done | bytes 122912 | tf_op jit(solution)/shard_map/ppermute | solution.py:20
  118.3 5.1 %collective-permute-done.17 = f32[640,128]{1,0:T(8,128)S(1)} collective-permute-done((f32[640,128]{1,0:T(8,128)S(1)}, f32[640,128]{1,0:T(8,128)S(1)}, u32[]{:S(2)}, u32[]{:S(2)}) %collective-permute-start.17) | collective-permute-done | bytes 327712 | tf_op jit(solution)/shard_map/ppermute | solution.py:20
  123.4 0.2 fusion.34
  123.5 2.2 %fusion.3 = bf16[64,1280]{1,0:T(8,128)(2,1)} fusion(s32[1280]{0:T(1024)S(1)} %concatenate.55, bf16[240,64]{1,0:T(8,128)(2,1)S(1)} %fusion.41, bf16[640,64]{1,0:T(8,128)(2,1)S(1)} %fusion.34, bf16[400,64]{1,0:T(8,128)(2,1)S(1)} %fusion.40), kind=kOutput, calls=%fused_computation.6 | convolution fusion | flops 211927040 | bytes 332800 | tf_op jit(solution)/shard_map/dot_general | solution.py:95
  (69 shorter events, 1.7 us)
Async XLA Ops:
  0.0 18.7 %collective-permute-start = (bf16[80,2048]{1,0:T(8,128)(2,1)}, bf16[80,2048]{1,0:T(8,128)(2,1)S(1)}, u32[]{:S(2)}, u32[]{:S(2)}) collective-permute-start(bf16[80,2048]{1,0:T(8,128)(2,1)} %param.2), channel_id=1, source_target_pairs={{0,16},{16,32},{32,48},{48,0},{1,17},{17,33},{33,49},{49,1},{2,18}... | collective-permute-start | bytes 983048 | tf_op jit(solution)/shard_map/ppermute | solution.py:12
  4.5 18.4 %collective-permute-start.1 = (bf16[80,2048]{1,0:T(8,128)(2,1)}, bf16[80,2048]{1,0:T(8,128)(2,1)S(1)}, u32[]{:S(2)}, u32[]{:S(2)}) collective-permute-start(bf16[80,2048]{1,0:T(8,128)(2,1)} %param.2), channel_id=1, source_target_pairs={{0,48},{16,0},{32,16},{48,32},{1,49},{17,1},{33,17},{49,33},{2,50}... | collective-permute-start | bytes 983048 | tf_op jit(solution)/shard_map/ppermute | solution.py:12
  4.5 21.8 %collective-permute-start.5 = (bf16[80,2048]{1,0:T(8,128)(2,1)}, bf16[80,2048]{1,0:T(8,128)(2,1)S(1)}, u32[]{:S(2)}, u32[]{:S(2)}) collective-permute-start(bf16[80,2048]{1,0:T(8,128)(2,1)} %param.2), channel_id=1, source_target_pairs={{0,64},{64,128},{128,192},{192,0},{1,65},{65,129},{129,193},{193,1... | collective-permute-start | bytes 983048 | tf_op jit(solution)/shard_map/ppermute | solution.py:12
  6.0 20.3 %collective-permute-start.6 = (bf16[80,2048]{1,0:T(8,128)(2,1)}, bf16[80,2048]{1,0:T(8,128)(2,1)S(1)}, u32[]{:S(2)}, u32[]{:S(2)}) collective-permute-start(bf16[80,2048]{1,0:T(8,128)(2,1)} %param.2), channel_id=1, source_target_pairs={{0,192},{64,0},{128,64},{192,128},{1,193},{65,1},{129,65},{193,129... | collective-permute-start | bytes 983048 | tf_op jit(solution)/shard_map/ppermute | solution.py:12
  7.7 7.1 %copy-start.2 = (bf16[80,2048]{1,0:T(8,128)(2,1)S(1)}, bf16[80,2048]{1,0:T(8,128)(2,1)}, u32[]{:S(2)}) copy-start(bf16[80,2048]{1,0:T(8,128)(2,1)} %param.2) | copy-start | bytes 983044
  14.8 26.4 %copy-start.3 = (bf16[2048,1024]{0,1:T(8,128)(2,1)}, bf16[2048,1024]{0,1:T(8,128)(2,1)S(1)}, u32[]{:S(2)}) copy-start(bf16[2048,1024]{0,1:T(8,128)(2,1)S(1)} %convert_bitcast_fusion) | copy-start | bytes 12582916
  22.9 17.0 %collective-permute-start.2 = (bf16[160,2048]{1,0:T(8,128)(2,1)S(1)}, bf16[160,2048]{1,0:T(8,128)(2,1)S(1)}, u32[]{:S(2)}, u32[]{:S(2)}) collective-permute-start(bf16[160,2048]{1,0:T(8,128)(2,1)S(1)} %constant_dynamic-update-slice_fusion), channel_id=1, source_target_pairs={{0,64},{64,128},{128,192},{192,0},{1,65},{65,129},{129,193},{193,1... | collective-permute-start | bytes 1966088 | tf_op jit(solution)/shard_map/ppermute | solution.py:12
  24.5 15.5 %collective-permute-start.8 = (bf16[160,2048]{1,0:T(8,128)(2,1)S(1)}, bf16[160,2048]{1,0:T(8,128)(2,1)S(1)}, u32[]{:S(2)}, u32[]{:S(2)}) collective-permute-start(bf16[160,2048]{1,0:T(8,128)(2,1)S(1)} %constant_dynamic-update-slice_fusion), channel_id=1, source_target_pairs={{0,192},{64,0},{128,64},{192,128},{1,193},{65,1},{129,65},{193,129... | collective-permute-start | bytes 1966088 | tf_op jit(solution)/shard_map/ppermute | solution.py:12
  26.3 7.6 %collective-permute-start.3 = (bf16[40,2048]{1,0:T(8,128)(2,1)S(1)}, bf16[40,2048]{1,0:T(8,128)(2,1)S(1)}, u32[]{:S(2)}, u32[]{:S(2)}) collective-permute-start(bf16[40,2048]{1,0:T(8,128)(2,1)S(1)} %slice.73), channel_id=1, source_target_pairs={{0,48},{16,0},{32,16},{48,32},{1,49},{17,1},{33,17},{49,33},{2,50}... | collective-permute-start | bytes 491528 | tf_op jit(solution)/shard_map/ppermute | solution.py:12
  26.4 8.0 %collective-permute-start.4 = (bf16[40,2048]{1,0:T(8,128)(2,1)S(1)}, bf16[40,2048]{1,0:T(8,128)(2,1)S(1)}, u32[]{:S(2)}, u32[]{:S(2)}) collective-permute-start(bf16[40,2048]{1,0:T(8,128)(2,1)S(1)} %slice.74), channel_id=1, source_target_pairs={{0,16},{16,32},{32,48},{48,0},{1,17},{17,33},{33,49},{49,1},{2,18}... | collective-permute-start | bytes 491528 | tf_op jit(solution)/shard_map/ppermute | solution.py:12
  31.7 9.5 %collective-permute-start.7 = (f32[400,512]{1,0:T(8,128)S(1)}, f32[400,512]{1,0:T(8,128)S(1)}, u32[]{:S(2)}, u32[]{:S(2)}) collective-permute-start(f32[400,512]{1,0:T(8,128)S(1)} %fusion.12), channel_id=1, source_target_pairs={{0,1},{1,0},{2,3},{3,2},{4,5},{5,4},{6,7},{7,6},{8,9},{9,8},{10,11... | collective-permute-start | bytes 2457608 | tf_op jit(solution)/shard_map/ppermute | solution.py:20
  40.1 1.1 copy-start.1
  43.1 9.5 %collective-permute-start.11 = (f32[160,512]{1,0:T(8,128)}, f32[160,512]{1,0:T(8,128)}, u32[]{:S(2)}, u32[]{:S(2)}) collective-permute-start(f32[160,512]{1,0:T(8,128)} %get-tuple-element.37), channel_id=1, source_target_pairs={{0,1},{1,0},{2,3},{3,2},{4,5},{5,4},{6,7},{7,6},{8,9},{9,8},{10,11... | collective-permute-start | bytes 983048 | tf_op jit(solution)/shard_map/ppermute | solution.py:20
  43.1 9.5 %collective-permute-start.12 = (f32[160,512]{1,0:T(8,128)S(1)}, f32[160,512]{1,0:T(8,128)}, u32[]{:S(2)}, u32[]{:S(2)}) collective-permute-start(f32[160,512]{1,0:T(8,128)S(1)} %get-tuple-element.38), channel_id=1, source_target_pairs={{0,1},{1,0},{2,3},{3,2},{4,5},{5,4},{6,7},{7,6},{8,9},{9,8},{10,11... | collective-permute-start | bytes 983048 | tf_op jit(solution)/shard_map/ppermute | solution.py:20
  44.2 13.9 %collective-permute-start.10 = (bf16[120,2048]{1,0:T(8,128)(2,1)}, bf16[120,2048]{1,0:T(8,128)(2,1)S(1)}, u32[]{:S(2)}, u32[]{:S(2)}) collective-permute-start(bf16[120,2048]{1,0:T(8,128)(2,1)} %get-tuple-element.25), channel_id=1, source_target_pairs={{0,192},{64,0},{128,64},{192,128},{1,193},{65,1},{129,65},{193,129... | collective-permute-start | bytes 1474568 | tf_op jit(solution)/shard_map/ppermute | solution.py:12
  47.1 14.3 %collective-permute-start.9 = (bf16[120,2048]{1,0:T(8,128)(2,1)}, bf16[120,2048]{1,0:T(8,128)(2,1)S(1)}, u32[]{:S(2)}, u32[]{:S(2)}) collective-permute-start(bf16[120,2048]{1,0:T(8,128)(2,1)} %get-tuple-element.24), channel_id=1, source_target_pairs={{0,64},{64,128},{128,192},{192,0},{1,65},{65,129},{129,193},{193,1... | collective-permute-start | bytes 1474568 | tf_op jit(solution)/shard_map/ppermute | solution.py:12
  48.1 18.2 %all-to-all-start = ((f32[4,400,128]{2,1,0:T(8,128)}), f32[4,400,128]{2,1,0:T(8,128)S(1)}, u32[]{:S(2)}, u32[]{:S(2)}) async-start(f32[4,400,128]{2,1,0:T(8,128)} %bitcast_bitcast_fusion.1), calls=%async_computation | async-start | bytes 1638400 | tf_op jit(solution)/shard_map/all_to_all | solution.py:41
  52.6 10.5 %copy-start.4 = (bf16[2048,1024]{0,1:T(8,128)(2,1)S(1)}, bf16[2048,1024]{0,1:T(8,128)(2,1)}, u32[]{:S(2)}) copy-start(bf16[2048,1024]{0,1:T(8,128)(2,1)} %copy-done.3) | copy-start | bytes 12582916
  66.1 3.6 %collective-permute-start.16 = (f32[320,512]{1,0:T(8,128)}, f32[320,512]{1,0:T(8,128)}, u32[]{:S(2)}, u32[]{:S(2)}) collective-permute-start(f32[320,512]{1,0:T(8,128)} %fusion.8), channel_id=1, source_target_pairs={{0,1},{1,0},{2,3},{3,2},{4,5},{5,4},{6,7},{7,6},{8,9},{9,8},{10,11... | collective-permute-start | bytes 1966088 | tf_op jit(solution)/shard_map/ppermute | solution.py:20
  66.4 14.9 %collective-permute-start.14 = (bf16[120,2048]{1,0:T(8,128)(2,1)S(1)}, bf16[120,2048]{1,0:T(8,128)(2,1)S(1)}, u32[]{:S(2)}, u32[]{:S(2)}) collective-permute-start(bf16[120,2048]{1,0:T(8,128)(2,1)S(1)} %get-tuple-element.32), channel_id=1, source_target_pairs={{0,64},{64,128},{128,192},{192,0},{1,65},{65,129},{129,193},{193,1... | collective-permute-start | bytes 1474568 | tf_op jit(solution)/shard_map/ppermute | solution.py:12
  66.5 14.8 %collective-permute-start.15 = (bf16[120,2048]{1,0:T(8,128)(2,1)S(1)}, bf16[120,2048]{1,0:T(8,128)(2,1)S(1)}, u32[]{:S(2)}, u32[]{:S(2)}) collective-permute-start(bf16[120,2048]{1,0:T(8,128)(2,1)S(1)} %get-tuple-element.33), channel_id=1, source_target_pairs={{0,192},{64,0},{128,64},{192,128},{1,193},{65,1},{129,65},{193,129... | collective-permute-start | bytes 1474568 | tf_op jit(solution)/shard_map/ppermute | solution.py:12
  69.7 11.7 %copy-start.5 = (bf16[2048,1024]{0,1:T(8,128)(2,1)S(1)}, bf16[2048,1024]{0,1:T(8,128)(2,1)}, u32[]{:S(2)}) copy-start(bf16[2048,1024]{0,1:T(8,128)(2,1)} %copy-done.3) | copy-start | bytes 12582916
  81.4 1.1 copy-start
  82.2 6.0 %collective-permute-start.18 = (f32[240,512]{1,0:T(8,128)S(1)}, f32[240,512]{1,0:T(8,128)}, u32[]{:S(2)}, u32[]{:S(2)}) collective-permute-start(f32[240,512]{1,0:T(8,128)S(1)} %fusion.6), channel_id=1, source_target_pairs={{0,1},{1,0},{2,3},{3,2},{4,5},{5,4},{6,7},{7,6},{8,9},{9,8},{10,11... | collective-permute-start | bytes 1474568 | tf_op jit(solution)/shard_map/ppermute | solution.py:20
  83.7 28.3 %all-to-all-start.1 = ((f32[4,640,128]{2,1,0:T(8,128)}), f32[4,640,128]{2,1,0:T(8,128)S(1)}, u32[]{:S(2)}, u32[]{:S(2)}) async-start(f32[4,640,128]{2,1,0:T(8,128)} %bitcast_bitcast_fusion), calls=%async_computation.1 | async-start | bytes 2621440 | tf_op jit(solution)/shard_map/all_to_all | solution.py:41
  90.6 18.8 %collective-permute-start.19 = (f32[240,128]{1,0:T(8,128)S(1)}, f32[240,128]{1,0:T(8,128)S(1)}, u32[]{:S(2)}, u32[]{:S(2)}) collective-permute-start(f32[240,128]{1,0:T(8,128)S(1)} %get-tuple-element.39), channel_id=1, source_target_pairs={{0,4},{4,8},{8,12},{12,0},{1,5},{5,9},{9,13},{13,1},{2,6},{6,10},{... | collective-permute-start | bytes 368648 | tf_op jit(solution)/shard_map/ppermute | solution.py:12
  93.0 16.5 %collective-permute-start.20 = (f32[240,128]{1,0:T(8,128)S(1)}, f32[240,128]{1,0:T(8,128)S(1)}, u32[]{:S(2)}, u32[]{:S(2)}) collective-permute-start(f32[240,128]{1,0:T(8,128)S(1)} %get-tuple-element.41), channel_id=1, source_target_pairs={{0,12},{4,0},{8,4},{12,8},{1,13},{5,1},{9,5},{13,9},{2,14},{6,2},{... | collective-permute-start | bytes 368648 | tf_op jit(solution)/shard_map/ppermute | solution.py:12
  94.3 17.6 %collective-permute-start.21 = (f32[240,128]{1,0:T(8,128)S(1)}, f32[240,128]{1,0:T(8,128)S(1)}, u32[]{:S(2)}, u32[]{:S(2)}) collective-permute-start(f32[240,128]{1,0:T(8,128)S(1)} %get-tuple-element.40), channel_id=1, source_target_pairs={{0,8},{4,12},{8,0},{12,4},{1,9},{5,13},{9,1},{13,5},{2,10},{6,14},... | collective-permute-start | bytes 368648 | tf_op jit(solution)/shard_map/ppermute | solution.py:12
  96.6 17.6 %collective-permute-start.13 = (f32[400,128]{1,0:T(8,128)S(1)}, f32[400,128]{1,0:T(8,128)S(1)}, u32[]{:S(2)}, u32[]{:S(2)}) collective-permute-start(f32[400,128]{1,0:T(8,128)S(1)} %reduce_sum.18), channel_id=1, source_target_pairs={{0,2},{2,0},{1,3},{3,1},{4,6},{6,4},{5,7},{7,5},{8,10},{10,8},{9,1... | collective-permute-start | bytes 614408 | tf_op jit(solution)/shard_map/ppermute | solution.py:20
  111.9 6.3 %collective-permute-start.22 = (f32[240,128]{1,0:T(8,128)S(1)}, f32[240,128]{1,0:T(8,128)S(1)}, u32[]{:S(2)}, u32[]{:S(2)}) collective-permute-start(f32[240,128]{1,0:T(8,128)S(1)} %add_add_fusion), channel_id=1, source_target_pairs={{0,2},{2,0},{1,3},{3,1},{4,6},{6,4},{5,7},{7,5},{8,10},{10,8},{9,1... | collective-permute-start | bytes 368648 | tf_op jit(solution)/shard_map/ppermute | solution.py:20
  112.1 11.3 %collective-permute-start.17 = (f32[640,128]{1,0:T(8,128)S(1)}, f32[640,128]{1,0:T(8,128)S(1)}, u32[]{:S(2)}, u32[]{:S(2)}) collective-permute-start(f32[640,128]{1,0:T(8,128)S(1)} %reduce_sum.19), channel_id=1, source_target_pairs={{0,2},{2,0},{1,3},{3,1},{4,6},{6,4},{5,7},{7,5},{8,10},{10,8},{9,1... | collective-permute-start | bytes 983048 | tf_op jit(solution)/shard_map/ppermute | solution.py:20

commit v7 on v6

--- a/solution.py
+++ b/solution.py
@@ -73,17 +73,21 @@
     )
     from_xm, from_xp = shift(after_xm, "x", 4, 1), shift(after_xp, "x", 4, -1)
     early = over_y(early)
-    late = dot(late_rows, mine) + joined(swap(away[:160], "core"), swap(away[160:], "core"))
+    kept_rows, early = lax.optimization_barrier((late_rows, early))
+    late = dot(kept_rows, mine) + joined(swap(away[:160], "core"), swap(away[160:], "core"))
     from_xm, from_xp, late = lax.optimization_barrier((from_xm, from_xp, late))
-    after_xm, after_xp, early = lax.optimization_barrier(
-        (joined(side_xm[80:], from_xm[40:80]), joined(side_xp[:80], from_xp[:40]), early)
-    )
-    last_xm, last_xp = shift(after_xm, "x", 4, 1), shift(after_xp, "x", 4, -1)
-    second = paired(joined(far, from_xm, from_xp))
+    last_xm = shift(joined(side_xm[80:], from_xm[40:80]), "x", 4, 1)
+    last_xp = shift(joined(side_xp[:80], from_xp[:40]), "x", 4, -1)
+    late = over_y(late)
+    rows = joined(far, from_xm, from_xp)
+    away = swap(dot(rows, theirs), "core")
+    rows, late = lax.optimization_barrier((rows, late))
+    second = dot(rows, mine) + away
     last_xm, last_xp, second = lax.optimization_barrier((last_xm, last_xp, second))
-    second = over_y(joined(late, second))
-    third = over_y_at_once(paired(joined(last_xm, last_xp)))
-    sums = [over_zl(part) for part in (early, second, third)]
+    second = over_y(second)
+    third, second = lax.optimization_barrier((paired(joined(last_xm, last_xp)), second))
+    third = over_y_at_once(third)
+    sums = [over_zl(part) for part in (joined(early, late), second, third)]
     sites = [
         [block(0, 0), block(-1, 0), block(1, 0), block(0, -1), block(0, 1)],
         [block(-1, -1), block(-1, 1), block(1, -1), block(1, 1)],

time: 126 us -> 135 us (1.071)
  waiting for transfers between devices: 51.5 us -> 57 us
  local copies, waits for them, and re-layouts: 5.68 us -> 9.44 us
    all_to_all x2 -> x3, waiting for transfers between devices: 0.01 us -> 19.1 us  [over_y(): lax.all_to_all(split, 'y', split_axis=0, concat_axis=0, tiled=True)]
    ppermute x15, waiting for transfers between devices: 42.5 us -> 33.1 us  [shift(): lax.ppermute(value, axis, [(i, (i + by) % size) for i in range(size)])]
    all_to_all x2 -> x3, starting transfers between devices: 8.93 us -> 14.1 us  [over_y(): lax.all_to_all(split, 'y', split_axis=0, concat_axis=0, tiled=True)]
    ppermute x8, waiting for transfers between devices: 8.99 us -> 4.76 us  [swap(): return lax.ppermute(value, axis, [(0, 1), (1, 0)])]
    ppermute x15, starting transfers between devices: 27.4 us -> 23.7 us  [shift(): lax.ppermute(value, axis, [(i, (i + by) % size) for i in range(size)])]
    ppermute x8, starting transfers between devices: 3.15 us -> 1.29 us  [swap(): return lax.ppermute(value, axis, [(0, 1), (1, 0)])]
    transpose x1 -> x3, local copies, waits for them, and re-layouts: 0.95 us -> 2.8 us  [over_y(): split = pair.reshape(pair.shape[0], 4, 128).transpose(1, 0, 2)]
    unnamed x21 -> x26, local copies, waits for them, and re-layouts: 2.69 us -> 3.47 us
  transfers between devices with their start and end apart: 25 -> 26, of which waited for: 12 -> 16; matrix products, arithmetic and copies ran while one was open for 23% -> 21% of each run, Pallas kernels for 0% -> 0%
where the time goes in v7:
time: 135 us
  waiting for transfers between devices  57 us (42%)
  starting transfers between devices  39 us (29%)
  matrix products  26.8 us (20%)
  local copies, waits for them, and re-layouts  9.44 us (7%)
  other arithmetic  1.82 us (1%)
    ppermute x15, waiting for transfers between devices, shift(): lax.ppermute(value, axis, [(i, (i + by) % size) for i in range(size)])  33.1 us
    dot_general x9, matrix products, dot(): return jnp.dot(left, right, preferred_element_type=F32)  24.6 us
    ppermute x15, starting transfers between devices, shift(): lax.ppermute(value, axis, [(i, (i + by) % size) for i in range(size)])  23.7 us
    all_to_all x3, waiting for transfers between devices, over_y(): lax.all_to_all(split, 'y', split_axis=0, concat_axis=0, tiled=True)  19.1 us
    all_to_all x3, starting transfers between devices, over_y(): lax.all_to_all(split, 'y', split_axis=0, concat_axis=0, tiled=True)  14.1 us
    ppermute x8, waiting for transfers between devices, swap(): return lax.ppermute(value, axis, [(0, 1), (1, 0)])  4.76 us
    unnamed x26, local copies, waits for them, and re-layouts  3.47 us
    transpose x3, local copies, waits for them, and re-layouts, over_y(): split = pair.reshape(pair.shape[0], 4, 128).transpose(1, 0, 2)  2.8 us
  transfers between devices with their start and end apart: 26, of which 16 were waited for; matrix products, arithmetic and copies ran while one was open for 21% of the time, Pallas kernels for 0%

profile of v7, /device:TPU:64, one launch (start us, length us, event | category | flops | bytes accessed | tf_op | source)
XLA Modules:
  0.0 134.6 jit_solution(10648316393905322009)
XLA Ops:
  0.0 4.5 %collective-permute-start = (bf16[80,2048]{1,0:T(8,128)(2,1)}, bf16[80,2048]{1,0:T(8,128)(2,1)S(1)}, u32[]{:S(2)}, u32[]{:S(2)}) collective-permute-start(bf16[80,2048]{1,0:T(8,128)(2,1)} %param.2), channel_id=1, source_target_pairs={{0,16},{16,32},{32,48},{48,0},{1,17},{17,33},{33,49},{49,1},{2,18}... | collective-permute-start | bytes 983048 | tf_op jit(solution)/shard_map/ppermute | solution.py:12
  4.5 1.5 %collective-permute-start.6 = (bf16[80,2048]{1,0:T(8,128)(2,1)}, bf16[80,2048]{1,0:T(8,128)(2,1)S(1)}, u32[]{:S(2)}, u32[]{:S(2)}) collective-permute-start(bf16[80,2048]{1,0:T(8,128)(2,1)} %param.2), channel_id=1, source_target_pairs={{0,64},{64,128},{128,192},{192,0},{1,65},{65,129},{129,193},{193,1... | collective-permute-start | bytes 983048 | tf_op jit(solution)/shard_map/ppermute | solution.py:12
  6.0 1.7 %collective-permute-start.7 = (bf16[80,2048]{1,0:T(8,128)(2,1)}, bf16[80,2048]{1,0:T(8,128)(2,1)S(1)}, u32[]{:S(2)}, u32[]{:S(2)}) collective-permute-start(bf16[80,2048]{1,0:T(8,128)(2,1)} %param.2), channel_id=1, source_target_pairs={{0,192},{64,0},{128,64},{192,128},{1,193},{65,1},{129,65},{193,129... | collective-permute-start | bytes 983048 | tf_op jit(solution)/shard_map/ppermute | solution.py:12
  7.8 7.1 %convert_bitcast_fusion = bf16[2048,1024]{0,1:T(8,128)(2,1)S(1)} fusion(bf16[2048,1024]{1,0:T(8,128)(2,1)} %param.3, s32[1024]{0:T(1024)S(1)} %and_add_fusion), kind=kOutput, calls=%fused_computation.2 | convolution fusion | flops 4299161600 | bytes 8392704 | tf_op jit(solution)/shard_map/dot_general | solution.py:24
  14.9 3.8 %collective-permute-done = bf16[80,2048]{1,0:T(8,128)(2,1)S(1)} collective-permute-done((bf16[80,2048]{1,0:T(8,128)(2,1)}, bf16[80,2048]{1,0:T(8,128)(2,1)S(1)}, u32[]{:S(2)}, u32[]{:S(2)}) %collective-permute-start) | collective-permute-done | bytes 327712 | tf_op jit(solution)/shard_map/ppermute | solution.py:12
  18.7 4.2 %collective-permute-done.1 = bf16[80,2048]{1,0:T(8,128)(2,1)S(1)} collective-permute-done((bf16[80,2048]{1,0:T(8,128)(2,1)}, bf16[80,2048]{1,0:T(8,128)(2,1)S(1)}, u32[]{:S(2)}, u32[]{:S(2)}) %collective-permute-start.1) | collective-permute-done | bytes 327712 | tf_op jit(solution)/shard_map/ppermute | solution.py:12
  22.9 1.6 %collective-permute-start.2 = (bf16[160,2048]{1,0:T(8,128)(2,1)S(1)}, bf16[160,2048]{1,0:T(8,128)(2,1)S(1)}, u32[]{:S(2)}, u32[]{:S(2)}) collective-permute-start(bf16[160,2048]{1,0:T(8,128)(2,1)S(1)} %constant_dynamic-update-slice_fusion), channel_id=1, source_target_pairs={{0,64},{64,128},{128,192},{192,0},{1,65},{65,129},{129,193},{193,1... | collective-permute-start | bytes 1966088 | tf_op jit(solution)/shard_map/ppermute | solution.py:12
  24.5 1.7 %collective-permute-start.3 = (bf16[160,2048]{1,0:T(8,128)(2,1)S(1)}, bf16[160,2048]{1,0:T(8,128)(2,1)S(1)}, u32[]{:S(2)}, u32[]{:S(2)}) collective-permute-start(bf16[160,2048]{1,0:T(8,128)(2,1)S(1)} %constant_dynamic-update-slice_fusion), channel_id=1, source_target_pairs={{0,192},{64,0},{128,64},{192,128},{1,193},{65,1},{129,65},{193,129... | collective-permute-start | bytes 1966088 | tf_op jit(solution)/shard_map/ppermute | solution.py:12
  26.4 4.2 %collective-permute-start.5 = (bf16[40,2048]{1,0:T(8,128)(2,1)S(1)}, bf16[40,2048]{1,0:T(8,128)(2,1)S(1)}, u32[]{:S(2)}, u32[]{:S(2)}) collective-permute-start(bf16[40,2048]{1,0:T(8,128)(2,1)S(1)} %slice.73), channel_id=1, source_target_pairs={{0,16},{16,32},{32,48},{48,0},{1,17},{17,33},{33,49},{49,1},{2,18}... | collective-permute-start | bytes 491528 | tf_op jit(solution)/shard_map/ppermute | solution.py:12
  30.7 1.0 fusion.12
  32.1 1.8 %collective-permute-done.4 = bf16[40,2048]{1,0:T(8,128)(2,1)S(1)} collective-permute-done((bf16[40,2048]{1,0:T(8,128)(2,1)S(1)}, bf16[40,2048]{1,0:T(8,128)(2,1)S(1)}, u32[]{:S(2)}, u32[]{:S(2)}) %collective-permute-start.4) | collective-permute-done | bytes 163872 | tf_op jit(solution)/shard_map/ppermute | solution.py:12
  34.4 1.1 pad_maximum_fusion.2
  35.4 4.5 %collective-permute-done.2 = bf16[160,2048]{1,0:T(8,128)(2,1)S(1)} collective-permute-done((bf16[160,2048]{1,0:T(8,128)(2,1)S(1)}, bf16[160,2048]{1,0:T(8,128)(2,1)S(1)}, u32[]{:S(2)}, u32[]{:S(2)}) %collective-permute-start.2) | collective-permute-done | bytes 655392 | tf_op jit(solution)/shard_map/ppermute | solution.py:12
  40.1 1.7 %fusion.10 = f32[320,512]{1,0:T(8,128)} fusion(bf16[320,2048]{1,0:T(8,128)(2,1)S(1)} %constant_dynamic-update-slice_fusion.2, bf16[2048,1024]{0,1:T(8,128)(2,1)S(1)} %convert_bitcast_fusion), kind=kOutput, calls=%fused_computation.12 | convolution fusion | flops 671088640 | bytes 4063232 | tf_op jit(solution)/shard_map/dot_general | solution.py:24
  41.9 1.0 fusion.25
  42.9 1.0 bitcast_bitcast_fusion
  43.9 4.5 %all-to-all-start = ((f32[4,400,128]{2,1,0:T(8,128)}), f32[4,400,128]{2,1,0:T(8,128)S(1)}, u32[]{:S(2)}, u32[]{:S(2)}) async-start(f32[4,400,128]{2,1,0:T(8,128)} %bitcast_bitcast_fusion), calls=%async_computation | async-start | bytes 1638400 | tf_op jit(solution)/shard_map/all_to_all | solution.py:41
  48.4 2.0 %fusion.40 = (f32[160,512]{1,0:T(8,128)}, f32[160,512]{1,0:T(8,128)}) fusion(f32[320,512]{1,0:T(8,128)} %fusion.10), kind=kLoop, calls=%fused_computation.88 | loop fusion | bytes 1310720 | tf_op jit(solution)/shard_map/slice | solution.py:77
  50.8 0.7 constant_dynamic-update-slice_fusion.11
  51.5 2.9 %collective-permute-start.10 = (bf16[120,2048]{1,0:T(8,128)(2,1)}, bf16[120,2048]{1,0:T(8,128)(2,1)S(1)}, u32[]{:S(2)}, u32[]{:S(2)}) collective-permute-start(bf16[120,2048]{1,0:T(8,128)(2,1)} %get-tuple-element.30), channel_id=1, source_target_pairs={{0,192},{64,0},{128,64},{192,128},{1,193},{65,1},{129,65},{193,129... | collective-permute-start | bytes 1474568 | tf_op jit(solution)/shard_map/ppermute | solution.py:12
  54.4 0.7 constant_dynamic-update-slice_fusion.10
  55.1 4.3 %all-to-all-done = f32[4,400,128]{2,1,0:T(8,128)S(1)} async-done(((f32[4,400,128]{2,1,0:T(8,128)}), f32[4,400,128]{2,1,0:T(8,128)S(1)}, u32[]{:S(2)}, u32[]{:S(2)}) %all-to-all-start) | async-done | bytes 819232 | tf_op jit(solution)/shard_map/all_to_all | solution.py:41
  59.4 3.0 %fusion.22 = f32[320,512]{1,0:T(8,128)S(1)} fusion(bf16[320,2048]{1,0:T(8,128)(2,1)} %copy-done.4, bf16[2048,1024]{0,1:T(8,128)(2,1)} %copy-done.6, f32[160,512]{1,0:T(8,128)} %collective-permute-done.12, f32[160,512]{1,0:T(8,128)} %collective-permute-done.11), kind=kOutput, calls=%fused_computation.24 | convolution fusion | flops 671416320 | bytes 4718592 | tf_op jit(solution)/shard_map/dot_general | solution.py:24
  62.4 3.0 %collective-permute-done.10 = bf16[120,2048]{1,0:T(8,128)(2,1)S(1)} collective-permute-done((bf16[120,2048]{1,0:T(8,128)(2,1)}, bf16[120,2048]{1,0:T(8,128)(2,1)S(1)}, u32[]{:S(2)}, u32[]{:S(2)}) %collective-permute-start.10) | collective-permute-done | bytes 491552 | tf_op jit(solution)/shard_map/ppermute | solution.py:12
  65.3 3.3 %collective-permute-done.9 = bf16[120,2048]{1,0:T(8,128)(2,1)S(1)} collective-permute-done((bf16[120,2048]{1,0:T(8,128)(2,1)}, bf16[120,2048]{1,0:T(8,128)(2,1)S(1)}, u32[]{:S(2)}, u32[]{:S(2)}) %collective-permute-start.9) | collective-permute-done | bytes 491552 | tf_op jit(solution)/shard_map/ppermute | solution.py:12
  68.7 0.9 constant_dynamic-update-slice_fusion.9
  69.5 0.8 constant_dynamic-update-slice_fusion.8
  70.3 0.9 bitcast_bitcast_fusion.2
  71.3 4.8 %all-to-all-start.1 = ((f32[4,320,128]{2,1,0:T(8,128)}), f32[4,320,128]{2,1,0:T(8,128)S(1)}, u32[]{:S(2)}, u32[]{:S(2)}) async-start(f32[4,320,128]{2,1,0:T(8,128)} %bitcast_bitcast_fusion.2), calls=%async_computation.1 | async-start | bytes 1310720 | tf_op jit(solution)/shard_map/all_to_all | solution.py:41
  76.1 3.8 %fusion.8 = f32[320,512]{1,0:T(8,128)} fusion(bf16[320,2048]{1,0:T(8,128)(2,1)} %constant_dynamic-update-slice_fusion.8, bf16[2048,1024]{0,1:T(8,128)(2,1)} %copy-done.6), kind=kOutput, calls=%fused_computation.10 | convolution fusion | flops 671088640 | bytes 4063232 | tf_op jit(solution)/shard_map/dot_general | solution.py:24
  80.3 1.8 %collective-permute-start.14 = (bf16[120,2048]{1,0:T(8,128)(2,1)S(1)}, bf16[120,2048]{1,0:T(8,128)(2,1)}, u32[]{:S(2)}, u32[]{:S(2)}) collective-permute-start(bf16[120,2048]{1,0:T(8,128)(2,1)S(1)} %pad_maximum_fusion.3), channel_id=1, source_target_pairs={{0,64},{64,128},{128,192},{192,0},{1,65},{65,129},{129,193},{193,1... | collective-permute-start | bytes 1474568 | tf_op jit(solution)/shard_map/ppermute | solution.py:12
  82.1 3.8 %all-to-all-done.1 = f32[4,320,128]{2,1,0:T(8,128)S(1)} async-done(((f32[4,320,128]{2,1,0:T(8,128)}), f32[4,320,128]{2,1,0:T(8,128)S(1)}, u32[]{:S(2)}, u32[]{:S(2)}) %all-to-all-start.1) | async-done | bytes 655392 | tf_op jit(solution)/shard_map/all_to_all | solution.py:41
  86.0 3.0 %fusion.16 = f32[320,512]{1,0:T(8,128)S(1)} fusion(bf16[320,2048]{1,0:T(8,128)(2,1)} %constant_dynamic-update-slice_fusion.8, bf16[2048,1024]{0,1:T(8,128)(2,1)} %copy-done.6), kind=kOutput, calls=%fused_computation.18 | convolution fusion | flops 671088640 | bytes 4063232 | tf_op jit(solution)/shard_map/dot_general | solution.py:24
  89.1 4.5 %collective-permute-done.15 = bf16[120,2048]{1,0:T(8,128)(2,1)S(1)} collective-permute-done((bf16[120,2048]{1,0:T(8,128)(2,1)S(1)}, bf16[120,2048]{1,0:T(8,128)(2,1)S(1)}, u32[]{:S(2)}, u32[]{:S(2)}) %collective-permute-start.15) | collective-permute-done | bytes 491552 | tf_op jit(solution)/shard_map/ppermute | solution.py:12
  93.6 1.5 %collective-permute-done.14 = bf16[120,2048]{1,0:T(8,128)(2,1)} collective-permute-done((bf16[120,2048]{1,0:T(8,128)(2,1)S(1)}, bf16[120,2048]{1,0:T(8,128)(2,1)}, u32[]{:S(2)}, u32[]{:S(2)}) %collective-permute-start.14) | collective-permute-done | bytes 491552 | tf_op jit(solution)/shard_map/ppermute | solution.py:12
  95.1 1.1 constant_dynamic-update-slice_fusion.15
  96.2 1.6 %fusion.6 = f32[240,512]{1,0:T(8,128)} fusion(bf16[240,2048]{1,0:T(8,128)(2,1)S(1)} %constant_dynamic-update-slice_fusion.14, bf16[2048,1024]{0,1:T(8,128)(2,1)S(1)} %copy-done.7), kind=kOutput, calls=%fused_computation.8 | convolution fusion | flops 503316480 | bytes 3571712 | tf_op jit(solution)/shard_map/dot_general | solution.py:24
  97.9 0.9 bitcast_bitcast_fusion.1
  98.8 4.8 %all-to-all-start.2 = ((f32[4,320,128]{2,1,0:T(8,128)}), f32[4,320,128]{2,1,0:T(8,128)S(1)}, u32[]{:S(2)}, u32[]{:S(2)}) async-start(f32[4,320,128]{2,1,0:T(8,128)} %bitcast_bitcast_fusion.1), calls=%async_computation.2 | async-start | bytes 1310720 | tf_op jit(solution)/shard_map/all_to_all | solution.py:41
  104.0 11.1 %all-to-all-done.2 = f32[4,320,128]{2,1,0:T(8,128)S(1)} async-done(((f32[4,320,128]{2,1,0:T(8,128)}), f32[4,320,128]{2,1,0:T(8,128)S(1)}, u32[]{:S(2)}, u32[]{:S(2)}) %all-to-all-start.2) | async-done | bytes 655392 | tf_op jit(solution)/shard_map/all_to_all | solution.py:41
  115.2 2.3 %fusion.28 = f32[240,512]{1,0:T(8,128)S(1)} fusion(f32[240,512]{1,0:T(8,128)S(1)} %collective-permute-done.17, bf16[240,2048]{1,0:T(8,128)(2,1)S(1)} %constant_dynamic-update-slice_fusion.14, bf16[2048,1024]{0,1:T(8,128)(2,1)} %copy-done.6), kind=kOutput, calls=%fused_computation.26 | convolution fusion | flops 503439360 | bytes 4063232 | tf_op jit(solution)/shard_map/dot_general | solution.py:24
  117.6 0.6 collective-permute-start.19
  118.2 2.7 %collective-permute-start.20 = (f32[240,128]{1,0:T(8,128)S(1)}, f32[240,128]{1,0:T(8,128)S(1)}, u32[]{:S(2)}, u32[]{:S(2)}) collective-permute-start(f32[240,128]{1,0:T(8,128)S(1)} %get-tuple-element.47), channel_id=1, source_target_pairs={{0,12},{4,0},{8,4},{12,8},{1,13},{5,1},{9,5},{13,9},{2,14},{6,2},{... | collective-permute-start | bytes 368648 | tf_op jit(solution)/shard_map/ppermute | solution.py:12
  121.2 2.6 %collective-permute-done.19 = f32[240,128]{1,0:T(8,128)S(1)} collective-permute-done((f32[240,128]{1,0:T(8,128)S(1)}, f32[240,128]{1,0:T(8,128)S(1)}, u32[]{:S(2)}, u32[]{:S(2)}) %collective-permute-start.19) | collective-permute-done | bytes 122912 | tf_op jit(solution)/shard_map/ppermute | solution.py:12
  123.7 1.7 %collective-permute-done.20 = f32[240,128]{1,0:T(8,128)S(1)} collective-permute-done((f32[240,128]{1,0:T(8,128)S(1)}, f32[240,128]{1,0:T(8,128)S(1)}, u32[]{:S(2)}, u32[]{:S(2)}) %collective-permute-start.20) | collective-permute-done | bytes 122912 | tf_op jit(solution)/shard_map/ppermute | solution.py:12
  125.4 1.8 %collective-permute-done.21 = f32[240,128]{1,0:T(8,128)S(1)} collective-permute-done((f32[240,128]{1,0:T(8,128)S(1)}, f32[240,128]{1,0:T(8,128)S(1)}, u32[]{:S(2)}, u32[]{:S(2)}) %collective-permute-start.21) | collective-permute-done | bytes 122912 | tf_op jit(solution)/shard_map/ppermute | solution.py:12
  127.5 4.7 %collective-permute-done.22 = f32[240,128]{1,0:T(8,128)S(1)} collective-permute-done((f32[240,128]{1,0:T(8,128)S(1)}, f32[240,128]{1,0:T(8,128)S(1)}, u32[]{:S(2)}, u32[]{:S(2)}) %collective-permute-start.22) | collective-permute-done | bytes 122912 | tf_op jit(solution)/shard_map/ppermute | solution.py:20
  132.4 2.2 %fusion.3 = bf16[64,1280]{1,0:T(8,128)(2,1)} fusion(s32[1280]{0:T(1024)S(1)} %concatenate.55, bf16[240,64]{1,0:T(8,128)(2,1)S(1)} %fusion.38, bf16[320,64]{1,0:T(8,128)(2,1)S(1)} %fusion.37, bf16[720,64]{1,0:T(8,128)(2,1)S(1)} %fusion.31), kind=kOutput, calls=%fused_computation.6 | convolution fusion | flops 211927040 | bytes 332800 | tf_op jit(solution)/shard_map/dot_general | solution.py:99
  (85 shorter events, 3.6 us)
Async XLA Ops:
  0.0 18.7 %collective-permute-start = (bf16[80,2048]{1,0:T(8,128)(2,1)}, bf16[80,2048]{1,0:T(8,128)(2,1)S(1)}, u32[]{:S(2)}, u32[]{:S(2)}) collective-permute-start(bf16[80,2048]{1,0:T(8,128)(2,1)} %param.2), channel_id=1, source_target_pairs={{0,16},{16,32},{32,48},{48,0},{1,17},{17,33},{33,49},{49,1},{2,18}... | collective-permute-start | bytes 983048 | tf_op jit(solution)/shard_map/ppermute | solution.py:12
  4.5 18.4 %collective-permute-start.1 = (bf16[80,2048]{1,0:T(8,128)(2,1)}, bf16[80,2048]{1,0:T(8,128)(2,1)S(1)}, u32[]{:S(2)}, u32[]{:S(2)}) collective-permute-start(bf16[80,2048]{1,0:T(8,128)(2,1)} %param.2), channel_id=1, source_target_pairs={{0,48},{16,0},{32,16},{48,32},{1,49},{17,1},{33,17},{49,33},{2,50}... | collective-permute-start | bytes 983048 | tf_op jit(solution)/shard_map/ppermute | solution.py:12
  4.5 21.8 %collective-permute-start.6 = (bf16[80,2048]{1,0:T(8,128)(2,1)}, bf16[80,2048]{1,0:T(8,128)(2,1)S(1)}, u32[]{:S(2)}, u32[]{:S(2)}) collective-permute-start(bf16[80,2048]{1,0:T(8,128)(2,1)} %param.2), channel_id=1, source_target_pairs={{0,64},{64,128},{128,192},{192,0},{1,65},{65,129},{129,193},{193,1... | collective-permute-start | bytes 983048 | tf_op jit(solution)/shard_map/ppermute | solution.py:12
  6.0 20.3 %collective-permute-start.7 = (bf16[80,2048]{1,0:T(8,128)(2,1)}, bf16[80,2048]{1,0:T(8,128)(2,1)S(1)}, u32[]{:S(2)}, u32[]{:S(2)}) collective-permute-start(bf16[80,2048]{1,0:T(8,128)(2,1)} %param.2), channel_id=1, source_target_pairs={{0,192},{64,0},{128,64},{192,128},{1,193},{65,1},{129,65},{193,129... | collective-permute-start | bytes 983048 | tf_op jit(solution)/shard_map/ppermute | solution.py:12
  7.7 7.1 %copy-start.5 = (bf16[80,2048]{1,0:T(8,128)(2,1)S(1)}, bf16[80,2048]{1,0:T(8,128)(2,1)}, u32[]{:S(2)}) copy-start(bf16[80,2048]{1,0:T(8,128)(2,1)} %param.2) | copy-start | bytes 983044
  14.8 27.0 %copy-start.6 = (bf16[2048,1024]{0,1:T(8,128)(2,1)}, bf16[2048,1024]{0,1:T(8,128)(2,1)S(1)}, u32[]{:S(2)}) copy-start(bf16[2048,1024]{0,1:T(8,128)(2,1)S(1)} %convert_bitcast_fusion) | copy-start | bytes 12582916
  22.9 17.0 %collective-permute-start.2 = (bf16[160,2048]{1,0:T(8,128)(2,1)S(1)}, bf16[160,2048]{1,0:T(8,128)(2,1)S(1)}, u32[]{:S(2)}, u32[]{:S(2)}) collective-permute-start(bf16[160,2048]{1,0:T(8,128)(2,1)S(1)} %constant_dynamic-update-slice_fusion), channel_id=1, source_target_pairs={{0,64},{64,128},{128,192},{192,0},{1,65},{65,129},{129,193},{193,1... | collective-permute-start | bytes 1966088 | tf_op jit(solution)/shard_map/ppermute | solution.py:12
  24.5 15.5 %collective-permute-start.3 = (bf16[160,2048]{1,0:T(8,128)(2,1)S(1)}, bf16[160,2048]{1,0:T(8,128)(2,1)S(1)}, u32[]{:S(2)}, u32[]{:S(2)}) collective-permute-start(bf16[160,2048]{1,0:T(8,128)(2,1)S(1)} %constant_dynamic-update-slice_fusion), channel_id=1, source_target_pairs={{0,192},{64,0},{128,64},{192,128},{1,193},{65,1},{129,65},{193,129... | collective-permute-start | bytes 1966088 | tf_op jit(solution)/shard_map/ppermute | solution.py:12
  26.3 7.6 %collective-permute-start.4 = (bf16[40,2048]{1,0:T(8,128)(2,1)S(1)}, bf16[40,2048]{1,0:T(8,128)(2,1)S(1)}, u32[]{:S(2)}, u32[]{:S(2)}) collective-permute-start(bf16[40,2048]{1,0:T(8,128)(2,1)S(1)} %slice.72), channel_id=1, source_target_pairs={{0,48},{16,0},{32,16},{48,32},{1,49},{17,1},{33,17},{49,33},{2,50}... | collective-permute-start | bytes 491528 | tf_op jit(solution)/shard_map/ppermute | solution.py:12
  26.4 8.0 %collective-permute-start.5 = (bf16[40,2048]{1,0:T(8,128)(2,1)S(1)}, bf16[40,2048]{1,0:T(8,128)(2,1)S(1)}, u32[]{:S(2)}, u32[]{:S(2)}) collective-permute-start(bf16[40,2048]{1,0:T(8,128)(2,1)S(1)} %slice.73), channel_id=1, source_target_pairs={{0,16},{16,32},{32,48},{48,0},{1,17},{17,33},{33,49},{49,1},{2,18}... | collective-permute-start | bytes 491528 | tf_op jit(solution)/shard_map/ppermute | solution.py:12
  31.7 10.1 %collective-permute-start.8 = (f32[400,512]{1,0:T(8,128)S(1)}, f32[400,512]{1,0:T(8,128)S(1)}, u32[]{:S(2)}, u32[]{:S(2)}) collective-permute-start(f32[400,512]{1,0:T(8,128)S(1)} %fusion.12), channel_id=1, source_target_pairs={{0,1},{1,0},{2,3},{3,2},{4,5},{5,4},{6,7},{7,6},{8,9},{9,8},{10,11... | collective-permute-start | bytes 2457608 | tf_op jit(solution)/shard_map/ppermute | solution.py:20
  40.0 15.1 %copy-start = (bf16[160,2048]{1,0:T(8,128)(2,1)}, bf16[160,2048]{1,0:T(8,128)(2,1)S(1)}, u32[]{:S(2)}) copy-start(bf16[160,2048]{1,0:T(8,128)(2,1)S(1)} %collective-permute-done.2) | copy-start | bytes 1966084
  40.0 15.0 %copy-start.1 = (bf16[160,2048]{1,0:T(8,128)(2,1)}, bf16[160,2048]{1,0:T(8,128)(2,1)S(1)}, u32[]{:S(2)}) copy-start(bf16[160,2048]{1,0:T(8,128)(2,1)S(1)} %collective-permute-done.3) | copy-start | bytes 1966084
  40.1 1.7 %copy-start.4 = (bf16[320,2048]{1,0:T(8,128)(2,1)}, bf16[320,2048]{1,0:T(8,128)(2,1)S(1)}, u32[]{:S(2)}) copy-start(bf16[320,2048]{1,0:T(8,128)(2,1)S(1)} %constant_dynamic-update-slice_fusion.2) | copy-start | bytes 3932164
  43.9 15.5 %all-to-all-start = ((f32[4,400,128]{2,1,0:T(8,128)}), f32[4,400,128]{2,1,0:T(8,128)S(1)}, u32[]{:S(2)}, u32[]{:S(2)}) async-start(f32[4,400,128]{2,1,0:T(8,128)} %bitcast_bitcast_fusion), calls=%async_computation | async-start | bytes 1638400 | tf_op jit(solution)/shard_map/all_to_all | solution.py:41
  50.3 9.1 %collective-permute-start.11 = (f32[160,512]{1,0:T(8,128)}, f32[160,512]{1,0:T(8,128)}, u32[]{:S(2)}, u32[]{:S(2)}) collective-permute-start(f32[160,512]{1,0:T(8,128)} %get-tuple-element.43), channel_id=1, source_target_pairs={{0,1},{1,0},{2,3},{3,2},{4,5},{5,4},{6,7},{7,6},{8,9},{9,8},{10,11... | collective-permute-start | bytes 983048 | tf_op jit(solution)/shard_map/ppermute | solution.py:20
  50.3 9.1 %collective-permute-start.12 = (f32[160,512]{1,0:T(8,128)}, f32[160,512]{1,0:T(8,128)}, u32[]{:S(2)}, u32[]{:S(2)}) collective-permute-start(f32[160,512]{1,0:T(8,128)} %get-tuple-element.44), channel_id=1, source_target_pairs={{0,1},{1,0},{2,3},{3,2},{4,5},{5,4},{6,7},{7,6},{8,9},{9,8},{10,11... | collective-permute-start | bytes 983048 | tf_op jit(solution)/shard_map/ppermute | solution.py:20
  51.5 13.8 %collective-permute-start.10 = (bf16[120,2048]{1,0:T(8,128)(2,1)}, bf16[120,2048]{1,0:T(8,128)(2,1)S(1)}, u32[]{:S(2)}, u32[]{:S(2)}) collective-permute-start(bf16[120,2048]{1,0:T(8,128)(2,1)} %get-tuple-element.30), channel_id=1, source_target_pairs={{0,192},{64,0},{128,64},{192,128},{1,193},{65,1},{129,65},{193,129... | collective-permute-start | bytes 1474568 | tf_op jit(solution)/shard_map/ppermute | solution.py:12
  54.4 14.3 %collective-permute-start.9 = (bf16[120,2048]{1,0:T(8,128)(2,1)}, bf16[120,2048]{1,0:T(8,128)(2,1)S(1)}, u32[]{:S(2)}, u32[]{:S(2)}) collective-permute-start(bf16[120,2048]{1,0:T(8,128)(2,1)} %get-tuple-element.29), channel_id=1, source_target_pairs={{0,64},{64,128},{128,192},{192,0},{1,65},{65,129},{129,193},{193,1... | collective-permute-start | bytes 1474568 | tf_op jit(solution)/shard_map/ppermute | solution.py:12
  65.3 5.9 %copy-start.2 = (bf16[120,2048]{1,0:T(8,128)(2,1)}, bf16[120,2048]{1,0:T(8,128)(2,1)S(1)}, u32[]{:S(2)}) copy-start(bf16[120,2048]{1,0:T(8,128)(2,1)S(1)} %collective-permute-done.10) | copy-start | bytes 1474564
  68.6 2.6 %copy-start.3 = (bf16[120,2048]{1,0:T(8,128)(2,1)}, bf16[120,2048]{1,0:T(8,128)(2,1)S(1)}, u32[]{:S(2)}) copy-start(bf16[120,2048]{1,0:T(8,128)(2,1)S(1)} %collective-permute-done.9) | copy-start | bytes 1474564
  71.3 14.7 %all-to-all-start.1 = ((f32[4,320,128]{2,1,0:T(8,128)}), f32[4,320,128]{2,1,0:T(8,128)S(1)}, u32[]{:S(2)}, u32[]{:S(2)}) async-start(f32[4,320,128]{2,1,0:T(8,128)} %bitcast_bitcast_fusion.2), calls=%async_computation.1 | async-start | bytes 1310720 | tf_op jit(solution)/shard_map/all_to_all | solution.py:41
  76.1 3.8 %slice-start.1 = ((bf16[160,2048]{1,0:T(8,128)(2,1)}), bf16[80,2048]{1,0:T(8,128)(2,1)S(1)}, s32[]{:S(2)}) async-start(bf16[160,2048]{1,0:T(8,128)(2,1)} %copy-done.1), calls=%async_computation.4 | async-start | bytes 655360 | tf_op jit(solution)/shard_map/slice | solution.py:80
  76.1 3.8 %slice-start.2 = ((bf16[120,2048]{1,0:T(8,128)(2,1)}), bf16[40,2048]{1,0:T(8,128)(2,1)S(1)}, s32[]{:S(2)}) async-start(bf16[120,2048]{1,0:T(8,128)(2,1)} %copy-done.2), calls=%async_computation.5 | async-start | bytes 327680 | tf_op jit(solution)/shard_map/slice | solution.py:80
  76.1 4.2 %slice-start = ((bf16[160,2048]{1,0:T(8,128)(2,1)}), bf16[80,2048]{1,0:T(8,128)(2,1)S(1)}, s32[]{:S(2)}) async-start(bf16[160,2048]{1,0:T(8,128)(2,1)} %copy-done), calls=%async_computation.3 | async-start | bytes 655360 | tf_op jit(solution)/shard_map/slice | solution.py:79
  76.1 4.2 %slice-start.3 = ((bf16[120,2048]{1,0:T(8,128)(2,1)}), bf16[40,2048]{1,0:T(8,128)(2,1)S(1)}, s32[]{:S(2)}) async-start(bf16[120,2048]{1,0:T(8,128)(2,1)} %copy-done.3), calls=%async_computation.6 | async-start | bytes 327680 | tf_op jit(solution)/shard_map/slice | solution.py:79
  79.9 9.1 %collective-permute-start.16 = (f32[320,512]{1,0:T(8,128)}, f32[320,512]{1,0:T(8,128)S(1)}, u32[]{:S(2)}, u32[]{:S(2)}) collective-permute-start(f32[320,512]{1,0:T(8,128)} %fusion.8), channel_id=1, source_target_pairs={{0,1},{1,0},{2,3},{3,2},{4,5},{5,4},{6,7},{7,6},{8,9},{9,8},{10,11... | collective-permute-start | bytes 1966088 | tf_op jit(solution)/shard_map/ppermute | solution.py:20
  79.9 13.7 %collective-permute-start.15 = (bf16[120,2048]{1,0:T(8,128)(2,1)S(1)}, bf16[120,2048]{1,0:T(8,128)(2,1)S(1)}, u32[]{:S(2)}, u32[]{:S(2)}) collective-permute-start(bf16[120,2048]{1,0:T(8,128)(2,1)S(1)} %pad_maximum_fusion.4), channel_id=1, source_target_pairs={{0,192},{64,0},{128,64},{192,128},{1,193},{65,1},{129,65},{193,129... | collective-permute-start | bytes 1474568 | tf_op jit(solution)/shard_map/ppermute | solution.py:12
  80.3 14.8 %collective-permute-start.14 = (bf16[120,2048]{1,0:T(8,128)(2,1)S(1)}, bf16[120,2048]{1,0:T(8,128)(2,1)}, u32[]{:S(2)}, u32[]{:S(2)}) collective-permute-start(bf16[120,2048]{1,0:T(8,128)(2,1)S(1)} %pad_maximum_fusion.3), channel_id=1, source_target_pairs={{0,64},{64,128},{128,192},{192,0},{1,65},{65,129},{129,193},{193,1... | collective-permute-start | bytes 1474568 | tf_op jit(solution)/shard_map/ppermute | solution.py:12
  86.0 10.2 %copy-start.7 = (bf16[2048,1024]{0,1:T(8,128)(2,1)S(1)}, bf16[2048,1024]{0,1:T(8,128)(2,1)}, u32[]{:S(2)}) copy-start(bf16[2048,1024]{0,1:T(8,128)(2,1)} %copy-done.6) | copy-start | bytes 12582916
  97.9 17.3 %collective-permute-start.17 = (f32[240,512]{1,0:T(8,128)}, f32[240,512]{1,0:T(8,128)S(1)}, u32[]{:S(2)}, u32[]{:S(2)}) collective-permute-start(f32[240,512]{1,0:T(8,128)} %fusion.6), channel_id=1, source_target_pairs={{0,1},{1,0},{2,3},{3,2},{4,5},{5,4},{6,7},{7,6},{8,9},{9,8},{10,11... | collective-permute-start | bytes 1474568 | tf_op jit(solution)/shard_map/ppermute | solution.py:20
  98.8 16.3 %all-to-all-start.2 = ((f32[4,320,128]{2,1,0:T(8,128)}), f32[4,320,128]{2,1,0:T(8,128)S(1)}, u32[]{:S(2)}, u32[]{:S(2)}) async-start(f32[4,320,128]{2,1,0:T(8,128)} %bitcast_bitcast_fusion.1), calls=%async_computation.2 | async-start | bytes 1310720 | tf_op jit(solution)/shard_map/all_to_all | solution.py:41
  103.7 17.2 %collective-permute-start.13 = (f32[720,128]{1,0:T(8,128)S(1)}, f32[720,128]{1,0:T(8,128)S(1)}, u32[]{:S(2)}, u32[]{:S(2)}) collective-permute-start(f32[720,128]{1,0:T(8,128)S(1)} %constant_dynamic-update-slice_fusion.12), channel_id=1, source_target_pairs={{0,2},{2,0},{1,3},{3,1},{4,6},{6,4},{5,7},{7,5},{8,10},{10,8},{9,1... | collective-permute-start | bytes 1105928 | tf_op jit(solution)/shard_map/ppermute | solution.py:20
  117.6 6.2 %collective-permute-start.19 = (f32[240,128]{1,0:T(8,128)S(1)}, f32[240,128]{1,0:T(8,128)S(1)}, u32[]{:S(2)}, u32[]{:S(2)}) collective-permute-start(f32[240,128]{1,0:T(8,128)S(1)} %get-tuple-element.45), channel_id=1, source_target_pairs={{0,4},{4,8},{8,12},{12,0},{1,5},{5,9},{9,13},{13,1},{2,6},{6,10},{... | collective-permute-start | bytes 368648 | tf_op jit(solution)/shard_map/ppermute | solution.py:12
  118.2 7.2 %collective-permute-start.20 = (f32[240,128]{1,0:T(8,128)S(1)}, f32[240,128]{1,0:T(8,128)S(1)}, u32[]{:S(2)}, u32[]{:S(2)}) collective-permute-start(f32[240,128]{1,0:T(8,128)S(1)} %get-tuple-element.47), channel_id=1, source_target_pairs={{0,12},{4,0},{8,4},{12,8},{1,13},{5,1},{9,5},{13,9},{2,14},{6,2},{... | collective-permute-start | bytes 368648 | tf_op jit(solution)/shard_map/ppermute | solution.py:12
  120.9 6.4 %collective-permute-start.21 = (f32[240,128]{1,0:T(8,128)S(1)}, f32[240,128]{1,0:T(8,128)S(1)}, u32[]{:S(2)}, u32[]{:S(2)}) collective-permute-start(f32[240,128]{1,0:T(8,128)S(1)} %get-tuple-element.46), channel_id=1, source_target_pairs={{0,8},{4,12},{8,0},{12,4},{1,9},{5,13},{9,1},{13,5},{2,10},{6,14},... | collective-permute-start | bytes 368648 | tf_op jit(solution)/shard_map/ppermute | solution.py:12
  121.1 6.4 %collective-permute-start.18 = (f32[320,128]{1,0:T(8,128)S(1)}, f32[320,128]{1,0:T(8,128)S(1)}, u32[]{:S(2)}, u32[]{:S(2)}) collective-permute-start(f32[320,128]{1,0:T(8,128)S(1)} %reduce_sum.29), channel_id=1, source_target_pairs={{0,2},{2,0},{1,3},{3,1},{4,6},{6,4},{5,7},{7,5},{8,10},{10,8},{9,1... | collective-permute-start | bytes 491528 | tf_op jit(solution)/shard_map/ppermute | solution.py:20
  127.3 5.0 %collective-permute-start.22 = (f32[240,128]{1,0:T(8,128)S(1)}, f32[240,128]{1,0:T(8,128)S(1)}, u32[]{:S(2)}, u32[]{:S(2)}) collective-permute-start(f32[240,128]{1,0:T(8,128)S(1)} %add_add_fusion), channel_id=1, source_target_pairs={{0,2},{2,0},{1,3},{3,1},{4,6},{6,4},{5,7},{7,5},{8,10},{10,8},{9,1... | collective-permute-start | bytes 368648 | tf_op jit(solution)/shard_map/ppermute | solution.py:20

commit v8 on v6

--- a/solution.py
+++ b/solution.py
@@ -1,6 +1,8 @@
 import jax
 import jax.numpy as jnp
 from jax import lax
+from jax.experimental import pallas as pl
+from jax.experimental.pallas import tpu as pltpu
 from jax.sharding import Mesh, PartitionSpec as P
 
 ROWS = 80
@@ -28,6 +30,42 @@
     return jnp.concatenate(parts, axis=0)
 
 
+def product(parts, values, away=None):
+    rows = sum(part.shape[0] for part in parts)
+    depth = values.shape[0]
+
+    def kernel(*refs):
+        held, out = refs[-1], refs[-2]
+
+        @pl.when(pl.program_id(0) == 0)
+        def _():
+            at = 0
+            for ref in refs[: len(parts)]:
+                held[at : at + ref.shape[0]] = ref[...]
+                at += ref.shape[0]
+
+        found = jnp.dot(held[...], refs[len(parts)][...], preferred_element_type=F32)
+        if away is None:
+            out[...] = found
+        else:
+            found += refs[len(parts) + 1][...]
+            out[0], out[1] = found[:, :128], found[:, 128:]
+
+    first = 0 if away is None else 2
+    whole = [pl.BlockSpec(part.shape, lambda i: (0, 0)) for part in parts]
+    half = pl.BlockSpec((rows, 256), lambda i: (0, i))
+    split = pl.BlockSpec((2, rows, 128), lambda i: (i, 0, 0))
+    return pl.pallas_call(
+        kernel,
+        grid=(2,),
+        in_specs=whole + [pl.BlockSpec((depth, 256), lambda i: (0, i + first))] + ([] if away is None else [half]),
+        out_specs=half if away is None else split,
+        out_shape=jax.ShapeDtypeStruct((rows, 512) if away is None else (4, rows, 128), F32),
+        scratch_shapes=[pltpu.VMEM((rows, depth), BF16)],
+        cost_estimate=pl.CostEstimate(flops=0, bytes_accessed=0, transcendentals=0),
+    )(*parts, values, *([] if away is None else [away]))
+
+
 def local(amplitudes, integrals):
     x, zh, y, zl, core = (lax.axis_index(n) for n in ("x", "zh", "y", "zl", "core"))
 
@@ -36,12 +74,11 @@
     level = jnp.where(at & 64 == 0, zl, 1 - zl)
     source = ((at >> 7) & 3) * 256 + level * 128 + owner * 64 + (at & 63)
 
-    def over_y(pair):
-        split = pair.reshape(pair.shape[0], 4, 128).transpose(1, 0, 2)
+    def over_y(split):
         return jnp.sum(lax.all_to_all(split, "y", split_axis=0, concat_axis=0, tiled=True), axis=0)
 
-    def over_y_at_once(pair):
-        part = lambda d: lax.dynamic_slice_in_dim(pair, ((y + d) % 4) * 128, 128, axis=1)
+    def over_y_at_once(split):
+        part = lambda d: lax.dynamic_index_in_dim(split, (y + d) % 4, 0, keepdims=False)
         others = [shift(part(d), "y", 4, d) for d in (1, 3, 2)]
         return part(0) + others[0] + others[1] + others[2]
 
@@ -57,33 +94,36 @@
     own_xm, own_xp = to_both(own, "x")
     order = (jnp.arange(1024)[:, None] == source[None, :]).astype(BF16)
     columns = dot(integrals, order).astype(BF16)
-    theirs, mine = columns[:, :512], columns[:, 512:]
 
-    def paired(rows):
-        return dot(rows, mine) + swap(dot(rows, theirs), "core")
+    def swapped(*parts):
+        return swap(product(parts, columns), "core")
 
     side = joined(zm, zp)
     side_xm, side_xp = to_both(side, "x")
     far = joined(shift(zp[:40], "zh", 4, -1), shift(zm[40:], "zh", 4, 1))
-    early = paired(joined(own, *lax.optimization_barrier((own_xm, own_xp, side))))
+    parts = (own, *lax.optimization_barrier((own_xm, own_xp, side)))
+    early = product(parts, columns, swapped(*parts))
 
-    late_rows = joined(side_xm, side_xp)
     after_xm, after_xp, early, away = lax.optimization_barrier(
-        (joined(far, own_xm[40:]), joined(far, own_xp[:40]), early, dot(late_rows, theirs))
+        (joined(far, own_xm[40:]), joined(far, own_xp[:40]), early, product((side_xm, side_xp), columns))
     )
     from_xm, from_xp = shift(after_xm, "x", 4, 1), shift(after_xp, "x", 4, -1)
     early = over_y(early)
-    late = dot(late_rows, mine) + joined(swap(away[:160], "core"), swap(away[160:], "core"))
+    late = product((side_xm, side_xp), columns, swap(away, "core"))
     from_xm, from_xp, late = lax.optimization_barrier((from_xm, from_xp, late))
+    late = over_y_at_once(late)
     after_xm, after_xp, early = lax.optimization_barrier(
         (joined(side_xm[80:], from_xm[40:80]), joined(side_xp[:80], from_xp[:40]), early)
     )
     last_xm, last_xp = shift(after_xm, "x", 4, 1), shift(after_xp, "x", 4, -1)
-    second = paired(joined(far, from_xm, from_xp))
+    parts = (far, from_xm, from_xp)
+    away, late = lax.optimization_barrier((swapped(*parts), late))
+    second = product(parts, columns, away)
     last_xm, last_xp, second = lax.optimization_barrier((last_xm, last_xp, second))
-    second = over_y(joined(late, second))
-    third = over_y_at_once(paired(joined(last_xm, last_xp)))
-    sums = [over_zl(part) for part in (early, second, third)]
+    second = over_y(second)
+    parts = (last_xm, last_xp)
+    last = over_y_at_once(product(parts, columns, swapped(*parts)))
+    sums = [over_zl(part) for part in (joined(early, late), second, last)]
     sites = [
         [block(0, 0), block(-1, 0), block(1, 0), block(0, -1), block(0, 1)],
         [block(-1, -1), block(-1, 1), block(1, -1), block(1, 1)],

time: 126 us -> 140 us (1.11)
  Pallas kernels: 0 us -> 28.5 us
  matrix products: 25.6 us -> 10.6 us
  waiting for transfers between devices: 51.5 us -> 44.4 us
  local copies, waits for them, and re-layouts: 5.68 us -> 11.6 us
  starting transfers between devices: 39.4 us -> 41 us
    pallas_call x0 -> x8, Pallas kernels: none -> 28.5 us  [product(): pl.pallas_call(kernel, grid=(2,), in_specs=whole + [pl.BlockSpec((depth,...]
    dot_general x9 -> x1, matrix products: 23.4 us -> 8.4 us  [dot(): return jnp.dot(left, right, preferred_element_type=F32)]
    ppermute x15 -> x18, waiting for transfers between devices: 42.5 us -> 29.7 us  [shift(): lax.ppermute(value, axis, [(i, (i + by) % size) for i in range(size)])]
    all_to_all x2, waiting for transfers between devices: 0.01 us -> 11.3 us  [over_y(): lax.all_to_all(split, 'y', split_axis=0, concat_axis=0, tiled=True)]
    ppermute x8 -> x7, waiting for transfers between devices: 8.99 us -> 3.4 us  [swap(): return lax.ppermute(value, axis, [(0, 1), (1, 0)])]
    unnamed x21 -> x29, local copies, waits for them, and re-layouts: 2.69 us -> 7.72 us
    ppermute x15 -> x18, starting transfers between devices: 27.4 us -> 29.4 us  [shift(): lax.ppermute(value, axis, [(i, (i + by) % size) for i in range(size)])]
    squeeze x0 -> x2, local copies, waits for them, and re-layouts: none -> 1.79 us  [over_y_at_once(): lax.dynamic_index_in_dim(split, (y + d) % 4, 0, keepdims=False)]
  transfers between devices with their start and end apart: 25 -> 27, of which waited for: 12 -> 14; matrix products, arithmetic and copies ran while one was open for 23% -> 11% of each run, Pallas kernels for 0% -> 10%
where the time goes in v8:
time: 140 us
  waiting for transfers between devices  44.4 us (32%)
  starting transfers between devices  41 us (29%)
  Pallas kernels  28.5 us (20%)
  local copies, waits for them, and re-layouts  11.6 us (8%)
  matrix products  10.6 us (8%)
  other arithmetic  3.17 us (2%)
    ppermute x18, waiting for transfers between devices, shift(): lax.ppermute(value, axis, [(i, (i + by) % size) for i in range(size)])  29.7 us
    ppermute x18, starting transfers between devices, shift(): lax.ppermute(value, axis, [(i, (i + by) % size) for i in range(size)])  29.4 us
    pallas_call x8, Pallas kernels, product(): pl.pallas_call(kernel, grid=(2,), in_specs=whole + [pl.BlockSpec((depth,...  28.5 us
    all_to_all x2, waiting for transfers between devices, over_y(): lax.all_to_all(split, 'y', split_axis=0, concat_axis=0, tiled=True)  11.3 us
    dot_general x1, matrix products, dot(): return jnp.dot(left, right, preferred_element_type=F32)  8.4 us
    all_to_all x2, starting transfers between devices, over_y(): lax.all_to_all(split, 'y', split_axis=0, concat_axis=0, tiled=True)  7.95 us
    unnamed x29, local copies, waits for them, and re-layouts  7.72 us
    ppermute x7, starting transfers between devices, swap(): return lax.ppermute(value, axis, [(0, 1), (1, 0)])  3.67 us
  transfers between devices with their start and end apart: 27, of which 14 were waited for; matrix products, arithmetic and copies ran while one was open for 11% of the time, Pallas kernels for 10%

profile of v8, /device:TPU:64, one launch (start us, length us, event | category | flops | bytes accessed | tf_op | source)
XLA Modules:
  0.0 139.5 jit_solution(3570095314164699810)
XLA Ops:
  0.0 2.8 %collective-permute-start.6 = (bf16[80,2048]{1,0:T(8,128)(2,1)}, bf16[80,2048]{1,0:T(8,128)(2,1)S(1)}, u32[]{:S(2)}, u32[]{:S(2)}) collective-permute-start(bf16[80,2048]{1,0:T(8,128)(2,1)} %refs_0_.3), channel_id=1, source_target_pairs={{0,192},{64,0},{128,64},{192,128},{1,193},{65,1},{129,65},{193,129... | collective-permute-start | bytes 983048 | tf_op jit(solution)/shard_map/ppermute | solution.py:14
  2.8 4.5 %collective-permute-start = (bf16[80,2048]{1,0:T(8,128)(2,1)}, bf16[80,2048]{1,0:T(8,128)(2,1)S(1)}, u32[]{:S(2)}, u32[]{:S(2)}) collective-permute-start(bf16[80,2048]{1,0:T(8,128)(2,1)} %refs_0_.3), channel_id=1, source_target_pairs={{0,16},{16,32},{32,48},{48,0},{1,17},{17,33},{33,49},{49,1},{2,18}... | collective-permute-start | bytes 983048 | tf_op jit(solution)/shard_map/ppermute | solution.py:14
  7.3 8.4 %convert_bitcast_fusion.refs_4_.refs_2_.refs_3_ = bf16[2048,1024]{1,0:T(8,128)(2,1)} fusion(bf16[2048,1024]{1,0:T(8,128)(2,1)} %param.3, s32[1024]{0:T(1024)S(1)} %and_add_fusion), kind=kOutput, calls=%fused_computation.2 | convolution fusion | flops 4298113024 | bytes 8392704 | tf_op jit(solution)/shard_map/dot_general | solution.py:26
  15.7 5.5 %collective-permute-done = bf16[80,2048]{1,0:T(8,128)(2,1)S(1)} collective-permute-done((bf16[80,2048]{1,0:T(8,128)(2,1)}, bf16[80,2048]{1,0:T(8,128)(2,1)S(1)}, u32[]{:S(2)}, u32[]{:S(2)}) %collective-permute-start) | collective-permute-done | bytes 327712 | tf_op jit(solution)/shard_map/ppermute | solution.py:14
  21.2 4.2 %collective-permute-done.1 = bf16[80,2048]{1,0:T(8,128)(2,1)S(1)} collective-permute-done((bf16[80,2048]{1,0:T(8,128)(2,1)}, bf16[80,2048]{1,0:T(8,128)(2,1)S(1)}, u32[]{:S(2)}, u32[]{:S(2)}) %collective-permute-start.1) | collective-permute-done | bytes 327712 | tf_op jit(solution)/shard_map/ppermute | solution.py:14
  25.5 0.9 copy-done
  27.2 3.9 %shard_map.28 = f32[400,512]{1,0:T(8,128)} custom-call(bf16[80,2048]{1,0:T(8,128)(2,1)} %refs_0_.3, bf16[80,2048]{1,0:T(8,128)(2,1)} %copy-done.7, bf16[80,2048]{1,0:T(8,128)(2,1)} %copy-done.6, bf16[160,2048]{1,0:T(8,128)(2,1)} %copy-done, bf16[2048,1024]{1,0:T(8,128)(2,1)} %convert_bitcast_fusion.refs_4_.refs_2_.refs_3_), custom_call_target="tpu_custom_call" | custom-call | tf_op jit(solution)/shard_map/pallas_call | solution.py:58
  31.1 3.2 %collective-permute-start.8 = (bf16[160,2048]{1,0:T(8,128)(2,1)}, bf16[160,2048]{1,0:T(8,128)(2,1)S(1)}, u32[]{:S(2)}, u32[]{:S(2)}) collective-permute-start(bf16[160,2048]{1,0:T(8,128)(2,1)} %copy-done), channel_id=1, source_target_pairs={{0,192},{64,0},{128,64},{192,128},{1,193},{65,1},{129,65},{193,129... | collective-permute-start | bytes 1966088 | tf_op jit(solution)/shard_map/ppermute | solution.py:14
  34.9 2.5 %collective-permute-start.3 = (bf16[40,2048]{1,0:T(8,128)(2,1)S(1)}, bf16[40,2048]{1,0:T(8,128)(2,1)S(1)}, u32[]{:S(2)}, u32[]{:S(2)}) collective-permute-start(bf16[40,2048]{1,0:T(8,128)(2,1)S(1)} %slice.57), channel_id=1, source_target_pairs={{0,48},{16,0},{32,16},{48,32},{1,49},{17,1},{33,17},{49,33},{2,50}... | collective-permute-start | bytes 491528 | tf_op jit(solution)/shard_map/ppermute | solution.py:14
  37.4 0.9 slice.60
  38.3 0.9 slice.59
  39.3 4.0 %collective-permute-done.4 = bf16[40,2048]{1,0:T(8,128)(2,1)S(1)} collective-permute-done((bf16[40,2048]{1,0:T(8,128)(2,1)S(1)}, bf16[40,2048]{1,0:T(8,128)(2,1)S(1)}, u32[]{:S(2)}, u32[]{:S(2)}) %collective-permute-start.4) | collective-permute-done | bytes 163872 | tf_op jit(solution)/shard_map/ppermute | solution.py:14
  43.3 1.9 %collective-permute-done.3 = bf16[40,2048]{1,0:T(8,128)(2,1)S(1)} collective-permute-done((bf16[40,2048]{1,0:T(8,128)(2,1)S(1)}, bf16[40,2048]{1,0:T(8,128)(2,1)S(1)}, u32[]{:S(2)}, u32[]{:S(2)}) %collective-permute-start.3) | collective-permute-done | bytes 163872 | tf_op jit(solution)/shard_map/ppermute | solution.py:14
  45.2 0.9 pad_maximum_fusion.2
  46.0 3.6 %collective-permute-done.2.refs_0_ = bf16[160,2048]{1,0:T(8,128)(2,1)S(1)} collective-permute-done((bf16[160,2048]{1,0:T(8,128)(2,1)}, bf16[160,2048]{1,0:T(8,128)(2,1)S(1)}, u32[]{:S(2)}, u32[]{:S(2)}) %collective-permute-start.2) | collective-permute-done | bytes 655392 | tf_op jit(solution)/shard_map/ppermute | solution.py:14
  49.6 0.9 copy-done.1
  50.5 0.8 copy-done.2
  51.3 3.5 %shard_map.30 = f32[320,512]{1,0:T(8,128)} custom-call(bf16[160,2048]{1,0:T(8,128)(2,1)} %copy-done.1, bf16[160,2048]{1,0:T(8,128)(2,1)} %copy-done.2, bf16[2048,1024]{1,0:T(8,128)(2,1)} %convert_bitcast_fusion.refs_4_.refs_2_.refs_3_), custom_call_target="tpu_custom_call" | custom-call | tf_op jit(solution)/shard_map/pallas_call | solution.py:58
  54.8 0.9 copy-done.11
  55.7 4.0 %shard_map.29 = f32[4,400,128]{2,1,0:T(8,128)} custom-call(bf16[80,2048]{1,0:T(8,128)(2,1)} %refs_0_.3, bf16[80,2048]{1,0:T(8,128)(2,1)} %copy-done.7, bf16[80,2048]{1,0:T(8,128)(2,1)} %copy-done.6, bf16[160,2048]{1,0:T(8,128)(2,1)} %copy-done, bf16[2048,1024]{1,0:T(8,128)(2,1)} %convert_bitcast_fusion.refs_4_.refs_2_.refs_3_, f32[400,512]{1,0:T(8,128)} %copy-done.11), custom_call_target="tpu_custom_call" | custom-call | tf_op jit(solution)/shard_map/pallas_call | solution.py:58
  59.7 4.5 %all-to-all-start = ((f32[4,400,128]{2,1,0:T(8,128)}), f32[4,400,128]{2,1,0:T(8,128)S(1)}, u32[]{:S(2)}, u32[]{:S(2)}) async-start(f32[4,400,128]{2,1,0:T(8,128)} %shard_map.29), calls=%async_computation | async-start | bytes 1638400 | tf_op jit(solution)/shard_map/all_to_all | solution.py:78
  64.2 3.2 %collective-permute-start.10 = (bf16[120,2048]{1,0:T(8,128)(2,1)S(1)}, bf16[120,2048]{1,0:T(8,128)(2,1)S(1)}, u32[]{:S(2)}, u32[]{:S(2)}) collective-permute-start(bf16[120,2048]{1,0:T(8,128)(2,1)S(1)} %get-tuple-element.27), channel_id=1, source_target_pairs={{0,192},{64,0},{128,64},{192,128},{1,193},{65,1},{129,65},{193,129... | collective-permute-start | bytes 1474568 | tf_op jit(solution)/shard_map/ppermute | solution.py:14
  67.5 10.0 %all-to-all-done = f32[4,400,128]{2,1,0:T(8,128)S(1)} async-done(((f32[4,400,128]{2,1,0:T(8,128)}), f32[4,400,128]{2,1,0:T(8,128)S(1)}, u32[]{:S(2)}, u32[]{:S(2)}) %all-to-all-start) | async-done | bytes 819232 | tf_op jit(solution)/shard_map/all_to_all | solution.py:78
  77.5 3.6 %shard_map.31 = f32[4,320,128]{2,1,0:T(8,128)} custom-call(bf16[160,2048]{1,0:T(8,128)(2,1)} %copy-done.1, bf16[160,2048]{1,0:T(8,128)(2,1)} %copy-done.2, bf16[2048,1024]{1,0:T(8,128)(2,1)} %convert_bitcast_fusion.refs_4_.refs_2_.refs_3_, f32[320,512]{1,0:T(8,128)} %collective-permute-done.11.refs_3_), custom_call_target="tpu_custom_call" | custom-call | tf_op jit(solution)/shard_map/pallas_call | solution.py:58
  82.3 3.5 %shard_map.32 = f32[320,512]{1,0:T(8,128)} custom-call(bf16[80,2048]{1,0:T(8,128)(2,1)} %copy-done.8, bf16[120,2048]{1,0:T(8,128)(2,1)} %copy-done.3, bf16[120,2048]{1,0:T(8,128)(2,1)} %copy-done.4, bf16[2048,1024]{1,0:T(8,128)(2,1)} %convert_bitcast_fusion.refs_4_.refs_2_.refs_3_), custom_call_target="tpu_custom_call" | custom-call | tf_op jit(solution)/shard_map/pallas_call | solution.py:58
  86.5 1.0 collective-permute-start.15
  87.5 0.9 pad_maximum_fusion.3
  88.4 3.2 %collective-permute-start.18 = (bf16[120,2048]{1,0:T(8,128)(2,1)S(1)}, bf16[120,2048]{1,0:T(8,128)(2,1)S(1)}, u32[]{:S(2)}, u32[]{:S(2)}) collective-permute-start(bf16[120,2048]{1,0:T(8,128)(2,1)S(1)} %get-tuple-element.36), channel_id=1, source_target_pairs={{0,192},{64,0},{128,64},{192,128},{1,193},{65,1},{129,65},{193,129... | collective-permute-start | bytes 1474568 | tf_op jit(solution)/shard_map/ppermute | solution.py:14
  91.6 2.2 %collective-permute-start.14 = (f32[320,128]{1,0:T(8,128)}, f32[320,128]{1,0:T(8,128)S(1)}, u32[]{:S(2)}, u32[]{:S(2)}) collective-permute-start(f32[320,128]{1,0:T(8,128)} %get-tuple-element.43), channel_id=1, source_target_pairs={{0,12},{4,0},{8,4},{12,8},{1,13},{5,1},{9,5},{13,9},{2,14},{6,2},{... | collective-permute-start | bytes 491528 | tf_op jit(solution)/shard_map/ppermute | solution.py:14
  93.8 1.0 collective-permute-done.15
  95.4 2.2 %collective-permute-done.14 = f32[320,128]{1,0:T(8,128)S(1)} collective-permute-done((f32[320,128]{1,0:T(8,128)}, f32[320,128]{1,0:T(8,128)S(1)}, u32[]{:S(2)}, u32[]{:S(2)}) %collective-permute-start.14) | collective-permute-done | bytes 163872 | tf_op jit(solution)/shard_map/ppermute | solution.py:14
  97.6 4.3 %collective-permute-done.13 = f32[320,128]{1,0:T(8,128)S(1)} collective-permute-done((f32[320,128]{1,0:T(8,128)S(1)}, f32[320,128]{1,0:T(8,128)S(1)}, u32[]{:S(2)}, u32[]{:S(2)}) %collective-permute-start.13) | collective-permute-done | bytes 163872 | tf_op jit(solution)/shard_map/ppermute | solution.py:14
  101.9 3.6 %shard_map.33 = f32[4,320,128]{2,1,0:T(8,128)} custom-call(bf16[80,2048]{1,0:T(8,128)(2,1)} %copy-done.8, bf16[120,2048]{1,0:T(8,128)(2,1)} %copy-done.3, bf16[120,2048]{1,0:T(8,128)(2,1)} %copy-done.4, bf16[2048,1024]{1,0:T(8,128)(2,1)} %convert_bitcast_fusion.refs_4_.refs_2_.refs_3_, f32[320,512]{1,0:T(8,128)} %collective-permute-done.12.refs_4_), custom_call_target="tpu_custom_call" | custom-call | tf_op jit(solution)/shard_map/pallas_call | solution.py:58
  107.1 3.2 %shard_map.34 = f32[240,512]{1,0:T(8,128)} custom-call(bf16[120,2048]{1,0:T(8,128)(2,1)} %copy-done.9, bf16[120,2048]{1,0:T(8,128)(2,1)} %copy-done.10, bf16[2048,1024]{1,0:T(8,128)(2,1)} %convert_bitcast_fusion.refs_4_.refs_2_.refs_3_), custom_call_target="tpu_custom_call" | custom-call | tf_op jit(solution)/shard_map/pallas_call | solution.py:58
  111.0 3.5 %all-to-all-start.1 = ((f32[4,320,128]{2,1,0:T(8,128)}), f32[4,320,128]{2,1,0:T(8,128)S(1)}, u32[]{:S(2)}, u32[]{:S(2)}) async-start(f32[4,320,128]{2,1,0:T(8,128)} %shard_map.33), calls=%async_computation.1 | async-start | bytes 1310720 | tf_op jit(solution)/shard_map/all_to_all | solution.py:78
  115.5 3.2 %shard_map.35 = f32[4,240,128]{2,1,0:T(8,128)} custom-call(bf16[120,2048]{1,0:T(8,128)(2,1)} %copy-done.9, bf16[120,2048]{1,0:T(8,128)(2,1)} %copy-done.10, bf16[2048,1024]{1,0:T(8,128)(2,1)} %convert_bitcast_fusion.refs_4_.refs_2_.refs_3_, f32[240,512]{1,0:T(8,128)} %copy-done.12), custom_call_target="tpu_custom_call" | custom-call | tf_op jit(solution)/shard_map/pallas_call | solution.py:58
  118.7 1.0 dynamic-slice_bitcast_fusion.5
  119.7 3.5 %collective-permute-start.23 = (f32[240,128]{1,0:T(8,128)S(1)}, f32[240,128]{1,0:T(8,128)S(1)}, u32[]{:S(2)}, u32[]{:S(2)}) collective-permute-start(f32[240,128]{1,0:T(8,128)S(1)} %get-tuple-element.45), channel_id=1, source_target_pairs={{0,8},{4,12},{8,0},{12,4},{1,9},{5,13},{9,1},{13,5},{2,10},{6,14},... | collective-permute-start | bytes 368648 | tf_op jit(solution)/shard_map/ppermute | solution.py:14
  123.3 1.2 collective-permute-start.22
  124.5 0.9 collective-permute-start.21
  125.5 1.3 all-to-all-done.1
  126.8 1.5 %collective-permute-start.19 = (f32[320,128]{1,0:T(8,128)S(1)}, f32[320,128]{1,0:T(8,128)S(1)}, u32[]{:S(2)}, u32[]{:S(2)}) collective-permute-start(f32[320,128]{1,0:T(8,128)S(1)} %reduce_sum.19), channel_id=1, source_target_pairs={{0,2},{2,0},{1,3},{3,1},{4,6},{6,4},{5,7},{7,5},{8,10},{10,8},{9,1... | collective-permute-start | bytes 491528 | tf_op jit(solution)/shard_map/ppermute | solution.py:22
  128.2 1.1 collective-permute-done.23
  129.8 1.5 %collective-permute-done.21 = f32[240,128]{1,0:T(8,128)S(1)} collective-permute-done((f32[240,128]{1,0:T(8,128)S(1)}, f32[240,128]{1,0:T(8,128)S(1)}, u32[]{:S(2)}, u32[]{:S(2)}) %collective-permute-start.21) | collective-permute-done | bytes 122912 | tf_op jit(solution)/shard_map/ppermute | solution.py:14
  131.3 0.9 fusion.16
  132.3 1.5 %collective-permute-start.24 = (f32[240,128]{1,0:T(8,128)S(1)}, f32[240,128]{1,0:T(8,128)S(1)}, u32[]{:S(2)}, u32[]{:S(2)}) collective-permute-start(f32[240,128]{1,0:T(8,128)S(1)} %fusion.16), channel_id=1, source_target_pairs={{0,2},{2,0},{1,3},{3,1},{4,6},{6,4},{5,7},{7,5},{8,10},{10,8},{9,1... | collective-permute-start | bytes 368648 | tf_op jit(solution)/shard_map/ppermute | solution.py:22
  133.8 3.4 %collective-permute-done.24 = f32[240,128]{1,0:T(8,128)S(1)} collective-permute-done((f32[240,128]{1,0:T(8,128)S(1)}, f32[240,128]{1,0:T(8,128)S(1)}, u32[]{:S(2)}, u32[]{:S(2)}) %collective-permute-start.24) | collective-permute-done | bytes 122912 | tf_op jit(solution)/shard_map/ppermute | solution.py:22
  137.3 2.2 %fusion.3 = bf16[64,1280]{1,0:T(8,128)(2,1)} fusion(s32[1280]{0:T(1024)S(1)} %concatenate.37, bf16[240,64]{1,0:T(8,128)(2,1)S(1)} %fusion.14, bf16[320,64]{1,0:T(8,128)(2,1)S(1)} %fusion.11, bf16[720,64]{1,0:T(8,128)(2,1)S(1)} %fusion.5), kind=kOutput, calls=%fused_computation.6 | convolution fusion | flops 211927040 | bytes 332800 | tf_op jit(solution)/shard_map/dot_general | solution.py:135
  (80 shorter events, 8.1 us)
Async XLA Ops:
  0.0 25.4 %collective-permute-start.6 = (bf16[80,2048]{1,0:T(8,128)(2,1)}, bf16[80,2048]{1,0:T(8,128)(2,1)S(1)}, u32[]{:S(2)}, u32[]{:S(2)}) collective-permute-start(bf16[80,2048]{1,0:T(8,128)(2,1)} %refs_0_.3), channel_id=1, source_target_pairs={{0,192},{64,0},{128,64},{192,128},{1,193},{65,1},{129,65},{193,129... | collective-permute-start | bytes 983048 | tf_op jit(solution)/shard_map/ppermute | solution.py:14
  2.8 18.4 %collective-permute-start = (bf16[80,2048]{1,0:T(8,128)(2,1)}, bf16[80,2048]{1,0:T(8,128)(2,1)S(1)}, u32[]{:S(2)}, u32[]{:S(2)}) collective-permute-start(bf16[80,2048]{1,0:T(8,128)(2,1)} %refs_0_.3), channel_id=1, source_target_pairs={{0,16},{16,32},{32,48},{48,0},{1,17},{17,33},{33,49},{49,1},{2,18}... | collective-permute-start | bytes 983048 | tf_op jit(solution)/shard_map/ppermute | solution.py:14
  7.2 18.1 %collective-permute-start.1 = (bf16[80,2048]{1,0:T(8,128)(2,1)}, bf16[80,2048]{1,0:T(8,128)(2,1)S(1)}, u32[]{:S(2)}, u32[]{:S(2)}) collective-permute-start(bf16[80,2048]{1,0:T(8,128)(2,1)} %refs_0_.3), channel_id=1, source_target_pairs={{0,48},{16,0},{32,16},{48,32},{1,49},{17,1},{33,17},{49,33},{2,50}... | collective-permute-start | bytes 983048 | tf_op jit(solution)/shard_map/ppermute | solution.py:14
  7.2 18.2 %collective-permute-start.5 = (bf16[80,2048]{1,0:T(8,128)(2,1)}, bf16[80,2048]{1,0:T(8,128)(2,1)S(1)}, u32[]{:S(2)}, u32[]{:S(2)}) collective-permute-start(bf16[80,2048]{1,0:T(8,128)(2,1)} %refs_0_.3), channel_id=1, source_target_pairs={{0,64},{64,128},{128,192},{192,0},{1,65},{65,129},{129,193},{193,1... | collective-permute-start | bytes 983048 | tf_op jit(solution)/shard_map/ppermute | solution.py:14
  25.4 0.9 copy-start
  25.4 1.0 copy-start.6
  26.5 0.7 copy-start.7
  31.1 23.8 %collective-permute-start.7 = (f32[400,512]{1,0:T(8,128)}, f32[400,512]{1,0:T(8,128)S(1)}, u32[]{:S(2)}, u32[]{:S(2)}) collective-permute-start(f32[400,512]{1,0:T(8,128)} %shard_map.28), channel_id=1, source_target_pairs={{0,1},{1,0},{2,3},{3,2},{4,5},{5,4},{6,7},{7,6},{8,9},{9,8},{10,11... | collective-permute-start | bytes 2457608 | tf_op jit(solution)/shard_map/ppermute | solution.py:22
  31.1 18.6 %collective-permute-start.2 = (bf16[160,2048]{1,0:T(8,128)(2,1)}, bf16[160,2048]{1,0:T(8,128)(2,1)S(1)}, u32[]{:S(2)}, u32[]{:S(2)}) collective-permute-start(bf16[160,2048]{1,0:T(8,128)(2,1)} %copy-done), channel_id=1, source_target_pairs={{0,64},{64,128},{128,192},{192,0},{1,65},{65,129},{129,193},{193,1... | collective-permute-start | bytes 1966088 | tf_op jit(solution)/shard_map/ppermute | solution.py:14
  31.1 18.6 %collective-permute-start.8 = (bf16[160,2048]{1,0:T(8,128)(2,1)}, bf16[160,2048]{1,0:T(8,128)(2,1)S(1)}, u32[]{:S(2)}, u32[]{:S(2)}) collective-permute-start(bf16[160,2048]{1,0:T(8,128)(2,1)} %copy-done), channel_id=1, source_target_pairs={{0,192},{64,0},{128,64},{192,128},{1,193},{65,1},{129,65},{193,129... | collective-permute-start | bytes 1966088 | tf_op jit(solution)/shard_map/ppermute | solution.py:14
  34.3 9.0 %collective-permute-start.4 = (bf16[40,2048]{1,0:T(8,128)(2,1)S(1)}, bf16[40,2048]{1,0:T(8,128)(2,1)S(1)}, u32[]{:S(2)}, u32[]{:S(2)}) collective-permute-start(bf16[40,2048]{1,0:T(8,128)(2,1)S(1)} %slice.58), channel_id=1, source_target_pairs={{0,16},{16,32},{32,48},{48,0},{1,17},{17,33},{33,49},{49,1},{2,18}... | collective-permute-start | bytes 491528 | tf_op jit(solution)/shard_map/ppermute | solution.py:14
  34.9 10.3 %collective-permute-start.3 = (bf16[40,2048]{1,0:T(8,128)(2,1)S(1)}, bf16[40,2048]{1,0:T(8,128)(2,1)S(1)}, u32[]{:S(2)}, u32[]{:S(2)}) collective-permute-start(bf16[40,2048]{1,0:T(8,128)(2,1)S(1)} %slice.57), channel_id=1, source_target_pairs={{0,48},{16,0},{32,16},{48,32},{1,49},{17,1},{33,17},{49,33},{2,50}... | collective-permute-start | bytes 491528 | tf_op jit(solution)/shard_map/ppermute | solution.py:14
  49.6 0.9 copy-start.1
  50.5 0.8 copy-start.2
  54.8 0.9 copy-start.11
  59.7 17.8 %collective-permute-start.11 = (f32[320,512]{1,0:T(8,128)}, f32[320,512]{1,0:T(8,128)}, u32[]{:S(2)}, u32[]{:S(2)}) collective-permute-start(f32[320,512]{1,0:T(8,128)} %shard_map.30), channel_id=1, source_target_pairs={{0,1},{1,0},{2,3},{3,2},{4,5},{5,4},{6,7},{7,6},{8,9},{9,8},{10,11... | collective-permute-start | bytes 1966088 | tf_op jit(solution)/shard_map/ppermute | solution.py:22
  59.7 17.8 %all-to-all-start = ((f32[4,400,128]{2,1,0:T(8,128)}), f32[4,400,128]{2,1,0:T(8,128)S(1)}, u32[]{:S(2)}, u32[]{:S(2)}) async-start(f32[4,400,128]{2,1,0:T(8,128)} %shard_map.29), calls=%async_computation | async-start | bytes 1638400 | tf_op jit(solution)/shard_map/all_to_all | solution.py:78
  64.2 17.0 %collective-permute-start.9 = (bf16[120,2048]{1,0:T(8,128)(2,1)}, bf16[120,2048]{1,0:T(8,128)(2,1)S(1)}, u32[]{:S(2)}, u32[]{:S(2)}) collective-permute-start(bf16[120,2048]{1,0:T(8,128)(2,1)} %get-tuple-element.26), channel_id=1, source_target_pairs={{0,64},{64,128},{128,192},{192,0},{1,65},{65,129},{129,193},{193,1... | collective-permute-start | bytes 1474568 | tf_op jit(solution)/shard_map/ppermute | solution.py:14
  64.2 17.0 %collective-permute-start.10 = (bf16[120,2048]{1,0:T(8,128)(2,1)S(1)}, bf16[120,2048]{1,0:T(8,128)(2,1)S(1)}, u32[]{:S(2)}, u32[]{:S(2)}) collective-permute-start(bf16[120,2048]{1,0:T(8,128)(2,1)S(1)} %get-tuple-element.27), channel_id=1, source_target_pairs={{0,192},{64,0},{128,64},{192,128},{1,193},{65,1},{129,65},{193,129... | collective-permute-start | bytes 1474568 | tf_op jit(solution)/shard_map/ppermute | solution.py:14
  67.4 13.7 %copy-start.8 = (bf16[80,2048]{1,0:T(8,128)(2,1)}, bf16[80,2048]{1,0:T(8,128)(2,1)S(1)}, u32[]{:S(2)}) copy-start(bf16[80,2048]{1,0:T(8,128)(2,1)S(1)} %constant_dynamic-update-slice_fusion.2.refs_0_) | copy-start | bytes 983044
  81.2 4.6 %copy-start.5 = (f32[4,320,128]{2,1,0:T(8,128)S(1)}, f32[4,320,128]{2,1,0:T(8,128)}, u32[]{:S(2)}) copy-start(f32[4,320,128]{2,1,0:T(8,128)} %shard_map.31) | copy-start | bytes 1966084
  81.2 6.3 %slice-start = ((bf16[160,2048]{1,0:T(8,128)(2,1)}), bf16[80,2048]{1,0:T(8,128)(2,1)S(1)}, s32[]{:S(2)}) async-start(bf16[160,2048]{1,0:T(8,128)(2,1)} %copy-done.1), calls=%async_computation.2 | async-start | bytes 655360 | tf_op jit(solution)/shard_map/slice | solution.py:116
  81.2 6.3 %slice-start.1 = ((bf16[160,2048]{1,0:T(8,128)(2,1)}), bf16[80,2048]{1,0:T(8,128)(2,1)S(1)}, s32[]{:S(2)}) async-start(bf16[160,2048]{1,0:T(8,128)(2,1)} %copy-done.2), calls=%async_computation.3 | async-start | bytes 655360 | tf_op jit(solution)/shard_map/slice | solution.py:116
  81.2 0.8 copy-start.3
  81.2 1.0 copy-start.4
  85.7 16.1 %collective-permute-start.12 = (f32[320,512]{1,0:T(8,128)}, f32[320,512]{1,0:T(8,128)}, u32[]{:S(2)}, u32[]{:S(2)}) collective-permute-start(f32[320,512]{1,0:T(8,128)} %shard_map.32), channel_id=1, source_target_pairs={{0,1},{1,0},{2,3},{3,2},{4,5},{5,4},{6,7},{7,6},{8,9},{9,8},{10,11... | collective-permute-start | bytes 1966088 | tf_op jit(solution)/shard_map/ppermute | solution.py:22
  86.5 8.3 %collective-permute-start.15 = (f32[320,128]{1,0:T(8,128)}, f32[320,128]{1,0:T(8,128)S(1)}, u32[]{:S(2)}, u32[]{:S(2)}) collective-permute-start(f32[320,128]{1,0:T(8,128)} %get-tuple-element.42), channel_id=1, source_target_pairs={{0,8},{4,12},{8,0},{12,4},{1,9},{5,13},{9,1},{13,5},{2,10},{6,14},... | collective-permute-start | bytes 491528 | tf_op jit(solution)/shard_map/ppermute | solution.py:14
  88.4 17.1 %collective-permute-start.17 = (bf16[120,2048]{1,0:T(8,128)(2,1)}, bf16[120,2048]{1,0:T(8,128)(2,1)S(1)}, u32[]{:S(2)}, u32[]{:S(2)}) collective-permute-start(bf16[120,2048]{1,0:T(8,128)(2,1)} %get-tuple-element.35), channel_id=1, source_target_pairs={{0,64},{64,128},{128,192},{192,0},{1,65},{65,129},{129,193},{193,1... | collective-permute-start | bytes 1474568 | tf_op jit(solution)/shard_map/ppermute | solution.py:14
  88.4 17.1 %collective-permute-start.18 = (bf16[120,2048]{1,0:T(8,128)(2,1)S(1)}, bf16[120,2048]{1,0:T(8,128)(2,1)S(1)}, u32[]{:S(2)}, u32[]{:S(2)}) collective-permute-start(bf16[120,2048]{1,0:T(8,128)(2,1)S(1)} %get-tuple-element.36), channel_id=1, source_target_pairs={{0,192},{64,0},{128,64},{192,128},{1,193},{65,1},{129,65},{193,129... | collective-permute-start | bytes 1474568 | tf_op jit(solution)/shard_map/ppermute | solution.py:14
  91.6 6.0 %collective-permute-start.14 = (f32[320,128]{1,0:T(8,128)}, f32[320,128]{1,0:T(8,128)S(1)}, u32[]{:S(2)}, u32[]{:S(2)}) collective-permute-start(f32[320,128]{1,0:T(8,128)} %get-tuple-element.43), channel_id=1, source_target_pairs={{0,12},{4,0},{8,4},{12,8},{1,13},{5,1},{9,5},{13,9},{2,14},{6,2},{... | collective-permute-start | bytes 491528 | tf_op jit(solution)/shard_map/ppermute | solution.py:14
  94.8 7.0 %collective-permute-start.13 = (f32[320,128]{1,0:T(8,128)S(1)}, f32[320,128]{1,0:T(8,128)S(1)}, u32[]{:S(2)}, u32[]{:S(2)}) collective-permute-start(f32[320,128]{1,0:T(8,128)S(1)} %get-tuple-element.41), channel_id=1, source_target_pairs={{0,4},{4,8},{8,12},{12,0},{1,5},{5,9},{9,13},{13,1},{2,6},{6,10},{... | collective-permute-start | bytes 491528 | tf_op jit(solution)/shard_map/ppermute | solution.py:14
  105.5 0.8 copy-start.9
  106.3 0.8 copy-start.10
  110.3 4.4 %collective-permute-start.20 = (f32[240,512]{1,0:T(8,128)}, f32[240,512]{1,0:T(8,128)S(1)}, u32[]{:S(2)}, u32[]{:S(2)}) collective-permute-start(f32[240,512]{1,0:T(8,128)} %shard_map.34), channel_id=1, source_target_pairs={{0,1},{1,0},{2,3},{3,2},{4,5},{5,4},{6,7},{7,6},{8,9},{9,8},{10,11... | collective-permute-start | bytes 1474568 | tf_op jit(solution)/shard_map/ppermute | solution.py:22
  110.3 15.0 %collective-permute-start.16 = (f32[720,128]{1,0:T(8,128)S(1)}, f32[720,128]{1,0:T(8,128)S(1)}, u32[]{:S(2)}, u32[]{:S(2)}) collective-permute-start(f32[720,128]{1,0:T(8,128)S(1)} %constant_dynamic-update-slice_fusion.4), channel_id=1, source_target_pairs={{0,2},{2,0},{1,3},{3,1},{4,6},{6,4},{5,7},{7,5},{8,10},{10,8},{9,1... | collective-permute-start | bytes 1105928 | tf_op jit(solution)/shard_map/ppermute | solution.py:22
  111.0 15.7 %all-to-all-start.1 = ((f32[4,320,128]{2,1,0:T(8,128)}), f32[4,320,128]{2,1,0:T(8,128)S(1)}, u32[]{:S(2)}, u32[]{:S(2)}) async-start(f32[4,320,128]{2,1,0:T(8,128)} %shard_map.33), calls=%async_computation.1 | async-start | bytes 1310720 | tf_op jit(solution)/shard_map/all_to_all | solution.py:78
  114.7 0.8 copy-start.12
  119.7 9.6 %collective-permute-start.23 = (f32[240,128]{1,0:T(8,128)S(1)}, f32[240,128]{1,0:T(8,128)S(1)}, u32[]{:S(2)}, u32[]{:S(2)}) collective-permute-start(f32[240,128]{1,0:T(8,128)S(1)} %get-tuple-element.45), channel_id=1, source_target_pairs={{0,8},{4,12},{8,0},{12,4},{1,9},{5,13},{9,1},{13,5},{2,10},{6,14},... | collective-permute-start | bytes 368648 | tf_op jit(solution)/shard_map/ppermute | solution.py:14
  123.3 6.5 %collective-permute-start.22 = (f32[240,128]{1,0:T(8,128)S(1)}, f32[240,128]{1,0:T(8,128)S(1)}, u32[]{:S(2)}, u32[]{:S(2)}) collective-permute-start(f32[240,128]{1,0:T(8,128)S(1)} %get-tuple-element.46), channel_id=1, source_target_pairs={{0,12},{4,0},{8,4},{12,8},{1,13},{5,1},{9,5},{13,9},{2,14},{6,2},{... | collective-permute-start | bytes 368648 | tf_op jit(solution)/shard_map/ppermute | solution.py:14
  124.5 6.9 %collective-permute-start.21 = (f32[240,128]{1,0:T(8,128)S(1)}, f32[240,128]{1,0:T(8,128)S(1)}, u32[]{:S(2)}, u32[]{:S(2)}) collective-permute-start(f32[240,128]{1,0:T(8,128)S(1)} %get-tuple-element.44), channel_id=1, source_target_pairs={{0,4},{4,8},{8,12},{12,0},{1,5},{5,9},{9,13},{13,1},{2,6},{6,10},{... | collective-permute-start | bytes 368648 | tf_op jit(solution)/shard_map/ppermute | solution.py:14
  126.8 6.9 %collective-permute-start.19 = (f32[320,128]{1,0:T(8,128)S(1)}, f32[320,128]{1,0:T(8,128)S(1)}, u32[]{:S(2)}, u32[]{:S(2)}) collective-permute-start(f32[320,128]{1,0:T(8,128)S(1)} %reduce_sum.19), channel_id=1, source_target_pairs={{0,2},{2,0},{1,3},{3,1},{4,6},{6,4},{5,7},{7,5},{8,10},{10,8},{9,1... | collective-permute-start | bytes 491528 | tf_op jit(solution)/shard_map/ppermute | solution.py:22
  132.3 5.0 %collective-permute-start.24 = (f32[240,128]{1,0:T(8,128)S(1)}, f32[240,128]{1,0:T(8,128)S(1)}, u32[]{:S(2)}, u32[]{:S(2)}) collective-permute-start(f32[240,128]{1,0:T(8,128)S(1)} %fusion.16), channel_id=1, source_target_pairs={{0,2},{2,0},{1,3},{3,1},{4,6},{6,4},{5,7},{7,5},{8,10},{10,8},{9,1... | collective-permute-start | bytes 368648 | tf_op jit(solution)/shard_map/ppermute | solution.py:22

commit v9 on v7

--- a/solution.py
+++ b/solution.py
@@ -72,22 +72,19 @@
         (joined(far, own_xm[40:]), joined(far, own_xp[:40]), early, dot(late_rows, theirs))
     )
     from_xm, from_xp = shift(after_xm, "x", 4, 1), shift(after_xp, "x", 4, -1)
-    early = over_y(early)
-    kept_rows, early = lax.optimization_barrier((late_rows, early))
-    late = dot(kept_rows, mine) + joined(swap(away[:160], "core"), swap(away[160:], "core"))
+    late = dot(late_rows, mine) + swap(away, "core")
+    early = over_y(joined(early, late))
     from_xm, from_xp, late = lax.optimization_barrier((from_xm, from_xp, late))
     last_xm = shift(joined(side_xm[80:], from_xm[40:80]), "x", 4, 1)
     last_xp = shift(joined(side_xp[:80], from_xp[:40]), "x", 4, -1)
-    late = over_y(late)
-    rows = joined(far, from_xm, from_xp)
-    away = swap(dot(rows, theirs), "core")
-    rows, late = lax.optimization_barrier((rows, late))
+    rows, early = lax.optimization_barrier((joined(far, from_xm, from_xp), early))
+    away = dot(rows, theirs)
+    away = joined(*[swap(piece, "core") for piece in (away[:104], away[104:208], away[208:])])
     second = dot(rows, mine) + away
     last_xm, last_xp, second = lax.optimization_barrier((last_xm, last_xp, second))
     second = over_y(second)
-    third, second = lax.optimization_barrier((paired(joined(last_xm, last_xp)), second))
-    third = over_y_at_once(third)
-    sums = [over_zl(part) for part in (joined(early, late), second, third)]
+    third = over_y_at_once(paired(joined(last_xm, last_xp)))
+    sums = [over_zl(part) for part in (early, second, third)]
     sites = [
         [block(0, 0), block(-1, 0), block(1, 0), block(0, -1), block(0, 1)],
         [block(-1, -1), block(-1, 1), block(1, -1), block(1, 1)],

time: 135 us -> 117 us (0.87)
  waiting for transfers between devices: 57 us -> 42.3 us
  local copies, waits for them, and re-layouts: 9.44 us -> 4.75 us
  other arithmetic: 1.82 us -> 5.9 us
  matrix products: 26.8 us -> 23.3 us
    ppermute x15, waiting for transfers between devices: 33.1 us -> 24.1 us  [shift(): lax.ppermute(value, axis, [(i, (i + by) % size) for i in range(size)])]
    all_to_all x3 -> x2, starting transfers between devices: 14.1 us -> 7.95 us  [over_y(): lax.all_to_all(split, 'y', split_axis=0, concat_axis=0, tiled=True)]
    all_to_all x3 -> x2, waiting for transfers between devices: 19.1 us -> 13.5 us  [over_y(): lax.all_to_all(split, 'y', split_axis=0, concat_axis=0, tiled=True)]
    ppermute x8 -> x9, starting transfers between devices: 1.29 us -> 5.6 us  [swap(): return lax.ppermute(value, axis, [(0, 1), (1, 0)])]
    dot_general x9, matrix products: 24.6 us -> 21.1 us  [dot(): return jnp.dot(left, right, preferred_element_type=F32)]
    concatenate x3 -> x4, other arithmetic: 1.14 us -> 4.1 us  [joined(): return jnp.concatenate(parts, axis=0)]
    ppermute x15, starting transfers between devices: 23.7 us -> 25.8 us  [shift(): lax.ppermute(value, axis, [(i, (i + by) % size) for i in range(size)])]
    unnamed x26 -> x20, local copies, waits for them, and re-layouts: 3.47 us -> 1.43 us
  transfers between devices with their start and end apart: 26 -> 26, of which waited for: 16 -> 14; matrix products, arithmetic and copies ran while one was open for 21% -> 24% of each run, Pallas kernels for 0% -> 0%
where the time goes in v9:
time: 117 us; the launch traced here: 116 us
  waiting for transfers between devices  42.3 us (36%)
  starting transfers between devices  39.3 us (34%)
  matrix products  23.3 us (20%)
  other arithmetic  5.9 us (5%)
  local copies, waits for them, and re-layouts  4.75 us (4%)
    ppermute x15, starting transfers between devices, shift(): lax.ppermute(value, axis, [(i, (i + by) % size) for i in range(size)])  25.8 us
    ppermute x15, waiting for transfers between devices, shift(): lax.ppermute(value, axis, [(i, (i + by) % size) for i in range(size)])  24.1 us
    dot_general x9, matrix products, dot(): return jnp.dot(left, right, preferred_element_type=F32)  21.1 us
    all_to_all x2, waiting for transfers between devices, over_y(): lax.all_to_all(split, 'y', split_axis=0, concat_axis=0, tiled=True)  13.5 us
    all_to_all x2, starting transfers between devices, over_y(): lax.all_to_all(split, 'y', split_axis=0, concat_axis=0, tiled=True)  7.95 us
    ppermute x9, starting transfers between devices, swap(): return lax.ppermute(value, axis, [(0, 1), (1, 0)])  5.6 us
    ppermute x9, waiting for transfers between devices, swap(): return lax.ppermute(value, axis, [(0, 1), (1, 0)])  4.77 us
    concatenate x4, other arithmetic, joined(): return jnp.concatenate(parts, axis=0)  4.1 us
  transfers between devices with their start and end apart: 26, of which 14 were waited for; matrix products, arithmetic and copies ran while one was open for 24% of the time, Pallas kernels for 0%

profile of v9, /device:TPU:64, one launch (start us, length us, event | category | flops | bytes accessed | tf_op | source)
XLA Modules:
  0.0 116.1 jit_solution(10157438058722285643)
XLA Ops:
  0.0 2.8 %collective-permute-start.5 = (bf16[80,2048]{1,0:T(8,128)(2,1)}, bf16[80,2048]{1,0:T(8,128)(2,1)S(1)}, u32[]{:S(2)}, u32[]{:S(2)}) collective-permute-start(bf16[80,2048]{1,0:T(8,128)(2,1)} %param.2), channel_id=1, source_target_pairs={{0,192},{64,0},{128,64},{192,128},{1,193},{65,1},{129,65},{193,129... | collective-permute-start | bytes 983048 | tf_op jit(solution)/shard_map/ppermute | solution.py:12
  2.8 4.5 %collective-permute-start.2 = (bf16[80,2048]{1,0:T(8,128)(2,1)}, bf16[80,2048]{1,0:T(8,128)(2,1)S(1)}, u32[]{:S(2)}, u32[]{:S(2)}) collective-permute-start(bf16[80,2048]{1,0:T(8,128)(2,1)} %param.2), channel_id=1, source_target_pairs={{0,16},{16,32},{32,48},{48,0},{1,17},{17,33},{33,49},{49,1},{2,18}... | collective-permute-start | bytes 983048 | tf_op jit(solution)/shard_map/ppermute | solution.py:12
  7.3 7.1 %convert_bitcast_fusion = bf16[2048,1024]{0,1:T(8,128)(2,1)S(1)} fusion(bf16[2048,1024]{1,0:T(8,128)(2,1)} %param.3, s32[1024]{0:T(1024)S(1)} %and_add_fusion), kind=kOutput, calls=%fused_computation.2 | convolution fusion | flops 4299161600 | bytes 8392704 | tf_op jit(solution)/shard_map/dot_general | solution.py:24
  14.4 6.8 %collective-permute-done.2 = bf16[80,2048]{1,0:T(8,128)(2,1)S(1)} collective-permute-done((bf16[80,2048]{1,0:T(8,128)(2,1)}, bf16[80,2048]{1,0:T(8,128)(2,1)S(1)}, u32[]{:S(2)}, u32[]{:S(2)}) %collective-permute-start.2) | collective-permute-done | bytes 327712 | tf_op jit(solution)/shard_map/ppermute | solution.py:12
  21.2 4.2 %collective-permute-done = bf16[80,2048]{1,0:T(8,128)(2,1)S(1)} collective-permute-done((bf16[80,2048]{1,0:T(8,128)(2,1)}, bf16[80,2048]{1,0:T(8,128)(2,1)S(1)}, u32[]{:S(2)}, u32[]{:S(2)}) %collective-permute-start) | collective-permute-done | bytes 327712 | tf_op jit(solution)/shard_map/ppermute | solution.py:12
  25.5 3.2 %collective-permute-start.8 = (bf16[160,2048]{1,0:T(8,128)(2,1)S(1)}, bf16[160,2048]{1,0:T(8,128)(2,1)S(1)}, u32[]{:S(2)}, u32[]{:S(2)}) collective-permute-start(bf16[160,2048]{1,0:T(8,128)(2,1)S(1)} %constant_dynamic-update-slice_fusion), channel_id=1, source_target_pairs={{0,192},{64,0},{128,64},{192,128},{1,193},{65,1},{129,65},{193,129... | collective-permute-start | bytes 1966088 | tf_op jit(solution)/shard_map/ppermute | solution.py:12
  28.7 0.5 collective-permute-start.3
  29.3 2.5 %collective-permute-start.1 = (bf16[40,2048]{1,0:T(8,128)(2,1)S(1)}, bf16[40,2048]{1,0:T(8,128)(2,1)S(1)}, u32[]{:S(2)}, u32[]{:S(2)}) collective-permute-start(bf16[40,2048]{1,0:T(8,128)(2,1)S(1)} %slice.76), channel_id=1, source_target_pairs={{0,48},{16,0},{32,16},{48,32},{1,49},{17,1},{33,17},{49,33},{2,50}... | collective-permute-start | bytes 491528 | tf_op jit(solution)/shard_map/ppermute | solution.py:12
  32.0 1.0 fusion.12
  33.3 3.3 %collective-permute-done.3 = bf16[40,2048]{1,0:T(8,128)(2,1)S(1)} collective-permute-done((bf16[40,2048]{1,0:T(8,128)(2,1)S(1)}, bf16[40,2048]{1,0:T(8,128)(2,1)S(1)}, u32[]{:S(2)}, u32[]{:S(2)}) %collective-permute-start.3) | collective-permute-done | bytes 163872 | tf_op jit(solution)/shard_map/ppermute | solution.py:12
  36.6 0.7 collective-permute-done.1
  37.3 1.1 pad_maximum_fusion.3
  38.4 4.0 %collective-permute-done.7 = bf16[160,2048]{1,0:T(8,128)(2,1)S(1)} collective-permute-done((bf16[160,2048]{1,0:T(8,128)(2,1)S(1)}, bf16[160,2048]{1,0:T(8,128)(2,1)S(1)}, u32[]{:S(2)}, u32[]{:S(2)}) %collective-permute-start.7) | collective-permute-done | bytes 655392 | tf_op jit(solution)/shard_map/ppermute | solution.py:12
  42.5 0.9 fusion.10
  43.6 1.0 fusion.25
  44.9 3.3 %collective-permute-start.10 = (bf16[120,2048]{1,0:T(8,128)(2,1)}, bf16[120,2048]{1,0:T(8,128)(2,1)}, u32[]{:S(2)}, u32[]{:S(2)}) collective-permute-start(bf16[120,2048]{1,0:T(8,128)(2,1)} %get-tuple-element.23), channel_id=1, source_target_pairs={{0,192},{64,0},{128,64},{192,128},{1,193},{65,1},{129,65},{193,129... | collective-permute-start | bytes 1474568 | tf_op jit(solution)/shard_map/ppermute | solution.py:12
  48.1 3.0 %fusion.22 = f32[320,512]{1,0:T(8,128)S(1)} fusion(f32[320,512]{1,0:T(8,128)} %collective-permute-done.11, bf16[320,2048]{1,0:T(8,128)(2,1)} %copy-done.3, bf16[2048,1024]{0,1:T(8,128)(2,1)} %copy-done.5), kind=kOutput, calls=%fused_computation.27 | convolution fusion | flops 671252480 | bytes 4718592 | tf_op jit(solution)/shard_map/dot_general | solution.py:24
  51.1 1.2 %bitcast_bitcast_fusion = f32[4,720,128]{2,1,0:T(8,128)} fusion(f32[320,512]{1,0:T(8,128)S(1)} %fusion.22, f32[400,512]{1,0:T(8,128)S(1)} %fusion.25), kind=kLoop, calls=%fused_computation.8 | loop fusion | flops 368640 | bytes 2949120 | tf_op jit(solution)/shard_map/transpose | solution.py:40
  52.3 4.5 %all-to-all-start = ((f32[4,720,128]{2,1,0:T(8,128)}), f32[4,720,128]{2,1,0:T(8,128)S(1)}, u32[]{:S(2)}, u32[]{:S(2)}) async-start(f32[4,720,128]{2,1,0:T(8,128)} %bitcast_bitcast_fusion), calls=%async_computation | async-start | bytes 2949120 | tf_op jit(solution)/shard_map/all_to_all | solution.py:41
  56.9 2.9 %collective-permute-done.9 = bf16[120,2048]{1,0:T(8,128)(2,1)S(1)} collective-permute-done((bf16[120,2048]{1,0:T(8,128)(2,1)}, bf16[120,2048]{1,0:T(8,128)(2,1)S(1)}, u32[]{:S(2)}, u32[]{:S(2)}) %collective-permute-start.9) | collective-permute-done | bytes 491552 | tf_op jit(solution)/shard_map/ppermute | solution.py:12
  59.8 0.9 pad_maximum_fusion.4
  60.7 1.1 collective-permute-start.13
  61.8 0.9 slice.68
  62.7 0.9 pad_maximum_fusion.5
  63.6 2.2 %collective-permute-start.14 = (bf16[120,2048]{1,0:T(8,128)(2,1)}, bf16[120,2048]{1,0:T(8,128)(2,1)}, u32[]{:S(2)}, u32[]{:S(2)}) collective-permute-start(bf16[120,2048]{1,0:T(8,128)(2,1)} %pad_maximum_fusion.5), channel_id=1, source_target_pairs={{0,192},{64,0},{128,64},{192,128},{1,193},{65,1},{129,65},{193,129... | collective-permute-start | bytes 1474568 | tf_op jit(solution)/shard_map/ppermute | solution.py:12
  65.8 1.3 %pad_maximum_fusion = bf16[320,2048]{1,0:T(8,128)(2,1)S(1)} fusion(bf16[120,2048]{1,0:T(8,128)(2,1)} %collective-permute-done.10, bf16[120,2048]{1,0:T(8,128)(2,1)} %copy-done, bf16[40,2048]{1,0:T(8,128)(2,1)S(1)} %collective-permute-done.3, bf16[40,2048]{1,0:T(8,128)(2,1)S(1)} %copy-done.2), kind=kLoop, calls=%fused_computation.26 | loop fusion | flops 5242880 | bytes 2621440 | tf_op jit(solution)/shard_map/concatenate | solution.py:28
  67.0 9.4 %all-to-all-done = f32[4,720,128]{2,1,0:T(8,128)S(1)} async-done(((f32[4,720,128]{2,1,0:T(8,128)}), f32[4,720,128]{2,1,0:T(8,128)S(1)}, u32[]{:S(2)}, u32[]{:S(2)}) %all-to-all-start) | async-done | bytes 1474592 | tf_op jit(solution)/shard_map/all_to_all | solution.py:41
  76.5 2.5 %fusion.8 = f32[320,512]{1,0:T(8,128)S(1)} fusion(bf16[320,2048]{1,0:T(8,128)(2,1)S(1)} %pad_maximum_fusion, bf16[2048,1024]{0,1:T(8,128)(2,1)} %copy-done.5), kind=kOutput, calls=%fused_computation.12 | convolution fusion | flops 671088640 | bytes 4063232 | tf_op jit(solution)/shard_map/dot_general | solution.py:24
  79.2 0.6 collective-permute-start.16
  79.9 1.1 collective-permute-done.16
  81.2 2.5 %maximum_add_fusion = f32[320,512]{1,0:T(8,128)S(1)} fusion(f32[112,512]{1,0:T(8,128)S(1)} %collective-permute-done.17, f32[104,512]{1,0:T(8,128)S(1)} %collective-permute-done.16, f32[104,512]{1,0:T(8,128)S(1)} %collective-permute-done.15, bf16[320,2048]{1,0:T(8,128)(2,1)S(1)} %pad_maximum_fusion, bf16[2048,1024]{0,1:T(8,128)(2,1)} %copy-done.5), kind=kOutput, calls=%fused_computation.31 | convolution fusion | flops 671580160 | bytes 4718592 | tf_op jit(solution)/shard_map/dot_general | solution.py:24
  83.7 1.1 constant_dynamic-update-slice_fusion.9
  84.8 1.1 constant_dynamic-update-slice_fusion.8
  85.9 0.7 fusion.6
  86.7 0.4 collective-permute-start.19
  87.3 0.9 bitcast_bitcast_fusion.1
  88.2 3.5 %all-to-all-start.1 = ((f32[4,320,128]{2,1,0:T(8,128)}), f32[4,320,128]{2,1,0:T(8,128)S(1)}, u32[]{:S(2)}, u32[]{:S(2)}) async-start(f32[4,320,128]{2,1,0:T(8,128)} %bitcast_bitcast_fusion.1), calls=%async_computation.1 | async-start | bytes 1310720 | tf_op jit(solution)/shard_map/all_to_all | solution.py:41
  91.7 2.4 %fusion.28 = f32[240,512]{1,0:T(8,128)S(1)} fusion(f32[240,512]{1,0:T(8,128)} %collective-permute-done.19, bf16[240,2048]{1,0:T(8,128)(2,1)S(1)} %constant_dynamic-update-slice_fusion.8, bf16[2048,1024]{0,1:T(8,128)(2,1)} %copy-done.5), kind=kOutput, calls=%fused_computation.29 | convolution fusion | flops 503439360 | bytes 4063232 | tf_op jit(solution)/shard_map/dot_general | solution.py:24
  94.1 3.6 %collective-permute-start.22 = (f32[240,128]{1,0:T(8,128)S(1)}, f32[240,128]{1,0:T(8,128)S(1)}, u32[]{:S(2)}, u32[]{:S(2)}) collective-permute-start(f32[240,128]{1,0:T(8,128)S(1)} %get-tuple-element.36), channel_id=1, source_target_pairs={{0,8},{4,12},{8,0},{12,4},{1,9},{5,13},{9,1},{13,5},{2,10},{6,14},... | collective-permute-start | bytes 368648 | tf_op jit(solution)/shard_map/ppermute | solution.py:12
  97.7 1.2 %collective-permute-start.21 = (f32[240,128]{1,0:T(8,128)S(1)}, f32[240,128]{1,0:T(8,128)S(1)}, u32[]{:S(2)}, u32[]{:S(2)}) collective-permute-start(f32[240,128]{1,0:T(8,128)S(1)} %get-tuple-element.37), channel_id=1, source_target_pairs={{0,12},{4,0},{8,4},{12,8},{1,13},{5,1},{9,5},{13,9},{2,14},{6,2},{... | collective-permute-start | bytes 368648 | tf_op jit(solution)/shard_map/ppermute | solution.py:12
  98.9 0.9 collective-permute-start.20
  99.9 4.1 %all-to-all-done.1 = f32[4,320,128]{2,1,0:T(8,128)S(1)} async-done(((f32[4,320,128]{2,1,0:T(8,128)}), f32[4,320,128]{2,1,0:T(8,128)S(1)}, u32[]{:S(2)}, u32[]{:S(2)}) %all-to-all-start.1) | async-done | bytes 655392 | tf_op jit(solution)/shard_map/all_to_all | solution.py:41
  104.0 2.1 %collective-permute-start.18 = (f32[320,128]{1,0:T(8,128)S(1)}, f32[320,128]{1,0:T(8,128)S(1)}, u32[]{:S(2)}, u32[]{:S(2)}) collective-permute-start(f32[320,128]{1,0:T(8,128)S(1)} %reduce_sum.19), channel_id=1, source_target_pairs={{0,2},{2,0},{1,3},{3,1},{4,6},{6,4},{5,7},{7,5},{8,10},{10,8},{9,1... | collective-permute-start | bytes 491528 | tf_op jit(solution)/shard_map/ppermute | solution.py:20
  106.2 0.4 collective-permute-done.22
  106.9 1.5 %collective-permute-done.20 = f32[240,128]{1,0:T(8,128)S(1)} collective-permute-done((f32[240,128]{1,0:T(8,128)S(1)}, f32[240,128]{1,0:T(8,128)S(1)}, u32[]{:S(2)}, u32[]{:S(2)}) %collective-permute-start.20) | collective-permute-done | bytes 122912 | tf_op jit(solution)/shard_map/ppermute | solution.py:12
  108.4 1.8 %collective-permute-start.23 = (f32[240,128]{1,0:T(8,128)S(1)}, f32[240,128]{1,0:T(8,128)S(1)}, u32[]{:S(2)}, u32[]{:S(2)}) collective-permute-start(f32[240,128]{1,0:T(8,128)S(1)} %add_add_fusion), channel_id=1, source_target_pairs={{0,2},{2,0},{1,3},{3,1},{4,6},{6,4},{5,7},{7,5},{8,10},{10,8},{9,1... | collective-permute-start | bytes 368648 | tf_op jit(solution)/shard_map/ppermute | solution.py:20
  110.4 3.4 %collective-permute-done.23 = f32[240,128]{1,0:T(8,128)S(1)} collective-permute-done((f32[240,128]{1,0:T(8,128)S(1)}, f32[240,128]{1,0:T(8,128)S(1)}, u32[]{:S(2)}, u32[]{:S(2)}) %collective-permute-start.23) | collective-permute-done | bytes 122912 | tf_op jit(solution)/shard_map/ppermute | solution.py:20
  113.9 2.2 %fusion.3 = bf16[64,1280]{1,0:T(8,128)(2,1)} fusion(s32[1280]{0:T(1024)S(1)} %concatenate.55, bf16[240,64]{1,0:T(8,128)(2,1)S(1)} %fusion.38, bf16[320,64]{1,0:T(8,128)(2,1)S(1)} %fusion.37, bf16[720,64]{1,0:T(8,128)(2,1)S(1)} %fusion.31), kind=kOutput, calls=%fused_computation.6 | convolution fusion | flops 211927040 | bytes 332800 | tf_op jit(solution)/shard_map/dot_general | solution.py:96
  (72 shorter events, 2.9 us)
Async XLA Ops:
  0.0 29.3 %collective-permute-start.5 = (bf16[80,2048]{1,0:T(8,128)(2,1)}, bf16[80,2048]{1,0:T(8,128)(2,1)S(1)}, u32[]{:S(2)}, u32[]{:S(2)}) collective-permute-start(bf16[80,2048]{1,0:T(8,128)(2,1)} %param.2), channel_id=1, source_target_pairs={{0,192},{64,0},{128,64},{192,128},{1,193},{65,1},{129,65},{193,129... | collective-permute-start | bytes 983048 | tf_op jit(solution)/shard_map/ppermute | solution.py:12
  2.8 18.4 %collective-permute-start.2 = (bf16[80,2048]{1,0:T(8,128)(2,1)}, bf16[80,2048]{1,0:T(8,128)(2,1)S(1)}, u32[]{:S(2)}, u32[]{:S(2)}) collective-permute-start(bf16[80,2048]{1,0:T(8,128)(2,1)} %param.2), channel_id=1, source_target_pairs={{0,16},{16,32},{32,48},{48,0},{1,17},{17,33},{33,49},{49,1},{2,18}... | collective-permute-start | bytes 983048 | tf_op jit(solution)/shard_map/ppermute | solution.py:12
  7.2 18.1 %collective-permute-start = (bf16[80,2048]{1,0:T(8,128)(2,1)}, bf16[80,2048]{1,0:T(8,128)(2,1)S(1)}, u32[]{:S(2)}, u32[]{:S(2)}) collective-permute-start(bf16[80,2048]{1,0:T(8,128)(2,1)} %param.2), channel_id=1, source_target_pairs={{0,48},{16,0},{32,16},{48,32},{1,49},{17,1},{33,17},{49,33},{2,50}... | collective-permute-start | bytes 983048 | tf_op jit(solution)/shard_map/ppermute | solution.py:12
  7.2 24.6 %collective-permute-start.4 = (bf16[80,2048]{1,0:T(8,128)(2,1)}, bf16[80,2048]{1,0:T(8,128)(2,1)S(1)}, u32[]{:S(2)}, u32[]{:S(2)}) collective-permute-start(bf16[80,2048]{1,0:T(8,128)(2,1)} %param.2), channel_id=1, source_target_pairs={{0,64},{64,128},{128,192},{192,0},{1,65},{65,129},{129,193},{193,1... | collective-permute-start | bytes 983048 | tf_op jit(solution)/shard_map/ppermute | solution.py:12
  7.3 7.1 %copy-start.4 = (bf16[80,2048]{1,0:T(8,128)(2,1)S(1)}, bf16[80,2048]{1,0:T(8,128)(2,1)}, u32[]{:S(2)}) copy-start(bf16[80,2048]{1,0:T(8,128)(2,1)} %param.2) | copy-start | bytes 983044
  14.4 29.2 %copy-start.5 = (bf16[2048,1024]{0,1:T(8,128)(2,1)}, bf16[2048,1024]{0,1:T(8,128)(2,1)S(1)}, u32[]{:S(2)}) copy-start(bf16[2048,1024]{0,1:T(8,128)(2,1)S(1)} %convert_bitcast_fusion) | copy-start | bytes 12582916
  25.4 17.0 %collective-permute-start.7 = (bf16[160,2048]{1,0:T(8,128)(2,1)S(1)}, bf16[160,2048]{1,0:T(8,128)(2,1)S(1)}, u32[]{:S(2)}, u32[]{:S(2)}) collective-permute-start(bf16[160,2048]{1,0:T(8,128)(2,1)S(1)} %constant_dynamic-update-slice_fusion), channel_id=1, source_target_pairs={{0,64},{64,128},{128,192},{192,0},{1,65},{65,129},{129,193},{193,1... | collective-permute-start | bytes 1966088 | tf_op jit(solution)/shard_map/ppermute | solution.py:12
  25.5 16.9 %collective-permute-start.8 = (bf16[160,2048]{1,0:T(8,128)(2,1)S(1)}, bf16[160,2048]{1,0:T(8,128)(2,1)S(1)}, u32[]{:S(2)}, u32[]{:S(2)}) collective-permute-start(bf16[160,2048]{1,0:T(8,128)(2,1)S(1)} %constant_dynamic-update-slice_fusion), channel_id=1, source_target_pairs={{0,192},{64,0},{128,64},{192,128},{1,193},{65,1},{129,65},{193,129... | collective-permute-start | bytes 1966088 | tf_op jit(solution)/shard_map/ppermute | solution.py:12
  28.7 7.9 %collective-permute-start.3 = (bf16[40,2048]{1,0:T(8,128)(2,1)S(1)}, bf16[40,2048]{1,0:T(8,128)(2,1)S(1)}, u32[]{:S(2)}, u32[]{:S(2)}) collective-permute-start(bf16[40,2048]{1,0:T(8,128)(2,1)S(1)} %slice.77), channel_id=1, source_target_pairs={{0,16},{16,32},{32,48},{48,0},{1,17},{17,33},{33,49},{49,1},{2,18}... | collective-permute-start | bytes 491528 | tf_op jit(solution)/shard_map/ppermute | solution.py:12
  29.3 8.0 %collective-permute-start.1 = (bf16[40,2048]{1,0:T(8,128)(2,1)S(1)}, bf16[40,2048]{1,0:T(8,128)(2,1)S(1)}, u32[]{:S(2)}, u32[]{:S(2)}) collective-permute-start(bf16[40,2048]{1,0:T(8,128)(2,1)S(1)} %slice.76), channel_id=1, source_target_pairs={{0,48},{16,0},{32,16},{48,32},{1,49},{17,1},{33,17},{49,33},{2,50}... | collective-permute-start | bytes 491528 | tf_op jit(solution)/shard_map/ppermute | solution.py:12
  33.0 10.6 %collective-permute-start.6 = (f32[400,512]{1,0:T(8,128)S(1)}, f32[400,512]{1,0:T(8,128)S(1)}, u32[]{:S(2)}, u32[]{:S(2)}) collective-permute-start(f32[400,512]{1,0:T(8,128)S(1)} %fusion.12), channel_id=1, source_target_pairs={{0,1},{1,0},{2,3},{3,2},{4,5},{5,4},{6,7},{7,6},{8,9},{9,8},{10,11... | collective-permute-start | bytes 2457608 | tf_op jit(solution)/shard_map/ppermute | solution.py:20
  37.3 5.2 %copy-start.1 = (bf16[40,2048]{1,0:T(8,128)(2,1)}, bf16[40,2048]{1,0:T(8,128)(2,1)S(1)}, u32[]{:S(2)}) copy-start(bf16[40,2048]{1,0:T(8,128)(2,1)S(1)} %collective-permute-done.1) | copy-start | bytes 491524
  42.5 1.1 copy-start.3
  44.7 3.5 %collective-permute-start.11 = (f32[320,512]{1,0:T(8,128)S(1)}, f32[320,512]{1,0:T(8,128)}, u32[]{:S(2)}, u32[]{:S(2)}) collective-permute-start(f32[320,512]{1,0:T(8,128)S(1)} %fusion.10), channel_id=1, source_target_pairs={{0,1},{1,0},{2,3},{3,2},{4,5},{5,4},{6,7},{7,6},{8,9},{9,8},{10,11... | collective-permute-start | bytes 1966088 | tf_op jit(solution)/shard_map/ppermute | solution.py:20
  44.8 15.0 %collective-permute-start.9 = (bf16[120,2048]{1,0:T(8,128)(2,1)}, bf16[120,2048]{1,0:T(8,128)(2,1)S(1)}, u32[]{:S(2)}, u32[]{:S(2)}) collective-permute-start(bf16[120,2048]{1,0:T(8,128)(2,1)} %get-tuple-element.22), channel_id=1, source_target_pairs={{0,64},{64,128},{128,192},{192,0},{1,65},{65,129},{129,193},{193,1... | collective-permute-start | bytes 1474568 | tf_op jit(solution)/shard_map/ppermute | solution.py:12
  44.9 14.9 %collective-permute-start.10 = (bf16[120,2048]{1,0:T(8,128)(2,1)}, bf16[120,2048]{1,0:T(8,128)(2,1)}, u32[]{:S(2)}, u32[]{:S(2)}) collective-permute-start(bf16[120,2048]{1,0:T(8,128)(2,1)} %get-tuple-element.23), channel_id=1, source_target_pairs={{0,192},{64,0},{128,64},{192,128},{1,193},{65,1},{129,65},{193,129... | collective-permute-start | bytes 1474568 | tf_op jit(solution)/shard_map/ppermute | solution.py:12
  52.3 24.1 %all-to-all-start = ((f32[4,720,128]{2,1,0:T(8,128)}), f32[4,720,128]{2,1,0:T(8,128)S(1)}, u32[]{:S(2)}, u32[]{:S(2)}) async-start(f32[4,720,128]{2,1,0:T(8,128)} %bitcast_bitcast_fusion), calls=%async_computation | async-start | bytes 2949120 | tf_op jit(solution)/shard_map/all_to_all | solution.py:41
  56.8 9.0 %copy-start.2 = (bf16[40,2048]{1,0:T(8,128)(2,1)S(1)}, bf16[40,2048]{1,0:T(8,128)(2,1)}, u32[]{:S(2)}) copy-start(bf16[40,2048]{1,0:T(8,128)(2,1)} %copy-done.1) | copy-start | bytes 491524
  59.8 3.8 %copy-start = (bf16[120,2048]{1,0:T(8,128)(2,1)}, bf16[120,2048]{1,0:T(8,128)(2,1)S(1)}, u32[]{:S(2)}) copy-start(bf16[120,2048]{1,0:T(8,128)(2,1)S(1)} %collective-permute-done.9) | copy-start | bytes 1474564
  60.7 23.0 %collective-permute-start.13 = (bf16[120,2048]{1,0:T(8,128)(2,1)}, bf16[120,2048]{1,0:T(8,128)(2,1)}, u32[]{:S(2)}, u32[]{:S(2)}) collective-permute-start(bf16[120,2048]{1,0:T(8,128)(2,1)} %pad_maximum_fusion.4), channel_id=1, source_target_pairs={{0,64},{64,128},{128,192},{192,0},{1,65},{65,129},{129,193},{193,1... | collective-permute-start | bytes 1474568 | tf_op jit(solution)/shard_map/ppermute | solution.py:12
  63.6 20.1 %collective-permute-start.14 = (bf16[120,2048]{1,0:T(8,128)(2,1)}, bf16[120,2048]{1,0:T(8,128)(2,1)}, u32[]{:S(2)}, u32[]{:S(2)}) collective-permute-start(bf16[120,2048]{1,0:T(8,128)(2,1)} %pad_maximum_fusion.5), channel_id=1, source_target_pairs={{0,192},{64,0},{128,64},{192,128},{1,193},{65,1},{129,65},{193,129... | collective-permute-start | bytes 1474568 | tf_op jit(solution)/shard_map/ppermute | solution.py:12
  79.0 2.2 %collective-permute-start.17 = (f32[112,512]{1,0:T(8,128)S(1)}, f32[112,512]{1,0:T(8,128)S(1)}, u32[]{:S(2)}, u32[]{:S(2)}) collective-permute-start(f32[112,512]{1,0:T(8,128)S(1)} %slice.87), channel_id=1, source_target_pairs={{0,1},{1,0},{2,3},{3,2},{4,5},{5,4},{6,7},{7,6},{8,9},{9,8},{10,11... | collective-permute-start | bytes 688136 | tf_op jit(solution)/shard_map/ppermute | solution.py:20
  79.2 1.7 %collective-permute-start.16 = (f32[104,512]{1,0:T(8,128)S(1)}, f32[104,512]{1,0:T(8,128)S(1)}, u32[]{:S(2)}, u32[]{:S(2)}) collective-permute-start(f32[104,512]{1,0:T(8,128)S(1)} %get-tuple-element.34), channel_id=1, source_target_pairs={{0,1},{1,0},{2,3},{3,2},{4,5},{5,4},{6,7},{7,6},{8,9},{9,8},{10,11... | collective-permute-start | bytes 638984 | tf_op jit(solution)/shard_map/ppermute | solution.py:20
  79.8 1.5 %collective-permute-start.15 = (f32[104,512]{1,0:T(8,128)S(1)}, f32[104,512]{1,0:T(8,128)S(1)}, u32[]{:S(2)}, u32[]{:S(2)}) collective-permute-start(f32[104,512]{1,0:T(8,128)S(1)} %get-tuple-element.33), channel_id=1, source_target_pairs={{0,1},{1,0},{2,3},{3,2},{4,5},{5,4},{6,7},{7,6},{8,9},{9,8},{10,11... | collective-permute-start | bytes 638984 | tf_op jit(solution)/shard_map/ppermute | solution.py:20
  79.9 6.0 %copy-start.6 = (bf16[2048,1024]{0,1:T(8,128)(2,1)S(1)}, bf16[2048,1024]{0,1:T(8,128)(2,1)}, u32[]{:S(2)}) copy-start(bf16[2048,1024]{0,1:T(8,128)(2,1)} %copy-done.5) | copy-start | bytes 12582916
  86.7 5.0 %collective-permute-start.19 = (f32[240,512]{1,0:T(8,128)S(1)}, f32[240,512]{1,0:T(8,128)}, u32[]{:S(2)}, u32[]{:S(2)}) collective-permute-start(f32[240,512]{1,0:T(8,128)S(1)} %fusion.6), channel_id=1, source_target_pairs={{0,1},{1,0},{2,3},{3,2},{4,5},{5,4},{6,7},{7,6},{8,9},{9,8},{10,11... | collective-permute-start | bytes 1474568 | tf_op jit(solution)/shard_map/ppermute | solution.py:20
  87.2 12.6 %collective-permute-start.12 = (f32[720,128]{1,0:T(8,128)S(1)}, f32[720,128]{1,0:T(8,128)S(1)}, u32[]{:S(2)}, u32[]{:S(2)}) collective-permute-start(f32[720,128]{1,0:T(8,128)S(1)} %reduce_sum.18), channel_id=1, source_target_pairs={{0,2},{2,0},{1,3},{3,1},{4,6},{6,4},{5,7},{7,5},{8,10},{10,8},{9,1... | collective-permute-start | bytes 1105928 | tf_op jit(solution)/shard_map/ppermute | solution.py:20
  88.2 15.8 %all-to-all-start.1 = ((f32[4,320,128]{2,1,0:T(8,128)}), f32[4,320,128]{2,1,0:T(8,128)S(1)}, u32[]{:S(2)}, u32[]{:S(2)}) async-start(f32[4,320,128]{2,1,0:T(8,128)} %bitcast_bitcast_fusion.1), calls=%async_computation.1 | async-start | bytes 1310720 | tf_op jit(solution)/shard_map/all_to_all | solution.py:41
  94.1 12.4 %collective-permute-start.22 = (f32[240,128]{1,0:T(8,128)S(1)}, f32[240,128]{1,0:T(8,128)S(1)}, u32[]{:S(2)}, u32[]{:S(2)}) collective-permute-start(f32[240,128]{1,0:T(8,128)S(1)} %get-tuple-element.36), channel_id=1, source_target_pairs={{0,8},{4,12},{8,0},{12,4},{1,9},{5,13},{9,1},{13,5},{2,10},{6,14},... | collective-permute-start | bytes 368648 | tf_op jit(solution)/shard_map/ppermute | solution.py:12
  97.7 9.2 %collective-permute-start.21 = (f32[240,128]{1,0:T(8,128)S(1)}, f32[240,128]{1,0:T(8,128)S(1)}, u32[]{:S(2)}, u32[]{:S(2)}) collective-permute-start(f32[240,128]{1,0:T(8,128)S(1)} %get-tuple-element.37), channel_id=1, source_target_pairs={{0,12},{4,0},{8,4},{12,8},{1,13},{5,1},{9,5},{13,9},{2,14},{6,2},{... | collective-permute-start | bytes 368648 | tf_op jit(solution)/shard_map/ppermute | solution.py:12
  98.9 9.5 %collective-permute-start.20 = (f32[240,128]{1,0:T(8,128)S(1)}, f32[240,128]{1,0:T(8,128)S(1)}, u32[]{:S(2)}, u32[]{:S(2)}) collective-permute-start(f32[240,128]{1,0:T(8,128)S(1)} %get-tuple-element.35), channel_id=1, source_target_pairs={{0,4},{4,8},{8,12},{12,0},{1,5},{5,9},{9,13},{13,1},{2,6},{6,10},{... | collective-permute-start | bytes 368648 | tf_op jit(solution)/shard_map/ppermute | solution.py:12
  104.0 6.2 %collective-permute-start.18 = (f32[320,128]{1,0:T(8,128)S(1)}, f32[320,128]{1,0:T(8,128)S(1)}, u32[]{:S(2)}, u32[]{:S(2)}) collective-permute-start(f32[320,128]{1,0:T(8,128)S(1)} %reduce_sum.19), channel_id=1, source_target_pairs={{0,2},{2,0},{1,3},{3,1},{4,6},{6,4},{5,7},{7,5},{8,10},{10,8},{9,1... | collective-permute-start | bytes 491528 | tf_op jit(solution)/shard_map/ppermute | solution.py:20
  108.4 5.3 %collective-permute-start.23 = (f32[240,128]{1,0:T(8,128)S(1)}, f32[240,128]{1,0:T(8,128)S(1)}, u32[]{:S(2)}, u32[]{:S(2)}) collective-permute-start(f32[240,128]{1,0:T(8,128)S(1)} %add_add_fusion), channel_id=1, source_target_pairs={{0,2},{2,0},{1,3},{3,1},{4,6},{6,4},{5,7},{7,5},{8,10},{10,8},{9,1... | collective-permute-start | bytes 368648 | tf_op jit(solution)/shard_map/ppermute | solution.py:20

commit v10 on v9

--- a/solution.py
+++ b/solution.py
@@ -93,9 +93,11 @@
     ]
     places = joined(*[p for ps in sites for p in ps])
     place = (places[:, None] == jnp.arange(1280)[None, :]).astype(BF16)
-    turned = lax.dot_general(
-        joined(*sums), place, (((0,), (0,)), ((), ())), preferred_element_type=F32
-    )
+
+    def put(some, where):
+        return lax.dot_general(some, where, (((0,), (0,)), ((), ())), preferred_element_type=F32)
+
+    turned = put(joined(*sums[:2]), place[:1040]) + put(sums[2], place[1040:])
     return turned.astype(BF16)
 
 

time: 117 us -> 116 us (level)
  waiting for transfers between devices: 42.3 us -> 35.7 us
  other arithmetic: 5.9 us -> 9.74 us
  matrix products: 23.3 us -> 24.9 us
    all_to_all x2, waiting for transfers between devices: 13.5 us -> 9.11 us  [over_y(): lax.all_to_all(split, 'y', split_axis=0, concat_axis=0, tiled=True)]
    dot_general x9, matrix products: 21.1 us -> 22.9 us  [dot(): return jnp.dot(left, right, preferred_element_type=F32)]
    ppermute x9, waiting for transfers between devices: 4.77 us -> 3.38 us  [swap(): return lax.ppermute(value, axis, [(0, 1), (1, 0)])]
  transfers between devices with their start and end apart: 26 -> 26, of which waited for: 14 -> 13; matrix products, arithmetic and copies ran while one was open for 24% -> 29% of each run, Pallas kernels for 0% -> 0%
where the time goes in v10:
time: 116 us
  starting transfers between devices  39.2 us (34%)
  waiting for transfers between devices  35.7 us (31%)
  matrix products  24.9 us (21%)
  other arithmetic  9.74 us (8%)
  local copies, waits for them, and re-layouts  5.49 us (5%)
    ppermute x15, starting transfers between devices, shift(): lax.ppermute(value, axis, [(i, (i + by) % size) for i in range(size)])  25.8 us
    ppermute x15, waiting for transfers between devices, shift(): lax.ppermute(value, axis, [(i, (i + by) % size) for i in range(size)])  23.2 us
    dot_general x9, matrix products, dot(): return jnp.dot(left, right, preferred_element_type=F32)  22.9 us
    all_to_all x2, waiting for transfers between devices, over_y(): lax.all_to_all(split, 'y', split_axis=0, concat_axis=0, tiled=True)  9.11 us
    all_to_all x2, starting transfers between devices, over_y(): lax.all_to_all(split, 'y', split_axis=0, concat_axis=0, tiled=True)  7.94 us
    ppermute x9, starting transfers between devices, swap(): return lax.ppermute(value, axis, [(0, 1), (1, 0)])  5.5 us
    concatenate x4, other arithmetic, joined(): return jnp.concatenate(parts, axis=0)  5.03 us
    ppermute x9, waiting for transfers between devices, swap(): return lax.ppermute(value, axis, [(0, 1), (1, 0)])  3.38 us
  transfers between devices with their start and end apart: 26, of which 13 were waited for; matrix products, arithmetic and copies ran while one was open for 29% of the time, Pallas kernels for 0%

profile of v10, /device:TPU:64, one launch (start us, length us, event | category | flops | bytes accessed | tf_op | source)
XLA Modules:
  0.0 115.6 jit_solution(12009499137641878248)
XLA Ops:
  0.0 4.5 %collective-permute-start.2 = (bf16[80,2048]{1,0:T(8,128)(2,1)}, bf16[80,2048]{1,0:T(8,128)(2,1)S(1)}, u32[]{:S(2)}, u32[]{:S(2)}) collective-permute-start(bf16[80,2048]{1,0:T(8,128)(2,1)} %param.2), channel_id=1, source_target_pairs={{0,16},{16,32},{32,48},{48,0},{1,17},{17,33},{33,49},{49,1},{2,18}... | collective-permute-start | bytes 983048 | tf_op jit(solution)/shard_map/ppermute | solution.py:12
  4.5 1.5 %collective-permute-start.4 = (bf16[80,2048]{1,0:T(8,128)(2,1)}, bf16[80,2048]{1,0:T(8,128)(2,1)S(1)}, u32[]{:S(2)}, u32[]{:S(2)}) collective-permute-start(bf16[80,2048]{1,0:T(8,128)(2,1)} %param.2), channel_id=1, source_target_pairs={{0,64},{64,128},{128,192},{192,0},{1,65},{65,129},{129,193},{193,1... | collective-permute-start | bytes 983048 | tf_op jit(solution)/shard_map/ppermute | solution.py:12
  6.0 1.7 %collective-permute-start.5 = (bf16[80,2048]{1,0:T(8,128)(2,1)}, bf16[80,2048]{1,0:T(8,128)(2,1)S(1)}, u32[]{:S(2)}, u32[]{:S(2)}) collective-permute-start(bf16[80,2048]{1,0:T(8,128)(2,1)} %param.2), channel_id=1, source_target_pairs={{0,192},{64,0},{128,64},{192,128},{1,193},{65,1},{129,65},{193,129... | collective-permute-start | bytes 983048 | tf_op jit(solution)/shard_map/ppermute | solution.py:12
  7.7 7.1 %convert_bitcast_fusion = bf16[2048,1024]{0,1:T(8,128)(2,1)S(1)} fusion(bf16[2048,1024]{1,0:T(8,128)(2,1)} %param.3, s32[1024]{0:T(1024)S(1)} %and_add_fusion), kind=kOutput, calls=%fused_computation.3 | convolution fusion | flops 4299161600 | bytes 8392704 | tf_op jit(solution)/shard_map/dot_general | solution.py:24
  14.9 3.8 %collective-permute-done.2 = bf16[80,2048]{1,0:T(8,128)(2,1)S(1)} collective-permute-done((bf16[80,2048]{1,0:T(8,128)(2,1)}, bf16[80,2048]{1,0:T(8,128)(2,1)S(1)}, u32[]{:S(2)}, u32[]{:S(2)}) %collective-permute-start.2) | collective-permute-done | bytes 327712 | tf_op jit(solution)/shard_map/ppermute | solution.py:12
  18.7 4.2 %collective-permute-done = bf16[80,2048]{1,0:T(8,128)(2,1)S(1)} collective-permute-done((bf16[80,2048]{1,0:T(8,128)(2,1)}, bf16[80,2048]{1,0:T(8,128)(2,1)S(1)}, u32[]{:S(2)}, u32[]{:S(2)}) %collective-permute-start) | collective-permute-done | bytes 327712 | tf_op jit(solution)/shard_map/ppermute | solution.py:12
  22.9 1.6 %collective-permute-start.7 = (bf16[160,2048]{1,0:T(8,128)(2,1)S(1)}, bf16[160,2048]{1,0:T(8,128)(2,1)S(1)}, u32[]{:S(2)}, u32[]{:S(2)}) collective-permute-start(bf16[160,2048]{1,0:T(8,128)(2,1)S(1)} %constant_dynamic-update-slice_fusion), channel_id=1, source_target_pairs={{0,64},{64,128},{128,192},{192,0},{1,65},{65,129},{129,193},{193,1... | collective-permute-start | bytes 1966088 | tf_op jit(solution)/shard_map/ppermute | solution.py:12
  24.5 1.7 %collective-permute-start.8 = (bf16[160,2048]{1,0:T(8,128)(2,1)S(1)}, bf16[160,2048]{1,0:T(8,128)(2,1)S(1)}, u32[]{:S(2)}, u32[]{:S(2)}) collective-permute-start(bf16[160,2048]{1,0:T(8,128)(2,1)S(1)} %constant_dynamic-update-slice_fusion), channel_id=1, source_target_pairs={{0,192},{64,0},{128,64},{192,128},{1,193},{65,1},{129,65},{193,129... | collective-permute-start | bytes 1966088 | tf_op jit(solution)/shard_map/ppermute | solution.py:12
  26.4 4.2 %collective-permute-start.3 = (bf16[40,2048]{1,0:T(8,128)(2,1)S(1)}, bf16[40,2048]{1,0:T(8,128)(2,1)S(1)}, u32[]{:S(2)}, u32[]{:S(2)}) collective-permute-start(bf16[40,2048]{1,0:T(8,128)(2,1)S(1)} %slice.85), channel_id=1, source_target_pairs={{0,16},{16,32},{32,48},{48,0},{1,17},{17,33},{33,49},{49,1},{2,18}... | collective-permute-start | bytes 491528 | tf_op jit(solution)/shard_map/ppermute | solution.py:12
  30.7 1.0 fusion.12
  32.1 1.8 %collective-permute-done.1 = bf16[40,2048]{1,0:T(8,128)(2,1)S(1)} collective-permute-done((bf16[40,2048]{1,0:T(8,128)(2,1)S(1)}, bf16[40,2048]{1,0:T(8,128)(2,1)S(1)}, u32[]{:S(2)}, u32[]{:S(2)}) %collective-permute-start.1) | collective-permute-done | bytes 163872 | tf_op jit(solution)/shard_map/ppermute | solution.py:12
  34.4 1.1 pad_maximum_fusion.3
  35.5 4.5 %collective-permute-done.7 = bf16[160,2048]{1,0:T(8,128)(2,1)S(1)} collective-permute-done((bf16[160,2048]{1,0:T(8,128)(2,1)S(1)}, bf16[160,2048]{1,0:T(8,128)(2,1)S(1)}, u32[]{:S(2)}, u32[]{:S(2)}) %collective-permute-start.7) | collective-permute-done | bytes 655392 | tf_op jit(solution)/shard_map/ppermute | solution.py:12
  40.1 0.9 fusion.10
  41.3 1.0 fusion.25
  42.6 2.9 %collective-permute-start.10 = (bf16[120,2048]{1,0:T(8,128)(2,1)}, bf16[120,2048]{1,0:T(8,128)(2,1)S(1)}, u32[]{:S(2)}, u32[]{:S(2)}) collective-permute-start(bf16[120,2048]{1,0:T(8,128)(2,1)} %get-tuple-element.23), channel_id=1, source_target_pairs={{0,192},{64,0},{128,64},{192,128},{1,193},{65,1},{129,65},{193,129... | collective-permute-start | bytes 1474568 | tf_op jit(solution)/shard_map/ppermute | solution.py:12
  45.5 3.0 %fusion.22 = f32[320,512]{1,0:T(8,128)S(1)} fusion(f32[320,512]{1,0:T(8,128)} %collective-permute-done.11, bf16[320,2048]{1,0:T(8,128)(2,1)} %copy-done.4, bf16[2048,1024]{0,1:T(8,128)(2,1)} %copy-done.7), kind=kOutput, calls=%fused_computation.28 | convolution fusion | flops 671252480 | bytes 4718592 | tf_op jit(solution)/shard_map/dot_general | solution.py:24
  48.5 1.2 %bitcast_bitcast_fusion = f32[4,720,128]{2,1,0:T(8,128)} fusion(f32[320,512]{1,0:T(8,128)S(1)} %fusion.22, f32[400,512]{1,0:T(8,128)S(1)} %fusion.25), kind=kLoop, calls=%fused_computation.9 | loop fusion | flops 368640 | bytes 2949120 | tf_op jit(solution)/shard_map/transpose | solution.py:40
  49.7 4.5 %all-to-all-start = ((f32[4,720,128]{2,1,0:T(8,128)}), f32[4,720,128]{2,1,0:T(8,128)S(1)}, u32[]{:S(2)}, u32[]{:S(2)}) async-start(f32[4,720,128]{2,1,0:T(8,128)} %bitcast_bitcast_fusion), calls=%async_computation | async-start | bytes 2949120 | tf_op jit(solution)/shard_map/all_to_all | solution.py:41
  54.3 2.5 %collective-permute-done.10 = bf16[120,2048]{1,0:T(8,128)(2,1)S(1)} collective-permute-done((bf16[120,2048]{1,0:T(8,128)(2,1)}, bf16[120,2048]{1,0:T(8,128)(2,1)S(1)}, u32[]{:S(2)}, u32[]{:S(2)}) %collective-permute-start.10) | collective-permute-done | bytes 491552 | tf_op jit(solution)/shard_map/ppermute | solution.py:12
  56.8 3.4 %collective-permute-done.9 = bf16[120,2048]{1,0:T(8,128)(2,1)} collective-permute-done((bf16[120,2048]{1,0:T(8,128)(2,1)}, bf16[120,2048]{1,0:T(8,128)(2,1)}, u32[]{:S(2)}, u32[]{:S(2)}) %collective-permute-start.9) | collective-permute-done | bytes 491552 | tf_op jit(solution)/shard_map/ppermute | solution.py:12
  60.2 0.9 pad_maximum_fusion.5
  61.3 0.9 slice.72
  63.1 1.8 %collective-permute-start.13 = (bf16[120,2048]{1,0:T(8,128)(2,1)}, bf16[120,2048]{1,0:T(8,128)(2,1)}, u32[]{:S(2)}, u32[]{:S(2)}) collective-permute-start(bf16[120,2048]{1,0:T(8,128)(2,1)} %pad_maximum_fusion.4), channel_id=1, source_target_pairs={{0,64},{64,128},{128,192},{192,0},{1,65},{65,129},{129,193},{193,1... | collective-permute-start | bytes 1474568 | tf_op jit(solution)/shard_map/ppermute | solution.py:12
  64.9 2.2 %pad_maximum_fusion = bf16[320,2048]{1,0:T(8,128)(2,1)} fusion(bf16[120,2048]{1,0:T(8,128)(2,1)S(1)} %collective-permute-done.10, bf16[120,2048]{1,0:T(8,128)(2,1)} %collective-permute-done.9, bf16[40,2048]{1,0:T(8,128)(2,1)S(1)} %copy-done.3, bf16[40,2048]{1,0:T(8,128)(2,1)S(1)} %collective-permute-done.1), kind=kLoop, calls=%fused_computation.27 | loop fusion | flops 5242880 | bytes 2621440 | tf_op jit(solution)/shard_map/concatenate | solution.py:28
  67.1 7.0 %all-to-all-done = f32[4,720,128]{2,1,0:T(8,128)S(1)} async-done(((f32[4,720,128]{2,1,0:T(8,128)}), f32[4,720,128]{2,1,0:T(8,128)S(1)}, u32[]{:S(2)}, u32[]{:S(2)}) %all-to-all-start) | async-done | bytes 1474592 | tf_op jit(solution)/shard_map/all_to_all | solution.py:41
  74.2 3.0 %fusion.8 = f32[320,512]{1,0:T(8,128)S(1)} fusion(bf16[320,2048]{1,0:T(8,128)(2,1)} %pad_maximum_fusion, bf16[2048,1024]{0,1:T(8,128)(2,1)} %copy-done.7), kind=kOutput, calls=%fused_computation.13 | convolution fusion | flops 671088640 | bytes 4063232 | tf_op jit(solution)/shard_map/dot_general | solution.py:24
  78.1 1.0 collective-permute-done.15
  79.4 2.6 %maximum_add_fusion = f32[320,512]{1,0:T(8,128)S(1)} fusion(f32[112,512]{1,0:T(8,128)} %collective-permute-done.17, f32[104,512]{1,0:T(8,128)S(1)} %collective-permute-done.16, f32[104,512]{1,0:T(8,128)S(1)} %collective-permute-done.15, bf16[320,2048]{1,0:T(8,128)(2,1)S(1)} %copy-done.1, bf16[2048,1024]{0,1:T(8,128)(2,1)} %copy-done.7), kind=kOutput, calls=%fused_computation.33 | convolution fusion | flops 671580160 | bytes 4718592 | tf_op jit(solution)/shard_map/dot_general | solution.py:24
  82.0 1.1 constant_dynamic-update-slice_fusion.9
  83.1 1.1 constant_dynamic-update-slice_fusion.8
  84.2 1.6 %fusion.6 = f32[240,512]{1,0:T(8,128)} fusion(bf16[240,2048]{1,0:T(8,128)(2,1)S(1)} %constant_dynamic-update-slice_fusion.8, bf16[2048,1024]{0,1:T(8,128)(2,1)S(1)} %copy-done.8), kind=kOutput, calls=%fused_computation.11 | convolution fusion | flops 503316480 | bytes 3571712 | tf_op jit(solution)/shard_map/dot_general | solution.py:24
  86.1 1.0 iota_compare_fusion
  87.3 0.9 bitcast_bitcast_fusion.1
  88.2 3.5 %all-to-all-start.1 = ((f32[4,320,128]{2,1,0:T(8,128)}), f32[4,320,128]{2,1,0:T(8,128)S(1)}, u32[]{:S(2)}, u32[]{:S(2)}) async-start(f32[4,320,128]{2,1,0:T(8,128)} %bitcast_bitcast_fusion.1), calls=%async_computation.1 | async-start | bytes 1310720 | tf_op jit(solution)/shard_map/all_to_all | solution.py:41
  91.7 2.7 %fusion.29 = f32[240,512]{1,0:T(8,128)S(1)} fusion(f32[240,512]{1,0:T(8,128)} %collective-permute-done.19, bf16[240,2048]{1,0:T(8,128)(2,1)} %copy-done.6, bf16[2048,1024]{0,1:T(8,128)(2,1)} %copy-done.7), kind=kOutput, calls=%fused_computation.31 | convolution fusion | flops 503439360 | bytes 4063232 | tf_op jit(solution)/shard_map/dot_general | solution.py:24
  95.1 2.0 %collective-permute-start.20 = (f32[240,128]{1,0:T(8,128)}, f32[240,128]{1,0:T(8,128)}, u32[]{:S(2)}, u32[]{:S(2)}) collective-permute-start(f32[240,128]{1,0:T(8,128)} %get-tuple-element.35), channel_id=1, source_target_pairs={{0,4},{4,8},{8,12},{12,0},{1,5},{5,9},{9,13},{13,1},{2,6},{6,10},{... | collective-permute-start | bytes 368648 | tf_op jit(solution)/shard_map/ppermute | solution.py:12
  97.1 1.3 %collective-permute-start.21 = (f32[240,128]{1,0:T(8,128)}, f32[240,128]{1,0:T(8,128)}, u32[]{:S(2)}, u32[]{:S(2)}) collective-permute-start(f32[240,128]{1,0:T(8,128)} %get-tuple-element.37), channel_id=1, source_target_pairs={{0,12},{4,0},{8,4},{12,8},{1,13},{5,1},{9,5},{13,9},{2,14},{6,2},{... | collective-permute-start | bytes 368648 | tf_op jit(solution)/shard_map/ppermute | solution.py:12
  98.3 2.3 %collective-permute-start.22 = (f32[240,128]{1,0:T(8,128)S(1)}, f32[240,128]{1,0:T(8,128)}, u32[]{:S(2)}, u32[]{:S(2)}) collective-permute-start(f32[240,128]{1,0:T(8,128)S(1)} %get-tuple-element.36), channel_id=1, source_target_pairs={{0,8},{4,12},{8,0},{12,4},{1,9},{5,13},{9,1},{13,5},{2,10},{6,14},... | collective-permute-start | bytes 368648 | tf_op jit(solution)/shard_map/ppermute | solution.py:12
  100.6 1.1 fusion.32
  101.8 2.1 %all-to-all-done.1 = f32[4,320,128]{2,1,0:T(8,128)S(1)} async-done(((f32[4,320,128]{2,1,0:T(8,128)}), f32[4,320,128]{2,1,0:T(8,128)S(1)}, u32[]{:S(2)}, u32[]{:S(2)}) %all-to-all-start.1) | async-done | bytes 655392 | tf_op jit(solution)/shard_map/all_to_all | solution.py:41
  104.0 2.1 %collective-permute-start.18 = (f32[320,128]{1,0:T(8,128)S(1)}, f32[320,128]{1,0:T(8,128)S(1)}, u32[]{:S(2)}, u32[]{:S(2)}) collective-permute-start(f32[320,128]{1,0:T(8,128)S(1)} %reduce_sum.19), channel_id=1, source_target_pairs={{0,2},{2,0},{1,3},{3,1},{4,6},{6,4},{5,7},{7,5},{8,10},{10,8},{9,1... | collective-permute-start | bytes 491528 | tf_op jit(solution)/shard_map/ppermute | solution.py:20
  106.1 2.5 %collective-permute-done.22 = f32[240,128]{1,0:T(8,128)} collective-permute-done((f32[240,128]{1,0:T(8,128)S(1)}, f32[240,128]{1,0:T(8,128)}, u32[]{:S(2)}, u32[]{:S(2)}) %collective-permute-start.22) | collective-permute-done | bytes 122912 | tf_op jit(solution)/shard_map/ppermute | solution.py:12
  108.6 1.1 add_add_fusion
  109.6 1.8 %collective-permute-start.23 = (f32[240,128]{1,0:T(8,128)S(1)}, f32[240,128]{1,0:T(8,128)S(1)}, u32[]{:S(2)}, u32[]{:S(2)}) collective-permute-start(f32[240,128]{1,0:T(8,128)S(1)} %add_add_fusion), channel_id=1, source_target_pairs={{0,2},{2,0},{1,3},{3,1},{4,6},{6,4},{5,7},{7,5},{8,10},{10,8},{9,1... | collective-permute-start | bytes 368648 | tf_op jit(solution)/shard_map/ppermute | solution.py:20
  111.6 0.9 fusion
  112.5 2.1 %collective-permute-done.23 = f32[240,128]{1,0:T(8,128)S(1)} collective-permute-done((f32[240,128]{1,0:T(8,128)S(1)}, f32[240,128]{1,0:T(8,128)S(1)}, u32[]{:S(2)}, u32[]{:S(2)}) %collective-permute-start.23) | collective-permute-done | bytes 122912 | tf_op jit(solution)/shard_map/ppermute | solution.py:20
  114.6 1.0 fusion.3
  (78 shorter events, 5.3 us)
Async XLA Ops:
  0.0 18.7 %collective-permute-start.2 = (bf16[80,2048]{1,0:T(8,128)(2,1)}, bf16[80,2048]{1,0:T(8,128)(2,1)S(1)}, u32[]{:S(2)}, u32[]{:S(2)}) collective-permute-start(bf16[80,2048]{1,0:T(8,128)(2,1)} %param.2), channel_id=1, source_target_pairs={{0,16},{16,32},{32,48},{48,0},{1,17},{17,33},{33,49},{49,1},{2,18}... | collective-permute-start | bytes 983048 | tf_op jit(solution)/shard_map/ppermute | solution.py:12
  4.5 18.4 %collective-permute-start = (bf16[80,2048]{1,0:T(8,128)(2,1)}, bf16[80,2048]{1,0:T(8,128)(2,1)S(1)}, u32[]{:S(2)}, u32[]{:S(2)}) collective-permute-start(bf16[80,2048]{1,0:T(8,128)(2,1)} %param.2), channel_id=1, source_target_pairs={{0,48},{16,0},{32,16},{48,32},{1,49},{17,1},{33,17},{49,33},{2,50}... | collective-permute-start | bytes 983048 | tf_op jit(solution)/shard_map/ppermute | solution.py:12
  4.5 21.8 %collective-permute-start.4 = (bf16[80,2048]{1,0:T(8,128)(2,1)}, bf16[80,2048]{1,0:T(8,128)(2,1)S(1)}, u32[]{:S(2)}, u32[]{:S(2)}) collective-permute-start(bf16[80,2048]{1,0:T(8,128)(2,1)} %param.2), channel_id=1, source_target_pairs={{0,64},{64,128},{128,192},{192,0},{1,65},{65,129},{129,193},{193,1... | collective-permute-start | bytes 983048 | tf_op jit(solution)/shard_map/ppermute | solution.py:12
  6.0 20.3 %collective-permute-start.5 = (bf16[80,2048]{1,0:T(8,128)(2,1)}, bf16[80,2048]{1,0:T(8,128)(2,1)S(1)}, u32[]{:S(2)}, u32[]{:S(2)}) collective-permute-start(bf16[80,2048]{1,0:T(8,128)(2,1)} %param.2), channel_id=1, source_target_pairs={{0,192},{64,0},{128,64},{192,128},{1,193},{65,1},{129,65},{193,129... | collective-permute-start | bytes 983048 | tf_op jit(solution)/shard_map/ppermute | solution.py:12
  7.7 7.1 %copy-start.5 = (bf16[80,2048]{1,0:T(8,128)(2,1)S(1)}, bf16[80,2048]{1,0:T(8,128)(2,1)}, u32[]{:S(2)}) copy-start(bf16[80,2048]{1,0:T(8,128)(2,1)} %param.2) | copy-start | bytes 983044
  14.8 26.4 %copy-start.7 = (bf16[2048,1024]{0,1:T(8,128)(2,1)}, bf16[2048,1024]{0,1:T(8,128)(2,1)S(1)}, u32[]{:S(2)}) copy-start(bf16[2048,1024]{0,1:T(8,128)(2,1)S(1)} %convert_bitcast_fusion) | copy-start | bytes 12582916
  22.9 17.0 %collective-permute-start.7 = (bf16[160,2048]{1,0:T(8,128)(2,1)S(1)}, bf16[160,2048]{1,0:T(8,128)(2,1)S(1)}, u32[]{:S(2)}, u32[]{:S(2)}) collective-permute-start(bf16[160,2048]{1,0:T(8,128)(2,1)S(1)} %constant_dynamic-update-slice_fusion), channel_id=1, source_target_pairs={{0,64},{64,128},{128,192},{192,0},{1,65},{65,129},{129,193},{193,1... | collective-permute-start | bytes 1966088 | tf_op jit(solution)/shard_map/ppermute | solution.py:12
  24.5 15.5 %collective-permute-start.8 = (bf16[160,2048]{1,0:T(8,128)(2,1)S(1)}, bf16[160,2048]{1,0:T(8,128)(2,1)S(1)}, u32[]{:S(2)}, u32[]{:S(2)}) collective-permute-start(bf16[160,2048]{1,0:T(8,128)(2,1)S(1)} %constant_dynamic-update-slice_fusion), channel_id=1, source_target_pairs={{0,192},{64,0},{128,64},{192,128},{1,193},{65,1},{129,65},{193,129... | collective-permute-start | bytes 1966088 | tf_op jit(solution)/shard_map/ppermute | solution.py:12
  26.3 7.6 %collective-permute-start.1 = (bf16[40,2048]{1,0:T(8,128)(2,1)S(1)}, bf16[40,2048]{1,0:T(8,128)(2,1)S(1)}, u32[]{:S(2)}, u32[]{:S(2)}) collective-permute-start(bf16[40,2048]{1,0:T(8,128)(2,1)S(1)} %slice.84), channel_id=1, source_target_pairs={{0,48},{16,0},{32,16},{48,32},{1,49},{17,1},{33,17},{49,33},{2,50}... | collective-permute-start | bytes 491528 | tf_op jit(solution)/shard_map/ppermute | solution.py:12
  26.4 8.0 %collective-permute-start.3 = (bf16[40,2048]{1,0:T(8,128)(2,1)S(1)}, bf16[40,2048]{1,0:T(8,128)(2,1)S(1)}, u32[]{:S(2)}, u32[]{:S(2)}) collective-permute-start(bf16[40,2048]{1,0:T(8,128)(2,1)S(1)} %slice.85), channel_id=1, source_target_pairs={{0,16},{16,32},{32,48},{48,0},{1,17},{17,33},{33,49},{49,1},{2,18}... | collective-permute-start | bytes 491528 | tf_op jit(solution)/shard_map/ppermute | solution.py:12
  31.7 9.5 %collective-permute-start.6 = (f32[400,512]{1,0:T(8,128)S(1)}, f32[400,512]{1,0:T(8,128)S(1)}, u32[]{:S(2)}, u32[]{:S(2)}) collective-permute-start(f32[400,512]{1,0:T(8,128)S(1)} %fusion.12), channel_id=1, source_target_pairs={{0,1},{1,0},{2,3},{3,2},{4,5},{5,4},{6,7},{7,6},{8,9},{9,8},{10,11... | collective-permute-start | bytes 2457608 | tf_op jit(solution)/shard_map/ppermute | solution.py:20
  34.4 5.7 %copy-start.2 = (bf16[40,2048]{1,0:T(8,128)(2,1)}, bf16[40,2048]{1,0:T(8,128)(2,1)S(1)}, u32[]{:S(2)}) copy-start(bf16[40,2048]{1,0:T(8,128)(2,1)S(1)} %collective-permute-done.3) | copy-start | bytes 491524
  40.0 14.3 %copy-start = (bf16[160,2048]{1,0:T(8,128)(2,1)}, bf16[160,2048]{1,0:T(8,128)(2,1)S(1)}, u32[]{:S(2)}) copy-start(bf16[160,2048]{1,0:T(8,128)(2,1)S(1)} %collective-permute-done.7) | copy-start | bytes 1966084
  40.1 1.1 copy-start.4
  42.3 3.2 %collective-permute-start.11 = (f32[320,512]{1,0:T(8,128)S(1)}, f32[320,512]{1,0:T(8,128)}, u32[]{:S(2)}, u32[]{:S(2)}) collective-permute-start(f32[320,512]{1,0:T(8,128)S(1)} %fusion.10), channel_id=1, source_target_pairs={{0,1},{1,0},{2,3},{3,2},{4,5},{5,4},{6,7},{7,6},{8,9},{9,8},{10,11... | collective-permute-start | bytes 1966088 | tf_op jit(solution)/shard_map/ppermute | solution.py:20
  42.6 14.2 %collective-permute-start.10 = (bf16[120,2048]{1,0:T(8,128)(2,1)}, bf16[120,2048]{1,0:T(8,128)(2,1)S(1)}, u32[]{:S(2)}, u32[]{:S(2)}) collective-permute-start(bf16[120,2048]{1,0:T(8,128)(2,1)} %get-tuple-element.23), channel_id=1, source_target_pairs={{0,192},{64,0},{128,64},{192,128},{1,193},{65,1},{129,65},{193,129... | collective-permute-start | bytes 1474568 | tf_op jit(solution)/shard_map/ppermute | solution.py:12
  45.5 14.7 %collective-permute-start.9 = (bf16[120,2048]{1,0:T(8,128)(2,1)}, bf16[120,2048]{1,0:T(8,128)(2,1)}, u32[]{:S(2)}, u32[]{:S(2)}) collective-permute-start(bf16[120,2048]{1,0:T(8,128)(2,1)} %get-tuple-element.22), channel_id=1, source_target_pairs={{0,64},{64,128},{128,192},{192,0},{1,65},{65,129},{129,193},{193,1... | collective-permute-start | bytes 1474568 | tf_op jit(solution)/shard_map/ppermute | solution.py:12
  49.7 24.4 %all-to-all-start = ((f32[4,720,128]{2,1,0:T(8,128)}), f32[4,720,128]{2,1,0:T(8,128)S(1)}, u32[]{:S(2)}, u32[]{:S(2)}) async-start(f32[4,720,128]{2,1,0:T(8,128)} %bitcast_bitcast_fusion), calls=%async_computation | async-start | bytes 2949120 | tf_op jit(solution)/shard_map/all_to_all | solution.py:41
  54.2 10.7 %copy-start.3 = (bf16[40,2048]{1,0:T(8,128)(2,1)S(1)}, bf16[40,2048]{1,0:T(8,128)(2,1)}, u32[]{:S(2)}) copy-start(bf16[40,2048]{1,0:T(8,128)(2,1)} %copy-done.2) | copy-start | bytes 491524
  54.3 7.9 %slice-start = ((bf16[160,2048]{1,0:T(8,128)(2,1)}), bf16[80,2048]{1,0:T(8,128)(2,1)S(1)}, s32[]{:S(2)}) async-start(bf16[160,2048]{1,0:T(8,128)(2,1)} %copy-done), calls=%async_computation.2 | async-start | bytes 655360 | tf_op jit(solution)/shard_map/slice | solution.py:78
  61.1 20.9 %collective-permute-start.14 = (bf16[120,2048]{1,0:T(8,128)(2,1)}, bf16[120,2048]{1,0:T(8,128)(2,1)}, u32[]{:S(2)}, u32[]{:S(2)}) collective-permute-start(bf16[120,2048]{1,0:T(8,128)(2,1)} %pad_maximum_fusion.5), channel_id=1, source_target_pairs={{0,192},{64,0},{128,64},{192,128},{1,193},{65,1},{129,65},{193,129... | collective-permute-start | bytes 1474568 | tf_op jit(solution)/shard_map/ppermute | solution.py:12
  63.1 19.0 %collective-permute-start.13 = (bf16[120,2048]{1,0:T(8,128)(2,1)}, bf16[120,2048]{1,0:T(8,128)(2,1)}, u32[]{:S(2)}, u32[]{:S(2)}) collective-permute-start(bf16[120,2048]{1,0:T(8,128)(2,1)} %pad_maximum_fusion.4), channel_id=1, source_target_pairs={{0,64},{64,128},{128,192},{192,0},{1,65},{65,129},{129,193},{193,1... | collective-permute-start | bytes 1474568 | tf_op jit(solution)/shard_map/ppermute | solution.py:12
  74.2 5.2 %copy-start.1 = (bf16[320,2048]{1,0:T(8,128)(2,1)S(1)}, bf16[320,2048]{1,0:T(8,128)(2,1)}, u32[]{:S(2)}) copy-start(bf16[320,2048]{1,0:T(8,128)(2,1)} %pad_maximum_fusion) | copy-start | bytes 3932164
  77.2 2.2 %collective-permute-start.17 = (f32[112,512]{1,0:T(8,128)S(1)}, f32[112,512]{1,0:T(8,128)}, u32[]{:S(2)}, u32[]{:S(2)}) collective-permute-start(f32[112,512]{1,0:T(8,128)S(1)} %slice.95), channel_id=1, source_target_pairs={{0,1},{1,0},{2,3},{3,2},{4,5},{5,4},{6,7},{7,6},{8,9},{9,8},{10,11... | collective-permute-start | bytes 688136 | tf_op jit(solution)/shard_map/ppermute | solution.py:20
  77.3 1.7 %collective-permute-start.15 = (f32[104,512]{1,0:T(8,128)S(1)}, f32[104,512]{1,0:T(8,128)S(1)}, u32[]{:S(2)}, u32[]{:S(2)}) collective-permute-start(f32[104,512]{1,0:T(8,128)S(1)} %get-tuple-element.33), channel_id=1, source_target_pairs={{0,1},{1,0},{2,3},{3,2},{4,5},{5,4},{6,7},{7,6},{8,9},{9,8},{10,11... | collective-permute-start | bytes 638984 | tf_op jit(solution)/shard_map/ppermute | solution.py:20
  77.9 1.5 %collective-permute-start.16 = (f32[104,512]{1,0:T(8,128)S(1)}, f32[104,512]{1,0:T(8,128)S(1)}, u32[]{:S(2)}, u32[]{:S(2)}) collective-permute-start(f32[104,512]{1,0:T(8,128)S(1)} %get-tuple-element.34), channel_id=1, source_target_pairs={{0,1},{1,0},{2,3},{3,2},{4,5},{5,4},{6,7},{7,6},{8,9},{9,8},{10,11... | collective-permute-start | bytes 638984 | tf_op jit(solution)/shard_map/ppermute | solution.py:20
  79.4 4.8 %copy-start.8 = (bf16[2048,1024]{0,1:T(8,128)(2,1)S(1)}, bf16[2048,1024]{0,1:T(8,128)(2,1)}, u32[]{:S(2)}) copy-start(bf16[2048,1024]{0,1:T(8,128)(2,1)} %copy-done.7) | copy-start | bytes 12582916
  84.2 1.6 %copy-start.6 = (bf16[240,2048]{1,0:T(8,128)(2,1)}, bf16[240,2048]{1,0:T(8,128)(2,1)S(1)}, u32[]{:S(2)}) copy-start(bf16[240,2048]{1,0:T(8,128)(2,1)S(1)} %constant_dynamic-update-slice_fusion.8) | copy-start | bytes 2949124
  85.8 5.8 %collective-permute-start.19 = (f32[240,512]{1,0:T(8,128)}, f32[240,512]{1,0:T(8,128)}, u32[]{:S(2)}, u32[]{:S(2)}) collective-permute-start(f32[240,512]{1,0:T(8,128)} %fusion.6), channel_id=1, source_target_pairs={{0,1},{1,0},{2,3},{3,2},{4,5},{5,4},{6,7},{7,6},{8,9},{9,8},{10,11... | collective-permute-start | bytes 1474568 | tf_op jit(solution)/shard_map/ppermute | solution.py:20
  87.2 13.5 %collective-permute-start.12 = (f32[720,128]{1,0:T(8,128)S(1)}, f32[720,128]{1,0:T(8,128)}, u32[]{:S(2)}, u32[]{:S(2)}) collective-permute-start(f32[720,128]{1,0:T(8,128)S(1)} %reduce_sum.18), channel_id=1, source_target_pairs={{0,2},{2,0},{1,3},{3,1},{4,6},{6,4},{5,7},{7,5},{8,10},{10,8},{9,1... | collective-permute-start | bytes 1105928 | tf_op jit(solution)/shard_map/ppermute | solution.py:20
  88.2 15.8 %all-to-all-start.1 = ((f32[4,320,128]{2,1,0:T(8,128)}), f32[4,320,128]{2,1,0:T(8,128)S(1)}, u32[]{:S(2)}, u32[]{:S(2)}) async-start(f32[4,320,128]{2,1,0:T(8,128)} %bitcast_bitcast_fusion.1), calls=%async_computation.1 | async-start | bytes 1310720 | tf_op jit(solution)/shard_map/all_to_all | solution.py:41
  95.1 11.0 %collective-permute-start.20 = (f32[240,128]{1,0:T(8,128)}, f32[240,128]{1,0:T(8,128)}, u32[]{:S(2)}, u32[]{:S(2)}) collective-permute-start(f32[240,128]{1,0:T(8,128)} %get-tuple-element.35), channel_id=1, source_target_pairs={{0,4},{4,8},{8,12},{12,0},{1,5},{5,9},{9,13},{13,1},{2,6},{6,10},{... | collective-permute-start | bytes 368648 | tf_op jit(solution)/shard_map/ppermute | solution.py:12
  97.1 9.0 %collective-permute-start.21 = (f32[240,128]{1,0:T(8,128)}, f32[240,128]{1,0:T(8,128)}, u32[]{:S(2)}, u32[]{:S(2)}) collective-permute-start(f32[240,128]{1,0:T(8,128)} %get-tuple-element.37), channel_id=1, source_target_pairs={{0,12},{4,0},{8,4},{12,8},{1,13},{5,1},{9,5},{13,9},{2,14},{6,2},{... | collective-permute-start | bytes 368648 | tf_op jit(solution)/shard_map/ppermute | solution.py:12
  98.3 10.2 %collective-permute-start.22 = (f32[240,128]{1,0:T(8,128)S(1)}, f32[240,128]{1,0:T(8,128)}, u32[]{:S(2)}, u32[]{:S(2)}) collective-permute-start(f32[240,128]{1,0:T(8,128)S(1)} %get-tuple-element.36), channel_id=1, source_target_pairs={{0,8},{4,12},{8,0},{12,4},{1,9},{5,13},{9,1},{13,5},{2,10},{6,14},... | collective-permute-start | bytes 368648 | tf_op jit(solution)/shard_map/ppermute | solution.py:12
  104.0 7.5 %collective-permute-start.18 = (f32[320,128]{1,0:T(8,128)S(1)}, f32[320,128]{1,0:T(8,128)S(1)}, u32[]{:S(2)}, u32[]{:S(2)}) collective-permute-start(f32[320,128]{1,0:T(8,128)S(1)} %reduce_sum.19), channel_id=1, source_target_pairs={{0,2},{2,0},{1,3},{3,1},{4,6},{6,4},{5,7},{7,5},{8,10},{10,8},{9,1... | collective-permute-start | bytes 491528 | tf_op jit(solution)/shard_map/ppermute | solution.py:20
  109.6 5.0 %collective-permute-start.23 = (f32[240,128]{1,0:T(8,128)S(1)}, f32[240,128]{1,0:T(8,128)S(1)}, u32[]{:S(2)}, u32[]{:S(2)}) collective-permute-start(f32[240,128]{1,0:T(8,128)S(1)} %add_add_fusion), channel_id=1, source_target_pairs={{0,2},{2,0},{1,3},{3,1},{4,6},{6,4},{5,7},{7,5},{8,10},{10,8},{9,1... | collective-permute-start | bytes 368648 | tf_op jit(solution)/shard_map/ppermute | solution.py:20

commit v11 on v10

--- a/solution.py
+++ b/solution.py
@@ -48,6 +48,12 @@
     def over_zl(some):
         return (some[:, :64] + swap(some, "zl")[:, 64:]).astype(BF16)
 
+    def over_zl_folded(some):
+        half = some.shape[0] // 2
+        other = some[:, 64:]
+        came = swap(jnp.concatenate([other[:half], other[half:]], axis=1), "zl")
+        return (some[:, :64] + joined(came[:, :64], came[:, 64:])).astype(BF16)
+
     def block(dx, dz, first=0, count=ROWS):
         start = (((x + dx) % 4) * 4 + (zh + dz) % 4) * ROWS + first
         return start + jnp.arange(count)
@@ -69,27 +75,32 @@
 
     late_rows = joined(side_xm, side_xp)
     after_xm, after_xp, early, away = lax.optimization_barrier(
-        (joined(far, own_xm[40:]), joined(far, own_xp[:40]), early, dot(late_rows, theirs))
+        (
+            joined(far, own_xm[40:], side_xm[80:]),
+            joined(far, own_xp[:40], side_xp[:80]),
+            early,
+            dot(late_rows, theirs),
+        )
     )
     from_xm, from_xp = shift(after_xm, "x", 4, 1), shift(after_xp, "x", 4, -1)
     late = dot(late_rows, mine) + swap(away, "core")
     early = over_y(joined(early, late))
     from_xm, from_xp, late = lax.optimization_barrier((from_xm, from_xp, late))
-    last_xm = shift(joined(side_xm[80:], from_xm[40:80]), "x", 4, 1)
-    last_xp = shift(joined(side_xp[:80], from_xp[:40]), "x", 4, -1)
-    rows, early = lax.optimization_barrier((joined(far, from_xm, from_xp), early))
-    away = dot(rows, theirs)
-    away = joined(*[swap(piece, "core") for piece in (away[:104], away[104:208], away[208:])])
-    second = dot(rows, mine) + away
-    last_xm, last_xp, second = lax.optimization_barrier((last_xm, last_xp, second))
-    second = over_y(second)
-    third = over_y_at_once(paired(joined(last_xm, last_xp)))
-    sums = [over_zl(part) for part in (early, second, third)]
+    last_xm = shift(from_xm[40:80], "x", 4, 1)
+    last_xp = shift(from_xp[:40], "x", 4, -1)
+    rows, early = lax.optimization_barrier(
+        (joined(far, from_xm, from_xp, last_xm, last_xp), early)
+    )
+    away = swap(dot(rows, theirs), "core")
+    kept = lax.optimization_barrier(dot(rows, mine))
+    last, early = lax.optimization_barrier((over_y_at_once(kept + away), over_zl(early)))
+    sums = [early, over_zl_folded(last)]
     sites = [
         [block(0, 0), block(-1, 0), block(1, 0), block(0, -1), block(0, 1)],
         [block(-1, -1), block(-1, 1), block(1, -1), block(1, 1)],
-        [block(0, 2), block(-1, 2), block(2, 0, 40, 40), block(1, 2), block(2, 0, 0, 40)],
-        [block(2, 1), block(2, 2, 40, 40), block(2, -1), block(2, 2, 0, 40)],
+        [block(0, 2), block(-1, 2), block(2, 0, 40, 40), block(2, 1)],
+        [block(1, 2), block(2, 0, 0, 40), block(2, -1)],
+        [block(2, 2, 40, 40), block(2, 2, 0, 40)],
     ]
     places = joined(*[p for ps in sites for p in ps])
     place = (places[:, None] == jnp.arange(1280)[None, :]).astype(BF16)
@@ -97,7 +108,7 @@
     def put(some, where):
         return lax.dot_general(some, where, (((0,), (0,)), ((), ())), preferred_element_type=F32)
 
-    turned = put(joined(*sums[:2]), place[:1040]) + put(sums[2], place[1040:])
+    turned = put(sums[0], place[:720]) + put(sums[1], place[720:])
     return turned.astype(BF16)
 
 

time: 116 us -> 112 us (0.966)
  waiting for transfers between devices: 35.7 us -> 43.5 us
  starting transfers between devices: 39.2 us -> 33.1 us
  other arithmetic: 9.74 us -> 5.36 us
  matrix products: 24.9 us -> 23.1 us
    ppermute x15, waiting for transfers between devices: 23.2 us -> 39.7 us  [shift(): lax.ppermute(value, axis, [(i, (i + by) % size) for i in range(size)])]
    all_to_all x2 -> x1, waiting for transfers between devices: 9.11 us -> 0.01 us  [over_y(): lax.all_to_all(split, 'y', split_axis=0, concat_axis=0, tiled=True)]
    concatenate x4 -> x1, other arithmetic: 5.03 us -> 1.42 us  [joined(): return jnp.concatenate(parts, axis=0)]
    all_to_all x2 -> x1, starting transfers between devices: 7.94 us -> 4.46 us  [over_y(): lax.all_to_all(split, 'y', split_axis=0, concat_axis=0, tiled=True)]
    ppermute x9 -> x5, starting transfers between devices: 5.5 us -> 2.19 us  [swap(): return lax.ppermute(value, axis, [(0, 1), (1, 0)])]
    unnamed x24 -> x20, local copies, waits for them, and re-layouts: 1.5 us -> 4.16 us
    dot_general x9 -> x7, matrix products: 22.9 us -> 21.3 us  [dot(): return jnp.dot(left, right, preferred_element_type=F32)]
    ppermute x9 -> x5, waiting for transfers between devices: 3.38 us -> 3.83 us  [swap(): return lax.ppermute(value, axis, [(0, 1), (1, 0)])]
  transfers between devices with their start and end apart: 26 -> 21, of which waited for: 13 -> 11; matrix products, arithmetic and copies ran while one was open for 29% -> 23% of each run, Pallas kernels for 0% -> 0%
where the time goes in v11:
time: 112 us
  waiting for transfers between devices  43.5 us (39%)
  starting transfers between devices  33.1 us (30%)
  matrix products  23.1 us (21%)
  local copies, waits for them, and re-layouts  6.26 us (6%)
  other arithmetic  5.36 us (5%)
    ppermute x15, waiting for transfers between devices, shift(): lax.ppermute(value, axis, [(i, (i + by) % size) for i in range(size)])  39.7 us
    ppermute x15, starting transfers between devices, shift(): lax.ppermute(value, axis, [(i, (i + by) % size) for i in range(size)])  26.5 us
    dot_general x7, matrix products, dot(): return jnp.dot(left, right, preferred_element_type=F32)  21.3 us
    all_to_all x1, starting transfers between devices, over_y(): lax.all_to_all(split, 'y', split_axis=0, concat_axis=0, tiled=True)  4.46 us
    unnamed x20, local copies, waits for them, and re-layouts  4.16 us
    ppermute x5, waiting for transfers between devices, swap(): return lax.ppermute(value, axis, [(0, 1), (1, 0)])  3.83 us
  transfers between devices with their start and end apart: 21, of which 11 were waited for; matrix products, arithmetic and copies ran while one was open for 23% of the time, Pallas kernels for 0%

profile of v11, /device:TPU:64, one launch (start us, length us, event | category | flops | bytes accessed | tf_op | source)
XLA Modules:
  0.0 112.0 jit_solution(3044304286627967426)
XLA Ops:
  0.0 4.5 %collective-permute-start.2 = (bf16[80,2048]{1,0:T(8,128)(2,1)}, bf16[80,2048]{1,0:T(8,128)(2,1)S(1)}, u32[]{:S(2)}, u32[]{:S(2)}) collective-permute-start(bf16[80,2048]{1,0:T(8,128)(2,1)} %param.2), channel_id=1, source_target_pairs={{0,16},{16,32},{32,48},{48,0},{1,17},{17,33},{33,49},{49,1},{2,18}... | collective-permute-start | bytes 983048 | tf_op jit(solution)/shard_map/ppermute | solution.py:12
  4.5 1.5 %collective-permute-start.4 = (bf16[80,2048]{1,0:T(8,128)(2,1)}, bf16[80,2048]{1,0:T(8,128)(2,1)S(1)}, u32[]{:S(2)}, u32[]{:S(2)}) collective-permute-start(bf16[80,2048]{1,0:T(8,128)(2,1)} %param.2), channel_id=1, source_target_pairs={{0,64},{64,128},{128,192},{192,0},{1,65},{65,129},{129,193},{193,1... | collective-permute-start | bytes 983048 | tf_op jit(solution)/shard_map/ppermute | solution.py:12
  6.0 1.7 %collective-permute-start.6 = (bf16[80,2048]{1,0:T(8,128)(2,1)}, bf16[80,2048]{1,0:T(8,128)(2,1)S(1)}, u32[]{:S(2)}, u32[]{:S(2)}) collective-permute-start(bf16[80,2048]{1,0:T(8,128)(2,1)} %param.2), channel_id=1, source_target_pairs={{0,192},{64,0},{128,64},{192,128},{1,193},{65,1},{129,65},{193,129... | collective-permute-start | bytes 983048 | tf_op jit(solution)/shard_map/ppermute | solution.py:12
  7.7 7.1 %convert_bitcast_fusion = bf16[2048,1024]{0,1:T(8,128)(2,1)S(1)} fusion(bf16[2048,1024]{1,0:T(8,128)(2,1)} %param.3, s32[1024]{0:T(1024)S(1)} %and_add_fusion), kind=kOutput, calls=%fused_computation.1 | convolution fusion | flops 4299161600 | bytes 8392704 | tf_op jit(solution)/shard_map/dot_general | solution.py:24
  14.9 3.8 %collective-permute-done.2 = bf16[80,2048]{1,0:T(8,128)(2,1)S(1)} collective-permute-done((bf16[80,2048]{1,0:T(8,128)(2,1)}, bf16[80,2048]{1,0:T(8,128)(2,1)S(1)}, u32[]{:S(2)}, u32[]{:S(2)}) %collective-permute-start.2) | collective-permute-done | bytes 327712 | tf_op jit(solution)/shard_map/ppermute | solution.py:12
  18.7 4.2 %collective-permute-done = bf16[80,2048]{1,0:T(8,128)(2,1)S(1)} collective-permute-done((bf16[80,2048]{1,0:T(8,128)(2,1)}, bf16[80,2048]{1,0:T(8,128)(2,1)S(1)}, u32[]{:S(2)}, u32[]{:S(2)}) %collective-permute-start) | collective-permute-done | bytes 327712 | tf_op jit(solution)/shard_map/ppermute | solution.py:12
  22.9 1.6 %collective-permute-start.5 = (bf16[160,2048]{1,0:T(8,128)(2,1)S(1)}, bf16[160,2048]{1,0:T(8,128)(2,1)S(1)}, u32[]{:S(2)}, u32[]{:S(2)}) collective-permute-start(bf16[160,2048]{1,0:T(8,128)(2,1)S(1)} %constant_dynamic-update-slice_fusion), channel_id=1, source_target_pairs={{0,64},{64,128},{128,192},{192,0},{1,65},{65,129},{129,193},{193,1... | collective-permute-start | bytes 1966088 | tf_op jit(solution)/shard_map/ppermute | solution.py:12
  24.5 1.7 %collective-permute-start.7 = (bf16[160,2048]{1,0:T(8,128)(2,1)S(1)}, bf16[160,2048]{1,0:T(8,128)(2,1)S(1)}, u32[]{:S(2)}, u32[]{:S(2)}) collective-permute-start(bf16[160,2048]{1,0:T(8,128)(2,1)S(1)} %constant_dynamic-update-slice_fusion), channel_id=1, source_target_pairs={{0,192},{64,0},{128,64},{192,128},{1,193},{65,1},{129,65},{193,129... | collective-permute-start | bytes 1966088 | tf_op jit(solution)/shard_map/ppermute | solution.py:12
  26.4 1.1 fusion.17
  27.7 4.4 %collective-permute-start.3 = (bf16[40,2048]{1,0:T(8,128)(2,1)S(1)}, bf16[40,2048]{1,0:T(8,128)(2,1)S(1)}, u32[]{:S(2)}, u32[]{:S(2)}) collective-permute-start(bf16[40,2048]{1,0:T(8,128)(2,1)S(1)} %slice.80), channel_id=1, source_target_pairs={{0,16},{16,32},{32,48},{48,0},{1,17},{17,33},{33,49},{49,1},{2,18}... | collective-permute-start | bytes 491528 | tf_op jit(solution)/shard_map/ppermute | solution.py:12
  32.1 7.9 %collective-permute-done.5 = bf16[160,2048]{1,0:T(8,128)(2,1)S(1)} collective-permute-done((bf16[160,2048]{1,0:T(8,128)(2,1)S(1)}, bf16[160,2048]{1,0:T(8,128)(2,1)S(1)}, u32[]{:S(2)}, u32[]{:S(2)}) %collective-permute-start.5) | collective-permute-done | bytes 655392 | tf_op jit(solution)/shard_map/ppermute | solution.py:12
  40.2 0.7 slice-done
  41.0 1.4 %pad_maximum_fusion.2 = (bf16[200,2048]{1,0:T(8,128)(2,1)}, bf16[200,2048]{1,0:T(8,128)(2,1)}) fusion(bf16[80,2048]{1,0:T(8,128)(2,1)S(1)} %slice.84, bf16[40,2048]{1,0:T(8,128)(2,1)S(1)} %slice-done.1, bf16[40,2048]{1,0:T(8,128)(2,1)S(1)} %collective-permute-done.3, bf16[40,2048]{1,0:T(8,128)(2,1)S(1)} %collective-permute-done.1, ...), kind=kLoop, calls=%fused_computation.29 | loop fusion | flops 5324800 | bytes 2949120 | tf_op jit(solution)/shard_map/concatenate | solution.py:28
  42.4 1.7 %fusion.15 = f32[320,512]{1,0:T(8,128)} fusion(bf16[320,2048]{1,0:T(8,128)(2,1)S(1)} %constant_dynamic-update-slice_fusion.6, bf16[2048,1024]{0,1:T(8,128)(2,1)S(1)} %convert_bitcast_fusion), kind=kOutput, calls=%fused_computation.13 | convolution fusion | flops 671088640 | bytes 4063232 | tf_op jit(solution)/shard_map/dot_general | solution.py:24
  44.1 1.1 fusion.28
  45.4 2.3 %collective-permute-start.10 = (bf16[200,2048]{1,0:T(8,128)(2,1)}, bf16[200,2048]{1,0:T(8,128)(2,1)S(1)}, u32[]{:S(2)}, u32[]{:S(2)}) collective-permute-start(bf16[200,2048]{1,0:T(8,128)(2,1)} %get-tuple-element.22), channel_id=1, source_target_pairs={{0,192},{64,0},{128,64},{192,128},{1,193},{65,1},{129,65},{193,129... | collective-permute-start | bytes 2457608 | tf_op jit(solution)/shard_map/ppermute | solution.py:12
  47.7 0.7 constant_dynamic-update-slice_fusion.13
  48.4 3.0 %fusion.25 = f32[320,512]{1,0:T(8,128)S(1)} fusion(f32[320,512]{1,0:T(8,128)} %collective-permute-done.11, bf16[320,2048]{1,0:T(8,128)(2,1)} %copy-done.2, bf16[2048,1024]{0,1:T(8,128)(2,1)} %copy-done.4), kind=kOutput, calls=%fused_computation.25 | convolution fusion | flops 671252480 | bytes 4718592 | tf_op jit(solution)/shard_map/dot_general | solution.py:24
  51.4 1.2 %bitcast_bitcast_fusion = f32[4,720,128]{2,1,0:T(8,128)} fusion(f32[320,512]{1,0:T(8,128)S(1)} %fusion.25, f32[400,512]{1,0:T(8,128)S(1)} %fusion.28), kind=kLoop, calls=%fused_computation.23 | loop fusion | flops 368640 | bytes 2949120 | tf_op jit(solution)/shard_map/transpose | solution.py:40
  52.6 4.5 %all-to-all-start = ((f32[4,720,128]{2,1,0:T(8,128)}), f32[4,720,128]{2,1,0:T(8,128)S(1)}, u32[]{:S(2)}, u32[]{:S(2)}) async-start(f32[4,720,128]{2,1,0:T(8,128)} %bitcast_bitcast_fusion), calls=%async_computation | async-start | bytes 2949120 | tf_op jit(solution)/shard_map/all_to_all | solution.py:41
  57.1 0.7 constant_dynamic-update-slice_fusion.12
  57.8 8.4 %collective-permute-done.10 = bf16[200,2048]{1,0:T(8,128)(2,1)S(1)} collective-permute-done((bf16[200,2048]{1,0:T(8,128)(2,1)}, bf16[200,2048]{1,0:T(8,128)(2,1)S(1)}, u32[]{:S(2)}, u32[]{:S(2)}) %collective-permute-start.10) | collective-permute-done | bytes 819232 | tf_op jit(solution)/shard_map/ppermute | solution.py:12
  66.2 3.2 %collective-permute-done.9 = bf16[200,2048]{1,0:T(8,128)(2,1)S(1)} collective-permute-done((bf16[200,2048]{1,0:T(8,128)(2,1)}, bf16[200,2048]{1,0:T(8,128)(2,1)S(1)}, u32[]{:S(2)}, u32[]{:S(2)}) %collective-permute-start.9) | collective-permute-done | bytes 819232 | tf_op jit(solution)/shard_map/ppermute | solution.py:12
  69.5 3.3 %collective-permute-start.13 = (bf16[40,2048]{1,0:T(8,128)(2,1)S(1)}, bf16[40,2048]{1,0:T(8,128)(2,1)S(1)}, u32[]{:S(2)}, u32[]{:S(2)}) collective-permute-start(bf16[40,2048]{1,0:T(8,128)(2,1)S(1)} %slice.69), channel_id=1, source_target_pairs={{0,192},{64,0},{128,64},{192,128},{1,193},{65,1},{129,65},{193,129... | collective-permute-start | bytes 491528 | tf_op jit(solution)/shard_map/ppermute | solution.py:12
  72.8 1.0 constant_dynamic-update-slice_fusion.11
  73.7 1.0 constant_dynamic-update-slice_fusion.10
  74.7 1.3 %collective-permute-done.12 = bf16[40,2048]{1,0:T(8,128)(2,1)S(1)} collective-permute-done((bf16[40,2048]{1,0:T(8,128)(2,1)S(1)}, bf16[40,2048]{1,0:T(8,128)(2,1)S(1)}, u32[]{:S(2)}, u32[]{:S(2)}) %collective-permute-start.12) | collective-permute-done | bytes 163872 | tf_op jit(solution)/shard_map/ppermute | solution.py:12
  76.0 0.7 constant_dynamic-update-slice_fusion.9
  76.7 0.7 constant_dynamic-update-slice_fusion.8
  77.4 3.7 %fusion.13 = f32[560,512]{1,0:T(8,128)S(1)} fusion(bf16[560,2048]{1,0:T(8,128)(2,1)} %constant_dynamic-update-slice_fusion.8, bf16[2048,1024]{0,1:T(8,128)(2,1)} %copy-done.4), kind=kOutput, calls=%fused_computation.11 | convolution fusion | flops 1174405120 | bytes 5537792 | tf_op jit(solution)/shard_map/dot_general | solution.py:24
  81.5 3.7 %fusion.19 = f32[560,512]{1,0:T(8,128)S(1)} fusion(bf16[560,2048]{1,0:T(8,128)(2,1)} %constant_dynamic-update-slice_fusion.8, bf16[2048,1024]{0,1:T(8,128)(2,1)} %copy-done.4), kind=kOutput, calls=%fused_computation.17 | convolution fusion | flops 1174405120 | bytes 5537792 | tf_op jit(solution)/shard_map/dot_general | solution.py:24
  85.2 0.2 add.342
  85.5 0.1 constant_dynamic-slice_fusion.2
  85.6 1.7 %collective-permute-start.15 = (f32[560,128]{1,0:T(8,128)S(1)}, f32[560,128]{1,0:T(8,128)S(1)}, u32[]{:S(2)}, u32[]{:S(2)}) collective-permute-start(f32[560,128]{1,0:T(8,128)S(1)} %get-tuple-element.31), channel_id=1, source_target_pairs={{0,4},{4,8},{8,12},{12,0},{1,5},{5,9},{9,13},{13,1},{2,6},{6,10},{... | collective-permute-start | bytes 860168 | tf_op jit(solution)/shard_map/ppermute | solution.py:12
  87.3 1.7 %collective-permute-start.16 = (f32[560,128]{1,0:T(8,128)S(1)}, f32[560,128]{1,0:T(8,128)S(1)}, u32[]{:S(2)}, u32[]{:S(2)}) collective-permute-start(f32[560,128]{1,0:T(8,128)S(1)} %get-tuple-element.33), channel_id=1, source_target_pairs={{0,12},{4,0},{8,4},{12,8},{1,13},{5,1},{9,5},{13,9},{2,14},{6,2},{... | collective-permute-start | bytes 860168 | tf_op jit(solution)/shard_map/ppermute | solution.py:12
  89.0 1.9 %collective-permute-start.17 = (f32[560,128]{1,0:T(8,128)S(1)}, f32[560,128]{1,0:T(8,128)}, u32[]{:S(2)}, u32[]{:S(2)}) collective-permute-start(f32[560,128]{1,0:T(8,128)S(1)} %get-tuple-element.32), channel_id=1, source_target_pairs={{0,8},{4,12},{8,0},{12,4},{1,9},{5,13},{9,1},{13,5},{2,10},{6,14},... | collective-permute-start | bytes 860168 | tf_op jit(solution)/shard_map/ppermute | solution.py:12
  91.0 1.4 %collective-permute-done.18 = f32[720,128]{1,0:T(8,128)S(1)} collective-permute-done((f32[720,128]{1,0:T(8,128)S(1)}, f32[720,128]{1,0:T(8,128)S(1)}, u32[]{:S(2)}, u32[]{:S(2)}) %collective-permute-start.18) | collective-permute-done | bytes 368672 | tf_op jit(solution)/shard_map/ppermute | solution.py:20
  92.4 0.2 fusion.31
  92.5 3.5 %collective-permute-done.15 = f32[560,128]{1,0:T(8,128)S(1)} collective-permute-done((f32[560,128]{1,0:T(8,128)S(1)}, f32[560,128]{1,0:T(8,128)S(1)}, u32[]{:S(2)}, u32[]{:S(2)}) %collective-permute-start.15) | collective-permute-done | bytes 286752 | tf_op jit(solution)/shard_map/ppermute | solution.py:12
  96.0 5.7 %collective-permute-done.16 = f32[560,128]{1,0:T(8,128)S(1)} collective-permute-done((f32[560,128]{1,0:T(8,128)S(1)}, f32[560,128]{1,0:T(8,128)S(1)}, u32[]{:S(2)}, u32[]{:S(2)}) %collective-permute-start.16) | collective-permute-done | bytes 286752 | tf_op jit(solution)/shard_map/ppermute | solution.py:12
  101.8 1.7 %collective-permute-done.17 = f32[560,128]{1,0:T(8,128)} collective-permute-done((f32[560,128]{1,0:T(8,128)S(1)}, f32[560,128]{1,0:T(8,128)}, u32[]{:S(2)}, u32[]{:S(2)}) %collective-permute-start.17) | collective-permute-done | bytes 286752 | tf_op jit(solution)/shard_map/ppermute | solution.py:12
  103.4 1.1 add_add_fusion
  104.5 0.1 fusion.35
  104.7 1.8 %collective-permute-start.19 = (f32[280,128]{1,0:T(8,128)S(1)}, f32[280,128]{1,0:T(8,128)S(1)}, u32[]{:S(2)}, u32[]{:S(2)}) collective-permute-start(f32[280,128]{1,0:T(8,128)S(1)} %pad_maximum_fusion.3), channel_id=1, source_target_pairs={{0,2},{2,0},{1,3},{3,1},{4,6},{6,4},{5,7},{7,5},{8,10},{10,8},{9,1... | collective-permute-start | bytes 430088 | tf_op jit(solution)/shard_map/ppermute | solution.py:20
  106.6 1.0 iota_compare_fusion
  107.5 2.5 %collective-permute-done.19 = f32[280,128]{1,0:T(8,128)S(1)} collective-permute-done((f32[280,128]{1,0:T(8,128)S(1)}, f32[280,128]{1,0:T(8,128)S(1)}, u32[]{:S(2)}, u32[]{:S(2)}) %collective-permute-start.19) | collective-permute-done | bytes 143392 | tf_op jit(solution)/shard_map/ppermute | solution.py:20
  110.1 0.6 fusion.3
  110.7 1.3 %fusion.8 = bf16[64,1280]{1,0:T(8,128)(2,1)} fusion(f32[64,1280]{1,0:T(8,128)S(1)} %fusion.3, bf16[720,64]{1,0:T(8,128)(2,1)S(1)} %fusion.31, pred[1280,1280]{1,0:T(8,128)(4,1)S(1)} %iota_compare_fusion), kind=kOutput, calls=%fused_computation.9 | convolution fusion | flops 118128640 | bytes 1597440 | tf_op jit(solution)/shard_map/dot_general | solution.py:109
  (59 shorter events, 1.5 us)
Async XLA Ops:
  0.0 18.7 %collective-permute-start.2 = (bf16[80,2048]{1,0:T(8,128)(2,1)}, bf16[80,2048]{1,0:T(8,128)(2,1)S(1)}, u32[]{:S(2)}, u32[]{:S(2)}) collective-permute-start(bf16[80,2048]{1,0:T(8,128)(2,1)} %param.2), channel_id=1, source_target_pairs={{0,16},{16,32},{32,48},{48,0},{1,17},{17,33},{33,49},{49,1},{2,18}... | collective-permute-start | bytes 983048 | tf_op jit(solution)/shard_map/ppermute | solution.py:12
  4.5 18.4 %collective-permute-start = (bf16[80,2048]{1,0:T(8,128)(2,1)}, bf16[80,2048]{1,0:T(8,128)(2,1)S(1)}, u32[]{:S(2)}, u32[]{:S(2)}) collective-permute-start(bf16[80,2048]{1,0:T(8,128)(2,1)} %param.2), channel_id=1, source_target_pairs={{0,48},{16,0},{32,16},{48,32},{1,49},{17,1},{33,17},{49,33},{2,50}... | collective-permute-start | bytes 983048 | tf_op jit(solution)/shard_map/ppermute | solution.py:12
  4.5 21.8 %collective-permute-start.4 = (bf16[80,2048]{1,0:T(8,128)(2,1)}, bf16[80,2048]{1,0:T(8,128)(2,1)S(1)}, u32[]{:S(2)}, u32[]{:S(2)}) collective-permute-start(bf16[80,2048]{1,0:T(8,128)(2,1)} %param.2), channel_id=1, source_target_pairs={{0,64},{64,128},{128,192},{192,0},{1,65},{65,129},{129,193},{193,1... | collective-permute-start | bytes 983048 | tf_op jit(solution)/shard_map/ppermute | solution.py:12
  6.0 20.3 %collective-permute-start.6 = (bf16[80,2048]{1,0:T(8,128)(2,1)}, bf16[80,2048]{1,0:T(8,128)(2,1)S(1)}, u32[]{:S(2)}, u32[]{:S(2)}) collective-permute-start(bf16[80,2048]{1,0:T(8,128)(2,1)} %param.2), channel_id=1, source_target_pairs={{0,192},{64,0},{128,64},{192,128},{1,193},{65,1},{129,65},{193,129... | collective-permute-start | bytes 983048 | tf_op jit(solution)/shard_map/ppermute | solution.py:12
  7.7 7.1 %copy-start.3 = (bf16[80,2048]{1,0:T(8,128)(2,1)S(1)}, bf16[80,2048]{1,0:T(8,128)(2,1)}, u32[]{:S(2)}) copy-start(bf16[80,2048]{1,0:T(8,128)(2,1)} %param.2) | copy-start | bytes 983044
  14.8 29.3 %copy-start.4 = (bf16[2048,1024]{0,1:T(8,128)(2,1)}, bf16[2048,1024]{0,1:T(8,128)(2,1)S(1)}, u32[]{:S(2)}) copy-start(bf16[2048,1024]{0,1:T(8,128)(2,1)S(1)} %convert_bitcast_fusion) | copy-start | bytes 12582916
  22.9 17.0 %collective-permute-start.5 = (bf16[160,2048]{1,0:T(8,128)(2,1)S(1)}, bf16[160,2048]{1,0:T(8,128)(2,1)S(1)}, u32[]{:S(2)}, u32[]{:S(2)}) collective-permute-start(bf16[160,2048]{1,0:T(8,128)(2,1)S(1)} %constant_dynamic-update-slice_fusion), channel_id=1, source_target_pairs={{0,64},{64,128},{128,192},{192,0},{1,65},{65,129},{129,193},{193,1... | collective-permute-start | bytes 1966088 | tf_op jit(solution)/shard_map/ppermute | solution.py:12
  24.5 15.6 %collective-permute-start.7 = (bf16[160,2048]{1,0:T(8,128)(2,1)S(1)}, bf16[160,2048]{1,0:T(8,128)(2,1)S(1)}, u32[]{:S(2)}, u32[]{:S(2)}) collective-permute-start(bf16[160,2048]{1,0:T(8,128)(2,1)S(1)} %constant_dynamic-update-slice_fusion), channel_id=1, source_target_pairs={{0,192},{64,0},{128,64},{192,128},{1,193},{65,1},{129,65},{193,129... | collective-permute-start | bytes 1966088 | tf_op jit(solution)/shard_map/ppermute | solution.py:12
  26.3 5.8 %copy-start = (bf16[80,2048]{1,0:T(8,128)(2,1)}, bf16[80,2048]{1,0:T(8,128)(2,1)S(1)}, u32[]{:S(2)}) copy-start(bf16[80,2048]{1,0:T(8,128)(2,1)S(1)} %collective-permute-done.4) | copy-start | bytes 983044
  26.3 5.8 %copy-start.1 = (bf16[80,2048]{1,0:T(8,128)(2,1)}, bf16[80,2048]{1,0:T(8,128)(2,1)S(1)}, u32[]{:S(2)}) copy-start(bf16[80,2048]{1,0:T(8,128)(2,1)S(1)} %collective-permute-done.6) | copy-start | bytes 983044
  27.5 16.7 %collective-permute-start.8 = (f32[400,512]{1,0:T(8,128)S(1)}, f32[400,512]{1,0:T(8,128)S(1)}, u32[]{:S(2)}, u32[]{:S(2)}) collective-permute-start(f32[400,512]{1,0:T(8,128)S(1)} %fusion.17), channel_id=1, source_target_pairs={{0,1},{1,0},{2,3},{3,2},{4,5},{5,4},{6,7},{7,6},{8,9},{9,8},{10,11... | collective-permute-start | bytes 2457608 | tf_op jit(solution)/shard_map/ppermute | solution.py:20
  27.6 12.6 %collective-permute-start.1 = (bf16[40,2048]{1,0:T(8,128)(2,1)S(1)}, bf16[40,2048]{1,0:T(8,128)(2,1)S(1)}, u32[]{:S(2)}, u32[]{:S(2)}) collective-permute-start(bf16[40,2048]{1,0:T(8,128)(2,1)S(1)} %slice.79), channel_id=1, source_target_pairs={{0,48},{16,0},{32,16},{48,32},{1,49},{17,1},{33,17},{49,33},{2,50}... | collective-permute-start | bytes 491528 | tf_op jit(solution)/shard_map/ppermute | solution.py:12
  27.7 12.5 %collective-permute-start.3 = (bf16[40,2048]{1,0:T(8,128)(2,1)S(1)}, bf16[40,2048]{1,0:T(8,128)(2,1)S(1)}, u32[]{:S(2)}, u32[]{:S(2)}) collective-permute-start(bf16[40,2048]{1,0:T(8,128)(2,1)S(1)} %slice.80), channel_id=1, source_target_pairs={{0,16},{16,32},{32,48},{48,0},{1,17},{17,33},{33,49},{49,1},{2,18}... | collective-permute-start | bytes 491528 | tf_op jit(solution)/shard_map/ppermute | solution.py:12
  40.0 0.9 slice-start
  40.0 1.0 slice-start.1
  40.2 4.0 %copy-start.2 = (bf16[320,2048]{1,0:T(8,128)(2,1)}, bf16[320,2048]{1,0:T(8,128)(2,1)S(1)}, u32[]{:S(2)}) copy-start(bf16[320,2048]{1,0:T(8,128)(2,1)S(1)} %constant_dynamic-update-slice_fusion.6) | copy-start | bytes 3932164
  45.2 3.2 %collective-permute-start.11 = (f32[320,512]{1,0:T(8,128)}, f32[320,512]{1,0:T(8,128)}, u32[]{:S(2)}, u32[]{:S(2)}) collective-permute-start(f32[320,512]{1,0:T(8,128)} %fusion.15), channel_id=1, source_target_pairs={{0,1},{1,0},{2,3},{3,2},{4,5},{5,4},{6,7},{7,6},{8,9},{9,8},{10,11... | collective-permute-start | bytes 1966088 | tf_op jit(solution)/shard_map/ppermute | solution.py:20
  45.4 20.8 %collective-permute-start.10 = (bf16[200,2048]{1,0:T(8,128)(2,1)}, bf16[200,2048]{1,0:T(8,128)(2,1)S(1)}, u32[]{:S(2)}, u32[]{:S(2)}) collective-permute-start(bf16[200,2048]{1,0:T(8,128)(2,1)} %get-tuple-element.22), channel_id=1, source_target_pairs={{0,192},{64,0},{128,64},{192,128},{1,193},{65,1},{129,65},{193,129... | collective-permute-start | bytes 2457608 | tf_op jit(solution)/shard_map/ppermute | solution.py:12
  47.7 21.6 %collective-permute-start.9 = (bf16[200,2048]{1,0:T(8,128)(2,1)}, bf16[200,2048]{1,0:T(8,128)(2,1)S(1)}, u32[]{:S(2)}, u32[]{:S(2)}) collective-permute-start(bf16[200,2048]{1,0:T(8,128)(2,1)} %get-tuple-element.21), channel_id=1, source_target_pairs={{0,64},{64,128},{128,192},{192,0},{1,65},{65,129},{129,193},{193,1... | collective-permute-start | bytes 2457608 | tf_op jit(solution)/shard_map/ppermute | solution.py:12
  52.6 24.7 %all-to-all-start = ((f32[4,720,128]{2,1,0:T(8,128)}), f32[4,720,128]{2,1,0:T(8,128)S(1)}, u32[]{:S(2)}, u32[]{:S(2)}) async-start(f32[4,720,128]{2,1,0:T(8,128)} %bitcast_bitcast_fusion), calls=%async_computation | async-start | bytes 2949120 | tf_op jit(solution)/shard_map/all_to_all | solution.py:41
  69.4 6.6 %collective-permute-start.12 = (bf16[40,2048]{1,0:T(8,128)(2,1)S(1)}, bf16[40,2048]{1,0:T(8,128)(2,1)S(1)}, u32[]{:S(2)}, u32[]{:S(2)}) collective-permute-start(bf16[40,2048]{1,0:T(8,128)(2,1)S(1)} %slice.68), channel_id=1, source_target_pairs={{0,64},{64,128},{128,192},{192,0},{1,65},{65,129},{129,193},{193,1... | collective-permute-start | bytes 491528 | tf_op jit(solution)/shard_map/ppermute | solution.py:12
  69.5 7.2 %collective-permute-start.13 = (bf16[40,2048]{1,0:T(8,128)(2,1)S(1)}, bf16[40,2048]{1,0:T(8,128)(2,1)S(1)}, u32[]{:S(2)}, u32[]{:S(2)}) collective-permute-start(bf16[40,2048]{1,0:T(8,128)(2,1)S(1)} %slice.69), channel_id=1, source_target_pairs={{0,192},{64,0},{128,64},{192,128},{1,193},{65,1},{129,65},{193,129... | collective-permute-start | bytes 491528 | tf_op jit(solution)/shard_map/ppermute | solution.py:12
  81.1 4.1 %collective-permute-start.14 = (f32[560,512]{1,0:T(8,128)S(1)}, f32[560,512]{1,0:T(8,128)S(1)}, u32[]{:S(2)}, u32[]{:S(2)}) collective-permute-start(f32[560,512]{1,0:T(8,128)S(1)} %fusion.13), channel_id=1, source_target_pairs={{0,1},{1,0},{2,3},{3,2},{4,5},{5,4},{6,7},{7,6},{8,9},{9,8},{10,11... | collective-permute-start | bytes 3440648 | tf_op jit(solution)/shard_map/ppermute | solution.py:20
  81.4 10.9 %collective-permute-start.18 = (f32[720,128]{1,0:T(8,128)S(1)}, f32[720,128]{1,0:T(8,128)S(1)}, u32[]{:S(2)}, u32[]{:S(2)}) collective-permute-start(f32[720,128]{1,0:T(8,128)S(1)} %reduce_sum.9), channel_id=1, source_target_pairs={{0,2},{2,0},{1,3},{3,1},{4,6},{6,4},{5,7},{7,5},{8,10},{10,8},{9,1... | collective-permute-start | bytes 1105928 | tf_op jit(solution)/shard_map/ppermute | solution.py:20
  85.6 10.4 %collective-permute-start.15 = (f32[560,128]{1,0:T(8,128)S(1)}, f32[560,128]{1,0:T(8,128)S(1)}, u32[]{:S(2)}, u32[]{:S(2)}) collective-permute-start(f32[560,128]{1,0:T(8,128)S(1)} %get-tuple-element.31), channel_id=1, source_target_pairs={{0,4},{4,8},{8,12},{12,0},{1,5},{5,9},{9,13},{13,1},{2,6},{6,10},{... | collective-permute-start | bytes 860168 | tf_op jit(solution)/shard_map/ppermute | solution.py:12
  87.3 14.5 %collective-permute-start.16 = (f32[560,128]{1,0:T(8,128)S(1)}, f32[560,128]{1,0:T(8,128)S(1)}, u32[]{:S(2)}, u32[]{:S(2)}) collective-permute-start(f32[560,128]{1,0:T(8,128)S(1)} %get-tuple-element.33), channel_id=1, source_target_pairs={{0,12},{4,0},{8,4},{12,8},{1,13},{5,1},{9,5},{13,9},{2,14},{6,2},{... | collective-permute-start | bytes 860168 | tf_op jit(solution)/shard_map/ppermute | solution.py:12
  89.0 14.4 %collective-permute-start.17 = (f32[560,128]{1,0:T(8,128)S(1)}, f32[560,128]{1,0:T(8,128)}, u32[]{:S(2)}, u32[]{:S(2)}) collective-permute-start(f32[560,128]{1,0:T(8,128)S(1)} %get-tuple-element.32), channel_id=1, source_target_pairs={{0,8},{4,12},{8,0},{12,4},{1,9},{5,13},{9,1},{13,5},{2,10},{6,14},... | collective-permute-start | bytes 860168 | tf_op jit(solution)/shard_map/ppermute | solution.py:12
  104.7 5.3 %collective-permute-start.19 = (f32[280,128]{1,0:T(8,128)S(1)}, f32[280,128]{1,0:T(8,128)S(1)}, u32[]{:S(2)}, u32[]{:S(2)}) collective-permute-start(f32[280,128]{1,0:T(8,128)S(1)} %pad_maximum_fusion.3), channel_id=1, source_target_pairs={{0,2},{2,0},{1,3},{3,1},{4,6},{6,4},{5,7},{7,5},{8,10},{10,8},{9,1... | collective-permute-start | bytes 430088 | tf_op jit(solution)/shard_map/ppermute | solution.py:20

commit v12 on v11

--- a/solution.py
+++ b/solution.py
@@ -73,15 +73,10 @@
     far = joined(shift(zp[:40], "zh", 4, -1), shift(zm[40:], "zh", 4, 1))
     early = paired(joined(own, *lax.optimization_barrier((own_xm, own_xp, side))))
 
-    late_rows = joined(side_xm, side_xp)
-    after_xm, after_xp, early, away = lax.optimization_barrier(
-        (
-            joined(far, own_xm[40:], side_xm[80:]),
-            joined(far, own_xp[:40], side_xp[:80]),
-            early,
-            dot(late_rows, theirs),
-        )
-    )
+    late_rows = joined(side_xm, side_xp, far)
+    away = dot(late_rows, theirs)
+    after_xm = joined(far, own_xm[40:], side_xm[80:])
+    after_xp = joined(far, own_xp[:40], side_xp[:80])
     from_xm, from_xp = shift(after_xm, "x", 4, 1), shift(after_xp, "x", 4, -1)
     late = dot(late_rows, mine) + swap(away, "core")
     early = over_y(joined(early, late))
@@ -89,7 +84,7 @@
     last_xm = shift(from_xm[40:80], "x", 4, 1)
     last_xp = shift(from_xp[:40], "x", 4, -1)
     rows, early = lax.optimization_barrier(
-        (joined(far, from_xm, from_xp, last_xm, last_xp), early)
+        (joined(from_xm, from_xp, last_xm, last_xp), early)
     )
     away = swap(dot(rows, theirs), "core")
     kept = lax.optimization_barrier(dot(rows, mine))
@@ -97,8 +92,8 @@
     sums = [early, over_zl_folded(last)]
     sites = [
         [block(0, 0), block(-1, 0), block(1, 0), block(0, -1), block(0, 1)],
-        [block(-1, -1), block(-1, 1), block(1, -1), block(1, 1)],
-        [block(0, 2), block(-1, 2), block(2, 0, 40, 40), block(2, 1)],
+        [block(-1, -1), block(-1, 1), block(1, -1), block(1, 1), block(0, 2)],
+        [block(-1, 2), block(2, 0, 40, 40), block(2, 1)],
         [block(1, 2), block(2, 0, 0, 40), block(2, -1)],
         [block(2, 2, 40, 40), block(2, 2, 0, 40)],
     ]
@@ -108,7 +103,7 @@
     def put(some, where):
         return lax.dot_general(some, where, (((0,), (0,)), ((), ())), preferred_element_type=F32)
 
-    turned = put(sums[0], place[:720]) + put(sums[1], place[720:])
+    turned = put(sums[0], place[:800]) + put(sums[1], place[800:])
     return turned.astype(BF16)
 
 

time: 112 us -> 108 us (0.964)
  local copies, waits for them, and re-layouts: 6.26 us -> 2.32 us
  matrix products: 23.1 us -> 20.8 us
  other arithmetic: 5.36 us -> 7.18 us
    unnamed x20 -> x15, local copies, waits for them, and re-layouts: 4.16 us -> 0.22 us
    dot_general x7, matrix products: 21.3 us -> 18.7 us  [dot(): return jnp.dot(left, right, preferred_element_type=F32)]
    ppermute x15, waiting for transfers between devices: 39.7 us -> 37.2 us  [shift(): lax.ppermute(value, axis, [(i, (i + by) % size) for i in range(size)])]
    concatenate x1 -> x2, other arithmetic: 1.42 us -> 3.83 us  [joined(): return jnp.concatenate(parts, axis=0)]
    ppermute x5, waiting for transfers between devices: 3.83 us -> 5.88 us  [swap(): return lax.ppermute(value, axis, [(0, 1), (1, 0)])]
  transfers between devices with their start and end apart: 21 -> 21, of which waited for: 11 -> 12; matrix products, arithmetic and copies ran while one was open for 23% -> 21% of each run, Pallas kernels for 0% -> 0%
where the time goes in v12:
time: 108 us; the launch traced here: 107 us
  waiting for transfers between devices  43.7 us (40%)
  starting transfers between devices  33.1 us (31%)
  matrix products  20.8 us (19%)
  other arithmetic  7.18 us (7%)
  local copies, waits for them, and re-layouts  2.32 us (2%)
    ppermute x15, waiting for transfers between devices, shift(): lax.ppermute(value, axis, [(i, (i + by) % size) for i in range(size)])  37.2 us
    ppermute x15, starting transfers between devices, shift(): lax.ppermute(value, axis, [(i, (i + by) % size) for i in range(size)])  26.5 us
    dot_general x7, matrix products, dot(): return jnp.dot(left, right, preferred_element_type=F32)  18.7 us
    ppermute x5, waiting for transfers between devices, swap(): return lax.ppermute(value, axis, [(0, 1), (1, 0)])  5.88 us
    all_to_all x1, starting transfers between devices, over_y(): lax.all_to_all(split, 'y', split_axis=0, concat_axis=0, tiled=True)  4.46 us
    concatenate x2, other arithmetic, joined(): return jnp.concatenate(parts, axis=0)  3.83 us
  transfers between devices with their start and end apart: 21, of which 12 were waited for; matrix products, arithmetic and copies ran while one was open for 21% of the time, Pallas kernels for 0%

profile of v12, /device:TPU:64, one launch (start us, length us, event | category | flops | bytes accessed | tf_op | source)
XLA Modules:
  0.0 107.5 jit_solution(5563415031005791949)
XLA Ops:
  0.0 4.5 %collective-permute-start.2 = (bf16[80,2048]{1,0:T(8,128)(2,1)}, bf16[80,2048]{1,0:T(8,128)(2,1)S(1)}, u32[]{:S(2)}, u32[]{:S(2)}) collective-permute-start(bf16[80,2048]{1,0:T(8,128)(2,1)} %param.2), channel_id=1, source_target_pairs={{0,16},{16,32},{32,48},{48,0},{1,17},{17,33},{33,49},{49,1},{2,18}... | collective-permute-start | bytes 983048 | tf_op jit(solution)/shard_map/ppermute | solution.py:12
  4.5 1.5 %collective-permute-start.4 = (bf16[80,2048]{1,0:T(8,128)(2,1)}, bf16[80,2048]{1,0:T(8,128)(2,1)S(1)}, u32[]{:S(2)}, u32[]{:S(2)}) collective-permute-start(bf16[80,2048]{1,0:T(8,128)(2,1)} %param.2), channel_id=1, source_target_pairs={{0,64},{64,128},{128,192},{192,0},{1,65},{65,129},{129,193},{193,1... | collective-permute-start | bytes 983048 | tf_op jit(solution)/shard_map/ppermute | solution.py:12
  6.0 1.7 %collective-permute-start.7 = (bf16[80,2048]{1,0:T(8,128)(2,1)}, bf16[80,2048]{1,0:T(8,128)(2,1)S(1)}, u32[]{:S(2)}, u32[]{:S(2)}) collective-permute-start(bf16[80,2048]{1,0:T(8,128)(2,1)} %param.2), channel_id=1, source_target_pairs={{0,192},{64,0},{128,64},{192,128},{1,193},{65,1},{129,65},{193,129... | collective-permute-start | bytes 983048 | tf_op jit(solution)/shard_map/ppermute | solution.py:12
  7.7 7.1 %convert_bitcast_fusion = bf16[2048,1024]{0,1:T(8,128)(2,1)S(1)} fusion(bf16[2048,1024]{1,0:T(8,128)(2,1)} %param.3, s32[1024]{0:T(1024)S(1)} %and_add_fusion), kind=kOutput, calls=%fused_computation.1 | convolution fusion | flops 4299161600 | bytes 8392704 | tf_op jit(solution)/shard_map/dot_general | solution.py:24
  14.9 3.8 %collective-permute-done.2 = bf16[80,2048]{1,0:T(8,128)(2,1)S(1)} collective-permute-done((bf16[80,2048]{1,0:T(8,128)(2,1)}, bf16[80,2048]{1,0:T(8,128)(2,1)S(1)}, u32[]{:S(2)}, u32[]{:S(2)}) %collective-permute-start.2) | collective-permute-done | bytes 327712 | tf_op jit(solution)/shard_map/ppermute | solution.py:12
  18.7 4.2 %collective-permute-done = bf16[80,2048]{1,0:T(8,128)(2,1)S(1)} collective-permute-done((bf16[80,2048]{1,0:T(8,128)(2,1)}, bf16[80,2048]{1,0:T(8,128)(2,1)S(1)}, u32[]{:S(2)}, u32[]{:S(2)}) %collective-permute-start) | collective-permute-done | bytes 327712 | tf_op jit(solution)/shard_map/ppermute | solution.py:12
  22.9 1.6 %collective-permute-start.5 = (bf16[160,2048]{1,0:T(8,128)(2,1)S(1)}, bf16[160,2048]{1,0:T(8,128)(2,1)S(1)}, u32[]{:S(2)}, u32[]{:S(2)}) collective-permute-start(bf16[160,2048]{1,0:T(8,128)(2,1)S(1)} %constant_dynamic-update-slice_fusion), channel_id=1, source_target_pairs={{0,64},{64,128},{128,192},{192,0},{1,65},{65,129},{129,193},{193,1... | collective-permute-start | bytes 1966088 | tf_op jit(solution)/shard_map/ppermute | solution.py:12
  24.5 1.7 %collective-permute-start.8 = (bf16[160,2048]{1,0:T(8,128)(2,1)S(1)}, bf16[160,2048]{1,0:T(8,128)(2,1)S(1)}, u32[]{:S(2)}, u32[]{:S(2)}) collective-permute-start(bf16[160,2048]{1,0:T(8,128)(2,1)S(1)} %constant_dynamic-update-slice_fusion), channel_id=1, source_target_pairs={{0,192},{64,0},{128,64},{192,128},{1,193},{65,1},{129,65},{193,129... | collective-permute-start | bytes 1966088 | tf_op jit(solution)/shard_map/ppermute | solution.py:12
  26.4 4.2 %collective-permute-start.3 = (bf16[40,2048]{1,0:T(8,128)(2,1)S(1)}, bf16[40,2048]{1,0:T(8,128)(2,1)S(1)}, u32[]{:S(2)}, u32[]{:S(2)}) collective-permute-start(bf16[40,2048]{1,0:T(8,128)(2,1)S(1)} %slice.80), channel_id=1, source_target_pairs={{0,16},{16,32},{32,48},{48,0},{1,17},{17,33},{33,49},{49,1},{2,18}... | collective-permute-start | bytes 491528 | tf_op jit(solution)/shard_map/ppermute | solution.py:12
  30.7 1.1 fusion.15
  31.9 8.1 %collective-permute-done.5 = bf16[160,2048]{1,0:T(8,128)(2,1)S(1)} collective-permute-done((bf16[160,2048]{1,0:T(8,128)(2,1)S(1)}, bf16[160,2048]{1,0:T(8,128)(2,1)S(1)}, u32[]{:S(2)}, u32[]{:S(2)}) %collective-permute-start.5) | collective-permute-done | bytes 655392 | tf_op jit(solution)/shard_map/ppermute | solution.py:12
  40.2 1.1 fusion.17
  41.4 0.8 slice-done
  42.3 1.4 %pad_maximum_fusion.3 = (bf16[200,2048]{1,0:T(8,128)(2,1)}, bf16[200,2048]{1,0:T(8,128)(2,1)}) fusion(bf16[80,2048]{1,0:T(8,128)(2,1)S(1)} %slice.84, bf16[40,2048]{1,0:T(8,128)(2,1)S(1)} %slice.83, bf16[40,2048]{1,0:T(8,128)(2,1)S(1)} %collective-permute-done.3, bf16[40,2048]{1,0:T(8,128)(2,1)S(1)} %collective-permute-done.1, ...), kind=kLoop, calls=%fused_computation.30 | loop fusion | flops 5324800 | bytes 2949120 | tf_op jit(solution)/shard_map/concatenate | solution.py:28
  43.6 1.4 %collective-permute-start.6 = (bf16[200,2048]{1,0:T(8,128)(2,1)}, bf16[200,2048]{1,0:T(8,128)(2,1)S(1)}, u32[]{:S(2)}, u32[]{:S(2)}) collective-permute-start(bf16[200,2048]{1,0:T(8,128)(2,1)} %get-tuple-element.27), channel_id=1, source_target_pairs={{0,64},{64,128},{128,192},{192,0},{1,65},{65,129},{129,193},{193,1... | collective-permute-start | bytes 2457608 | tf_op jit(solution)/shard_map/ppermute | solution.py:12
  45.1 1.8 %collective-permute-start.9 = (bf16[200,2048]{1,0:T(8,128)(2,1)}, bf16[200,2048]{1,0:T(8,128)(2,1)S(1)}, u32[]{:S(2)}, u32[]{:S(2)}) collective-permute-start(bf16[200,2048]{1,0:T(8,128)(2,1)} %get-tuple-element.26), channel_id=1, source_target_pairs={{0,192},{64,0},{128,64},{192,128},{1,193},{65,1},{129,65},{193,129... | collective-permute-start | bytes 2457608 | tf_op jit(solution)/shard_map/ppermute | solution.py:12
  46.9 1.1 fusion.28
  48.0 1.1 %fusion.25 = f32[400,512]{1,0:T(8,128)S(1)} fusion(f32[400,512]{1,0:T(8,128)S(1)} %collective-permute-done.10, bf16[400,2048]{1,0:T(8,128)(2,1)S(1)} %constant_dynamic-update-slice_fusion.2, bf16[2048,1024]{0,1:T(8,128)(2,1)S(1)} %convert_bitcast_fusion), kind=kOutput, calls=%fused_computation.26 | convolution fusion | flops 839065600 | bytes 5373952 | tf_op jit(solution)/shard_map/dot_general | solution.py:24
  49.1 1.3 %bitcast_bitcast_fusion = f32[4,800,128]{2,1,0:T(8,128)} fusion(f32[400,512]{1,0:T(8,128)S(1)} %fusion.25, f32[400,512]{1,0:T(8,128)S(1)} %fusion.28), kind=kLoop, calls=%fused_computation.12 | loop fusion | flops 409600 | bytes 3276800 | tf_op jit(solution)/shard_map/transpose | solution.py:40
  50.3 4.5 %all-to-all-start = ((f32[4,800,128]{2,1,0:T(8,128)}), f32[4,800,128]{2,1,0:T(8,128)S(1)}, u32[]{:S(2)}, u32[]{:S(2)}) async-start(f32[4,800,128]{2,1,0:T(8,128)} %bitcast_bitcast_fusion), calls=%async_computation | async-start | bytes 3276800 | tf_op jit(solution)/shard_map/all_to_all | solution.py:41
  54.8 10.9 %collective-permute-done.6 = bf16[200,2048]{1,0:T(8,128)(2,1)S(1)} collective-permute-done((bf16[200,2048]{1,0:T(8,128)(2,1)}, bf16[200,2048]{1,0:T(8,128)(2,1)S(1)}, u32[]{:S(2)}, u32[]{:S(2)}) %collective-permute-start.6) | collective-permute-done | bytes 819232 | tf_op jit(solution)/shard_map/ppermute | solution.py:12
  65.7 1.2 %collective-permute-start.11 = (bf16[40,2048]{1,0:T(8,128)(2,1)S(1)}, bf16[40,2048]{1,0:T(8,128)(2,1)}, u32[]{:S(2)}, u32[]{:S(2)}) collective-permute-start(bf16[40,2048]{1,0:T(8,128)(2,1)S(1)} %slice.68), channel_id=1, source_target_pairs={{0,64},{64,128},{128,192},{192,0},{1,65},{65,129},{129,193},{193,1... | collective-permute-start | bytes 491528 | tf_op jit(solution)/shard_map/ppermute | solution.py:12
  66.9 0.7 slice.69
  67.6 2.1 %collective-permute-start.12 = (bf16[40,2048]{1,0:T(8,128)(2,1)}, bf16[40,2048]{1,0:T(8,128)(2,1)}, u32[]{:S(2)}, u32[]{:S(2)}) collective-permute-start(bf16[40,2048]{1,0:T(8,128)(2,1)} %slice.69), channel_id=1, source_target_pairs={{0,192},{64,0},{128,64},{192,128},{1,193},{65,1},{129,65},{193,129... | collective-permute-start | bytes 491528 | tf_op jit(solution)/shard_map/ppermute | solution.py:12
  69.7 3.2 %collective-permute-done.11 = bf16[40,2048]{1,0:T(8,128)(2,1)} collective-permute-done((bf16[40,2048]{1,0:T(8,128)(2,1)S(1)}, bf16[40,2048]{1,0:T(8,128)(2,1)}, u32[]{:S(2)}, u32[]{:S(2)}) %collective-permute-start.11) | collective-permute-done | bytes 163872 | tf_op jit(solution)/shard_map/ppermute | solution.py:12
  72.9 0.3 collective-permute-done.12
  73.2 2.5 %pad_maximum_fusion = bf16[480,2048]{1,0:T(8,128)(2,1)} fusion(bf16[40,2048]{1,0:T(8,128)(2,1)} %collective-permute-done.12, bf16[40,2048]{1,0:T(8,128)(2,1)} %collective-permute-done.11, bf16[200,2048]{1,0:T(8,128)(2,1)S(1)} %collective-permute-done.9, bf16[200,2048]{1,0:T(8,128)(2,1)S(1)} %collective-permute-done.6), kind=kLoop, calls=%fused_computation.11 | loop fusion | flops 7864320 | bytes 3932160 | tf_op jit(solution)/shard_map/concatenate | solution.py:28
  75.7 0.6 all-to-all-done
  76.3 0.1 reduce_sum.9
  76.4 4.5 %fusion.13 = f32[480,512]{1,0:T(8,128)} fusion(bf16[480,2048]{1,0:T(8,128)(2,1)} %pad_maximum_fusion, bf16[2048,1024]{0,1:T(8,128)(2,1)} %copy-done.3), kind=kOutput, calls=%fused_computation.14 | convolution fusion | flops 1006632960 | bytes 5046272 | tf_op jit(solution)/shard_map/dot_general | solution.py:24
  81.2 2.8 %fusion.19 = f32[480,512]{1,0:T(8,128)S(1)} fusion(bf16[480,2048]{1,0:T(8,128)(2,1)S(1)} %copy-done, bf16[2048,1024]{0,1:T(8,128)(2,1)} %copy-done.3), kind=kOutput, calls=%fused_computation.20 | convolution fusion | flops 1006632960 | bytes 5046272 | tf_op jit(solution)/shard_map/dot_general | solution.py:24
  84.0 0.2 add.342
  84.2 0.1 constant_dynamic-slice_fusion.2
  84.3 1.0 collective-permute-start.15
  85.4 2.3 %collective-permute-start.16 = (f32[480,128]{1,0:T(8,128)S(1)}, f32[480,128]{1,0:T(8,128)S(1)}, u32[]{:S(2)}, u32[]{:S(2)}) collective-permute-start(f32[480,128]{1,0:T(8,128)S(1)} %get-tuple-element.25), channel_id=1, source_target_pairs={{0,12},{4,0},{8,4},{12,8},{1,13},{5,1},{9,5},{13,9},{2,14},{6,2},{... | collective-permute-start | bytes 737288 | tf_op jit(solution)/shard_map/ppermute | solution.py:12
  87.6 1.4 %collective-permute-start.17 = (f32[480,128]{1,0:T(8,128)S(1)}, f32[480,128]{1,0:T(8,128)S(1)}, u32[]{:S(2)}, u32[]{:S(2)}) collective-permute-start(f32[480,128]{1,0:T(8,128)S(1)} %get-tuple-element.24), channel_id=1, source_target_pairs={{0,8},{4,12},{8,0},{12,4},{1,9},{5,13},{9,1},{13,5},{2,10},{6,14},... | collective-permute-start | bytes 737288 | tf_op jit(solution)/shard_map/ppermute | solution.py:12
  89.0 4.0 %collective-permute-done.18 = f32[800,128]{1,0:T(8,128)S(1)} collective-permute-done((f32[800,128]{1,0:T(8,128)S(1)}, f32[800,128]{1,0:T(8,128)S(1)}, u32[]{:S(2)}, u32[]{:S(2)}) %collective-permute-start.18) | collective-permute-done | bytes 409632 | tf_op jit(solution)/shard_map/ppermute | solution.py:20
  93.0 0.2 fusion.31
  93.2 0.8 collective-permute-done.15
  94.0 4.6 %collective-permute-done.16 = f32[480,128]{1,0:T(8,128)S(1)} collective-permute-done((f32[480,128]{1,0:T(8,128)S(1)}, f32[480,128]{1,0:T(8,128)S(1)}, u32[]{:S(2)}, u32[]{:S(2)}) %collective-permute-start.16) | collective-permute-done | bytes 245792 | tf_op jit(solution)/shard_map/ppermute | solution.py:12
  98.5 1.3 %collective-permute-done.17 = f32[480,128]{1,0:T(8,128)S(1)} collective-permute-done((f32[480,128]{1,0:T(8,128)S(1)}, f32[480,128]{1,0:T(8,128)S(1)}, u32[]{:S(2)}, u32[]{:S(2)}) %collective-permute-start.17) | collective-permute-done | bytes 245792 | tf_op jit(solution)/shard_map/ppermute | solution.py:12
  99.9 0.1 fusion.35
  100.1 0.1 pad_maximum_fusion.4
  100.2 1.8 %collective-permute-start.19 = (f32[240,128]{1,0:T(8,128)S(1)}, f32[240,128]{1,0:T(8,128)S(1)}, u32[]{:S(2)}, u32[]{:S(2)}) collective-permute-start(f32[240,128]{1,0:T(8,128)S(1)} %pad_maximum_fusion.4), channel_id=1, source_target_pairs={{0,2},{2,0},{1,3},{3,1},{4,6},{6,4},{5,7},{7,5},{8,10},{10,8},{9,1... | collective-permute-start | bytes 368648 | tf_op jit(solution)/shard_map/ppermute | solution.py:20
  102.0 1.4 %iota_compare_fusion = pred[1280,1280]{1,0:T(32,128)(4,1)S(1)} fusion(s32[1280]{0:T(1024)S(1)} %concatenate.41), kind=kLoop, calls=%fused_computation | loop fusion | flops 1638400 | bytes 1643520 | tf_op jit(solution)/shard_map/eq | solution.py:101
  103.4 1.8 %collective-permute-done.19 = f32[240,128]{1,0:T(8,128)S(1)} collective-permute-done((f32[240,128]{1,0:T(8,128)S(1)}, f32[240,128]{1,0:T(8,128)S(1)}, u32[]{:S(2)}, u32[]{:S(2)}) %collective-permute-start.19) | collective-permute-done | bytes 122912 | tf_op jit(solution)/shard_map/ppermute | solution.py:20
  105.3 0.6 fusion.3
  105.9 1.5 %fusion.8 = bf16[64,1280]{1,0:T(8,128)(2,1)} fusion(f32[64,1280]{1,0:T(8,128)S(1)} %fusion.3, bf16[800,64]{1,0:T(8,128)(2,1)S(1)} %fusion.31, pred[1280,1280]{1,0:T(32,128)(4,1)S(1)} %iota_compare_fusion), kind=kOutput, calls=%fused_computation.9 | convolution fusion | flops 131235840 | bytes 1720320 | tf_op jit(solution)/shard_map/dot_general | solution.py:104
  (53 shorter events, 1.1 us)
Async XLA Ops:
  0.0 18.7 %collective-permute-start.2 = (bf16[80,2048]{1,0:T(8,128)(2,1)}, bf16[80,2048]{1,0:T(8,128)(2,1)S(1)}, u32[]{:S(2)}, u32[]{:S(2)}) collective-permute-start(bf16[80,2048]{1,0:T(8,128)(2,1)} %param.2), channel_id=1, source_target_pairs={{0,16},{16,32},{32,48},{48,0},{1,17},{17,33},{33,49},{49,1},{2,18}... | collective-permute-start | bytes 983048 | tf_op jit(solution)/shard_map/ppermute | solution.py:12
  4.5 18.4 %collective-permute-start = (bf16[80,2048]{1,0:T(8,128)(2,1)}, bf16[80,2048]{1,0:T(8,128)(2,1)S(1)}, u32[]{:S(2)}, u32[]{:S(2)}) collective-permute-start(bf16[80,2048]{1,0:T(8,128)(2,1)} %param.2), channel_id=1, source_target_pairs={{0,48},{16,0},{32,16},{48,32},{1,49},{17,1},{33,17},{49,33},{2,50}... | collective-permute-start | bytes 983048 | tf_op jit(solution)/shard_map/ppermute | solution.py:12
  4.5 21.9 %collective-permute-start.4 = (bf16[80,2048]{1,0:T(8,128)(2,1)}, bf16[80,2048]{1,0:T(8,128)(2,1)S(1)}, u32[]{:S(2)}, u32[]{:S(2)}) collective-permute-start(bf16[80,2048]{1,0:T(8,128)(2,1)} %param.2), channel_id=1, source_target_pairs={{0,64},{64,128},{128,192},{192,0},{1,65},{65,129},{129,193},{193,1... | collective-permute-start | bytes 983048 | tf_op jit(solution)/shard_map/ppermute | solution.py:12
  6.0 24.6 %collective-permute-start.7 = (bf16[80,2048]{1,0:T(8,128)(2,1)}, bf16[80,2048]{1,0:T(8,128)(2,1)S(1)}, u32[]{:S(2)}, u32[]{:S(2)}) collective-permute-start(bf16[80,2048]{1,0:T(8,128)(2,1)} %param.2), channel_id=1, source_target_pairs={{0,192},{64,0},{128,64},{192,128},{1,193},{65,1},{129,65},{193,129... | collective-permute-start | bytes 983048 | tf_op jit(solution)/shard_map/ppermute | solution.py:12
  7.7 7.1 %copy-start.2 = (bf16[80,2048]{1,0:T(8,128)(2,1)S(1)}, bf16[80,2048]{1,0:T(8,128)(2,1)}, u32[]{:S(2)}) copy-start(bf16[80,2048]{1,0:T(8,128)(2,1)} %param.2) | copy-start | bytes 983044
  14.8 33.2 %copy-start.3 = (bf16[2048,1024]{0,1:T(8,128)(2,1)}, bf16[2048,1024]{0,1:T(8,128)(2,1)S(1)}, u32[]{:S(2)}) copy-start(bf16[2048,1024]{0,1:T(8,128)(2,1)S(1)} %convert_bitcast_fusion) | copy-start | bytes 12582916
  22.9 17.0 %collective-permute-start.5 = (bf16[160,2048]{1,0:T(8,128)(2,1)S(1)}, bf16[160,2048]{1,0:T(8,128)(2,1)S(1)}, u32[]{:S(2)}, u32[]{:S(2)}) collective-permute-start(bf16[160,2048]{1,0:T(8,128)(2,1)S(1)} %constant_dynamic-update-slice_fusion), channel_id=1, source_target_pairs={{0,64},{64,128},{128,192},{192,0},{1,65},{65,129},{129,193},{193,1... | collective-permute-start | bytes 1966088 | tf_op jit(solution)/shard_map/ppermute | solution.py:12
  24.5 15.5 %collective-permute-start.8 = (bf16[160,2048]{1,0:T(8,128)(2,1)S(1)}, bf16[160,2048]{1,0:T(8,128)(2,1)S(1)}, u32[]{:S(2)}, u32[]{:S(2)}) collective-permute-start(bf16[160,2048]{1,0:T(8,128)(2,1)S(1)} %constant_dynamic-update-slice_fusion), channel_id=1, source_target_pairs={{0,192},{64,0},{128,64},{192,128},{1,193},{65,1},{129,65},{193,129... | collective-permute-start | bytes 1966088 | tf_op jit(solution)/shard_map/ppermute | solution.py:12
  26.3 13.8 %collective-permute-start.1 = (bf16[40,2048]{1,0:T(8,128)(2,1)S(1)}, bf16[40,2048]{1,0:T(8,128)(2,1)S(1)}, u32[]{:S(2)}, u32[]{:S(2)}) collective-permute-start(bf16[40,2048]{1,0:T(8,128)(2,1)S(1)} %slice.79), channel_id=1, source_target_pairs={{0,48},{16,0},{32,16},{48,32},{1,49},{17,1},{33,17},{49,33},{2,50}... | collective-permute-start | bytes 491528 | tf_op jit(solution)/shard_map/ppermute | solution.py:12
  26.4 15.0 %copy-start.1 = (bf16[80,2048]{1,0:T(8,128)(2,1)}, bf16[80,2048]{1,0:T(8,128)(2,1)S(1)}, u32[]{:S(2)}) copy-start(bf16[80,2048]{1,0:T(8,128)(2,1)S(1)} %collective-permute-done.4) | copy-start | bytes 983044
  26.4 13.7 %collective-permute-start.3 = (bf16[40,2048]{1,0:T(8,128)(2,1)S(1)}, bf16[40,2048]{1,0:T(8,128)(2,1)S(1)}, u32[]{:S(2)}, u32[]{:S(2)}) collective-permute-start(bf16[40,2048]{1,0:T(8,128)(2,1)S(1)} %slice.80), channel_id=1, source_target_pairs={{0,16},{16,32},{32,48},{48,0},{1,17},{17,33},{33,49},{49,1},{2,18}... | collective-permute-start | bytes 491528 | tf_op jit(solution)/shard_map/ppermute | solution.py:12
  31.8 15.1 %collective-permute-start.13 = (f32[400,512]{1,0:T(8,128)S(1)}, f32[400,512]{1,0:T(8,128)S(1)}, u32[]{:S(2)}, u32[]{:S(2)}) collective-permute-start(f32[400,512]{1,0:T(8,128)S(1)} %fusion.15), channel_id=1, source_target_pairs={{0,1},{1,0},{2,3},{3,2},{4,5},{5,4},{6,7},{7,6},{8,9},{9,8},{10,11... | collective-permute-start | bytes 2457608 | tf_op jit(solution)/shard_map/ppermute | solution.py:20
  41.2 6.7 %collective-permute-start.10 = (f32[400,512]{1,0:T(8,128)S(1)}, f32[400,512]{1,0:T(8,128)S(1)}, u32[]{:S(2)}, u32[]{:S(2)}) collective-permute-start(f32[400,512]{1,0:T(8,128)S(1)} %fusion.17), channel_id=1, source_target_pairs={{0,1},{1,0},{2,3},{3,2},{4,5},{5,4},{6,7},{7,6},{8,9},{9,8},{10,11... | collective-permute-start | bytes 2457608 | tf_op jit(solution)/shard_map/ppermute | solution.py:20
  41.4 0.9 slice-start
  43.6 22.1 %collective-permute-start.6 = (bf16[200,2048]{1,0:T(8,128)(2,1)}, bf16[200,2048]{1,0:T(8,128)(2,1)S(1)}, u32[]{:S(2)}, u32[]{:S(2)}) collective-permute-start(bf16[200,2048]{1,0:T(8,128)(2,1)} %get-tuple-element.27), channel_id=1, source_target_pairs={{0,64},{64,128},{128,192},{192,0},{1,65},{65,129},{129,193},{193,1... | collective-permute-start | bytes 2457608 | tf_op jit(solution)/shard_map/ppermute | solution.py:12
  45.1 20.6 %collective-permute-start.9 = (bf16[200,2048]{1,0:T(8,128)(2,1)}, bf16[200,2048]{1,0:T(8,128)(2,1)S(1)}, u32[]{:S(2)}, u32[]{:S(2)}) collective-permute-start(bf16[200,2048]{1,0:T(8,128)(2,1)} %get-tuple-element.26), channel_id=1, source_target_pairs={{0,192},{64,0},{128,64},{192,128},{1,193},{65,1},{129,65},{193,129... | collective-permute-start | bytes 2457608 | tf_op jit(solution)/shard_map/ppermute | solution.py:12
  50.3 26.0 %all-to-all-start = ((f32[4,800,128]{2,1,0:T(8,128)}), f32[4,800,128]{2,1,0:T(8,128)S(1)}, u32[]{:S(2)}, u32[]{:S(2)}) async-start(f32[4,800,128]{2,1,0:T(8,128)} %bitcast_bitcast_fusion), calls=%async_computation | async-start | bytes 3276800 | tf_op jit(solution)/shard_map/all_to_all | solution.py:41
  65.7 7.2 %collective-permute-start.11 = (bf16[40,2048]{1,0:T(8,128)(2,1)S(1)}, bf16[40,2048]{1,0:T(8,128)(2,1)}, u32[]{:S(2)}, u32[]{:S(2)}) collective-permute-start(bf16[40,2048]{1,0:T(8,128)(2,1)S(1)} %slice.68), channel_id=1, source_target_pairs={{0,64},{64,128},{128,192},{192,0},{1,65},{65,129},{129,193},{193,1... | collective-permute-start | bytes 491528 | tf_op jit(solution)/shard_map/ppermute | solution.py:12
  67.6 5.6 %collective-permute-start.12 = (bf16[40,2048]{1,0:T(8,128)(2,1)}, bf16[40,2048]{1,0:T(8,128)(2,1)}, u32[]{:S(2)}, u32[]{:S(2)}) collective-permute-start(bf16[40,2048]{1,0:T(8,128)(2,1)} %slice.69), channel_id=1, source_target_pairs={{0,192},{64,0},{128,64},{192,128},{1,193},{65,1},{129,65},{193,129... | collective-permute-start | bytes 491528 | tf_op jit(solution)/shard_map/ppermute | solution.py:12
  76.4 4.7 %copy-start = (bf16[480,2048]{1,0:T(8,128)(2,1)S(1)}, bf16[480,2048]{1,0:T(8,128)(2,1)}, u32[]{:S(2)}) copy-start(bf16[480,2048]{1,0:T(8,128)(2,1)} %pad_maximum_fusion) | copy-start | bytes 5898244
  80.9 3.1 %collective-permute-start.14 = (f32[480,512]{1,0:T(8,128)}, f32[480,512]{1,0:T(8,128)S(1)}, u32[]{:S(2)}, u32[]{:S(2)}) collective-permute-start(f32[480,512]{1,0:T(8,128)} %fusion.13), channel_id=1, source_target_pairs={{0,1},{1,0},{2,3},{3,2},{4,5},{5,4},{6,7},{7,6},{8,9},{9,8},{10,11... | collective-permute-start | bytes 2949128 | tf_op jit(solution)/shard_map/ppermute | solution.py:20
  81.1 12.0 %collective-permute-start.18 = (f32[800,128]{1,0:T(8,128)S(1)}, f32[800,128]{1,0:T(8,128)S(1)}, u32[]{:S(2)}, u32[]{:S(2)}) collective-permute-start(f32[800,128]{1,0:T(8,128)S(1)} %reduce_sum.9), channel_id=1, source_target_pairs={{0,2},{2,0},{1,3},{3,1},{4,6},{6,4},{5,7},{7,5},{8,10},{10,8},{9,1... | collective-permute-start | bytes 1228808 | tf_op jit(solution)/shard_map/ppermute | solution.py:20
  84.3 9.6 %collective-permute-start.15 = (f32[480,128]{1,0:T(8,128)S(1)}, f32[480,128]{1,0:T(8,128)S(1)}, u32[]{:S(2)}, u32[]{:S(2)}) collective-permute-start(f32[480,128]{1,0:T(8,128)S(1)} %get-tuple-element.23), channel_id=1, source_target_pairs={{0,4},{4,8},{8,12},{12,0},{1,5},{5,9},{9,13},{13,1},{2,6},{6,10},{... | collective-permute-start | bytes 737288 | tf_op jit(solution)/shard_map/ppermute | solution.py:12
  85.4 13.2 %collective-permute-start.16 = (f32[480,128]{1,0:T(8,128)S(1)}, f32[480,128]{1,0:T(8,128)S(1)}, u32[]{:S(2)}, u32[]{:S(2)}) collective-permute-start(f32[480,128]{1,0:T(8,128)S(1)} %get-tuple-element.25), channel_id=1, source_target_pairs={{0,12},{4,0},{8,4},{12,8},{1,13},{5,1},{9,5},{13,9},{2,14},{6,2},{... | collective-permute-start | bytes 737288 | tf_op jit(solution)/shard_map/ppermute | solution.py:12
  87.6 12.2 %collective-permute-start.17 = (f32[480,128]{1,0:T(8,128)S(1)}, f32[480,128]{1,0:T(8,128)S(1)}, u32[]{:S(2)}, u32[]{:S(2)}) collective-permute-start(f32[480,128]{1,0:T(8,128)S(1)} %get-tuple-element.24), channel_id=1, source_target_pairs={{0,8},{4,12},{8,0},{12,4},{1,9},{5,13},{9,1},{13,5},{2,10},{6,14},... | collective-permute-start | bytes 737288 | tf_op jit(solution)/shard_map/ppermute | solution.py:12
  100.2 5.0 %collective-permute-start.19 = (f32[240,128]{1,0:T(8,128)S(1)}, f32[240,128]{1,0:T(8,128)S(1)}, u32[]{:S(2)}, u32[]{:S(2)}) collective-permute-start(f32[240,128]{1,0:T(8,128)S(1)} %pad_maximum_fusion.4), channel_id=1, source_target_pairs={{0,2},{2,0},{1,3},{3,1},{4,6},{6,4},{5,7},{7,5},{8,10},{10,8},{9,1... | collective-permute-start | bytes 368648 | tf_op jit(solution)/shard_map/ppermute | solution.py:20

commit v13 on v12

--- a/solution.py
+++ b/solution.py
@@ -81,12 +81,10 @@
     late = dot(late_rows, mine) + swap(away, "core")
     early = over_y(joined(early, late))
     from_xm, from_xp, late = lax.optimization_barrier((from_xm, from_xp, late))
-    last_xm = shift(from_xm[40:80], "x", 4, 1)
-    last_xp = shift(from_xp[:40], "x", 4, -1)
-    rows, early = lax.optimization_barrier(
-        (joined(from_xm, from_xp, last_xm, last_xp), early)
-    )
-    away = swap(dot(rows, theirs), "core")
+    opposite = shift(far, "x", 4, 2)
+    rows = joined(from_xm, from_xp, opposite)
+    away, early = lax.optimization_barrier((dot(rows, theirs), early))
+    away = swap(away, "core")
     kept = lax.optimization_barrier(dot(rows, mine))
     last, early = lax.optimization_barrier((over_y_at_once(kept + away), over_zl(early)))
     sums = [early, over_zl_folded(last)]
@@ -95,7 +93,7 @@
         [block(-1, -1), block(-1, 1), block(1, -1), block(1, 1), block(0, 2)],
         [block(-1, 2), block(2, 0, 40, 40), block(2, 1)],
         [block(1, 2), block(2, 0, 0, 40), block(2, -1)],
-        [block(2, 2, 40, 40), block(2, 2, 0, 40)],
+        [block(2, 2)],
     ]
     places = joined(*[p for ps in sites for p in ps])
     place = (places[:, None] == jnp.arange(1280)[None, :]).astype(BF16)

time: 108 us -> 107 us (level)
  matrix products: 20.8 us -> 24.1 us
  local copies, waits for them, and re-layouts: 2.32 us -> 5.36 us
  starting transfers between devices: 33.1 us -> 30.2 us
  other arithmetic: 7.18 us -> 4.58 us
  waiting for transfers between devices: 43.7 us -> 41.8 us
    ppermute x15 -> x14, waiting for transfers between devices: 37.2 us -> 32.7 us  [shift(): lax.ppermute(value, axis, [(i, (i + by) % size) for i in range(size)])]
    unnamed x15 -> x29, local copies, waits for them, and re-layouts: 0.22 us -> 3.93 us
    dot_general x7, matrix products: 18.7 us -> 22 us  [dot(): return jnp.dot(left, right, preferred_element_type=F32)]
    ppermute x15 -> x14, starting transfers between devices: 26.5 us -> 23.7 us  [shift(): lax.ppermute(value, axis, [(i, (i + by) % size) for i in range(size)])]
    concatenate x2, other arithmetic: 3.83 us -> 1.19 us  [joined(): return jnp.concatenate(parts, axis=0)]
    all_to_all x1, waiting for transfers between devices: 0.62 us -> 2.64 us  [over_y(): lax.all_to_all(split, 'y', split_axis=0, concat_axis=0, tiled=True)]
  transfers between devices with their start and end apart: 21 -> 20, of which waited for: 12 -> 9; matrix products, arithmetic and copies ran while one was open for 21% -> 27% of each run, Pallas kernels for 0% -> 0%
where the time goes in v13:
time: 107 us
  waiting for transfers between devices  41.8 us (39%)
  starting transfers between devices  30.2 us (28%)
  matrix products  24.1 us (23%)
  local copies, waits for them, and re-layouts  5.36 us (5%)
  other arithmetic  4.58 us (4%)
    ppermute x14, waiting for transfers between devices, shift(): lax.ppermute(value, axis, [(i, (i + by) % size) for i in range(size)])  32.7 us
    ppermute x14, starting transfers between devices, shift(): lax.ppermute(value, axis, [(i, (i + by) % size) for i in range(size)])  23.7 us
    dot_general x7, matrix products, dot(): return jnp.dot(left, right, preferred_element_type=F32)  22 us
    ppermute x5, waiting for transfers between devices, swap(): return lax.ppermute(value, axis, [(0, 1), (1, 0)])  6.44 us
    all_to_all x1, starting transfers between devices, over_y(): lax.all_to_all(split, 'y', split_axis=0, concat_axis=0, tiled=True)  4.46 us
    unnamed x29, local copies, waits for them, and re-layouts  3.93 us
    all_to_all x1, waiting for transfers between devices, over_y(): lax.all_to_all(split, 'y', split_axis=0, concat_axis=0, tiled=True)  2.64 us
  transfers between devices with their start and end apart: 20, of which 9 were waited for; matrix products, arithmetic and copies ran while one was open for 27% of the time, Pallas kernels for 0%

profile of v13, /device:TPU:64, one launch (start us, length us, event | category | flops | bytes accessed | tf_op | source)
XLA Modules:
  0.0 106.7 jit_solution(9355097908909681349)
XLA Ops:
  0.0 4.5 %collective-permute-start.2 = (bf16[80,2048]{1,0:T(8,128)(2,1)}, bf16[80,2048]{1,0:T(8,128)(2,1)S(1)}, u32[]{:S(2)}, u32[]{:S(2)}) collective-permute-start(bf16[80,2048]{1,0:T(8,128)(2,1)} %param.2), channel_id=1, source_target_pairs={{0,16},{16,32},{32,48},{48,0},{1,17},{17,33},{33,49},{49,1},{2,18}... | collective-permute-start | bytes 983048 | tf_op jit(solution)/shard_map/ppermute | solution.py:12
  4.5 1.5 %collective-permute-start.4 = (bf16[80,2048]{1,0:T(8,128)(2,1)}, bf16[80,2048]{1,0:T(8,128)(2,1)S(1)}, u32[]{:S(2)}, u32[]{:S(2)}) collective-permute-start(bf16[80,2048]{1,0:T(8,128)(2,1)} %param.2), channel_id=1, source_target_pairs={{0,64},{64,128},{128,192},{192,0},{1,65},{65,129},{129,193},{193,1... | collective-permute-start | bytes 983048 | tf_op jit(solution)/shard_map/ppermute | solution.py:12
  6.0 1.7 %collective-permute-start.7 = (bf16[80,2048]{1,0:T(8,128)(2,1)}, bf16[80,2048]{1,0:T(8,128)(2,1)S(1)}, u32[]{:S(2)}, u32[]{:S(2)}) collective-permute-start(bf16[80,2048]{1,0:T(8,128)(2,1)} %param.2), channel_id=1, source_target_pairs={{0,192},{64,0},{128,64},{192,128},{1,193},{65,1},{129,65},{193,129... | collective-permute-start | bytes 983048 | tf_op jit(solution)/shard_map/ppermute | solution.py:12
  7.7 8.4 %convert_bitcast_fusion = bf16[2048,1024]{0,1:T(8,128)(2,1)} fusion(bf16[2048,1024]{1,0:T(8,128)(2,1)} %param.3, s32[1024]{0:T(1024)S(1)} %and_add_fusion), kind=kOutput, calls=%fused_computation.1 | convolution fusion | flops 4299161600 | bytes 8392704 | tf_op jit(solution)/shard_map/dot_general | solution.py:24
  16.2 2.5 %collective-permute-done.2 = bf16[80,2048]{1,0:T(8,128)(2,1)S(1)} collective-permute-done((bf16[80,2048]{1,0:T(8,128)(2,1)}, bf16[80,2048]{1,0:T(8,128)(2,1)S(1)}, u32[]{:S(2)}, u32[]{:S(2)}) %collective-permute-start.2) | collective-permute-done | bytes 327712 | tf_op jit(solution)/shard_map/ppermute | solution.py:12
  18.7 4.2 %collective-permute-done = bf16[80,2048]{1,0:T(8,128)(2,1)S(1)} collective-permute-done((bf16[80,2048]{1,0:T(8,128)(2,1)}, bf16[80,2048]{1,0:T(8,128)(2,1)S(1)}, u32[]{:S(2)}, u32[]{:S(2)}) %collective-permute-start) | collective-permute-done | bytes 327712 | tf_op jit(solution)/shard_map/ppermute | solution.py:12
  22.9 1.6 %collective-permute-start.5 = (bf16[160,2048]{1,0:T(8,128)(2,1)S(1)}, bf16[160,2048]{1,0:T(8,128)(2,1)S(1)}, u32[]{:S(2)}, u32[]{:S(2)}) collective-permute-start(bf16[160,2048]{1,0:T(8,128)(2,1)S(1)} %constant_dynamic-update-slice_fusion), channel_id=1, source_target_pairs={{0,64},{64,128},{128,192},{192,0},{1,65},{65,129},{129,193},{193,1... | collective-permute-start | bytes 1966088 | tf_op jit(solution)/shard_map/ppermute | solution.py:12
  24.5 1.7 %collective-permute-start.8 = (bf16[160,2048]{1,0:T(8,128)(2,1)S(1)}, bf16[160,2048]{1,0:T(8,128)(2,1)S(1)}, u32[]{:S(2)}, u32[]{:S(2)}) collective-permute-start(bf16[160,2048]{1,0:T(8,128)(2,1)S(1)} %constant_dynamic-update-slice_fusion), channel_id=1, source_target_pairs={{0,192},{64,0},{128,64},{192,128},{1,193},{65,1},{129,65},{193,129... | collective-permute-start | bytes 1966088 | tf_op jit(solution)/shard_map/ppermute | solution.py:12
  26.4 4.2 %collective-permute-start.3 = (bf16[40,2048]{1,0:T(8,128)(2,1)S(1)}, bf16[40,2048]{1,0:T(8,128)(2,1)S(1)}, u32[]{:S(2)}, u32[]{:S(2)}) collective-permute-start(bf16[40,2048]{1,0:T(8,128)(2,1)S(1)} %slice.72), channel_id=1, source_target_pairs={{0,16},{16,32},{32,48},{48,0},{1,17},{17,33},{33,49},{49,1},{2,18}... | collective-permute-start | bytes 491528 | tf_op jit(solution)/shard_map/ppermute | solution.py:12
  30.7 2.0 %fusion.13 = f32[400,512]{1,0:T(8,128)} fusion(bf16[400,2048]{1,0:T(8,128)(2,1)S(1)} %constant_dynamic-update-slice_fusion.9, bf16[2048,1024]{0,1:T(8,128)(2,1)S(1)} %copy-done.7), kind=kOutput, calls=%fused_computation.13 | convolution fusion | flops 838860800 | bytes 4554752 | tf_op jit(solution)/shard_map/dot_general | solution.py:24
  32.7 7.2 %collective-permute-done.5 = bf16[160,2048]{1,0:T(8,128)(2,1)S(1)} collective-permute-done((bf16[160,2048]{1,0:T(8,128)(2,1)S(1)}, bf16[160,2048]{1,0:T(8,128)(2,1)S(1)}, u32[]{:S(2)}, u32[]{:S(2)}) %collective-permute-start.5) | collective-permute-done | bytes 655392 | tf_op jit(solution)/shard_map/ppermute | solution.py:12
  40.2 2.0 %fusion.17 = f32[400,512]{1,0:T(8,128)} fusion(bf16[400,2048]{1,0:T(8,128)(2,1)S(1)} %constant_dynamic-update-slice_fusion.2, bf16[2048,1024]{0,1:T(8,128)(2,1)S(1)} %copy-done.7), kind=kOutput, calls=%fused_computation.17 | convolution fusion | flops 838860800 | bytes 4554752 | tf_op jit(solution)/shard_map/dot_general | solution.py:24
  42.3 0.8 slice-done
  43.1 1.2 %pad_maximum_fusion.2 = (bf16[200,2048]{1,0:T(8,128)(2,1)S(1)}, bf16[200,2048]{1,0:T(8,128)(2,1)}) fusion(bf16[80,2048]{1,0:T(8,128)(2,1)S(1)} %slice.76, bf16[40,2048]{1,0:T(8,128)(2,1)S(1)} %slice.75, bf16[40,2048]{1,0:T(8,128)(2,1)S(1)} %collective-permute-done.3, bf16[40,2048]{1,0:T(8,128)(2,1)S(1)} %collective-permute-done.1, ...), kind=kLoop, calls=%fused_computation.29 | loop fusion | flops 5324800 | bytes 2949120 | tf_op jit(solution)/shard_map/concatenate | solution.py:28
  44.3 1.4 %collective-permute-start.6 = (bf16[200,2048]{1,0:T(8,128)(2,1)}, bf16[200,2048]{1,0:T(8,128)(2,1)}, u32[]{:S(2)}, u32[]{:S(2)}) collective-permute-start(bf16[200,2048]{1,0:T(8,128)(2,1)} %get-tuple-element.27), channel_id=1, source_target_pairs={{0,64},{64,128},{128,192},{192,0},{1,65},{65,129},{129,193},{193,1... | collective-permute-start | bytes 2457608 | tf_op jit(solution)/shard_map/ppermute | solution.py:12
  45.7 1.8 %collective-permute-start.9 = (bf16[200,2048]{1,0:T(8,128)(2,1)S(1)}, bf16[200,2048]{1,0:T(8,128)(2,1)}, u32[]{:S(2)}, u32[]{:S(2)}) collective-permute-start(bf16[200,2048]{1,0:T(8,128)(2,1)S(1)} %get-tuple-element.26), channel_id=1, source_target_pairs={{0,192},{64,0},{128,64},{192,128},{1,193},{65,1},{129,65},{193,129... | collective-permute-start | bytes 2457608 | tf_op jit(solution)/shard_map/ppermute | solution.py:12
  47.6 2.8 %fusion.28 = f32[400,512]{1,0:T(8,128)S(1)} fusion(f32[400,512]{1,0:T(8,128)} %collective-permute-done.12, bf16[400,2048]{1,0:T(8,128)(2,1)S(1)} %copy-done.6, bf16[2048,1024]{0,1:T(8,128)(2,1)} %convert_bitcast_fusion), kind=kOutput, calls=%fused_computation.26 | convolution fusion | flops 839065600 | bytes 5373952 | tf_op jit(solution)/shard_map/dot_general | solution.py:24
  50.4 2.2 %fusion.25 = f32[400,512]{1,0:T(8,128)S(1)} fusion(f32[400,512]{1,0:T(8,128)} %collective-permute-done.10, bf16[400,2048]{1,0:T(8,128)(2,1)S(1)} %copy-done.4, bf16[2048,1024]{0,1:T(8,128)(2,1)S(1)} %copy-done.8), kind=kOutput, calls=%fused_computation.25 | convolution fusion | flops 839065600 | bytes 5373952 | tf_op jit(solution)/shard_map/dot_general | solution.py:24
  52.6 1.3 %bitcast_bitcast_fusion = f32[4,800,128]{2,1,0:T(8,128)} fusion(f32[400,512]{1,0:T(8,128)S(1)} %fusion.25, f32[400,512]{1,0:T(8,128)S(1)} %fusion.28), kind=kLoop, calls=%fused_computation.11 | loop fusion | flops 409600 | bytes 3276800 | tf_op jit(solution)/shard_map/transpose | solution.py:40
  54.0 4.5 %all-to-all-start = ((f32[4,800,128]{2,1,0:T(8,128)}), f32[4,800,128]{2,1,0:T(8,128)S(1)}, u32[]{:S(2)}, u32[]{:S(2)}) async-start(f32[4,800,128]{2,1,0:T(8,128)} %bitcast_bitcast_fusion), calls=%async_computation | async-start | bytes 3276800 | tf_op jit(solution)/shard_map/all_to_all | solution.py:41
  58.4 1.9 %collective-permute-start.11 = (bf16[80,2048]{1,0:T(8,128)(2,1)S(1)}, bf16[80,2048]{1,0:T(8,128)(2,1)S(1)}, u32[]{:S(2)}, u32[]{:S(2)}) collective-permute-start(bf16[80,2048]{1,0:T(8,128)(2,1)S(1)} %pad_maximum_fusion.3), channel_id=1, source_target_pairs={{0,128},{64,192},{128,0},{192,64},{1,129},{65,193},{129,1},{193,65... | collective-permute-start | bytes 983048 | tf_op jit(solution)/shard_map/ppermute | solution.py:12
  60.3 6.1 %collective-permute-done.6 = bf16[200,2048]{1,0:T(8,128)(2,1)} collective-permute-done((bf16[200,2048]{1,0:T(8,128)(2,1)}, bf16[200,2048]{1,0:T(8,128)(2,1)}, u32[]{:S(2)}, u32[]{:S(2)}) %collective-permute-start.6) | collective-permute-done | bytes 819232 | tf_op jit(solution)/shard_map/ppermute | solution.py:12
  66.4 6.0 %collective-permute-done.9 = bf16[200,2048]{1,0:T(8,128)(2,1)} collective-permute-done((bf16[200,2048]{1,0:T(8,128)(2,1)S(1)}, bf16[200,2048]{1,0:T(8,128)(2,1)}, u32[]{:S(2)}, u32[]{:S(2)}) %collective-permute-start.9) | collective-permute-done | bytes 819232 | tf_op jit(solution)/shard_map/ppermute | solution.py:12
  72.4 1.2 %constant_dynamic-update-slice_fusion.8 = bf16[480,2048]{1,0:T(8,128)(2,1)S(1)} fusion(bf16[200,2048]{1,0:T(8,128)(2,1)} %collective-permute-done.6), kind=kLoop, calls=%fused_computation.45 | loop fusion | bytes 1638400
  73.6 1.2 %constant_dynamic-update-slice_fusion.7 = bf16[480,2048]{1,0:T(8,128)(2,1)S(1)} fusion(bf16[480,2048]{1,0:T(8,128)(2,1)S(1)} %constant_dynamic-update-slice_fusion.8, bf16[200,2048]{1,0:T(8,128)(2,1)} %collective-permute-done.9), kind=kLoop, calls=%fused_computation.44 | loop fusion | bytes 1638400
  74.9 1.3 %copy-done.1 = bf16[480,2048]{1,0:T(8,128)(2,1)} copy-done((bf16[480,2048]{1,0:T(8,128)(2,1)}, bf16[480,2048]{1,0:T(8,128)(2,1)S(1)}, u32[]{:S(2)}) %copy-start.1) | copy-done | bytes 1966104
  76.2 1.2 %fusion.15 = f32[480,512]{1,0:T(8,128)S(1)} fusion(bf16[480,2048]{1,0:T(8,128)(2,1)S(1)} %constant_dynamic-update-slice_fusion.6, bf16[2048,1024]{0,1:T(8,128)(2,1)S(1)} %copy-done.9), kind=kOutput, calls=%fused_computation.15 | convolution fusion | flops 1006632960 | bytes 5046272 | tf_op jit(solution)/shard_map/dot_general | solution.py:24
  77.4 2.6 %all-to-all-done = f32[4,800,128]{2,1,0:T(8,128)S(1)} async-done(((f32[4,800,128]{2,1,0:T(8,128)}), f32[4,800,128]{2,1,0:T(8,128)S(1)}, u32[]{:S(2)}, u32[]{:S(2)}) %all-to-all-start) | async-done | bytes 1638432 | tf_op jit(solution)/shard_map/all_to_all | solution.py:41
  80.1 0.1 reduce_sum.9
  80.2 0.1 collective-permute-start.13
  80.4 0.1 concatenate.44
  80.5 0.1 collective-permute-start.17
  80.6 3.4 %fusion.21 = f32[480,512]{1,0:T(8,128)S(1)} fusion(bf16[480,2048]{1,0:T(8,128)(2,1)} %copy-done.1, bf16[2048,1024]{0,1:T(8,128)(2,1)} %convert_bitcast_fusion), kind=kOutput, calls=%fused_computation.21 | convolution fusion | flops 1006632960 | bytes 5046272 | tf_op jit(solution)/shard_map/dot_general | solution.py:24
  84.1 0.2 add.328
  84.3 0.1 constant_dynamic-slice_fusion.2
  84.4 0.7 collective-permute-start.14
  85.0 2.7 %collective-permute-start.15 = (f32[480,128]{1,0:T(8,128)S(1)}, f32[480,128]{1,0:T(8,128)S(1)}, u32[]{:S(2)}, u32[]{:S(2)}) collective-permute-start(f32[480,128]{1,0:T(8,128)S(1)} %get-tuple-element.25), channel_id=1, source_target_pairs={{0,12},{4,0},{8,4},{12,8},{1,13},{5,1},{9,5},{13,9},{2,14},{6,2},{... | collective-permute-start | bytes 737288 | tf_op jit(solution)/shard_map/ppermute | solution.py:12
  87.7 4.7 %collective-permute-done.17 = f32[800,128]{1,0:T(8,128)S(1)} collective-permute-done((f32[800,128]{1,0:T(8,128)S(1)}, f32[800,128]{1,0:T(8,128)S(1)}, u32[]{:S(2)}, u32[]{:S(2)}) %collective-permute-start.17) | collective-permute-done | bytes 409632 | tf_op jit(solution)/shard_map/ppermute | solution.py:20
  92.4 0.2 fusion.31
  92.5 6.6 %collective-permute-done.14 = f32[480,128]{1,0:T(8,128)S(1)} collective-permute-done((f32[480,128]{1,0:T(8,128)S(1)}, f32[480,128]{1,0:T(8,128)S(1)}, u32[]{:S(2)}, u32[]{:S(2)}) %collective-permute-start.14) | collective-permute-done | bytes 245792 | tf_op jit(solution)/shard_map/ppermute | solution.py:12
  99.2 0.1 fusion.35
  99.4 0.1 pad_maximum_fusion.4
  99.5 1.8 %collective-permute-start.18 = (f32[240,128]{1,0:T(8,128)S(1)}, f32[240,128]{1,0:T(8,128)S(1)}, u32[]{:S(2)}, u32[]{:S(2)}) collective-permute-start(f32[240,128]{1,0:T(8,128)S(1)} %pad_maximum_fusion.4), channel_id=1, source_target_pairs={{0,2},{2,0},{1,3},{3,1},{4,6},{6,4},{5,7},{7,5},{8,10},{10,8},{9,1... | collective-permute-start | bytes 368648 | tf_op jit(solution)/shard_map/ppermute | solution.py:20
  101.3 1.4 %iota_compare_fusion = pred[1280,1280]{1,0:T(32,128)(4,1)S(1)} fusion(s32[1280]{0:T(1024)S(1)} %concatenate.44), kind=kLoop, calls=%fused_computation | loop fusion | flops 1638400 | bytes 1643520 | tf_op jit(solution)/shard_map/eq | solution.py:99
  102.7 1.8 %collective-permute-done.18 = f32[240,128]{1,0:T(8,128)S(1)} collective-permute-done((f32[240,128]{1,0:T(8,128)S(1)}, f32[240,128]{1,0:T(8,128)S(1)}, u32[]{:S(2)}, u32[]{:S(2)}) %collective-permute-start.18) | collective-permute-done | bytes 122912 | tf_op jit(solution)/shard_map/ppermute | solution.py:20
  104.5 0.1 fusion.36
  104.5 0.6 fusion.3
  105.1 1.5 %fusion.8 = bf16[64,1280]{1,0:T(8,128)(2,1)} fusion(f32[64,1280]{1,0:T(8,128)S(1)} %fusion.3, bf16[800,64]{1,0:T(8,128)(2,1)S(1)} %fusion.31, pred[1280,1280]{1,0:T(32,128)(4,1)S(1)} %iota_compare_fusion), kind=kOutput, calls=%fused_computation.9 | convolution fusion | flops 131235840 | bytes 1720320 | tf_op jit(solution)/shard_map/dot_general | solution.py:102
  (64 shorter events, 0.7 us)
Async XLA Ops:
  0.0 18.7 %collective-permute-start.2 = (bf16[80,2048]{1,0:T(8,128)(2,1)}, bf16[80,2048]{1,0:T(8,128)(2,1)S(1)}, u32[]{:S(2)}, u32[]{:S(2)}) collective-permute-start(bf16[80,2048]{1,0:T(8,128)(2,1)} %param.2), channel_id=1, source_target_pairs={{0,16},{16,32},{32,48},{48,0},{1,17},{17,33},{33,49},{49,1},{2,18}... | collective-permute-start | bytes 983048 | tf_op jit(solution)/shard_map/ppermute | solution.py:12
  4.5 18.4 %collective-permute-start = (bf16[80,2048]{1,0:T(8,128)(2,1)}, bf16[80,2048]{1,0:T(8,128)(2,1)S(1)}, u32[]{:S(2)}, u32[]{:S(2)}) collective-permute-start(bf16[80,2048]{1,0:T(8,128)(2,1)} %param.2), channel_id=1, source_target_pairs={{0,48},{16,0},{32,16},{48,32},{1,49},{17,1},{33,17},{49,33},{2,50}... | collective-permute-start | bytes 983048 | tf_op jit(solution)/shard_map/ppermute | solution.py:12
  4.5 21.9 %collective-permute-start.4 = (bf16[80,2048]{1,0:T(8,128)(2,1)}, bf16[80,2048]{1,0:T(8,128)(2,1)S(1)}, u32[]{:S(2)}, u32[]{:S(2)}) collective-permute-start(bf16[80,2048]{1,0:T(8,128)(2,1)} %param.2), channel_id=1, source_target_pairs={{0,64},{64,128},{128,192},{192,0},{1,65},{65,129},{129,193},{193,1... | collective-permute-start | bytes 983048 | tf_op jit(solution)/shard_map/ppermute | solution.py:12
  6.0 24.6 %collective-permute-start.7 = (bf16[80,2048]{1,0:T(8,128)(2,1)}, bf16[80,2048]{1,0:T(8,128)(2,1)S(1)}, u32[]{:S(2)}, u32[]{:S(2)}) collective-permute-start(bf16[80,2048]{1,0:T(8,128)(2,1)} %param.2), channel_id=1, source_target_pairs={{0,192},{64,0},{128,64},{192,128},{1,193},{65,1},{129,65},{193,129... | collective-permute-start | bytes 983048 | tf_op jit(solution)/shard_map/ppermute | solution.py:12
  7.7 8.4 %copy-start.2 = (bf16[80,2048]{1,0:T(8,128)(2,1)S(1)}, bf16[80,2048]{1,0:T(8,128)(2,1)}, u32[]{:S(2)}) copy-start(bf16[80,2048]{1,0:T(8,128)(2,1)} %param.2) | copy-start | bytes 983044
  18.7 12.0 %copy-start.7 = (bf16[2048,1024]{0,1:T(8,128)(2,1)S(1)}, bf16[2048,1024]{0,1:T(8,128)(2,1)}, u32[]{:S(2)}) copy-start(bf16[2048,1024]{0,1:T(8,128)(2,1)} %convert_bitcast_fusion) | copy-start | bytes 12582916
  22.9 17.0 %collective-permute-start.5 = (bf16[160,2048]{1,0:T(8,128)(2,1)S(1)}, bf16[160,2048]{1,0:T(8,128)(2,1)S(1)}, u32[]{:S(2)}, u32[]{:S(2)}) collective-permute-start(bf16[160,2048]{1,0:T(8,128)(2,1)S(1)} %constant_dynamic-update-slice_fusion), channel_id=1, source_target_pairs={{0,64},{64,128},{128,192},{192,0},{1,65},{65,129},{129,193},{193,1... | collective-permute-start | bytes 1966088 | tf_op jit(solution)/shard_map/ppermute | solution.py:12
  24.5 15.5 %collective-permute-start.8 = (bf16[160,2048]{1,0:T(8,128)(2,1)S(1)}, bf16[160,2048]{1,0:T(8,128)(2,1)S(1)}, u32[]{:S(2)}, u32[]{:S(2)}) collective-permute-start(bf16[160,2048]{1,0:T(8,128)(2,1)S(1)} %constant_dynamic-update-slice_fusion), channel_id=1, source_target_pairs={{0,192},{64,0},{128,64},{192,128},{1,193},{65,1},{129,65},{193,129... | collective-permute-start | bytes 1966088 | tf_op jit(solution)/shard_map/ppermute | solution.py:12
  26.3 13.8 %collective-permute-start.1 = (bf16[40,2048]{1,0:T(8,128)(2,1)S(1)}, bf16[40,2048]{1,0:T(8,128)(2,1)S(1)}, u32[]{:S(2)}, u32[]{:S(2)}) collective-permute-start(bf16[40,2048]{1,0:T(8,128)(2,1)S(1)} %slice.71), channel_id=1, source_target_pairs={{0,48},{16,0},{32,16},{48,32},{1,49},{17,1},{33,17},{49,33},{2,50}... | collective-permute-start | bytes 491528 | tf_op jit(solution)/shard_map/ppermute | solution.py:12
  26.4 15.8 %copy-start = (bf16[80,2048]{1,0:T(8,128)(2,1)}, bf16[80,2048]{1,0:T(8,128)(2,1)S(1)}, u32[]{:S(2)}) copy-start(bf16[80,2048]{1,0:T(8,128)(2,1)S(1)} %collective-permute-done.4) | copy-start | bytes 983044
  26.4 13.7 %collective-permute-start.3 = (bf16[40,2048]{1,0:T(8,128)(2,1)S(1)}, bf16[40,2048]{1,0:T(8,128)(2,1)S(1)}, u32[]{:S(2)}, u32[]{:S(2)}) collective-permute-start(bf16[40,2048]{1,0:T(8,128)(2,1)S(1)} %slice.72), channel_id=1, source_target_pairs={{0,16},{16,32},{32,48},{48,0},{1,17},{17,33},{33,49},{49,1},{2,18}... | collective-permute-start | bytes 491528 | tf_op jit(solution)/shard_map/ppermute | solution.py:12
  30.7 2.0 %copy-start.5 = (bf16[400,2048]{1,0:T(8,128)(2,1)}, bf16[400,2048]{1,0:T(8,128)(2,1)S(1)}, u32[]{:S(2)}) copy-start(bf16[400,2048]{1,0:T(8,128)(2,1)S(1)} %constant_dynamic-update-slice_fusion.9) | copy-start | bytes 4915204
  32.7 14.8 %collective-permute-start.12 = (f32[400,512]{1,0:T(8,128)}, f32[400,512]{1,0:T(8,128)}, u32[]{:S(2)}, u32[]{:S(2)}) collective-permute-start(f32[400,512]{1,0:T(8,128)} %fusion.13), channel_id=1, source_target_pairs={{0,1},{1,0},{2,3},{3,2},{4,5},{5,4},{6,7},{7,6},{8,9},{9,8},{10,11... | collective-permute-start | bytes 2457608 | tf_op jit(solution)/shard_map/ppermute | solution.py:20
  40.2 2.0 %copy-start.3 = (bf16[400,2048]{1,0:T(8,128)(2,1)}, bf16[400,2048]{1,0:T(8,128)(2,1)S(1)}, u32[]{:S(2)}) copy-start(bf16[400,2048]{1,0:T(8,128)(2,1)S(1)} %constant_dynamic-update-slice_fusion.2) | copy-start | bytes 4915204
  42.1 8.3 %collective-permute-start.10 = (f32[400,512]{1,0:T(8,128)}, f32[400,512]{1,0:T(8,128)}, u32[]{:S(2)}, u32[]{:S(2)}) collective-permute-start(f32[400,512]{1,0:T(8,128)} %fusion.17), channel_id=1, source_target_pairs={{0,1},{1,0},{2,3},{3,2},{4,5},{5,4},{6,7},{7,6},{8,9},{9,8},{10,11... | collective-permute-start | bytes 2457608 | tf_op jit(solution)/shard_map/ppermute | solution.py:20
  42.2 0.9 slice-start
  43.1 4.4 %copy-start.6 = (bf16[400,2048]{1,0:T(8,128)(2,1)S(1)}, bf16[400,2048]{1,0:T(8,128)(2,1)}, u32[]{:S(2)}) copy-start(bf16[400,2048]{1,0:T(8,128)(2,1)} %copy-done.5) | copy-start | bytes 4915204
  44.3 22.1 %collective-permute-start.6 = (bf16[200,2048]{1,0:T(8,128)(2,1)}, bf16[200,2048]{1,0:T(8,128)(2,1)}, u32[]{:S(2)}, u32[]{:S(2)}) collective-permute-start(bf16[200,2048]{1,0:T(8,128)(2,1)} %get-tuple-element.27), channel_id=1, source_target_pairs={{0,64},{64,128},{128,192},{192,0},{1,65},{65,129},{129,193},{193,1... | collective-permute-start | bytes 2457608 | tf_op jit(solution)/shard_map/ppermute | solution.py:12
  45.7 4.7 %copy-start.4 = (bf16[400,2048]{1,0:T(8,128)(2,1)S(1)}, bf16[400,2048]{1,0:T(8,128)(2,1)}, u32[]{:S(2)}) copy-start(bf16[400,2048]{1,0:T(8,128)(2,1)} %copy-done.3) | copy-start | bytes 4915204
  45.7 4.7 %copy-start.8 = (bf16[2048,1024]{0,1:T(8,128)(2,1)S(1)}, bf16[2048,1024]{0,1:T(8,128)(2,1)}, u32[]{:S(2)}) copy-start(bf16[2048,1024]{0,1:T(8,128)(2,1)} %convert_bitcast_fusion) | copy-start | bytes 12582916
  45.7 26.7 %collective-permute-start.9 = (bf16[200,2048]{1,0:T(8,128)(2,1)S(1)}, bf16[200,2048]{1,0:T(8,128)(2,1)}, u32[]{:S(2)}, u32[]{:S(2)}) collective-permute-start(bf16[200,2048]{1,0:T(8,128)(2,1)S(1)} %get-tuple-element.26), channel_id=1, source_target_pairs={{0,192},{64,0},{128,64},{192,128},{1,193},{65,1},{129,65},{193,129... | collective-permute-start | bytes 2457608 | tf_op jit(solution)/shard_map/ppermute | solution.py:12
  54.0 26.1 %all-to-all-start = ((f32[4,800,128]{2,1,0:T(8,128)}), f32[4,800,128]{2,1,0:T(8,128)S(1)}, u32[]{:S(2)}, u32[]{:S(2)}) async-start(f32[4,800,128]{2,1,0:T(8,128)} %bitcast_bitcast_fusion), calls=%async_computation | async-start | bytes 3276800 | tf_op jit(solution)/shard_map/all_to_all | solution.py:41
  58.4 17.8 %copy-start.9 = (bf16[2048,1024]{0,1:T(8,128)(2,1)S(1)}, bf16[2048,1024]{0,1:T(8,128)(2,1)}, u32[]{:S(2)}) copy-start(bf16[2048,1024]{0,1:T(8,128)(2,1)} %convert_bitcast_fusion) | copy-start | bytes 12582916
  58.4 16.4 %collective-permute-start.11 = (bf16[80,2048]{1,0:T(8,128)(2,1)S(1)}, bf16[80,2048]{1,0:T(8,128)(2,1)S(1)}, u32[]{:S(2)}, u32[]{:S(2)}) collective-permute-start(bf16[80,2048]{1,0:T(8,128)(2,1)S(1)} %pad_maximum_fusion.3), channel_id=1, source_target_pairs={{0,128},{64,192},{128,0},{192,64},{1,129},{65,193},{129,1},{193,65... | collective-permute-start | bytes 983048 | tf_op jit(solution)/shard_map/ppermute | solution.py:12
  74.9 1.3 %copy-start.1 = (bf16[480,2048]{1,0:T(8,128)(2,1)}, bf16[480,2048]{1,0:T(8,128)(2,1)S(1)}, u32[]{:S(2)}) copy-start(bf16[480,2048]{1,0:T(8,128)(2,1)S(1)} %constant_dynamic-update-slice_fusion.6) | copy-start | bytes 5898244
  80.2 3.9 %collective-permute-start.13 = (f32[480,512]{1,0:T(8,128)S(1)}, f32[480,512]{1,0:T(8,128)S(1)}, u32[]{:S(2)}, u32[]{:S(2)}) collective-permute-start(f32[480,512]{1,0:T(8,128)S(1)} %fusion.15), channel_id=1, source_target_pairs={{0,1},{1,0},{2,3},{3,2},{4,5},{5,4},{6,7},{7,6},{8,9},{9,8},{10,11... | collective-permute-start | bytes 2949128 | tf_op jit(solution)/shard_map/ppermute | solution.py:20
  80.5 11.8 %collective-permute-start.17 = (f32[800,128]{1,0:T(8,128)S(1)}, f32[800,128]{1,0:T(8,128)S(1)}, u32[]{:S(2)}, u32[]{:S(2)}) collective-permute-start(f32[800,128]{1,0:T(8,128)S(1)} %reduce_sum.9), channel_id=1, source_target_pairs={{0,2},{2,0},{1,3},{3,1},{4,6},{6,4},{5,7},{7,5},{8,10},{10,8},{9,1... | collective-permute-start | bytes 1228808 | tf_op jit(solution)/shard_map/ppermute | solution.py:20
  84.4 14.8 %collective-permute-start.14 = (f32[480,128]{1,0:T(8,128)S(1)}, f32[480,128]{1,0:T(8,128)S(1)}, u32[]{:S(2)}, u32[]{:S(2)}) collective-permute-start(f32[480,128]{1,0:T(8,128)S(1)} %get-tuple-element.23), channel_id=1, source_target_pairs={{0,4},{4,8},{8,12},{12,0},{1,5},{5,9},{9,13},{13,1},{2,6},{6,10},{... | collective-permute-start | bytes 737288 | tf_op jit(solution)/shard_map/ppermute | solution.py:12
  85.0 14.1 %collective-permute-start.15 = (f32[480,128]{1,0:T(8,128)S(1)}, f32[480,128]{1,0:T(8,128)S(1)}, u32[]{:S(2)}, u32[]{:S(2)}) collective-permute-start(f32[480,128]{1,0:T(8,128)S(1)} %get-tuple-element.25), channel_id=1, source_target_pairs={{0,12},{4,0},{8,4},{12,8},{1,13},{5,1},{9,5},{13,9},{2,14},{6,2},{... | collective-permute-start | bytes 737288 | tf_op jit(solution)/shard_map/ppermute | solution.py:12
  87.7 11.5 %collective-permute-start.16 = (f32[480,128]{1,0:T(8,128)S(1)}, f32[480,128]{1,0:T(8,128)S(1)}, u32[]{:S(2)}, u32[]{:S(2)}) collective-permute-start(f32[480,128]{1,0:T(8,128)S(1)} %get-tuple-element.24), channel_id=1, source_target_pairs={{0,8},{4,12},{8,0},{12,4},{1,9},{5,13},{9,1},{13,5},{2,10},{6,14},... | collective-permute-start | bytes 737288 | tf_op jit(solution)/shard_map/ppermute | solution.py:12
  99.5 5.0 %collective-permute-start.18 = (f32[240,128]{1,0:T(8,128)S(1)}, f32[240,128]{1,0:T(8,128)S(1)}, u32[]{:S(2)}, u32[]{:S(2)}) collective-permute-start(f32[240,128]{1,0:T(8,128)S(1)} %pad_maximum_fusion.4), channel_id=1, source_target_pairs={{0,2},{2,0},{1,3},{3,1},{4,6},{6,4},{5,7},{7,5},{8,10},{10,8},{9,1... | collective-permute-start | bytes 368648 | tf_op jit(solution)/shard_map/ppermute | solution.py:20

commit v14 on v13

--- a/solution.py
+++ b/solution.py
@@ -75,8 +75,8 @@
 
     late_rows = joined(side_xm, side_xp, far)
     away = dot(late_rows, theirs)
-    after_xm = joined(far, own_xm[40:], side_xm[80:])
-    after_xp = joined(far, own_xp[:40], side_xp[:80])
+    halves = lax.optimization_barrier((joined(far, own_xm[40:]), joined(far, own_xp[:40])))
+    after_xm, after_xp = joined(halves[0], side_xm[80:]), joined(halves[1], side_xp[:80])
     from_xm, from_xp = shift(after_xm, "x", 4, 1), shift(after_xp, "x", 4, -1)
     late = dot(late_rows, mine) + swap(away, "core")
     early = over_y(joined(early, late))

time: 107 us -> 111 us (1.037)
  waiting for transfers between devices: 41.8 us -> 47.3 us
  matrix products: 24.1 us -> 20.7 us
  starting transfers between devices: 30.2 us -> 32.2 us
    ppermute x14, waiting for transfers between devices: 32.7 us -> 42.9 us  [shift(): lax.ppermute(value, axis, [(i, (i + by) % size) for i in range(size)])]
    dot_general x7, matrix products: 22 us -> 18.6 us  [dot(): return jnp.dot(left, right, preferred_element_type=F32)]
    all_to_all x1, waiting for transfers between devices: 2.64 us -> 0.01 us  [over_y(): lax.all_to_all(split, 'y', split_axis=0, concat_axis=0, tiled=True)]
    ppermute x5, waiting for transfers between devices: 6.44 us -> 4.45 us  [swap(): return lax.ppermute(value, axis, [(0, 1), (1, 0)])]
    ppermute x14, starting transfers between devices: 23.7 us -> 25.4 us  [shift(): lax.ppermute(value, axis, [(i, (i + by) % size) for i in range(size)])]
    unnamed x29 -> x15, local copies, waits for them, and re-layouts: 3.93 us -> 3.29 us
  transfers between devices with their start and end apart: 20 -> 20, of which waited for: 9 -> 12; matrix products, arithmetic and copies ran while one was open for 27% -> 25% of each run, Pallas kernels for 0% -> 0%
where the time goes in v14:
time: 111 us
  waiting for transfers between devices  47.3 us (43%)
  starting transfers between devices  32.2 us (29%)
  matrix products  20.7 us (19%)
  other arithmetic  5.4 us (5%)
  local copies, waits for them, and re-layouts  4.62 us (4%)
    ppermute x14, waiting for transfers between devices, shift(): lax.ppermute(value, axis, [(i, (i + by) % size) for i in range(size)])  42.9 us
    ppermute x14, starting transfers between devices, shift(): lax.ppermute(value, axis, [(i, (i + by) % size) for i in range(size)])  25.4 us
    dot_general x7, matrix products, dot(): return jnp.dot(left, right, preferred_element_type=F32)  18.6 us
    all_to_all x1, starting transfers between devices, over_y(): lax.all_to_all(split, 'y', split_axis=0, concat_axis=0, tiled=True)  4.47 us
    ppermute x5, waiting for transfers between devices, swap(): return lax.ppermute(value, axis, [(0, 1), (1, 0)])  4.45 us
    unnamed x15, local copies, waits for them, and re-layouts  3.29 us
    ppermute x5, starting transfers between devices, swap(): return lax.ppermute(value, axis, [(0, 1), (1, 0)])  2.36 us
  transfers between devices with their start and end apart: 20, of which 12 were waited for; matrix products, arithmetic and copies ran while one was open for 25% of the time, Pallas kernels for 0%

profile of v14, /device:TPU:64, one launch (start us, length us, event | category | flops | bytes accessed | tf_op | source)
XLA Modules:
  0.0 110.8 jit_solution(2525137243356801412)
XLA Ops:
  0.0 4.5 %collective-permute-start.2 = (bf16[80,2048]{1,0:T(8,128)(2,1)}, bf16[80,2048]{1,0:T(8,128)(2,1)S(1)}, u32[]{:S(2)}, u32[]{:S(2)}) collective-permute-start(bf16[80,2048]{1,0:T(8,128)(2,1)} %param.2), channel_id=1, source_target_pairs={{0,16},{16,32},{32,48},{48,0},{1,17},{17,33},{33,49},{49,1},{2,18}... | collective-permute-start | bytes 983048 | tf_op jit(solution)/shard_map/ppermute | solution.py:12
  4.5 1.5 %collective-permute-start.4 = (bf16[80,2048]{1,0:T(8,128)(2,1)}, bf16[80,2048]{1,0:T(8,128)(2,1)S(1)}, u32[]{:S(2)}, u32[]{:S(2)}) collective-permute-start(bf16[80,2048]{1,0:T(8,128)(2,1)} %param.2), channel_id=1, source_target_pairs={{0,64},{64,128},{128,192},{192,0},{1,65},{65,129},{129,193},{193,1... | collective-permute-start | bytes 983048 | tf_op jit(solution)/shard_map/ppermute | solution.py:12
  6.0 1.7 %collective-permute-start.5 = (bf16[80,2048]{1,0:T(8,128)(2,1)}, bf16[80,2048]{1,0:T(8,128)(2,1)S(1)}, u32[]{:S(2)}, u32[]{:S(2)}) collective-permute-start(bf16[80,2048]{1,0:T(8,128)(2,1)} %param.2), channel_id=1, source_target_pairs={{0,192},{64,0},{128,64},{192,128},{1,193},{65,1},{129,65},{193,129... | collective-permute-start | bytes 983048 | tf_op jit(solution)/shard_map/ppermute | solution.py:12
  7.7 7.1 %convert_bitcast_fusion = bf16[2048,1024]{0,1:T(8,128)(2,1)S(1)} fusion(bf16[2048,1024]{1,0:T(8,128)(2,1)} %param.3, s32[1024]{0:T(1024)S(1)} %and_add_fusion), kind=kOutput, calls=%fused_computation.1 | convolution fusion | flops 4299161600 | bytes 8392704 | tf_op jit(solution)/shard_map/dot_general | solution.py:24
  14.9 3.8 %collective-permute-done.2 = bf16[80,2048]{1,0:T(8,128)(2,1)S(1)} collective-permute-done((bf16[80,2048]{1,0:T(8,128)(2,1)}, bf16[80,2048]{1,0:T(8,128)(2,1)S(1)}, u32[]{:S(2)}, u32[]{:S(2)}) %collective-permute-start.2) | collective-permute-done | bytes 327712 | tf_op jit(solution)/shard_map/ppermute | solution.py:12
  18.7 4.2 %collective-permute-done = bf16[80,2048]{1,0:T(8,128)(2,1)S(1)} collective-permute-done((bf16[80,2048]{1,0:T(8,128)(2,1)}, bf16[80,2048]{1,0:T(8,128)(2,1)S(1)}, u32[]{:S(2)}, u32[]{:S(2)}) %collective-permute-start) | collective-permute-done | bytes 327712 | tf_op jit(solution)/shard_map/ppermute | solution.py:12
  22.9 1.6 %collective-permute-start.6 = (bf16[160,2048]{1,0:T(8,128)(2,1)S(1)}, bf16[160,2048]{1,0:T(8,128)(2,1)S(1)}, u32[]{:S(2)}, u32[]{:S(2)}) collective-permute-start(bf16[160,2048]{1,0:T(8,128)(2,1)S(1)} %constant_dynamic-update-slice_fusion), channel_id=1, source_target_pairs={{0,64},{64,128},{128,192},{192,0},{1,65},{65,129},{129,193},{193,1... | collective-permute-start | bytes 1966088 | tf_op jit(solution)/shard_map/ppermute | solution.py:12
  24.5 1.7 %collective-permute-start.8 = (bf16[160,2048]{1,0:T(8,128)(2,1)S(1)}, bf16[160,2048]{1,0:T(8,128)(2,1)S(1)}, u32[]{:S(2)}, u32[]{:S(2)}) collective-permute-start(bf16[160,2048]{1,0:T(8,128)(2,1)S(1)} %constant_dynamic-update-slice_fusion), channel_id=1, source_target_pairs={{0,192},{64,0},{128,64},{192,128},{1,193},{65,1},{129,65},{193,129... | collective-permute-start | bytes 1966088 | tf_op jit(solution)/shard_map/ppermute | solution.py:12
  26.4 4.2 %collective-permute-start.3 = (bf16[40,2048]{1,0:T(8,128)(2,1)S(1)}, bf16[40,2048]{1,0:T(8,128)(2,1)S(1)}, u32[]{:S(2)}, u32[]{:S(2)}) collective-permute-start(bf16[40,2048]{1,0:T(8,128)(2,1)S(1)} %slice.72), channel_id=1, source_target_pairs={{0,16},{16,32},{32,48},{48,0},{1,17},{17,33},{33,49},{49,1},{2,18}... | collective-permute-start | bytes 491528 | tf_op jit(solution)/shard_map/ppermute | solution.py:12
  30.7 1.1 fusion.13
  31.9 2.0 %collective-permute-done.1 = bf16[40,2048]{1,0:T(8,128)(2,1)S(1)} collective-permute-done((bf16[40,2048]{1,0:T(8,128)(2,1)S(1)}, bf16[40,2048]{1,0:T(8,128)(2,1)S(1)}, u32[]{:S(2)}, u32[]{:S(2)}) %collective-permute-start.1) | collective-permute-done | bytes 163872 | tf_op jit(solution)/shard_map/ppermute | solution.py:12
  33.9 0.5 collective-permute-done.3
  34.5 5.5 %collective-permute-done.6 = bf16[160,2048]{1,0:T(8,128)(2,1)S(1)} collective-permute-done((bf16[160,2048]{1,0:T(8,128)(2,1)S(1)}, bf16[160,2048]{1,0:T(8,128)(2,1)S(1)}, u32[]{:S(2)}, u32[]{:S(2)}) %collective-permute-start.6) | collective-permute-done | bytes 655392 | tf_op jit(solution)/shard_map/ppermute | solution.py:12
  40.1 1.1 fusion.17
  41.2 0.3 collective-permute-start.10
  41.5 1.0 pad_maximum_fusion.1
  42.5 2.9 %collective-permute-start.9 = (bf16[200,2048]{1,0:T(8,128)(2,1)}, bf16[200,2048]{1,0:T(8,128)(2,1)S(1)}, u32[]{:S(2)}, u32[]{:S(2)}) collective-permute-start(bf16[200,2048]{1,0:T(8,128)(2,1)} %pad_maximum_fusion.1), channel_id=1, source_target_pairs={{0,192},{64,0},{128,64},{192,128},{1,193},{65,1},{129,65},{193,129... | collective-permute-start | bytes 2457608 | tf_op jit(solution)/shard_map/ppermute | solution.py:12
  45.4 1.0 pad_maximum_fusion
  46.4 1.1 fusion.28
  47.5 1.1 fusion.25
  48.5 1.3 %bitcast_bitcast_fusion = f32[4,800,128]{2,1,0:T(8,128)} fusion(f32[400,512]{1,0:T(8,128)S(1)} %fusion.25, f32[400,512]{1,0:T(8,128)S(1)} %fusion.28), kind=kLoop, calls=%fused_computation.11 | loop fusion | flops 409600 | bytes 3276800 | tf_op jit(solution)/shard_map/transpose | solution.py:40
  49.8 4.5 %all-to-all-start = ((f32[4,800,128]{2,1,0:T(8,128)}), f32[4,800,128]{2,1,0:T(8,128)S(1)}, u32[]{:S(2)}, u32[]{:S(2)}) async-start(f32[4,800,128]{2,1,0:T(8,128)} %bitcast_bitcast_fusion), calls=%async_computation | async-start | bytes 3276800 | tf_op jit(solution)/shard_map/all_to_all | solution.py:41
  54.3 1.9 %collective-permute-start.11 = (bf16[80,2048]{1,0:T(8,128)(2,1)S(1)}, bf16[80,2048]{1,0:T(8,128)(2,1)S(1)}, u32[]{:S(2)}, u32[]{:S(2)}) collective-permute-start(bf16[80,2048]{1,0:T(8,128)(2,1)S(1)} %pad_maximum_fusion.5), channel_id=1, source_target_pairs={{0,128},{64,192},{128,0},{192,64},{1,129},{65,193},{129,1},{193,65... | collective-permute-start | bytes 983048 | tf_op jit(solution)/shard_map/ppermute | solution.py:12
  56.2 14.7 %collective-permute-done.9 = bf16[200,2048]{1,0:T(8,128)(2,1)S(1)} collective-permute-done((bf16[200,2048]{1,0:T(8,128)(2,1)}, bf16[200,2048]{1,0:T(8,128)(2,1)S(1)}, u32[]{:S(2)}, u32[]{:S(2)}) %collective-permute-start.9) | collective-permute-done | bytes 819232 | tf_op jit(solution)/shard_map/ppermute | solution.py:12
  70.9 4.4 %collective-permute-done.7 = bf16[200,2048]{1,0:T(8,128)(2,1)} collective-permute-done((bf16[200,2048]{1,0:T(8,128)(2,1)}, bf16[200,2048]{1,0:T(8,128)(2,1)}, u32[]{:S(2)}, u32[]{:S(2)}) %collective-permute-start.7) | collective-permute-done | bytes 819232 | tf_op jit(solution)/shard_map/ppermute | solution.py:12
  75.3 2.1 %constant_dynamic-update-slice_fusion.8 = bf16[480,2048]{1,0:T(8,128)(2,1)} fusion(bf16[200,2048]{1,0:T(8,128)(2,1)} %collective-permute-done.7), kind=kLoop, calls=%fused_computation.47 | loop fusion | bytes 1638400
  77.4 1.0 constant_dynamic-update-slice_fusion.7
  78.4 0.7 constant_dynamic-update-slice_fusion.6
  79.1 3.8 %fusion.15 = f32[480,512]{1,0:T(8,128)} fusion(bf16[480,2048]{1,0:T(8,128)(2,1)} %constant_dynamic-update-slice_fusion.6, bf16[2048,1024]{0,1:T(8,128)(2,1)S(1)} %copy-done.2), kind=kOutput, calls=%fused_computation.15 | convolution fusion | flops 1006632960 | bytes 5046272 | tf_op jit(solution)/shard_map/dot_general | solution.py:24
  82.9 0.1 reduce_sum.9
  83.5 3.4 %fusion.21 = f32[480,512]{1,0:T(8,128)S(1)} fusion(bf16[480,2048]{1,0:T(8,128)(2,1)} %constant_dynamic-update-slice_fusion.6, bf16[2048,1024]{0,1:T(8,128)(2,1)} %copy-done.1), kind=kOutput, calls=%fused_computation.21 | convolution fusion | flops 1006632960 | bytes 5046272 | tf_op jit(solution)/shard_map/dot_general | solution.py:24
  86.9 0.2 add.328
  87.1 0.1 constant_dynamic-slice_fusion.2
  87.2 1.7 %collective-permute-start.14 = (f32[480,128]{1,0:T(8,128)S(1)}, f32[480,128]{1,0:T(8,128)S(1)}, u32[]{:S(2)}, u32[]{:S(2)}) collective-permute-start(f32[480,128]{1,0:T(8,128)S(1)} %get-tuple-element.27), channel_id=1, source_target_pairs={{0,4},{4,8},{8,12},{12,0},{1,5},{5,9},{9,13},{13,1},{2,6},{6,10},{... | collective-permute-start | bytes 737288 | tf_op jit(solution)/shard_map/ppermute | solution.py:12
  88.9 1.7 %collective-permute-start.15 = (f32[480,128]{1,0:T(8,128)S(1)}, f32[480,128]{1,0:T(8,128)S(1)}, u32[]{:S(2)}, u32[]{:S(2)}) collective-permute-start(f32[480,128]{1,0:T(8,128)S(1)} %get-tuple-element.29), channel_id=1, source_target_pairs={{0,12},{4,0},{8,4},{12,8},{1,13},{5,1},{9,5},{13,9},{2,14},{6,2},{... | collective-permute-start | bytes 737288 | tf_op jit(solution)/shard_map/ppermute | solution.py:12
  90.6 2.0 %collective-permute-start.16 = (f32[480,128]{1,0:T(8,128)S(1)}, f32[480,128]{1,0:T(8,128)S(1)}, u32[]{:S(2)}, u32[]{:S(2)}) collective-permute-start(f32[480,128]{1,0:T(8,128)S(1)} %get-tuple-element.28), channel_id=1, source_target_pairs={{0,8},{4,12},{8,0},{12,4},{1,9},{5,13},{9,1},{13,5},{2,10},{6,14},... | collective-permute-start | bytes 737288 | tf_op jit(solution)/shard_map/ppermute | solution.py:12
  92.6 2.7 %collective-permute-done.17 = f32[800,128]{1,0:T(8,128)S(1)} collective-permute-done((f32[800,128]{1,0:T(8,128)S(1)}, f32[800,128]{1,0:T(8,128)S(1)}, u32[]{:S(2)}, u32[]{:S(2)}) %collective-permute-start.17) | collective-permute-done | bytes 409632 | tf_op jit(solution)/shard_map/ppermute | solution.py:20
  95.2 0.2 fusion.31
  95.4 1.4 %collective-permute-done.14 = f32[480,128]{1,0:T(8,128)S(1)} collective-permute-done((f32[480,128]{1,0:T(8,128)S(1)}, f32[480,128]{1,0:T(8,128)S(1)}, u32[]{:S(2)}, u32[]{:S(2)}) %collective-permute-start.14) | collective-permute-done | bytes 245792 | tf_op jit(solution)/shard_map/ppermute | solution.py:12
  96.8 4.6 %collective-permute-done.15 = f32[480,128]{1,0:T(8,128)S(1)} collective-permute-done((f32[480,128]{1,0:T(8,128)S(1)}, f32[480,128]{1,0:T(8,128)S(1)}, u32[]{:S(2)}, u32[]{:S(2)}) %collective-permute-start.15) | collective-permute-done | bytes 245792 | tf_op jit(solution)/shard_map/ppermute | solution.py:12
  101.5 1.8 %collective-permute-done.16 = f32[480,128]{1,0:T(8,128)S(1)} collective-permute-done((f32[480,128]{1,0:T(8,128)S(1)}, f32[480,128]{1,0:T(8,128)S(1)}, u32[]{:S(2)}, u32[]{:S(2)}) %collective-permute-start.16) | collective-permute-done | bytes 245792 | tf_op jit(solution)/shard_map/ppermute | solution.py:12
  103.4 0.1 fusion.35
  103.5 0.1 pad_maximum_fusion.6
  103.6 1.8 %collective-permute-start.18 = (f32[240,128]{1,0:T(8,128)S(1)}, f32[240,128]{1,0:T(8,128)S(1)}, u32[]{:S(2)}, u32[]{:S(2)}) collective-permute-start(f32[240,128]{1,0:T(8,128)S(1)} %pad_maximum_fusion.6), channel_id=1, source_target_pairs={{0,2},{2,0},{1,3},{3,1},{4,6},{6,4},{5,7},{7,5},{8,10},{10,8},{9,1... | collective-permute-start | bytes 368648 | tf_op jit(solution)/shard_map/ppermute | solution.py:20
  105.4 1.4 %iota_compare_fusion = pred[1280,1280]{1,0:T(32,128)(4,1)S(1)} fusion(s32[1280]{0:T(1024)S(1)} %concatenate.52), kind=kLoop, calls=%fused_computation | loop fusion | flops 1638400 | bytes 1643520 | tf_op jit(solution)/shard_map/eq | solution.py:99
  106.8 1.8 %collective-permute-done.18 = f32[240,128]{1,0:T(8,128)S(1)} collective-permute-done((f32[240,128]{1,0:T(8,128)S(1)}, f32[240,128]{1,0:T(8,128)S(1)}, u32[]{:S(2)}, u32[]{:S(2)}) %collective-permute-start.18) | collective-permute-done | bytes 122912 | tf_op jit(solution)/shard_map/ppermute | solution.py:20
  108.7 0.6 fusion.3
  109.2 1.5 %fusion.8 = bf16[64,1280]{1,0:T(8,128)(2,1)} fusion(f32[64,1280]{1,0:T(8,128)S(1)} %fusion.3, bf16[800,64]{1,0:T(8,128)(2,1)S(1)} %fusion.31, pred[1280,1280]{1,0:T(32,128)(4,1)S(1)} %iota_compare_fusion), kind=kOutput, calls=%fused_computation.9 | convolution fusion | flops 131235840 | bytes 1720320 | tf_op jit(solution)/shard_map/dot_general | solution.py:102
  (51 shorter events, 1.2 us)
Async XLA Ops:
  0.0 18.7 %collective-permute-start.2 = (bf16[80,2048]{1,0:T(8,128)(2,1)}, bf16[80,2048]{1,0:T(8,128)(2,1)S(1)}, u32[]{:S(2)}, u32[]{:S(2)}) collective-permute-start(bf16[80,2048]{1,0:T(8,128)(2,1)} %param.2), channel_id=1, source_target_pairs={{0,16},{16,32},{32,48},{48,0},{1,17},{17,33},{33,49},{49,1},{2,18}... | collective-permute-start | bytes 983048 | tf_op jit(solution)/shard_map/ppermute | solution.py:12
  4.5 18.4 %collective-permute-start = (bf16[80,2048]{1,0:T(8,128)(2,1)}, bf16[80,2048]{1,0:T(8,128)(2,1)S(1)}, u32[]{:S(2)}, u32[]{:S(2)}) collective-permute-start(bf16[80,2048]{1,0:T(8,128)(2,1)} %param.2), channel_id=1, source_target_pairs={{0,48},{16,0},{32,16},{48,32},{1,49},{17,1},{33,17},{49,33},{2,50}... | collective-permute-start | bytes 983048 | tf_op jit(solution)/shard_map/ppermute | solution.py:12
  4.5 21.9 %collective-permute-start.4 = (bf16[80,2048]{1,0:T(8,128)(2,1)}, bf16[80,2048]{1,0:T(8,128)(2,1)S(1)}, u32[]{:S(2)}, u32[]{:S(2)}) collective-permute-start(bf16[80,2048]{1,0:T(8,128)(2,1)} %param.2), channel_id=1, source_target_pairs={{0,64},{64,128},{128,192},{192,0},{1,65},{65,129},{129,193},{193,1... | collective-permute-start | bytes 983048 | tf_op jit(solution)/shard_map/ppermute | solution.py:12
  6.0 24.6 %collective-permute-start.5 = (bf16[80,2048]{1,0:T(8,128)(2,1)}, bf16[80,2048]{1,0:T(8,128)(2,1)S(1)}, u32[]{:S(2)}, u32[]{:S(2)}) collective-permute-start(bf16[80,2048]{1,0:T(8,128)(2,1)} %param.2), channel_id=1, source_target_pairs={{0,192},{64,0},{128,64},{192,128},{1,193},{65,1},{129,65},{193,129... | collective-permute-start | bytes 983048 | tf_op jit(solution)/shard_map/ppermute | solution.py:12
  7.7 7.1 %copy-start = (bf16[80,2048]{1,0:T(8,128)(2,1)S(1)}, bf16[80,2048]{1,0:T(8,128)(2,1)}, u32[]{:S(2)}) copy-start(bf16[80,2048]{1,0:T(8,128)(2,1)} %param.2) | copy-start | bytes 983044
  14.8 32.6 %copy-start.1 = (bf16[2048,1024]{0,1:T(8,128)(2,1)}, bf16[2048,1024]{0,1:T(8,128)(2,1)S(1)}, u32[]{:S(2)}) copy-start(bf16[2048,1024]{0,1:T(8,128)(2,1)S(1)} %convert_bitcast_fusion) | copy-start | bytes 12582916
  22.9 17.0 %collective-permute-start.6 = (bf16[160,2048]{1,0:T(8,128)(2,1)S(1)}, bf16[160,2048]{1,0:T(8,128)(2,1)S(1)}, u32[]{:S(2)}, u32[]{:S(2)}) collective-permute-start(bf16[160,2048]{1,0:T(8,128)(2,1)S(1)} %constant_dynamic-update-slice_fusion), channel_id=1, source_target_pairs={{0,64},{64,128},{128,192},{192,0},{1,65},{65,129},{129,193},{193,1... | collective-permute-start | bytes 1966088 | tf_op jit(solution)/shard_map/ppermute | solution.py:12
  24.5 15.5 %collective-permute-start.8 = (bf16[160,2048]{1,0:T(8,128)(2,1)S(1)}, bf16[160,2048]{1,0:T(8,128)(2,1)S(1)}, u32[]{:S(2)}, u32[]{:S(2)}) collective-permute-start(bf16[160,2048]{1,0:T(8,128)(2,1)S(1)} %constant_dynamic-update-slice_fusion), channel_id=1, source_target_pairs={{0,192},{64,0},{128,64},{192,128},{1,193},{65,1},{129,65},{193,129... | collective-permute-start | bytes 1966088 | tf_op jit(solution)/shard_map/ppermute | solution.py:12
  26.3 7.6 %collective-permute-start.1 = (bf16[40,2048]{1,0:T(8,128)(2,1)S(1)}, bf16[40,2048]{1,0:T(8,128)(2,1)S(1)}, u32[]{:S(2)}, u32[]{:S(2)}) collective-permute-start(bf16[40,2048]{1,0:T(8,128)(2,1)S(1)} %slice.71), channel_id=1, source_target_pairs={{0,48},{16,0},{32,16},{48,32},{1,49},{17,1},{33,17},{49,33},{2,50}... | collective-permute-start | bytes 491528 | tf_op jit(solution)/shard_map/ppermute | solution.py:12
  26.4 8.0 %collective-permute-start.3 = (bf16[40,2048]{1,0:T(8,128)(2,1)S(1)}, bf16[40,2048]{1,0:T(8,128)(2,1)S(1)}, u32[]{:S(2)}, u32[]{:S(2)}) collective-permute-start(bf16[40,2048]{1,0:T(8,128)(2,1)S(1)} %slice.72), channel_id=1, source_target_pairs={{0,16},{16,32},{32,48},{48,0},{1,17},{17,33},{33,49},{49,1},{2,18}... | collective-permute-start | bytes 491528 | tf_op jit(solution)/shard_map/ppermute | solution.py:12
  31.8 14.6 %collective-permute-start.12 = (f32[400,512]{1,0:T(8,128)S(1)}, f32[400,512]{1,0:T(8,128)S(1)}, u32[]{:S(2)}, u32[]{:S(2)}) collective-permute-start(f32[400,512]{1,0:T(8,128)S(1)} %fusion.13), channel_id=1, source_target_pairs={{0,1},{1,0},{2,3},{3,2},{4,5},{5,4},{6,7},{7,6},{8,9},{9,8},{10,11... | collective-permute-start | bytes 2457608 | tf_op jit(solution)/shard_map/ppermute | solution.py:20
  41.2 6.2 %collective-permute-start.10 = (f32[400,512]{1,0:T(8,128)S(1)}, f32[400,512]{1,0:T(8,128)S(1)}, u32[]{:S(2)}, u32[]{:S(2)}) collective-permute-start(f32[400,512]{1,0:T(8,128)S(1)} %fusion.17), channel_id=1, source_target_pairs={{0,1},{1,0},{2,3},{3,2},{4,5},{5,4},{6,7},{7,6},{8,9},{9,8},{10,11... | collective-permute-start | bytes 2457608 | tf_op jit(solution)/shard_map/ppermute | solution.py:20
  42.5 28.4 %collective-permute-start.9 = (bf16[200,2048]{1,0:T(8,128)(2,1)}, bf16[200,2048]{1,0:T(8,128)(2,1)S(1)}, u32[]{:S(2)}, u32[]{:S(2)}) collective-permute-start(bf16[200,2048]{1,0:T(8,128)(2,1)} %pad_maximum_fusion.1), channel_id=1, source_target_pairs={{0,192},{64,0},{128,64},{192,128},{1,193},{65,1},{129,65},{193,129... | collective-permute-start | bytes 2457608 | tf_op jit(solution)/shard_map/ppermute | solution.py:12
  46.4 28.9 %collective-permute-start.7 = (bf16[200,2048]{1,0:T(8,128)(2,1)}, bf16[200,2048]{1,0:T(8,128)(2,1)}, u32[]{:S(2)}, u32[]{:S(2)}) collective-permute-start(bf16[200,2048]{1,0:T(8,128)(2,1)} %pad_maximum_fusion), channel_id=1, source_target_pairs={{0,64},{64,128},{128,192},{192,0},{1,65},{65,129},{129,193},{193,1... | collective-permute-start | bytes 2457608 | tf_op jit(solution)/shard_map/ppermute | solution.py:12
  49.8 33.1 %all-to-all-start = ((f32[4,800,128]{2,1,0:T(8,128)}), f32[4,800,128]{2,1,0:T(8,128)S(1)}, u32[]{:S(2)}, u32[]{:S(2)}) async-start(f32[4,800,128]{2,1,0:T(8,128)} %bitcast_bitcast_fusion), calls=%async_computation | async-start | bytes 3276800 | tf_op jit(solution)/shard_map/all_to_all | solution.py:41
  54.3 24.8 %copy-start.2 = (bf16[2048,1024]{0,1:T(8,128)(2,1)S(1)}, bf16[2048,1024]{0,1:T(8,128)(2,1)}, u32[]{:S(2)}) copy-start(bf16[2048,1024]{0,1:T(8,128)(2,1)} %copy-done.1) | copy-start | bytes 12582916
  54.3 24.0 %collective-permute-start.11 = (bf16[80,2048]{1,0:T(8,128)(2,1)S(1)}, bf16[80,2048]{1,0:T(8,128)(2,1)S(1)}, u32[]{:S(2)}, u32[]{:S(2)}) collective-permute-start(bf16[80,2048]{1,0:T(8,128)(2,1)S(1)} %pad_maximum_fusion.5), channel_id=1, source_target_pairs={{0,128},{64,192},{128,0},{192,64},{1,129},{65,193},{129,1},{193,65... | collective-permute-start | bytes 983048 | tf_op jit(solution)/shard_map/ppermute | solution.py:12
  83.0 3.9 %collective-permute-start.13 = (f32[480,512]{1,0:T(8,128)}, f32[480,512]{1,0:T(8,128)S(1)}, u32[]{:S(2)}, u32[]{:S(2)}) collective-permute-start(f32[480,512]{1,0:T(8,128)} %fusion.15), channel_id=1, source_target_pairs={{0,1},{1,0},{2,3},{3,2},{4,5},{5,4},{6,7},{7,6},{8,9},{9,8},{10,11... | collective-permute-start | bytes 2949128 | tf_op jit(solution)/shard_map/ppermute | solution.py:20
  83.4 11.8 %collective-permute-start.17 = (f32[800,128]{1,0:T(8,128)S(1)}, f32[800,128]{1,0:T(8,128)S(1)}, u32[]{:S(2)}, u32[]{:S(2)}) collective-permute-start(f32[800,128]{1,0:T(8,128)S(1)} %reduce_sum.9), channel_id=1, source_target_pairs={{0,2},{2,0},{1,3},{3,1},{4,6},{6,4},{5,7},{7,5},{8,10},{10,8},{9,1... | collective-permute-start | bytes 1228808 | tf_op jit(solution)/shard_map/ppermute | solution.py:20
  87.2 9.6 %collective-permute-start.14 = (f32[480,128]{1,0:T(8,128)S(1)}, f32[480,128]{1,0:T(8,128)S(1)}, u32[]{:S(2)}, u32[]{:S(2)}) collective-permute-start(f32[480,128]{1,0:T(8,128)S(1)} %get-tuple-element.27), channel_id=1, source_target_pairs={{0,4},{4,8},{8,12},{12,0},{1,5},{5,9},{9,13},{13,1},{2,6},{6,10},{... | collective-permute-start | bytes 737288 | tf_op jit(solution)/shard_map/ppermute | solution.py:12
  88.9 12.6 %collective-permute-start.15 = (f32[480,128]{1,0:T(8,128)S(1)}, f32[480,128]{1,0:T(8,128)S(1)}, u32[]{:S(2)}, u32[]{:S(2)}) collective-permute-start(f32[480,128]{1,0:T(8,128)S(1)} %get-tuple-element.29), channel_id=1, source_target_pairs={{0,12},{4,0},{8,4},{12,8},{1,13},{5,1},{9,5},{13,9},{2,14},{6,2},{... | collective-permute-start | bytes 737288 | tf_op jit(solution)/shard_map/ppermute | solution.py:12
  90.6 12.7 %collective-permute-start.16 = (f32[480,128]{1,0:T(8,128)S(1)}, f32[480,128]{1,0:T(8,128)S(1)}, u32[]{:S(2)}, u32[]{:S(2)}) collective-permute-start(f32[480,128]{1,0:T(8,128)S(1)} %get-tuple-element.28), channel_id=1, source_target_pairs={{0,8},{4,12},{8,0},{12,4},{1,9},{5,13},{9,1},{13,5},{2,10},{6,14},... | collective-permute-start | bytes 737288 | tf_op jit(solution)/shard_map/ppermute | solution.py:12
  103.6 5.0 %collective-permute-start.18 = (f32[240,128]{1,0:T(8,128)S(1)}, f32[240,128]{1,0:T(8,128)S(1)}, u32[]{:S(2)}, u32[]{:S(2)}) collective-permute-start(f32[240,128]{1,0:T(8,128)S(1)} %pad_maximum_fusion.6), channel_id=1, source_target_pairs={{0,2},{2,0},{1,3},{3,1},{4,6},{6,4},{5,7},{7,5},{8,10},{10,8},{9,1... | collective-permute-start | bytes 368648 | tf_op jit(solution)/shard_map/ppermute | solution.py:20

commit v15 on v12

--- a/solution.py
+++ b/solution.py
@@ -75,8 +75,8 @@
 
     late_rows = joined(side_xm, side_xp, far)
     away = dot(late_rows, theirs)
-    after_xm = joined(far, own_xm[40:], side_xm[80:])
-    after_xp = joined(far, own_xp[:40], side_xp[:80])
+    halves = lax.optimization_barrier((joined(far, own_xm[40:]), joined(far, own_xp[:40])))
+    after_xm, after_xp = joined(halves[0], side_xm[80:]), joined(halves[1], side_xp[:80])
     from_xm, from_xp = shift(after_xm, "x", 4, 1), shift(after_xp, "x", 4, -1)
     late = dot(late_rows, mine) + swap(away, "core")
     early = over_y(joined(early, late))

time: 108 us -> 110 us (1.019)
  waiting for transfers between devices: 43.7 us -> 45.6 us
    ppermute x15, waiting for transfers between devices: 37.2 us -> 40.3 us  [shift(): lax.ppermute(value, axis, [(i, (i + by) % size) for i in range(size)])]
    concatenate x2 -> x4, other arithmetic: 3.83 us -> 4.48 us  [joined(): return jnp.concatenate(parts, axis=0)]
  transfers between devices with their start and end apart: 21 -> 21, of which waited for: 12 -> 14; matrix products, arithmetic and copies ran while one was open for 21% -> 21% of each run, Pallas kernels for 0% -> 0%
where the time goes in v15:
time: 110 us; the launch traced here: 109 us
  waiting for transfers between devices  45.6 us (41%)
  starting transfers between devices  33.4 us (30%)
  matrix products  20.7 us (19%)
  other arithmetic  7.83 us (7%)
  local copies, waits for them, and re-layouts  1.5 us (1%)
    ppermute x15, waiting for transfers between devices, shift(): lax.ppermute(value, axis, [(i, (i + by) % size) for i in range(size)])  40.3 us
    ppermute x15, starting transfers between devices, shift(): lax.ppermute(value, axis, [(i, (i + by) % size) for i in range(size)])  26.8 us
    dot_general x7, matrix products, dot(): return jnp.dot(left, right, preferred_element_type=F32)  18.5 us
    ppermute x5, waiting for transfers between devices, swap(): return lax.ppermute(value, axis, [(0, 1), (1, 0)])  5.24 us
    concatenate x4, other arithmetic, joined(): return jnp.concatenate(parts, axis=0)  4.48 us
    all_to_all x1, starting transfers between devices, over_y(): lax.all_to_all(split, 'y', split_axis=0, concat_axis=0, tiled=True)  4.46 us
  transfers between devices with their start and end apart: 21, of which 14 were waited for; matrix products, arithmetic and copies ran while one was open for 21% of the time, Pallas kernels for 0%

profile of v15, /device:TPU:64, one launch (start us, length us, event | category | flops | bytes accessed | tf_op | source)
XLA Modules:
  0.0 109.3 jit_solution(5817656739367517696)
XLA Ops:
  0.0 4.5 %collective-permute-start.2 = (bf16[80,2048]{1,0:T(8,128)(2,1)}, bf16[80,2048]{1,0:T(8,128)(2,1)S(1)}, u32[]{:S(2)}, u32[]{:S(2)}) collective-permute-start(bf16[80,2048]{1,0:T(8,128)(2,1)} %param.2), channel_id=1, source_target_pairs={{0,16},{16,32},{32,48},{48,0},{1,17},{17,33},{33,49},{49,1},{2,18}... | collective-permute-start | bytes 983048 | tf_op jit(solution)/shard_map/ppermute | solution.py:12
  4.5 1.5 %collective-permute-start.4 = (bf16[80,2048]{1,0:T(8,128)(2,1)}, bf16[80,2048]{1,0:T(8,128)(2,1)S(1)}, u32[]{:S(2)}, u32[]{:S(2)}) collective-permute-start(bf16[80,2048]{1,0:T(8,128)(2,1)} %param.2), channel_id=1, source_target_pairs={{0,64},{64,128},{128,192},{192,0},{1,65},{65,129},{129,193},{193,1... | collective-permute-start | bytes 983048 | tf_op jit(solution)/shard_map/ppermute | solution.py:12
  6.0 1.7 %collective-permute-start.5 = (bf16[80,2048]{1,0:T(8,128)(2,1)}, bf16[80,2048]{1,0:T(8,128)(2,1)S(1)}, u32[]{:S(2)}, u32[]{:S(2)}) collective-permute-start(bf16[80,2048]{1,0:T(8,128)(2,1)} %param.2), channel_id=1, source_target_pairs={{0,192},{64,0},{128,64},{192,128},{1,193},{65,1},{129,65},{193,129... | collective-permute-start | bytes 983048 | tf_op jit(solution)/shard_map/ppermute | solution.py:12
  7.7 7.1 %convert_bitcast_fusion = bf16[2048,1024]{0,1:T(8,128)(2,1)S(1)} fusion(bf16[2048,1024]{1,0:T(8,128)(2,1)} %param.3, s32[1024]{0:T(1024)S(1)} %and_add_fusion), kind=kOutput, calls=%fused_computation.1 | convolution fusion | flops 4299161600 | bytes 8392704 | tf_op jit(solution)/shard_map/dot_general | solution.py:24
  14.9 3.8 %collective-permute-done.2 = bf16[80,2048]{1,0:T(8,128)(2,1)S(1)} collective-permute-done((bf16[80,2048]{1,0:T(8,128)(2,1)}, bf16[80,2048]{1,0:T(8,128)(2,1)S(1)}, u32[]{:S(2)}, u32[]{:S(2)}) %collective-permute-start.2) | collective-permute-done | bytes 327712 | tf_op jit(solution)/shard_map/ppermute | solution.py:12
  18.7 4.2 %collective-permute-done = bf16[80,2048]{1,0:T(8,128)(2,1)S(1)} collective-permute-done((bf16[80,2048]{1,0:T(8,128)(2,1)}, bf16[80,2048]{1,0:T(8,128)(2,1)S(1)}, u32[]{:S(2)}, u32[]{:S(2)}) %collective-permute-start) | collective-permute-done | bytes 327712 | tf_op jit(solution)/shard_map/ppermute | solution.py:12
  22.9 1.6 %collective-permute-start.6 = (bf16[160,2048]{1,0:T(8,128)(2,1)S(1)}, bf16[160,2048]{1,0:T(8,128)(2,1)S(1)}, u32[]{:S(2)}, u32[]{:S(2)}) collective-permute-start(bf16[160,2048]{1,0:T(8,128)(2,1)S(1)} %constant_dynamic-update-slice_fusion), channel_id=1, source_target_pairs={{0,64},{64,128},{128,192},{192,0},{1,65},{65,129},{129,193},{193,1... | collective-permute-start | bytes 1966088 | tf_op jit(solution)/shard_map/ppermute | solution.py:12
  24.5 1.7 %collective-permute-start.8 = (bf16[160,2048]{1,0:T(8,128)(2,1)S(1)}, bf16[160,2048]{1,0:T(8,128)(2,1)S(1)}, u32[]{:S(2)}, u32[]{:S(2)}) collective-permute-start(bf16[160,2048]{1,0:T(8,128)(2,1)S(1)} %constant_dynamic-update-slice_fusion), channel_id=1, source_target_pairs={{0,192},{64,0},{128,64},{192,128},{1,193},{65,1},{129,65},{193,129... | collective-permute-start | bytes 1966088 | tf_op jit(solution)/shard_map/ppermute | solution.py:12
  26.4 4.2 %collective-permute-start.3 = (bf16[40,2048]{1,0:T(8,128)(2,1)S(1)}, bf16[40,2048]{1,0:T(8,128)(2,1)S(1)}, u32[]{:S(2)}, u32[]{:S(2)}) collective-permute-start(bf16[40,2048]{1,0:T(8,128)(2,1)S(1)} %slice.80), channel_id=1, source_target_pairs={{0,16},{16,32},{32,48},{48,0},{1,17},{17,33},{33,49},{49,1},{2,18}... | collective-permute-start | bytes 491528 | tf_op jit(solution)/shard_map/ppermute | solution.py:12
  30.7 1.0 fusion.15
  31.9 2.0 %collective-permute-done.1 = bf16[40,2048]{1,0:T(8,128)(2,1)S(1)} collective-permute-done((bf16[40,2048]{1,0:T(8,128)(2,1)S(1)}, bf16[40,2048]{1,0:T(8,128)(2,1)S(1)}, u32[]{:S(2)}, u32[]{:S(2)}) %collective-permute-start.1) | collective-permute-done | bytes 163872 | tf_op jit(solution)/shard_map/ppermute | solution.py:12
  33.9 0.5 collective-permute-done.3
  34.5 5.5 %collective-permute-done.6 = bf16[160,2048]{1,0:T(8,128)(2,1)S(1)} collective-permute-done((bf16[160,2048]{1,0:T(8,128)(2,1)S(1)}, bf16[160,2048]{1,0:T(8,128)(2,1)S(1)}, u32[]{:S(2)}, u32[]{:S(2)}) %collective-permute-start.6) | collective-permute-done | bytes 655392 | tf_op jit(solution)/shard_map/ppermute | solution.py:12
  40.1 1.0 fusion.17
  41.3 1.0 pad_maximum_fusion.2
  42.3 2.9 %collective-permute-start.9 = (bf16[200,2048]{1,0:T(8,128)(2,1)}, bf16[200,2048]{1,0:T(8,128)(2,1)S(1)}, u32[]{:S(2)}, u32[]{:S(2)}) collective-permute-start(bf16[200,2048]{1,0:T(8,128)(2,1)} %pad_maximum_fusion.2), channel_id=1, source_target_pairs={{0,192},{64,0},{128,64},{192,128},{1,193},{65,1},{129,65},{193,129... | collective-permute-start | bytes 2457608 | tf_op jit(solution)/shard_map/ppermute | solution.py:12
  45.2 1.0 pad_maximum_fusion.1
  46.2 1.0 fusion.28
  47.2 1.0 fusion.25
  48.3 1.3 %bitcast_bitcast_fusion = f32[4,800,128]{2,1,0:T(8,128)} fusion(f32[400,512]{1,0:T(8,128)S(1)} %fusion.25, f32[400,512]{1,0:T(8,128)S(1)} %fusion.28), kind=kLoop, calls=%fused_computation.12 | loop fusion | flops 409600 | bytes 3276800 | tf_op jit(solution)/shard_map/transpose | solution.py:40
  49.6 4.5 %all-to-all-start = ((f32[4,800,128]{2,1,0:T(8,128)}), f32[4,800,128]{2,1,0:T(8,128)S(1)}, u32[]{:S(2)}, u32[]{:S(2)}) async-start(f32[4,800,128]{2,1,0:T(8,128)} %bitcast_bitcast_fusion), calls=%async_computation | async-start | bytes 3276800 | tf_op jit(solution)/shard_map/all_to_all | solution.py:41
  54.0 9.6 %collective-permute-done.9 = bf16[200,2048]{1,0:T(8,128)(2,1)S(1)} collective-permute-done((bf16[200,2048]{1,0:T(8,128)(2,1)}, bf16[200,2048]{1,0:T(8,128)(2,1)S(1)}, u32[]{:S(2)}, u32[]{:S(2)}) %collective-permute-start.9) | collective-permute-done | bytes 819232 | tf_op jit(solution)/shard_map/ppermute | solution.py:12
  63.7 4.3 %collective-permute-done.7 = bf16[200,2048]{1,0:T(8,128)(2,1)S(1)} collective-permute-done((bf16[200,2048]{1,0:T(8,128)(2,1)}, bf16[200,2048]{1,0:T(8,128)(2,1)S(1)}, u32[]{:S(2)}, u32[]{:S(2)}) %collective-permute-start.7) | collective-permute-done | bytes 819232 | tf_op jit(solution)/shard_map/ppermute | solution.py:12
  68.1 0.7 slice.69
  68.7 3.2 %collective-permute-start.12 = (bf16[40,2048]{1,0:T(8,128)(2,1)}, bf16[40,2048]{1,0:T(8,128)(2,1)}, u32[]{:S(2)}, u32[]{:S(2)}) collective-permute-start(bf16[40,2048]{1,0:T(8,128)(2,1)} %slice.69), channel_id=1, source_target_pairs={{0,192},{64,0},{128,64},{192,128},{1,193},{65,1},{129,65},{193,129... | collective-permute-start | bytes 491528 | tf_op jit(solution)/shard_map/ppermute | solution.py:12
  72.0 2.9 %collective-permute-done.11 = bf16[40,2048]{1,0:T(8,128)(2,1)} collective-permute-done((bf16[40,2048]{1,0:T(8,128)(2,1)S(1)}, bf16[40,2048]{1,0:T(8,128)(2,1)}, u32[]{:S(2)}, u32[]{:S(2)}) %collective-permute-start.11) | collective-permute-done | bytes 163872 | tf_op jit(solution)/shard_map/ppermute | solution.py:12
  74.9 0.3 collective-permute-done.12
  75.1 2.5 %pad_maximum_fusion = bf16[480,2048]{1,0:T(8,128)(2,1)} fusion(bf16[40,2048]{1,0:T(8,128)(2,1)} %collective-permute-done.12, bf16[40,2048]{1,0:T(8,128)(2,1)} %collective-permute-done.11, bf16[200,2048]{1,0:T(8,128)(2,1)S(1)} %collective-permute-done.9, bf16[200,2048]{1,0:T(8,128)(2,1)S(1)} %collective-permute-done.7), kind=kLoop, calls=%fused_computation.11 | loop fusion | flops 7864320 | bytes 3932160 | tf_op jit(solution)/shard_map/concatenate | solution.py:28
  77.6 0.1 reduce_sum.9
  77.7 4.5 %fusion.13 = f32[480,512]{1,0:T(8,128)} fusion(bf16[480,2048]{1,0:T(8,128)(2,1)} %pad_maximum_fusion, bf16[2048,1024]{0,1:T(8,128)(2,1)} %copy-done.2), kind=kOutput, calls=%fused_computation.14 | convolution fusion | flops 1006632960 | bytes 5046272 | tf_op jit(solution)/shard_map/dot_general | solution.py:24
  82.4 2.8 %fusion.19 = f32[480,512]{1,0:T(8,128)S(1)} fusion(bf16[480,2048]{1,0:T(8,128)(2,1)S(1)} %copy-done, bf16[2048,1024]{0,1:T(8,128)(2,1)} %copy-done.2), kind=kOutput, calls=%fused_computation.20 | convolution fusion | flops 1006632960 | bytes 5046272 | tf_op jit(solution)/shard_map/dot_general | solution.py:24
  85.3 0.2 add.342
  85.5 0.1 constant_dynamic-slice_fusion.2
  85.6 1.7 %collective-permute-start.15 = (f32[480,128]{1,0:T(8,128)S(1)}, f32[480,128]{1,0:T(8,128)S(1)}, u32[]{:S(2)}, u32[]{:S(2)}) collective-permute-start(f32[480,128]{1,0:T(8,128)S(1)} %get-tuple-element.27), channel_id=1, source_target_pairs={{0,4},{4,8},{8,12},{12,0},{1,5},{5,9},{9,13},{13,1},{2,6},{6,10},{... | collective-permute-start | bytes 737288 | tf_op jit(solution)/shard_map/ppermute | solution.py:12
  87.2 1.7 %collective-permute-start.16 = (f32[480,128]{1,0:T(8,128)S(1)}, f32[480,128]{1,0:T(8,128)S(1)}, u32[]{:S(2)}, u32[]{:S(2)}) collective-permute-start(f32[480,128]{1,0:T(8,128)S(1)} %get-tuple-element.29), channel_id=1, source_target_pairs={{0,12},{4,0},{8,4},{12,8},{1,13},{5,1},{9,5},{13,9},{2,14},{6,2},{... | collective-permute-start | bytes 737288 | tf_op jit(solution)/shard_map/ppermute | solution.py:12
  88.9 2.0 %collective-permute-start.17 = (f32[480,128]{1,0:T(8,128)S(1)}, f32[480,128]{1,0:T(8,128)S(1)}, u32[]{:S(2)}, u32[]{:S(2)}) collective-permute-start(f32[480,128]{1,0:T(8,128)S(1)} %get-tuple-element.28), channel_id=1, source_target_pairs={{0,8},{4,12},{8,0},{12,4},{1,9},{5,13},{9,1},{13,5},{2,10},{6,14},... | collective-permute-start | bytes 737288 | tf_op jit(solution)/shard_map/ppermute | solution.py:12
  90.9 3.4 %collective-permute-done.18 = f32[800,128]{1,0:T(8,128)S(1)} collective-permute-done((f32[800,128]{1,0:T(8,128)S(1)}, f32[800,128]{1,0:T(8,128)S(1)}, u32[]{:S(2)}, u32[]{:S(2)}) %collective-permute-start.18) | collective-permute-done | bytes 409632 | tf_op jit(solution)/shard_map/ppermute | solution.py:20
  94.3 0.2 fusion.31
  94.5 0.8 collective-permute-done.15
  95.3 4.6 %collective-permute-done.16 = f32[480,128]{1,0:T(8,128)S(1)} collective-permute-done((f32[480,128]{1,0:T(8,128)S(1)}, f32[480,128]{1,0:T(8,128)S(1)}, u32[]{:S(2)}, u32[]{:S(2)}) %collective-permute-start.16) | collective-permute-done | bytes 245792 | tf_op jit(solution)/shard_map/ppermute | solution.py:12
  99.9 1.8 %collective-permute-done.17 = f32[480,128]{1,0:T(8,128)S(1)} collective-permute-done((f32[480,128]{1,0:T(8,128)S(1)}, f32[480,128]{1,0:T(8,128)S(1)}, u32[]{:S(2)}, u32[]{:S(2)}) %collective-permute-start.17) | collective-permute-done | bytes 245792 | tf_op jit(solution)/shard_map/ppermute | solution.py:12
  101.8 0.1 fusion.35
  102.0 0.1 pad_maximum_fusion.6
  102.1 1.8 %collective-permute-start.19 = (f32[240,128]{1,0:T(8,128)S(1)}, f32[240,128]{1,0:T(8,128)S(1)}, u32[]{:S(2)}, u32[]{:S(2)}) collective-permute-start(f32[240,128]{1,0:T(8,128)S(1)} %pad_maximum_fusion.6), channel_id=1, source_target_pairs={{0,2},{2,0},{1,3},{3,1},{4,6},{6,4},{5,7},{7,5},{8,10},{10,8},{9,1... | collective-permute-start | bytes 368648 | tf_op jit(solution)/shard_map/ppermute | solution.py:20
  103.9 1.4 %iota_compare_fusion = pred[1280,1280]{1,0:T(32,128)(4,1)S(1)} fusion(s32[1280]{0:T(1024)S(1)} %concatenate.49), kind=kLoop, calls=%fused_computation | loop fusion | flops 1638400 | bytes 1643520 | tf_op jit(solution)/shard_map/eq | solution.py:101
  105.3 1.8 %collective-permute-done.19 = f32[240,128]{1,0:T(8,128)S(1)} collective-permute-done((f32[240,128]{1,0:T(8,128)S(1)}, f32[240,128]{1,0:T(8,128)S(1)}, u32[]{:S(2)}, u32[]{:S(2)}) %collective-permute-start.19) | collective-permute-done | bytes 122912 | tf_op jit(solution)/shard_map/ppermute | solution.py:20
  107.2 0.6 fusion.3
  107.8 1.5 %fusion.8 = bf16[64,1280]{1,0:T(8,128)(2,1)} fusion(f32[64,1280]{1,0:T(8,128)S(1)} %fusion.3, bf16[800,64]{1,0:T(8,128)(2,1)S(1)} %fusion.31, pred[1280,1280]{1,0:T(32,128)(4,1)S(1)} %iota_compare_fusion), kind=kOutput, calls=%fused_computation.9 | convolution fusion | flops 131235840 | bytes 1720320 | tf_op jit(solution)/shard_map/dot_general | solution.py:104
  (52 shorter events, 1.3 us)
Async XLA Ops:
  0.0 18.7 %collective-permute-start.2 = (bf16[80,2048]{1,0:T(8,128)(2,1)}, bf16[80,2048]{1,0:T(8,128)(2,1)S(1)}, u32[]{:S(2)}, u32[]{:S(2)}) collective-permute-start(bf16[80,2048]{1,0:T(8,128)(2,1)} %param.2), channel_id=1, source_target_pairs={{0,16},{16,32},{32,48},{48,0},{1,17},{17,33},{33,49},{49,1},{2,18}... | collective-permute-start | bytes 983048 | tf_op jit(solution)/shard_map/ppermute | solution.py:12
  4.5 18.4 %collective-permute-start = (bf16[80,2048]{1,0:T(8,128)(2,1)}, bf16[80,2048]{1,0:T(8,128)(2,1)S(1)}, u32[]{:S(2)}, u32[]{:S(2)}) collective-permute-start(bf16[80,2048]{1,0:T(8,128)(2,1)} %param.2), channel_id=1, source_target_pairs={{0,48},{16,0},{32,16},{48,32},{1,49},{17,1},{33,17},{49,33},{2,50}... | collective-permute-start | bytes 983048 | tf_op jit(solution)/shard_map/ppermute | solution.py:12
  4.5 21.9 %collective-permute-start.4 = (bf16[80,2048]{1,0:T(8,128)(2,1)}, bf16[80,2048]{1,0:T(8,128)(2,1)S(1)}, u32[]{:S(2)}, u32[]{:S(2)}) collective-permute-start(bf16[80,2048]{1,0:T(8,128)(2,1)} %param.2), channel_id=1, source_target_pairs={{0,64},{64,128},{128,192},{192,0},{1,65},{65,129},{129,193},{193,1... | collective-permute-start | bytes 983048 | tf_op jit(solution)/shard_map/ppermute | solution.py:12
  6.0 24.6 %collective-permute-start.5 = (bf16[80,2048]{1,0:T(8,128)(2,1)}, bf16[80,2048]{1,0:T(8,128)(2,1)S(1)}, u32[]{:S(2)}, u32[]{:S(2)}) collective-permute-start(bf16[80,2048]{1,0:T(8,128)(2,1)} %param.2), channel_id=1, source_target_pairs={{0,192},{64,0},{128,64},{192,128},{1,193},{65,1},{129,65},{193,129... | collective-permute-start | bytes 983048 | tf_op jit(solution)/shard_map/ppermute | solution.py:12
  7.7 7.1 %copy-start.1 = (bf16[80,2048]{1,0:T(8,128)(2,1)S(1)}, bf16[80,2048]{1,0:T(8,128)(2,1)}, u32[]{:S(2)}) copy-start(bf16[80,2048]{1,0:T(8,128)(2,1)} %param.2) | copy-start | bytes 983044
  14.8 32.4 %copy-start.2 = (bf16[2048,1024]{0,1:T(8,128)(2,1)}, bf16[2048,1024]{0,1:T(8,128)(2,1)S(1)}, u32[]{:S(2)}) copy-start(bf16[2048,1024]{0,1:T(8,128)(2,1)S(1)} %convert_bitcast_fusion) | copy-start | bytes 12582916
  22.9 17.0 %collective-permute-start.6 = (bf16[160,2048]{1,0:T(8,128)(2,1)S(1)}, bf16[160,2048]{1,0:T(8,128)(2,1)S(1)}, u32[]{:S(2)}, u32[]{:S(2)}) collective-permute-start(bf16[160,2048]{1,0:T(8,128)(2,1)S(1)} %constant_dynamic-update-slice_fusion), channel_id=1, source_target_pairs={{0,64},{64,128},{128,192},{192,0},{1,65},{65,129},{129,193},{193,1... | collective-permute-start | bytes 1966088 | tf_op jit(solution)/shard_map/ppermute | solution.py:12
  24.5 15.5 %collective-permute-start.8 = (bf16[160,2048]{1,0:T(8,128)(2,1)S(1)}, bf16[160,2048]{1,0:T(8,128)(2,1)S(1)}, u32[]{:S(2)}, u32[]{:S(2)}) collective-permute-start(bf16[160,2048]{1,0:T(8,128)(2,1)S(1)} %constant_dynamic-update-slice_fusion), channel_id=1, source_target_pairs={{0,192},{64,0},{128,64},{192,128},{1,193},{65,1},{129,65},{193,129... | collective-permute-start | bytes 1966088 | tf_op jit(solution)/shard_map/ppermute | solution.py:12
  26.3 7.6 %collective-permute-start.1 = (bf16[40,2048]{1,0:T(8,128)(2,1)S(1)}, bf16[40,2048]{1,0:T(8,128)(2,1)S(1)}, u32[]{:S(2)}, u32[]{:S(2)}) collective-permute-start(bf16[40,2048]{1,0:T(8,128)(2,1)S(1)} %slice.79), channel_id=1, source_target_pairs={{0,48},{16,0},{32,16},{48,32},{1,49},{17,1},{33,17},{49,33},{2,50}... | collective-permute-start | bytes 491528 | tf_op jit(solution)/shard_map/ppermute | solution.py:12
  26.4 8.0 %collective-permute-start.3 = (bf16[40,2048]{1,0:T(8,128)(2,1)S(1)}, bf16[40,2048]{1,0:T(8,128)(2,1)S(1)}, u32[]{:S(2)}, u32[]{:S(2)}) collective-permute-start(bf16[40,2048]{1,0:T(8,128)(2,1)S(1)} %slice.80), channel_id=1, source_target_pairs={{0,16},{16,32},{32,48},{48,0},{1,17},{17,33},{33,49},{49,1},{2,18}... | collective-permute-start | bytes 491528 | tf_op jit(solution)/shard_map/ppermute | solution.py:12
  31.8 14.4 %collective-permute-start.13 = (f32[400,512]{1,0:T(8,128)S(1)}, f32[400,512]{1,0:T(8,128)S(1)}, u32[]{:S(2)}, u32[]{:S(2)}) collective-permute-start(f32[400,512]{1,0:T(8,128)S(1)} %fusion.15), channel_id=1, source_target_pairs={{0,1},{1,0},{2,3},{3,2},{4,5},{5,4},{6,7},{7,6},{8,9},{9,8},{10,11... | collective-permute-start | bytes 2457608 | tf_op jit(solution)/shard_map/ppermute | solution.py:20
  41.2 6.0 %collective-permute-start.10 = (f32[400,512]{1,0:T(8,128)S(1)}, f32[400,512]{1,0:T(8,128)S(1)}, u32[]{:S(2)}, u32[]{:S(2)}) collective-permute-start(f32[400,512]{1,0:T(8,128)S(1)} %fusion.17), channel_id=1, source_target_pairs={{0,1},{1,0},{2,3},{3,2},{4,5},{5,4},{6,7},{7,6},{8,9},{9,8},{10,11... | collective-permute-start | bytes 2457608 | tf_op jit(solution)/shard_map/ppermute | solution.py:20
  42.3 21.4 %collective-permute-start.9 = (bf16[200,2048]{1,0:T(8,128)(2,1)}, bf16[200,2048]{1,0:T(8,128)(2,1)S(1)}, u32[]{:S(2)}, u32[]{:S(2)}) collective-permute-start(bf16[200,2048]{1,0:T(8,128)(2,1)} %pad_maximum_fusion.2), channel_id=1, source_target_pairs={{0,192},{64,0},{128,64},{192,128},{1,193},{65,1},{129,65},{193,129... | collective-permute-start | bytes 2457608 | tf_op jit(solution)/shard_map/ppermute | solution.py:12
  46.2 21.8 %collective-permute-start.7 = (bf16[200,2048]{1,0:T(8,128)(2,1)}, bf16[200,2048]{1,0:T(8,128)(2,1)S(1)}, u32[]{:S(2)}, u32[]{:S(2)}) collective-permute-start(bf16[200,2048]{1,0:T(8,128)(2,1)} %pad_maximum_fusion.1), channel_id=1, source_target_pairs={{0,64},{64,128},{128,192},{192,0},{1,65},{65,129},{129,193},{193,1... | collective-permute-start | bytes 2457608 | tf_op jit(solution)/shard_map/ppermute | solution.py:12
  49.6 28.0 %all-to-all-start = ((f32[4,800,128]{2,1,0:T(8,128)}), f32[4,800,128]{2,1,0:T(8,128)S(1)}, u32[]{:S(2)}, u32[]{:S(2)}) async-start(f32[4,800,128]{2,1,0:T(8,128)} %bitcast_bitcast_fusion), calls=%async_computation | async-start | bytes 3276800 | tf_op jit(solution)/shard_map/all_to_all | solution.py:41
  68.0 6.9 %collective-permute-start.11 = (bf16[40,2048]{1,0:T(8,128)(2,1)S(1)}, bf16[40,2048]{1,0:T(8,128)(2,1)}, u32[]{:S(2)}, u32[]{:S(2)}) collective-permute-start(bf16[40,2048]{1,0:T(8,128)(2,1)S(1)} %slice.68), channel_id=1, source_target_pairs={{0,64},{64,128},{128,192},{192,0},{1,65},{65,129},{129,193},{193,1... | collective-permute-start | bytes 491528 | tf_op jit(solution)/shard_map/ppermute | solution.py:12
  68.7 6.4 %collective-permute-start.12 = (bf16[40,2048]{1,0:T(8,128)(2,1)}, bf16[40,2048]{1,0:T(8,128)(2,1)}, u32[]{:S(2)}, u32[]{:S(2)}) collective-permute-start(bf16[40,2048]{1,0:T(8,128)(2,1)} %slice.69), channel_id=1, source_target_pairs={{0,192},{64,0},{128,64},{192,128},{1,193},{65,1},{129,65},{193,129... | collective-permute-start | bytes 491528 | tf_op jit(solution)/shard_map/ppermute | solution.py:12
  77.7 4.8 %copy-start = (bf16[480,2048]{1,0:T(8,128)(2,1)S(1)}, bf16[480,2048]{1,0:T(8,128)(2,1)}, u32[]{:S(2)}) copy-start(bf16[480,2048]{1,0:T(8,128)(2,1)} %pad_maximum_fusion) | copy-start | bytes 5898244
  82.2 3.1 %collective-permute-start.14 = (f32[480,512]{1,0:T(8,128)}, f32[480,512]{1,0:T(8,128)S(1)}, u32[]{:S(2)}, u32[]{:S(2)}) collective-permute-start(f32[480,512]{1,0:T(8,128)} %fusion.13), channel_id=1, source_target_pairs={{0,1},{1,0},{2,3},{3,2},{4,5},{5,4},{6,7},{7,6},{8,9},{9,8},{10,11... | collective-permute-start | bytes 2949128 | tf_op jit(solution)/shard_map/ppermute | solution.py:20
  82.3 12.0 %collective-permute-start.18 = (f32[800,128]{1,0:T(8,128)S(1)}, f32[800,128]{1,0:T(8,128)S(1)}, u32[]{:S(2)}, u32[]{:S(2)}) collective-permute-start(f32[800,128]{1,0:T(8,128)S(1)} %reduce_sum.9), channel_id=1, source_target_pairs={{0,2},{2,0},{1,3},{3,1},{4,6},{6,4},{5,7},{7,5},{8,10},{10,8},{9,1... | collective-permute-start | bytes 1228808 | tf_op jit(solution)/shard_map/ppermute | solution.py:20
  85.6 9.7 %collective-permute-start.15 = (f32[480,128]{1,0:T(8,128)S(1)}, f32[480,128]{1,0:T(8,128)S(1)}, u32[]{:S(2)}, u32[]{:S(2)}) collective-permute-start(f32[480,128]{1,0:T(8,128)S(1)} %get-tuple-element.27), channel_id=1, source_target_pairs={{0,4},{4,8},{8,12},{12,0},{1,5},{5,9},{9,13},{13,1},{2,6},{6,10},{... | collective-permute-start | bytes 737288 | tf_op jit(solution)/shard_map/ppermute | solution.py:12
  87.2 12.7 %collective-permute-start.16 = (f32[480,128]{1,0:T(8,128)S(1)}, f32[480,128]{1,0:T(8,128)S(1)}, u32[]{:S(2)}, u32[]{:S(2)}) collective-permute-start(f32[480,128]{1,0:T(8,128)S(1)} %get-tuple-element.29), channel_id=1, source_target_pairs={{0,12},{4,0},{8,4},{12,8},{1,13},{5,1},{9,5},{13,9},{2,14},{6,2},{... | collective-permute-start | bytes 737288 | tf_op jit(solution)/shard_map/ppermute | solution.py:12
  88.9 12.8 %collective-permute-start.17 = (f32[480,128]{1,0:T(8,128)S(1)}, f32[480,128]{1,0:T(8,128)S(1)}, u32[]{:S(2)}, u32[]{:S(2)}) collective-permute-start(f32[480,128]{1,0:T(8,128)S(1)} %get-tuple-element.28), channel_id=1, source_target_pairs={{0,8},{4,12},{8,0},{12,4},{1,9},{5,13},{9,1},{13,5},{2,10},{6,14},... | collective-permute-start | bytes 737288 | tf_op jit(solution)/shard_map/ppermute | solution.py:12
  102.1 5.0 %collective-permute-start.19 = (f32[240,128]{1,0:T(8,128)S(1)}, f32[240,128]{1,0:T(8,128)S(1)}, u32[]{:S(2)}, u32[]{:S(2)}) collective-permute-start(f32[240,128]{1,0:T(8,128)S(1)} %pad_maximum_fusion.6), channel_id=1, source_target_pairs={{0,2},{2,0},{1,3},{3,1},{4,6},{6,4},{5,7},{7,5},{8,10},{10,8},{9,1... | collective-permute-start | bytes 368648 | tf_op jit(solution)/shard_map/ppermute | solution.py:20

commit v16 on v13

--- a/solution.py
+++ b/solution.py
@@ -85,7 +85,7 @@
     rows = joined(from_xm, from_xp, opposite)
     away, early = lax.optimization_barrier((dot(rows, theirs), early))
     away = swap(away, "core")
-    kept = lax.optimization_barrier(dot(rows, mine))
+    kept = dot(rows, mine)
     last, early = lax.optimization_barrier((over_y_at_once(kept + away), over_zl(early)))
     sums = [early, over_zl_folded(last)]
     sites = [

time: 107 us -> 109 us (1.019)
  waiting for transfers between devices: 41.8 us -> 46.9 us
  starting transfers between devices: 30.2 us -> 28.5 us
  matrix products: 24.1 us -> 22.8 us
    ppermute x14, waiting for transfers between devices: 32.7 us -> 35.8 us  [shift(): lax.ppermute(value, axis, [(i, (i + by) % size) for i in range(size)])]
    ppermute x5, waiting for transfers between devices: 6.44 us -> 8.45 us  [swap(): return lax.ppermute(value, axis, [(0, 1), (1, 0)])]
    ppermute x5, starting transfers between devices: 2.01 us -> 0.28 us  [swap(): return lax.ppermute(value, axis, [(0, 1), (1, 0)])]
    dot_general x7, matrix products: 22 us -> 20.7 us  [dot(): return jnp.dot(left, right, preferred_element_type=F32)]
  transfers between devices with their start and end apart: 20 -> 20, of which waited for: 9 -> 10; matrix products, arithmetic and copies ran while one was open for 27% -> 26% of each run, Pallas kernels for 0% -> 0%
where the time goes in v16:
time: 109 us; the launch traced here: 108 us
  waiting for transfers between devices  46.9 us (43%)
  starting transfers between devices  28.5 us (26%)
  matrix products  22.8 us (21%)
  local copies, waits for them, and re-layouts  5.36 us (5%)
  other arithmetic  4.41 us (4%)
    ppermute x14, waiting for transfers between devices, shift(): lax.ppermute(value, axis, [(i, (i + by) % size) for i in range(size)])  35.8 us
    ppermute x14, starting transfers between devices, shift(): lax.ppermute(value, axis, [(i, (i + by) % size) for i in range(size)])  23.7 us
    dot_general x7, matrix products, dot(): return jnp.dot(left, right, preferred_element_type=F32)  20.7 us
    ppermute x5, waiting for transfers between devices, swap(): return lax.ppermute(value, axis, [(0, 1), (1, 0)])  8.45 us
    all_to_all x1, starting transfers between devices, over_y(): lax.all_to_all(split, 'y', split_axis=0, concat_axis=0, tiled=True)  4.47 us
    unnamed x29, local copies, waits for them, and re-layouts  3.93 us
    all_to_all x1, waiting for transfers between devices, over_y(): lax.all_to_all(split, 'y', split_axis=0, concat_axis=0, tiled=True)  2.64 us
  transfers between devices with their start and end apart: 20, of which 10 were waited for; matrix products, arithmetic and copies ran while one was open for 26% of the time, Pallas kernels for 0%

profile of v16, /device:TPU:64, one launch (start us, length us, event | category | flops | bytes accessed | tf_op | source)
XLA Modules:
  0.0 108.4 jit_solution(2174644500225891026)
XLA Ops:
  0.0 4.5 %collective-permute-start.2 = (bf16[80,2048]{1,0:T(8,128)(2,1)}, bf16[80,2048]{1,0:T(8,128)(2,1)S(1)}, u32[]{:S(2)}, u32[]{:S(2)}) collective-permute-start(bf16[80,2048]{1,0:T(8,128)(2,1)} %param.2), channel_id=1, source_target_pairs={{0,16},{16,32},{32,48},{48,0},{1,17},{17,33},{33,49},{49,1},{2,18}... | collective-permute-start | bytes 983048 | tf_op jit(solution)/shard_map/ppermute | solution.py:12
  4.5 1.5 %collective-permute-start.4 = (bf16[80,2048]{1,0:T(8,128)(2,1)}, bf16[80,2048]{1,0:T(8,128)(2,1)S(1)}, u32[]{:S(2)}, u32[]{:S(2)}) collective-permute-start(bf16[80,2048]{1,0:T(8,128)(2,1)} %param.2), channel_id=1, source_target_pairs={{0,64},{64,128},{128,192},{192,0},{1,65},{65,129},{129,193},{193,1... | collective-permute-start | bytes 983048 | tf_op jit(solution)/shard_map/ppermute | solution.py:12
  6.0 1.7 %collective-permute-start.7 = (bf16[80,2048]{1,0:T(8,128)(2,1)}, bf16[80,2048]{1,0:T(8,128)(2,1)S(1)}, u32[]{:S(2)}, u32[]{:S(2)}) collective-permute-start(bf16[80,2048]{1,0:T(8,128)(2,1)} %param.2), channel_id=1, source_target_pairs={{0,192},{64,0},{128,64},{192,128},{1,193},{65,1},{129,65},{193,129... | collective-permute-start | bytes 983048 | tf_op jit(solution)/shard_map/ppermute | solution.py:12
  7.7 7.1 %convert_bitcast_fusion = bf16[2048,1024]{0,1:T(8,128)(2,1)S(1)} fusion(bf16[2048,1024]{1,0:T(8,128)(2,1)} %param.3, s32[1024]{0:T(1024)S(1)} %and_add_fusion), kind=kOutput, calls=%fused_computation.1 | convolution fusion | flops 4299161600 | bytes 8392704 | tf_op jit(solution)/shard_map/dot_general | solution.py:24
  14.9 3.8 %collective-permute-done.2 = bf16[80,2048]{1,0:T(8,128)(2,1)S(1)} collective-permute-done((bf16[80,2048]{1,0:T(8,128)(2,1)}, bf16[80,2048]{1,0:T(8,128)(2,1)S(1)}, u32[]{:S(2)}, u32[]{:S(2)}) %collective-permute-start.2) | collective-permute-done | bytes 327712 | tf_op jit(solution)/shard_map/ppermute | solution.py:12
  18.7 4.2 %collective-permute-done = bf16[80,2048]{1,0:T(8,128)(2,1)S(1)} collective-permute-done((bf16[80,2048]{1,0:T(8,128)(2,1)}, bf16[80,2048]{1,0:T(8,128)(2,1)S(1)}, u32[]{:S(2)}, u32[]{:S(2)}) %collective-permute-start) | collective-permute-done | bytes 327712 | tf_op jit(solution)/shard_map/ppermute | solution.py:12
  22.9 1.6 %collective-permute-start.5 = (bf16[160,2048]{1,0:T(8,128)(2,1)S(1)}, bf16[160,2048]{1,0:T(8,128)(2,1)S(1)}, u32[]{:S(2)}, u32[]{:S(2)}) collective-permute-start(bf16[160,2048]{1,0:T(8,128)(2,1)S(1)} %constant_dynamic-update-slice_fusion), channel_id=1, source_target_pairs={{0,64},{64,128},{128,192},{192,0},{1,65},{65,129},{129,193},{193,1... | collective-permute-start | bytes 1966088 | tf_op jit(solution)/shard_map/ppermute | solution.py:12
  24.5 1.7 %collective-permute-start.8 = (bf16[160,2048]{1,0:T(8,128)(2,1)S(1)}, bf16[160,2048]{1,0:T(8,128)(2,1)S(1)}, u32[]{:S(2)}, u32[]{:S(2)}) collective-permute-start(bf16[160,2048]{1,0:T(8,128)(2,1)S(1)} %constant_dynamic-update-slice_fusion), channel_id=1, source_target_pairs={{0,192},{64,0},{128,64},{192,128},{1,193},{65,1},{129,65},{193,129... | collective-permute-start | bytes 1966088 | tf_op jit(solution)/shard_map/ppermute | solution.py:12
  26.4 4.2 %collective-permute-start.3 = (bf16[40,2048]{1,0:T(8,128)(2,1)S(1)}, bf16[40,2048]{1,0:T(8,128)(2,1)S(1)}, u32[]{:S(2)}, u32[]{:S(2)}) collective-permute-start(bf16[40,2048]{1,0:T(8,128)(2,1)S(1)} %slice.72), channel_id=1, source_target_pairs={{0,16},{16,32},{32,48},{48,0},{1,17},{17,33},{33,49},{49,1},{2,18}... | collective-permute-start | bytes 491528 | tf_op jit(solution)/shard_map/ppermute | solution.py:12
  30.7 2.0 %fusion.13 = f32[400,512]{1,0:T(8,128)} fusion(bf16[400,2048]{1,0:T(8,128)(2,1)S(1)} %constant_dynamic-update-slice_fusion.9, bf16[2048,1024]{0,1:T(8,128)(2,1)S(1)} %convert_bitcast_fusion), kind=kOutput, calls=%fused_computation.13 | convolution fusion | flops 838860800 | bytes 4554752 | tf_op jit(solution)/shard_map/dot_general | solution.py:24
  32.7 7.2 %collective-permute-done.5 = bf16[160,2048]{1,0:T(8,128)(2,1)S(1)} collective-permute-done((bf16[160,2048]{1,0:T(8,128)(2,1)S(1)}, bf16[160,2048]{1,0:T(8,128)(2,1)S(1)}, u32[]{:S(2)}, u32[]{:S(2)}) %collective-permute-start.5) | collective-permute-done | bytes 655392 | tf_op jit(solution)/shard_map/ppermute | solution.py:12
  40.2 2.0 %fusion.17 = f32[400,512]{1,0:T(8,128)} fusion(bf16[400,2048]{1,0:T(8,128)(2,1)S(1)} %constant_dynamic-update-slice_fusion.2, bf16[2048,1024]{0,1:T(8,128)(2,1)S(1)} %convert_bitcast_fusion), kind=kOutput, calls=%fused_computation.17 | convolution fusion | flops 838860800 | bytes 4554752 | tf_op jit(solution)/shard_map/dot_general | solution.py:24
  42.3 0.8 slice-done
  43.1 1.2 %pad_maximum_fusion.2 = (bf16[200,2048]{1,0:T(8,128)(2,1)S(1)}, bf16[200,2048]{1,0:T(8,128)(2,1)}) fusion(bf16[80,2048]{1,0:T(8,128)(2,1)S(1)} %slice.76, bf16[40,2048]{1,0:T(8,128)(2,1)S(1)} %slice.75, bf16[40,2048]{1,0:T(8,128)(2,1)S(1)} %collective-permute-done.3, bf16[40,2048]{1,0:T(8,128)(2,1)S(1)} %collective-permute-done.1, ...), kind=kLoop, calls=%fused_computation.30 | loop fusion | flops 5324800 | bytes 2949120 | tf_op jit(solution)/shard_map/concatenate | solution.py:28
  44.3 1.4 %collective-permute-start.6 = (bf16[200,2048]{1,0:T(8,128)(2,1)}, bf16[200,2048]{1,0:T(8,128)(2,1)}, u32[]{:S(2)}, u32[]{:S(2)}) collective-permute-start(bf16[200,2048]{1,0:T(8,128)(2,1)} %get-tuple-element.27), channel_id=1, source_target_pairs={{0,64},{64,128},{128,192},{192,0},{1,65},{65,129},{129,193},{193,1... | collective-permute-start | bytes 2457608 | tf_op jit(solution)/shard_map/ppermute | solution.py:12
  45.7 1.8 %collective-permute-start.9 = (bf16[200,2048]{1,0:T(8,128)(2,1)S(1)}, bf16[200,2048]{1,0:T(8,128)(2,1)}, u32[]{:S(2)}, u32[]{:S(2)}) collective-permute-start(bf16[200,2048]{1,0:T(8,128)(2,1)S(1)} %get-tuple-element.26), channel_id=1, source_target_pairs={{0,192},{64,0},{128,64},{192,128},{1,193},{65,1},{129,65},{193,129... | collective-permute-start | bytes 2457608 | tf_op jit(solution)/shard_map/ppermute | solution.py:12
  47.5 2.8 %fusion.31 = f32[400,512]{1,0:T(8,128)S(1)} fusion(f32[400,512]{1,0:T(8,128)} %collective-permute-done.12, bf16[400,2048]{1,0:T(8,128)(2,1)S(1)} %copy-done.6, bf16[2048,1024]{0,1:T(8,128)(2,1)} %copy-done.7), kind=kOutput, calls=%fused_computation.27 | convolution fusion | flops 839065600 | bytes 5373952 | tf_op jit(solution)/shard_map/dot_general | solution.py:24
  50.4 2.2 %fusion.28 = f32[400,512]{1,0:T(8,128)S(1)} fusion(f32[400,512]{1,0:T(8,128)} %collective-permute-done.10, bf16[400,2048]{1,0:T(8,128)(2,1)S(1)} %copy-done.4, bf16[2048,1024]{0,1:T(8,128)(2,1)S(1)} %copy-done.8), kind=kOutput, calls=%fused_computation.26 | convolution fusion | flops 839065600 | bytes 5373952 | tf_op jit(solution)/shard_map/dot_general | solution.py:24
  52.6 1.3 %bitcast_bitcast_fusion = f32[4,800,128]{2,1,0:T(8,128)} fusion(f32[400,512]{1,0:T(8,128)S(1)} %fusion.28, f32[400,512]{1,0:T(8,128)S(1)} %fusion.31), kind=kLoop, calls=%fused_computation.11 | loop fusion | flops 409600 | bytes 3276800 | tf_op jit(solution)/shard_map/transpose | solution.py:40
  53.9 4.5 %all-to-all-start = ((f32[4,800,128]{2,1,0:T(8,128)}), f32[4,800,128]{2,1,0:T(8,128)S(1)}, u32[]{:S(2)}, u32[]{:S(2)}) async-start(f32[4,800,128]{2,1,0:T(8,128)} %bitcast_bitcast_fusion), calls=%async_computation | async-start | bytes 3276800 | tf_op jit(solution)/shard_map/all_to_all | solution.py:41
  58.4 1.9 %collective-permute-start.11 = (bf16[80,2048]{1,0:T(8,128)(2,1)S(1)}, bf16[80,2048]{1,0:T(8,128)(2,1)S(1)}, u32[]{:S(2)}, u32[]{:S(2)}) collective-permute-start(bf16[80,2048]{1,0:T(8,128)(2,1)S(1)} %pad_maximum_fusion.3), channel_id=1, source_target_pairs={{0,128},{64,192},{128,0},{192,64},{1,129},{65,193},{129,1},{193,65... | collective-permute-start | bytes 983048 | tf_op jit(solution)/shard_map/ppermute | solution.py:12
  60.3 6.2 %collective-permute-done.6 = bf16[200,2048]{1,0:T(8,128)(2,1)} collective-permute-done((bf16[200,2048]{1,0:T(8,128)(2,1)}, bf16[200,2048]{1,0:T(8,128)(2,1)}, u32[]{:S(2)}, u32[]{:S(2)}) %collective-permute-start.6) | collective-permute-done | bytes 819232 | tf_op jit(solution)/shard_map/ppermute | solution.py:12
  66.4 6.0 %collective-permute-done.9 = bf16[200,2048]{1,0:T(8,128)(2,1)} collective-permute-done((bf16[200,2048]{1,0:T(8,128)(2,1)S(1)}, bf16[200,2048]{1,0:T(8,128)(2,1)}, u32[]{:S(2)}, u32[]{:S(2)}) %collective-permute-start.9) | collective-permute-done | bytes 819232 | tf_op jit(solution)/shard_map/ppermute | solution.py:12
  72.4 1.2 %constant_dynamic-update-slice_fusion.8 = bf16[480,2048]{1,0:T(8,128)(2,1)S(1)} fusion(bf16[200,2048]{1,0:T(8,128)(2,1)} %collective-permute-done.6), kind=kLoop, calls=%fused_computation.46 | loop fusion | bytes 1638400
  73.6 1.2 %constant_dynamic-update-slice_fusion.7 = bf16[480,2048]{1,0:T(8,128)(2,1)S(1)} fusion(bf16[480,2048]{1,0:T(8,128)(2,1)S(1)} %constant_dynamic-update-slice_fusion.8, bf16[200,2048]{1,0:T(8,128)(2,1)} %collective-permute-done.9), kind=kLoop, calls=%fused_computation.45 | loop fusion | bytes 1638400
  74.9 1.3 %copy-done.1 = bf16[480,2048]{1,0:T(8,128)(2,1)} copy-done((bf16[480,2048]{1,0:T(8,128)(2,1)}, bf16[480,2048]{1,0:T(8,128)(2,1)S(1)}, u32[]{:S(2)}) %copy-start.1) | copy-done | bytes 1966104
  76.2 1.2 %fusion.15 = f32[480,512]{1,0:T(8,128)S(1)} fusion(bf16[480,2048]{1,0:T(8,128)(2,1)S(1)} %constant_dynamic-update-slice_fusion.6, bf16[2048,1024]{0,1:T(8,128)(2,1)S(1)} %copy-done.9), kind=kOutput, calls=%fused_computation.15 | convolution fusion | flops 1006632960 | bytes 5046272 | tf_op jit(solution)/shard_map/dot_general | solution.py:24
  77.4 2.6 %all-to-all-done = f32[4,800,128]{2,1,0:T(8,128)S(1)} async-done(((f32[4,800,128]{2,1,0:T(8,128)}), f32[4,800,128]{2,1,0:T(8,128)S(1)}, u32[]{:S(2)}, u32[]{:S(2)}) %all-to-all-start) | async-done | bytes 1638432 | tf_op jit(solution)/shard_map/all_to_all | solution.py:41
  80.1 0.1 reduce_sum.9
  80.2 0.1 collective-permute-start.13
  80.4 0.1 concatenate.44
  80.5 0.1 collective-permute-start.17
  80.6 2.2 %collective-permute-done.13 = f32[480,512]{1,0:T(8,128)S(1)} collective-permute-done((f32[480,512]{1,0:T(8,128)S(1)}, f32[480,512]{1,0:T(8,128)S(1)}, u32[]{:S(2)}, u32[]{:S(2)}) %collective-permute-start.13) | collective-permute-done | bytes 983072 | tf_op jit(solution)/shard_map/ppermute | solution.py:20
  82.8 3.4 %fusion.25 = f32[480,512]{1,0:T(8,128)S(1)} fusion(f32[480,512]{1,0:T(8,128)S(1)} %collective-permute-done.13, bf16[480,2048]{1,0:T(8,128)(2,1)} %copy-done.1, bf16[2048,1024]{0,1:T(8,128)(2,1)} %copy-done.7), kind=kOutput, calls=%fused_computation.25 | convolution fusion | flops 1006878720 | bytes 6029312 | tf_op jit(solution)/shard_map/dot_general | solution.py:24
  86.2 0.1 constant_dynamic-slice_fusion.2
  86.3 0.6 collective-permute-start.14
  87.0 2.7 %collective-permute-start.15 = (f32[480,128]{1,0:T(8,128)S(1)}, f32[480,128]{1,0:T(8,128)S(1)}, u32[]{:S(2)}, u32[]{:S(2)}) collective-permute-start(f32[480,128]{1,0:T(8,128)S(1)} %get-tuple-element.25), channel_id=1, source_target_pairs={{0,12},{4,0},{8,4},{12,8},{1,13},{5,1},{9,5},{13,9},{2,14},{6,2},{... | collective-permute-start | bytes 737288 | tf_op jit(solution)/shard_map/ppermute | solution.py:12
  89.7 2.7 %collective-permute-done.17 = f32[800,128]{1,0:T(8,128)S(1)} collective-permute-done((f32[800,128]{1,0:T(8,128)S(1)}, f32[800,128]{1,0:T(8,128)S(1)}, u32[]{:S(2)}, u32[]{:S(2)}) %collective-permute-start.17) | collective-permute-done | bytes 409632 | tf_op jit(solution)/shard_map/ppermute | solution.py:20
  92.4 0.2 fusion.34
  92.6 8.3 %collective-permute-done.14 = f32[480,128]{1,0:T(8,128)S(1)} collective-permute-done((f32[480,128]{1,0:T(8,128)S(1)}, f32[480,128]{1,0:T(8,128)S(1)}, u32[]{:S(2)}, u32[]{:S(2)}) %collective-permute-start.14) | collective-permute-done | bytes 245792 | tf_op jit(solution)/shard_map/ppermute | solution.py:12
  101.0 0.1 fusion.38
  101.1 0.1 pad_maximum_fusion.4
  101.2 0.1 collective-permute-start.18
  101.3 1.4 %iota_compare_fusion = pred[1280,1280]{1,0:T(32,128)(4,1)S(1)} fusion(s32[1280]{0:T(1024)S(1)} %concatenate.44), kind=kLoop, calls=%fused_computation | loop fusion | flops 1638400 | bytes 1643520 | tf_op jit(solution)/shard_map/eq | solution.py:99
  102.7 3.5 %collective-permute-done.18 = f32[240,128]{1,0:T(8,128)S(1)} collective-permute-done((f32[240,128]{1,0:T(8,128)S(1)}, f32[240,128]{1,0:T(8,128)S(1)}, u32[]{:S(2)}, u32[]{:S(2)}) %collective-permute-start.18) | collective-permute-done | bytes 122912 | tf_op jit(solution)/shard_map/ppermute | solution.py:20
  106.2 0.1 fusion.39
  106.3 0.6 fusion.3
  106.9 1.5 %fusion.8 = bf16[64,1280]{1,0:T(8,128)(2,1)} fusion(f32[64,1280]{1,0:T(8,128)S(1)} %fusion.3, bf16[800,64]{1,0:T(8,128)(2,1)S(1)} %fusion.34, pred[1280,1280]{1,0:T(32,128)(4,1)S(1)} %iota_compare_fusion), kind=kOutput, calls=%fused_computation.9 | convolution fusion | flops 131235840 | bytes 1720320 | tf_op jit(solution)/shard_map/dot_general | solution.py:102
  (63 shorter events, 0.7 us)
Async XLA Ops:
  0.0 18.7 %collective-permute-start.2 = (bf16[80,2048]{1,0:T(8,128)(2,1)}, bf16[80,2048]{1,0:T(8,128)(2,1)S(1)}, u32[]{:S(2)}, u32[]{:S(2)}) collective-permute-start(bf16[80,2048]{1,0:T(8,128)(2,1)} %param.2), channel_id=1, source_target_pairs={{0,16},{16,32},{32,48},{48,0},{1,17},{17,33},{33,49},{49,1},{2,18}... | collective-permute-start | bytes 983048 | tf_op jit(solution)/shard_map/ppermute | solution.py:12
  4.5 18.4 %collective-permute-start = (bf16[80,2048]{1,0:T(8,128)(2,1)}, bf16[80,2048]{1,0:T(8,128)(2,1)S(1)}, u32[]{:S(2)}, u32[]{:S(2)}) collective-permute-start(bf16[80,2048]{1,0:T(8,128)(2,1)} %param.2), channel_id=1, source_target_pairs={{0,48},{16,0},{32,16},{48,32},{1,49},{17,1},{33,17},{49,33},{2,50}... | collective-permute-start | bytes 983048 | tf_op jit(solution)/shard_map/ppermute | solution.py:12
  4.5 21.9 %collective-permute-start.4 = (bf16[80,2048]{1,0:T(8,128)(2,1)}, bf16[80,2048]{1,0:T(8,128)(2,1)S(1)}, u32[]{:S(2)}, u32[]{:S(2)}) collective-permute-start(bf16[80,2048]{1,0:T(8,128)(2,1)} %param.2), channel_id=1, source_target_pairs={{0,64},{64,128},{128,192},{192,0},{1,65},{65,129},{129,193},{193,1... | collective-permute-start | bytes 983048 | tf_op jit(solution)/shard_map/ppermute | solution.py:12
  6.0 24.6 %collective-permute-start.7 = (bf16[80,2048]{1,0:T(8,128)(2,1)}, bf16[80,2048]{1,0:T(8,128)(2,1)S(1)}, u32[]{:S(2)}, u32[]{:S(2)}) collective-permute-start(bf16[80,2048]{1,0:T(8,128)(2,1)} %param.2), channel_id=1, source_target_pairs={{0,192},{64,0},{128,64},{192,128},{1,193},{65,1},{129,65},{193,129... | collective-permute-start | bytes 983048 | tf_op jit(solution)/shard_map/ppermute | solution.py:12
  7.7 7.1 %copy-start.2 = (bf16[80,2048]{1,0:T(8,128)(2,1)S(1)}, bf16[80,2048]{1,0:T(8,128)(2,1)}, u32[]{:S(2)}) copy-start(bf16[80,2048]{1,0:T(8,128)(2,1)} %param.2) | copy-start | bytes 983044
  14.8 25.3 %copy-start.7 = (bf16[2048,1024]{0,1:T(8,128)(2,1)}, bf16[2048,1024]{0,1:T(8,128)(2,1)S(1)}, u32[]{:S(2)}) copy-start(bf16[2048,1024]{0,1:T(8,128)(2,1)S(1)} %convert_bitcast_fusion) | copy-start | bytes 12582916
  22.9 17.0 %collective-permute-start.5 = (bf16[160,2048]{1,0:T(8,128)(2,1)S(1)}, bf16[160,2048]{1,0:T(8,128)(2,1)S(1)}, u32[]{:S(2)}, u32[]{:S(2)}) collective-permute-start(bf16[160,2048]{1,0:T(8,128)(2,1)S(1)} %constant_dynamic-update-slice_fusion), channel_id=1, source_target_pairs={{0,64},{64,128},{128,192},{192,0},{1,65},{65,129},{129,193},{193,1... | collective-permute-start | bytes 1966088 | tf_op jit(solution)/shard_map/ppermute | solution.py:12
  24.5 15.5 %collective-permute-start.8 = (bf16[160,2048]{1,0:T(8,128)(2,1)S(1)}, bf16[160,2048]{1,0:T(8,128)(2,1)S(1)}, u32[]{:S(2)}, u32[]{:S(2)}) collective-permute-start(bf16[160,2048]{1,0:T(8,128)(2,1)S(1)} %constant_dynamic-update-slice_fusion), channel_id=1, source_target_pairs={{0,192},{64,0},{128,64},{192,128},{1,193},{65,1},{129,65},{193,129... | collective-permute-start | bytes 1966088 | tf_op jit(solution)/shard_map/ppermute | solution.py:12
  26.3 13.8 %collective-permute-start.1 = (bf16[40,2048]{1,0:T(8,128)(2,1)S(1)}, bf16[40,2048]{1,0:T(8,128)(2,1)S(1)}, u32[]{:S(2)}, u32[]{:S(2)}) collective-permute-start(bf16[40,2048]{1,0:T(8,128)(2,1)S(1)} %slice.71), channel_id=1, source_target_pairs={{0,48},{16,0},{32,16},{48,32},{1,49},{17,1},{33,17},{49,33},{2,50}... | collective-permute-start | bytes 491528 | tf_op jit(solution)/shard_map/ppermute | solution.py:12
  26.4 15.8 %copy-start = (bf16[80,2048]{1,0:T(8,128)(2,1)}, bf16[80,2048]{1,0:T(8,128)(2,1)S(1)}, u32[]{:S(2)}) copy-start(bf16[80,2048]{1,0:T(8,128)(2,1)S(1)} %collective-permute-done.4) | copy-start | bytes 983044
  26.4 13.7 %collective-permute-start.3 = (bf16[40,2048]{1,0:T(8,128)(2,1)S(1)}, bf16[40,2048]{1,0:T(8,128)(2,1)S(1)}, u32[]{:S(2)}, u32[]{:S(2)}) collective-permute-start(bf16[40,2048]{1,0:T(8,128)(2,1)S(1)} %slice.72), channel_id=1, source_target_pairs={{0,16},{16,32},{32,48},{48,0},{1,17},{17,33},{33,49},{49,1},{2,18}... | collective-permute-start | bytes 491528 | tf_op jit(solution)/shard_map/ppermute | solution.py:12
  30.7 2.0 %copy-start.5 = (bf16[400,2048]{1,0:T(8,128)(2,1)}, bf16[400,2048]{1,0:T(8,128)(2,1)S(1)}, u32[]{:S(2)}) copy-start(bf16[400,2048]{1,0:T(8,128)(2,1)S(1)} %constant_dynamic-update-slice_fusion.9) | copy-start | bytes 4915204
  32.7 14.8 %collective-permute-start.12 = (f32[400,512]{1,0:T(8,128)}, f32[400,512]{1,0:T(8,128)}, u32[]{:S(2)}, u32[]{:S(2)}) collective-permute-start(f32[400,512]{1,0:T(8,128)} %fusion.13), channel_id=1, source_target_pairs={{0,1},{1,0},{2,3},{3,2},{4,5},{5,4},{6,7},{7,6},{8,9},{9,8},{10,11... | collective-permute-start | bytes 2457608 | tf_op jit(solution)/shard_map/ppermute | solution.py:20
  40.2 2.0 %copy-start.3 = (bf16[400,2048]{1,0:T(8,128)(2,1)}, bf16[400,2048]{1,0:T(8,128)(2,1)S(1)}, u32[]{:S(2)}) copy-start(bf16[400,2048]{1,0:T(8,128)(2,1)S(1)} %constant_dynamic-update-slice_fusion.2) | copy-start | bytes 4915204
  42.2 8.2 %collective-permute-start.10 = (f32[400,512]{1,0:T(8,128)}, f32[400,512]{1,0:T(8,128)}, u32[]{:S(2)}, u32[]{:S(2)}) collective-permute-start(f32[400,512]{1,0:T(8,128)} %fusion.17), channel_id=1, source_target_pairs={{0,1},{1,0},{2,3},{3,2},{4,5},{5,4},{6,7},{7,6},{8,9},{9,8},{10,11... | collective-permute-start | bytes 2457608 | tf_op jit(solution)/shard_map/ppermute | solution.py:20
  42.2 0.9 slice-start
  43.1 4.4 %copy-start.6 = (bf16[400,2048]{1,0:T(8,128)(2,1)S(1)}, bf16[400,2048]{1,0:T(8,128)(2,1)}, u32[]{:S(2)}) copy-start(bf16[400,2048]{1,0:T(8,128)(2,1)} %copy-done.5) | copy-start | bytes 4915204
  44.3 22.2 %collective-permute-start.6 = (bf16[200,2048]{1,0:T(8,128)(2,1)}, bf16[200,2048]{1,0:T(8,128)(2,1)}, u32[]{:S(2)}, u32[]{:S(2)}) collective-permute-start(bf16[200,2048]{1,0:T(8,128)(2,1)} %get-tuple-element.27), channel_id=1, source_target_pairs={{0,64},{64,128},{128,192},{192,0},{1,65},{65,129},{129,193},{193,1... | collective-permute-start | bytes 2457608 | tf_op jit(solution)/shard_map/ppermute | solution.py:12
  45.7 4.7 %copy-start.4 = (bf16[400,2048]{1,0:T(8,128)(2,1)S(1)}, bf16[400,2048]{1,0:T(8,128)(2,1)}, u32[]{:S(2)}) copy-start(bf16[400,2048]{1,0:T(8,128)(2,1)} %copy-done.3) | copy-start | bytes 4915204
  45.7 4.7 %copy-start.8 = (bf16[2048,1024]{0,1:T(8,128)(2,1)S(1)}, bf16[2048,1024]{0,1:T(8,128)(2,1)}, u32[]{:S(2)}) copy-start(bf16[2048,1024]{0,1:T(8,128)(2,1)} %copy-done.7) | copy-start | bytes 12582916
  45.7 26.8 %collective-permute-start.9 = (bf16[200,2048]{1,0:T(8,128)(2,1)S(1)}, bf16[200,2048]{1,0:T(8,128)(2,1)}, u32[]{:S(2)}, u32[]{:S(2)}) collective-permute-start(bf16[200,2048]{1,0:T(8,128)(2,1)S(1)} %get-tuple-element.26), channel_id=1, source_target_pairs={{0,192},{64,0},{128,64},{192,128},{1,193},{65,1},{129,65},{193,129... | collective-permute-start | bytes 2457608 | tf_op jit(solution)/shard_map/ppermute | solution.py:12
  53.9 26.2 %all-to-all-start = ((f32[4,800,128]{2,1,0:T(8,128)}), f32[4,800,128]{2,1,0:T(8,128)S(1)}, u32[]{:S(2)}, u32[]{:S(2)}) async-start(f32[4,800,128]{2,1,0:T(8,128)} %bitcast_bitcast_fusion), calls=%async_computation | async-start | bytes 3276800 | tf_op jit(solution)/shard_map/all_to_all | solution.py:41
  58.4 17.8 %copy-start.9 = (bf16[2048,1024]{0,1:T(8,128)(2,1)S(1)}, bf16[2048,1024]{0,1:T(8,128)(2,1)}, u32[]{:S(2)}) copy-start(bf16[2048,1024]{0,1:T(8,128)(2,1)} %copy-done.7) | copy-start | bytes 12582916
  58.4 16.5 %collective-permute-start.11 = (bf16[80,2048]{1,0:T(8,128)(2,1)S(1)}, bf16[80,2048]{1,0:T(8,128)(2,1)S(1)}, u32[]{:S(2)}, u32[]{:S(2)}) collective-permute-start(bf16[80,2048]{1,0:T(8,128)(2,1)S(1)} %pad_maximum_fusion.3), channel_id=1, source_target_pairs={{0,128},{64,192},{128,0},{192,64},{1,129},{65,193},{129,1},{193,65... | collective-permute-start | bytes 983048 | tf_op jit(solution)/shard_map/ppermute | solution.py:12
  74.9 1.3 %copy-start.1 = (bf16[480,2048]{1,0:T(8,128)(2,1)}, bf16[480,2048]{1,0:T(8,128)(2,1)S(1)}, u32[]{:S(2)}) copy-start(bf16[480,2048]{1,0:T(8,128)(2,1)S(1)} %constant_dynamic-update-slice_fusion.6) | copy-start | bytes 5898244
  80.2 2.7 %collective-permute-start.13 = (f32[480,512]{1,0:T(8,128)S(1)}, f32[480,512]{1,0:T(8,128)S(1)}, u32[]{:S(2)}, u32[]{:S(2)}) collective-permute-start(f32[480,512]{1,0:T(8,128)S(1)} %fusion.15), channel_id=1, source_target_pairs={{0,1},{1,0},{2,3},{3,2},{4,5},{5,4},{6,7},{7,6},{8,9},{9,8},{10,11... | collective-permute-start | bytes 2949128 | tf_op jit(solution)/shard_map/ppermute | solution.py:20
  80.5 11.9 %collective-permute-start.17 = (f32[800,128]{1,0:T(8,128)S(1)}, f32[800,128]{1,0:T(8,128)S(1)}, u32[]{:S(2)}, u32[]{:S(2)}) collective-permute-start(f32[800,128]{1,0:T(8,128)S(1)} %reduce_sum.9), channel_id=1, source_target_pairs={{0,2},{2,0},{1,3},{3,1},{4,6},{6,4},{5,7},{7,5},{8,10},{10,8},{9,1... | collective-permute-start | bytes 1228808 | tf_op jit(solution)/shard_map/ppermute | solution.py:20
  86.3 14.6 %collective-permute-start.14 = (f32[480,128]{1,0:T(8,128)S(1)}, f32[480,128]{1,0:T(8,128)S(1)}, u32[]{:S(2)}, u32[]{:S(2)}) collective-permute-start(f32[480,128]{1,0:T(8,128)S(1)} %get-tuple-element.23), channel_id=1, source_target_pairs={{0,4},{4,8},{8,12},{12,0},{1,5},{5,9},{9,13},{13,1},{2,6},{6,10},{... | collective-permute-start | bytes 737288 | tf_op jit(solution)/shard_map/ppermute | solution.py:12
  87.0 13.9 %collective-permute-start.15 = (f32[480,128]{1,0:T(8,128)S(1)}, f32[480,128]{1,0:T(8,128)S(1)}, u32[]{:S(2)}, u32[]{:S(2)}) collective-permute-start(f32[480,128]{1,0:T(8,128)S(1)} %get-tuple-element.25), channel_id=1, source_target_pairs={{0,12},{4,0},{8,4},{12,8},{1,13},{5,1},{9,5},{13,9},{2,14},{6,2},{... | collective-permute-start | bytes 737288 | tf_op jit(solution)/shard_map/ppermute | solution.py:12
  89.7 11.2 %collective-permute-start.16 = (f32[480,128]{1,0:T(8,128)S(1)}, f32[480,128]{1,0:T(8,128)S(1)}, u32[]{:S(2)}, u32[]{:S(2)}) collective-permute-start(f32[480,128]{1,0:T(8,128)S(1)} %get-tuple-element.24), channel_id=1, source_target_pairs={{0,8},{4,12},{8,0},{12,4},{1,9},{5,13},{9,1},{13,5},{2,10},{6,14},... | collective-permute-start | bytes 737288 | tf_op jit(solution)/shard_map/ppermute | solution.py:12
  101.2 5.0 %collective-permute-start.18 = (f32[240,128]{1,0:T(8,128)S(1)}, f32[240,128]{1,0:T(8,128)S(1)}, u32[]{:S(2)}, u32[]{:S(2)}) collective-permute-start(f32[240,128]{1,0:T(8,128)S(1)} %pad_maximum_fusion.4), channel_id=1, source_target_pairs={{0,2},{2,0},{1,3},{3,1},{4,6},{6,4},{5,7},{7,5},{8,10},{10,8},{9,1... | collective-permute-start | bytes 368648 | tf_op jit(solution)/shard_map/ppermute | solution.py:20
